TPU v7x, 32 devices: a whole 2x2x4 slice. The times are simulated.
32 devices in a mesh: seq: 4 (over z), dp: 8 (over y, x, core).
Axes of the slice: x: 2, y: 2, z: 4, core: 2. Of those that a mesh axis runs over, the one named last changes fastest.
Arguments:
- tokens: bfloat16 [8, 512, 2048], P('dp', 'seq'), may hold values from -6 to 6
- doc_lengths: int32 [8, 12], P('dp'), may hold values from 1 to 256, 512 in all within a row
- qkv_weight: bfloat16 [2048, 6144], P(('seq', 'dp')), may hold values from -0.125 to 0.125
- qv_bias: bfloat16 [4096], P(('seq', 'dp')), may hold values from -3 to 3
- out_weight: bfloat16 [2048, 2048], P(('seq', 'dp')), may hold values from -1.5 to 1.5
- out_bias: bfloat16 [2048], P(('seq', 'dp')), may hold values from -3 to 3
- norm1_gain: bfloat16 [2048], P(('seq', 'dp')), may hold values from 0.5 to 1.5
- norm1_bias: bfloat16 [2048], P(('seq', 'dp')), may hold values from -3 to 3
- in_weight: bfloat16 [2048, 8192], P(('seq', 'dp')), may hold values from -0.125 to 0.125
- in_bias: bfloat16 [8192], P(('seq', 'dp')), may hold values from -3 to 3
- down_weight: bfloat16 [8192, 2048], P(('seq', 'dp')), may hold values from -0.0625 to 0.0625
- down_bias: bfloat16 [2048], P(('seq', 'dp')), may hold values from -3 to 3
- norm2_gain: bfloat16 [2048], P(('seq', 'dp')), may hold values from 0.5 to 1.5
- norm2_bias: bfloat16 [2048], P(('seq', 'dp')), may hold values from -3 to 3
- cotangent: bfloat16 [8, 512, 2048], P('dp', 'seq'), may hold values from -6 to 6
Outputs:
- output: bfloat16 [8, 512, 2048], P('dp', 'seq')
- input_grad: bfloat16 [8, 512, 2048], P('dp', 'seq')
- qkv_weight_grad: float32 [2048, 6144], P(('seq', 'dp'))
- qv_bias_grad: float32 [4096], P(('seq', 'dp'))
- out_weight_grad: float32 [2048, 2048], P(('seq', 'dp'))
- out_bias_grad: float32 [2048], P(('seq', 'dp'))
- norm1_gain_grad: float32 [2048], P(('seq', 'dp'))
- norm1_bias_grad: float32 [2048], P(('seq', 'dp'))
- in_weight_grad: float32 [2048, 8192], P(('seq', 'dp'))
- in_bias_grad: float32 [8192], P(('seq', 'dp'))
- down_weight_grad: float32 [8192, 2048], P(('seq', 'dp'))
- down_bias_grad: float32 [2048], P(('seq', 'dp'))
- norm2_gain_grad: float32 [2048], P(('seq', 'dp'))
- norm2_bias_grad: float32 [2048], P(('seq', 'dp'))
Inputs may be any that keep to these rules, and one draw needn't show every extreme that they name: `doc_lengths`: each row sums to 512, and its largest entry is exactly 256.
All inputs are finite; a program needn't handle non-finite values.
Results may differ from a plain program's by a relative error of at most 0.015.
Values may be sent and summed in bfloat16 or wider, within the bound.
No kernel may reach another device: no remote copies, remote signals or barrier semaphores. Data moves between devices by JAX's collectives and lax.ppermute only.
A program may use at most 384 MiB of HBM per device.

v0:
```python
import jax
import jax.numpy as jnp
from jax import lax
from jax.sharding import PartitionSpec as P

HEAD_DIM = 128


eps_norm = 1e-06


def gather_attention(qkv_weight, qv_bias, out_weight, out_bias, norm1_gain, norm1_bias):
    return (
        lax.all_gather(qkv_weight, ("seq", "dp"), axis=0, tiled=True),
        lax.all_gather(qv_bias, ("seq", "dp"), axis=0, tiled=True),
        lax.all_gather(out_weight, ("seq", "dp"), axis=0, tiled=True),
        lax.all_gather(out_bias, ("seq", "dp"), axis=0, tiled=True),
        lax.all_gather(norm1_gain, ("seq", "dp"), axis=0, tiled=True),
        lax.all_gather(norm1_bias, ("seq", "dp"), axis=0, tiled=True),
    )


def gather_feed(in_weight, in_bias, down_weight, down_bias, norm2_gain, norm2_bias):
    return (
        lax.all_gather(in_weight, ("seq", "dp"), axis=0, tiled=True),
        lax.all_gather(in_bias, ("seq", "dp"), axis=0, tiled=True),
        lax.all_gather(down_weight, ("seq", "dp"), axis=0, tiled=True),
        lax.all_gather(down_bias, ("seq", "dp"), axis=0, tiled=True),
        lax.all_gather(norm2_gain, ("seq", "dp"), axis=0, tiled=True),
        lax.all_gather(norm2_bias, ("seq", "dp"), axis=0, tiled=True),
    )


def normalize(hidden):
    center = hidden - jnp.mean(hidden, axis=-1, keepdims=True)
    spread = jnp.mean(center * center, axis=-1, keepdims=True)
    recip = lax.rsqrt(spread + eps_norm)
    return (center * recip, recip)


def norm_back(grad_out, normed, recip, gain):
    scaled = grad_out * gain
    return recip * (
        scaled
        - jnp.mean(scaled, axis=-1, keepdims=True)
        - normed * jnp.mean(scaled * normed, axis=-1, keepdims=True)
    )


def score_block(queries, key_block):
    scale = queries.shape[2] ** (-0.5)
    return (
        jnp.einsum("thd,khd->htk", queries, key_block, preferred_element_type=jnp.float32) * scale
    )


def probabilities(queries, key_block, seg_query, seg_block, log_total):
    matches = (seg_query[:, None] == seg_block[None, :])[None]
    return jnp.where(matches, jnp.exp(score_block(queries, key_block) - log_total[:, :, None]), 0.0)


def log_totals(queries, seg_query, key_blocks, seg_blocks):
    head_count = queries.shape[1]
    row_count = queries.shape[0]
    initial = (
        jnp.full((head_count, row_count), -1e30, jnp.float32),
        jnp.zeros((head_count, row_count), jnp.float32),
    )

    def advance(carried, pieces):
        key_block, seg_block = pieces

        def compute(running):
            running_max, running_sum = running
            matches = (seg_query[:, None] == seg_block[None, :])[None]
            scores = jnp.where(matches, score_block(queries, key_block), -1e30)
            new_max = jnp.maximum(running_max, jnp.max(scores, axis=2))
            terms = jnp.where(matches, jnp.exp(scores - new_max[:, :, None]), 0.0)
            new_sum = running_sum * jnp.exp(running_max - new_max) + jnp.sum(terms, axis=2)
            return (new_max, new_sum)

        return (compute(carried), None)

    (final_max, final_sum), unused_out = lax.scan(advance, initial, (key_blocks, seg_blocks))
    return final_max + jnp.log(final_sum)


def attend(queries, seg_query, key_blocks, value_blocks, seg_blocks, log_total):
    initial = jnp.zeros(queries.shape, jnp.float32)

    def advance(carried, pieces):
        key_block, value_block, seg_block = pieces

        def compute(accum):
            probs_low = probabilities(queries, key_block, seg_query, seg_block, log_total).astype(
                jnp.bfloat16
            )
            return accum + jnp.einsum(
                "htk,khd->thd", probs_low, value_block, preferred_element_type=jnp.float32
            )

        return (compute(carried), None)

    result, unused_out = lax.scan(advance, initial, (key_blocks, value_blocks, seg_blocks))
    return result


def prob_products(queries, grad_mixed, seg_query, key_blocks, value_blocks, seg_blocks, log_total):
    initial = jnp.zeros(log_total.shape, jnp.float32)

    def advance(carried, pieces):
        key_block, value_block, seg_block = pieces

        def compute(accum):
            probs = probabilities(queries, key_block, seg_query, seg_block, log_total)
            grad_probs = jnp.einsum(
                "thd,khd->htk", grad_mixed, value_block, preferred_element_type=jnp.float32
            )
            return accum + jnp.sum(probs * grad_probs, axis=2)

        return (compute(carried), None)

    result, unused_out = lax.scan(advance, initial, (key_blocks, value_blocks, seg_blocks))
    return result


def attend_back(
    queries, grad_mixed, seg_query, key_blocks, value_blocks, seg_blocks, log_total, products
):
    scale = queries.shape[2] ** (-0.5)
    initial = jnp.zeros(queries.shape, jnp.float32)
    pair_width = 2 * queries.shape[1] * queries.shape[2]

    def advance(carried, pieces):
        key_block, value_block, seg_block = pieces
        block_rows = key_block.shape[0]

        def compute(grad_query):
            probs = probabilities(queries, key_block, seg_query, seg_block, log_total)
            grad_probs = jnp.einsum(
                "thd,khd->htk", grad_mixed, value_block, preferred_element_type=jnp.float32
            )
            grad_scores = (probs * (grad_probs - products[:, :, None])).astype(jnp.bfloat16)
            new_grad = (
                grad_query
                + jnp.einsum(
                    "htk,khd->thd", grad_scores, key_block, preferred_element_type=jnp.float32
                )
                * scale
            )
            key_grad = (
                jnp.einsum("htk,thd->khd", grad_scores, queries, preferred_element_type=jnp.float32)
                * scale
            )
            value_grad = jnp.einsum(
                "htk,thd->khd",
                probs.astype(jnp.bfloat16),
                grad_mixed,
                preferred_element_type=jnp.float32,
            )
            return (
                new_grad,
                jnp.concatenate(
                    [key_grad.reshape(block_rows, -1), value_grad.reshape(block_rows, -1)], axis=1
                ),
            )

        return compute(carried)

    grad_query, pair_grads = lax.scan(advance, initial, (key_blocks, value_blocks, seg_blocks))
    return (grad_query, pair_grads.reshape(-1, pair_width))


def per_device(
    tokens,
    doc_lengths,
    qkv_weight,
    qv_bias,
    out_weight,
    out_bias,
    norm1_gain,
    norm1_bias,
    in_weight,
    in_bias,
    down_weight,
    down_bias,
    norm2_gain,
    norm2_bias,
    cotangent,
):
    row_count = tokens.shape[1]
    model_width = tokens.shape[2]
    head_size = HEAD_DIM
    head_count = model_width // head_size
    seq_length = row_count * lax.axis_size("seq")
    key_rows = min(512, seq_length)
    block_count = seq_length // key_rows
    tok_rows = tokens[0]
    tok_float = tok_rows.astype(jnp.float32)
    ends = jnp.cumsum(doc_lengths[0])
    places = jnp.arange(seq_length, dtype=jnp.int32)
    seg_all = jnp.sum((places[:, None] >= ends[None, :]).astype(jnp.int32), axis=1)
    seg_query = lax.dynamic_slice_in_dim(seg_all, lax.axis_index("seq") * row_count, row_count)
    seg_blocks = seg_all.reshape(block_count, key_rows)
    attn_params = gather_attention(
        qkv_weight, qv_bias, out_weight, out_bias, norm1_gain, norm1_bias
    )
    qkv_full, qv_full, out_full, out_b_full, gain_one, shift_one = attn_params
    zero_bias = jnp.zeros((model_width,), jnp.float32)
    qv_float = qv_full.astype(jnp.float32)
    full_bias = jnp.concatenate([qv_float[:model_width], zero_bias, qv_float[model_width:]])
    qkv_low = (jnp.dot(tok_rows, qkv_full, preferred_element_type=jnp.float32) + full_bias).astype(
        jnp.bfloat16
    )
    queries = qkv_low[:, :model_width].reshape(row_count, head_count, head_size)
    pair_all = lax.all_gather(qkv_low[:, model_width:], "seq", axis=0, tiled=True)
    key_blocks = pair_all[:, :model_width].reshape(block_count, key_rows, head_count, head_size)
    value_blocks = pair_all[:, model_width:].reshape(block_count, key_rows, head_count, head_size)
    log_total = log_totals(queries, seg_query, key_blocks, seg_blocks)
    mixed = attend(queries, seg_query, key_blocks, value_blocks, seg_blocks, log_total)
    mixed_low = mixed.reshape(row_count, model_width).astype(jnp.bfloat16)
    attn = jnp.dot(mixed_low, out_full, preferred_element_type=jnp.float32) + out_b_full.astype(
        jnp.float32
    )
    normed_one, recip_one = normalize(tok_float + attn)
    gain_one_f = gain_one.astype(jnp.float32)
    first = normed_one * gain_one_f + shift_one.astype(jnp.float32)
    first_low = first.astype(jnp.bfloat16)
    feed_params = gather_feed(in_weight, in_bias, down_weight, down_bias, norm2_gain, norm2_bias)
    in_full, in_b_full, down_full, down_b_full, gain_two, shift_two = feed_params
    pre = jnp.dot(first_low, in_full, preferred_element_type=jnp.float32) + in_b_full.astype(
        jnp.float32
    )
    act_low = jax.nn.gelu(pre, approximate=True).astype(jnp.bfloat16)
    ffn = jnp.dot(act_low, down_full, preferred_element_type=jnp.float32) + down_b_full.astype(
        jnp.float32
    )
    normed_two, recip_two = normalize(first + ffn)
    gain_two_f = gain_two.astype(jnp.float32)
    result = (normed_two * gain_two_f + shift_two.astype(jnp.float32)).astype(jnp.bfloat16)
    in_full, in_b_full, down_full, down_b_full, gain_two, shift_two = gather_feed(
        in_weight, in_bias, down_weight, down_bias, norm2_gain, norm2_bias
    )
    grad_out = cotangent[0].astype(jnp.float32)
    shift_two_grad = jnp.sum(grad_out, axis=0)
    gain_two_grad = jnp.sum(grad_out * normed_two, axis=0)
    grad_h2 = norm_back(grad_out, normed_two, recip_two, gain_two.astype(jnp.float32))
    grad_ffn = grad_h2.astype(jnp.bfloat16)
    down_b_grad = jnp.sum(grad_ffn.astype(jnp.float32), axis=0)
    down_w_grad = jnp.einsum("tf,td->fd", act_low, grad_ffn, preferred_element_type=jnp.float32)
    grad_act = jnp.einsum("td,fd->tf", grad_ffn, down_full, preferred_element_type=jnp.float32)
    unused_value, gelu_pull = jax.vjp(lambda inner: jax.nn.gelu(inner, approximate=True), pre)
    grad_pre = gelu_pull(grad_act)[0].astype(jnp.bfloat16)
    in_b_grad = jnp.sum(grad_pre.astype(jnp.float32), axis=0)
    in_w_grad = jnp.einsum("td,tf->df", first_low, grad_pre, preferred_element_type=jnp.float32)
    grad_first = grad_h2 + jnp.einsum(
        "tf,df->td", grad_pre, in_full, preferred_element_type=jnp.float32
    )
    feed_grads = (
        lax.psum_scatter(in_w_grad, ("seq", "dp"), scatter_dimension=0, tiled=True),
        lax.psum_scatter(in_b_grad, ("seq", "dp"), scatter_dimension=0, tiled=True),
        lax.psum_scatter(down_w_grad, ("seq", "dp"), scatter_dimension=0, tiled=True),
        lax.psum_scatter(down_b_grad, ("seq", "dp"), scatter_dimension=0, tiled=True),
        lax.psum_scatter(gain_two_grad, ("seq", "dp"), scatter_dimension=0, tiled=True),
        lax.psum_scatter(shift_two_grad, ("seq", "dp"), scatter_dimension=0, tiled=True),
    )
    qkv_full, qv_full, out_full, out_b_full, gain_one, shift_one = gather_attention(
        qkv_weight, qv_bias, out_weight, out_bias, norm1_gain, norm1_bias
    )
    shift_one_grad = jnp.sum(grad_first, axis=0)
    gain_one_grad = jnp.sum(grad_first * normed_one, axis=0)
    grad_h1 = norm_back(grad_first, normed_one, recip_one, gain_one.astype(jnp.float32))
    grad_attn = grad_h1.astype(jnp.bfloat16)
    out_b_grad = jnp.sum(grad_attn.astype(jnp.float32), axis=0)
    out_w_grad = jnp.einsum("td,te->de", mixed_low, grad_attn, preferred_element_type=jnp.float32)
    grad_mixed = jnp.einsum(
        "te,de->td", grad_attn, out_full, preferred_element_type=jnp.float32
    ).astype(jnp.bfloat16)
    grad_mixed = grad_mixed.reshape(row_count, head_count, head_size)
    products = prob_products(
        queries, grad_mixed, seg_query, key_blocks, value_blocks, seg_blocks, log_total
    )
    grad_query, pair_grads = attend_back(
        queries, grad_mixed, seg_query, key_blocks, value_blocks, seg_blocks, log_total, products
    )
    pair_mine = lax.psum_scatter(
        pair_grads.astype(jnp.bfloat16), "seq", scatter_dimension=0, tiled=True
    ).astype(jnp.float32)
    grad_qkv = jnp.concatenate(
        [grad_query.reshape(row_count, model_width), pair_mine], axis=1
    ).astype(jnp.bfloat16)
    column_sums = jnp.sum(grad_qkv.astype(jnp.float32), axis=0)
    qv_grad = jnp.concatenate([column_sums[:model_width], column_sums[2 * model_width :]])
    qkv_w_grad = jnp.einsum("td,te->de", tok_rows, grad_qkv, preferred_element_type=jnp.float32)
    input_grad = (
        grad_h1 + jnp.einsum("te,de->td", grad_qkv, qkv_full, preferred_element_type=jnp.float32)
    ).astype(jnp.bfloat16)
    attn_grads = (
        lax.psum_scatter(qkv_w_grad, ("seq", "dp"), scatter_dimension=0, tiled=True),
        lax.psum_scatter(qv_grad, ("seq", "dp"), scatter_dimension=0, tiled=True),
        lax.psum_scatter(out_w_grad, ("seq", "dp"), scatter_dimension=0, tiled=True),
        lax.psum_scatter(out_b_grad, ("seq", "dp"), scatter_dimension=0, tiled=True),
        lax.psum_scatter(gain_one_grad, ("seq", "dp"), scatter_dimension=0, tiled=True),
        lax.psum_scatter(shift_one_grad, ("seq", "dp"), scatter_dimension=0, tiled=True),
    )
    return (
        result[None],
        input_grad[None],
        attn_grads[0],
        attn_grads[1],
        attn_grads[2],
        attn_grads[3],
        attn_grads[4],
        attn_grads[5],
        feed_grads[0],
        feed_grads[1],
        feed_grads[2],
        feed_grads[3],
        feed_grads[4],
        feed_grads[5],
    )


def solution(mesh):
    placed = (
        P("dp", "seq", None),
        P("dp", None),
        P(("seq", "dp"), None),
        P(("seq", "dp")),
        P(("seq", "dp"), None),
        P(("seq", "dp")),
        P(("seq", "dp")),
        P(("seq", "dp")),
        P(("seq", "dp"), None),
        P(("seq", "dp")),
        P(("seq", "dp"), None),
        P(("seq", "dp")),
        P(("seq", "dp")),
        P(("seq", "dp")),
        P("dp", "seq", None),
    )
    return jax.shard_map(
        per_device,
        mesh=mesh,
        in_specs=placed,
        out_specs=(
            P("dp", "seq", None),
            P("dp", "seq", None),
            P(("seq", "dp"), None),
            P(("seq", "dp")),
            P(("seq", "dp"), None),
            P(("seq", "dp")),
            P(("seq", "dp")),
            P(("seq", "dp")),
            P(("seq", "dp"), None),
            P(("seq", "dp")),
            P(("seq", "dp"), None),
            P(("seq", "dp")),
            P(("seq", "dp")),
            P(("seq", "dp")),
        ),
        check_vma=False,
    )
```

profile of v0, /device:TPU:0, one launch (start us, length us, event | category | flops | bytes accessed | tf_op | source)
XLA Modules:
  0.0 3076.2 jit_solution(15687262694008455717)
XLA Ops:
  8.0 43.4 %all-gather = bf16[32,1,128]{2,1,0:T(2,128)(2,1)S(1)} all-gather(bf16[1,1,128]{2,1,0:T(2,128)(2,1)} %bitcast.103), channel_id=1, replica_groups=mesh['seq'=4,'dp'=8] {'seq','dp'}, dimensions={0}, use_global_device_ids=true | all-gather | bytes 8448 | tf_op jit(solution)/shard_map/all_gather | solution.py:15
  51.4 116.9 %all-gather.8.cloned.1.call-done = bf16[2048,6144]{1,0:T(8,128)(2,1)} async-done(((bf16[64,6144]{1,0:T(8,128)(2,1)}), bf16[2048,6144]{1,0:T(8,128)(2,1)}) %all-gather.8.cloned.1.call-update) | async-done | bytes 25165840 | tf_op jit(solution)/shard_map/all_gather | solution.py:14
  168.3 11.8 fusion
  184.7 42.2 %all-reduce.15 = (bf16[2048]{0:T(1024)(128)(2,1)S(1)}, bf16[2048]{0:T(1024)(128)(2,1)S(1)}, bf16[2048]{0:T(1024)(128)(2,1)S(1)}, bf16[2048]{0:T(1024)(128)(2,1)S...) all-reduce(bf16[2048]{0:T(1024)(128)(2,1)S(1)} %dynamic-update-slic, ...), channel_id=1, replica_groups=mesh['seq'=4,'dp'=8] {'seq','dp'}, use_global_device_ids=true, to_apply=%add | all-reduce | flops 12288 | bytes 49152
  226.9 44.4 %all-gather.1 = bf16[32,1,256]{2,1,0:T(2,128)(2,1)S(1)} all-gather(bf16[1,1,256]{2,1,0:T(2,128)(2,1)S(1)} %reshape.193), channel_id=1, replica_groups=mesh['seq'=4,'dp'=8] {'seq','dp'}, dimensions={0}, use_global_device_ids=true | all-gather | bytes 16896 | tf_op jit(solution)/shard_map/all_gather | solution.py:26
  272.2 5.0 fusion.57
  277.2 2.9 copy.61
  281.1 1.3 select_reduce_fusion
  283.3 1.7 fusion.25
  285.0 55.2 %all-gather.12.cloned.1.call-done = bf16[2048,2048]{1,0:T(8,128)(2,1)} async-done(((bf16[64,2048]{1,0:T(8,128)(2,1)}), bf16[2048,2048]{1,0:T(8,128)(2,1)}) %all-gather.12.cloned.1.call-update) | async-done | bytes 8388624 | tf_op jit(solution)/shard_map/all_gather | solution.py:16
  340.2 4.7 fusion.60
  345.3 191.1 %all-gather.14.cloned.1.call-done = bf16[2048,8192]{1,0:T(8,128)(2,1)} async-done(((bf16[64,8192]{1,0:T(8,128)(2,1)}), bf16[2048,8192]{1,0:T(8,128)(2,1)}) %all-gather.14.cloned.1.call-update) | async-done | bytes 33554448 | tf_op jit(solution)/shard_map/all_gather | solution.py:25
  536.4 17.9 convolution_add_fusion
  554.2 177.8 %all-gather.16.cloned.1.call-done = bf16[8192,2048]{1,0:T(8,128)(2,1)} async-done(((bf16[256,2048]{1,0:T(8,128)(2,1)}), bf16[8192,2048]{1,0:T(8,128)(2,1)}) %all-gather.16.cloned.1.call-update) | async-done | bytes 33554448 | tf_op jit(solution)/shard_map/all_gather | solution.py:27
  732.0 15.1 fusion.61
  748.4 2.2 convert_reduce_fusion.3
  750.7 18.9 convert_reduce_fusion
  769.5 19.1 multiply_reduce_fusion.1
  788.6 2.2 convert_reduce_fusion.4
  791.8 7.1 convolution_convert_fusion
  798.9 2.2 copy.62
  801.1 3.6 convolution_convert_fusion.1
  804.8 2.0 multiply_reduce_fusion
  806.8 1.5 multiply_convert_fusion.1
  809.0 2.2 pad_maximum_fusion
  811.2 6.4 copy.56
  817.7 1.7 convert_reduce_fusion.2
  819.4 3.1 fusion.24
  822.5 70.2 %reduce-scatter.16.cloned.1.call-done = bf16[128,4096]{1,0:T(8,128)(2,1)} async-done(((bf16[512,4096]{1,0:T(8,128)(2,1)}), bf16[128,4096]{1,0:T(8,128)(2,1)}) %reduce-scatter.16.cloned.1.call-update) | async-done | bytes 1048592
  892.7 1.6 copy.57
  894.4 1.5 convert_reduce_fusion.1
  896.6 9.1 fusion.40
  905.7 20.9 convolution_bitcast_fusion
  926.7 48.9 %copy.58 = f32[2048,6144]{1,0:T(8,128)} copy(f32[2048,6144]{0,1:T(8,128)} %convolution_bitcast_fusion) | data formatting | bytes 100663296
  975.7 24.8 fusion.53
  1001.8 25.7 fusion.43
  1028.5 16.6 fusion.11
  1045.0 1.3 dynamic-slice.2
  1046.3 1.3 dynamic-slice.3
  1047.6 1.3 dynamic-slice.4
  1048.8 1.3 dynamic-slice.6
  1051.3 1.3 dynamic-slice.8
  1052.6 1.3 dynamic-slice.1
  1053.9 1.3 dynamic-slice.5
  1055.2 156.3 %reduce-scatter.10.cloned.1.call-done = f32[64,2048]{1,0:T(8,128)} async-done(((f32[2048,2048]{1,0:T(8,128)}), f32[64,2048]{1,0:T(8,128)}) %reduce-scatter.10.cloned.1.call-update) | async-done | bytes 524304 | tf_op jit(solution)/shard_map/reduce_scatter | solution.py:301
  1211.5 440.2 %reduce-scatter.18.cloned.1.call-done = f32[64,6144]{1,0:T(8,128)} async-done(((f32[2048,6144]{1,0:T(8,128)}), f32[64,6144]{1,0:T(8,128)}) %reduce-scatter.18.cloned.1.call-update) | async-done | bytes 1572880
  1651.6 704.4 %reduce-scatter.12.cloned.1.call-done = f32[64,8192]{1,0:T(8,128)} async-done(((f32[2048,8192]{1,0:T(8,128)}), f32[64,8192]{1,0:T(8,128)}) %reduce-scatter.12.cloned.1.call-update) | async-done | bytes 2097168 | tf_op jit(solution)/shard_map/reduce_scatter | solution.py:260
  2356.0 713.2 %reduce-scatter.14.cloned.1.call-done = f32[256,2048]{1,0:T(8,128)} async-done(((f32[8192,2048]{1,0:T(8,128)}), f32[256,2048]{1,0:T(8,128)}) %reduce-scatter.14.cloned.1.call-update) | async-done | bytes 2097168 | tf_op jit(solution)/shard_map/reduce_scatter | solution.py:262
  (119 shorter events, 15.7 us)
Async XLA Ops:
  7.2 161.1 %all-gather.8.cloned.1.call-start = ((), (), s32[]{:S(2)}) async-start(), calls=%async_computation.5 | async-start | bytes 25952256 | tf_op jit(solution)/shard_map/all_gather | solution.py:14
  7.9 264.3 %all-gather.10.cloned.1.call-start = ((), (), s32[]{:S(2)}) async-start(), calls=%async_computation.6 | async-start | bytes 5242880 | tf_op jit(solution)/shard_map/all_gather | solution.py:216
  180.1 3.1 copy-start.16
  180.1 3.4 copy-start.17
  180.1 3.6 copy-start.18
  180.1 3.9 copy-start.19
  180.1 4.1 copy-start.20
  180.1 4.3 copy-start.21
  180.1 46.8 %copy-start.22 = (bf16[256]{0:T(256)(128)(2,1)S(1)}, bf16[256]{0:T(256)(128)(2,1)}, u32[]{:S(2)}) copy-start(bf16[256]{0:T(256)(128)(2,1)} %param.24) | copy-start | bytes 1540
  180.2 91.2 %copy-start.23 = (s32[1,12]{1,0:T(1,128)S(1)}, s32[1,12]{1,0:T(1,128)}, u32[]{:S(2)}) copy-start(s32[1,12]{1,0:T(1,128)} %param.16) | copy-start | bytes 148
  181.2 159.0 %all-gather.12.cloned.1.call-start = ((), (), s32[]{:S(2)}) async-start(), calls=%async_computation.7 | async-start | bytes 8650752 | tf_op jit(solution)/shard_map/all_gather | solution.py:16
  182.0 354.4 %all-gather.14.cloned.1.call-start = ((), (), s32[]{:S(2)}) async-start(), calls=%async_computation.8 | async-start | bytes 34603008 | tf_op jit(solution)/shard_map/all_gather | solution.py:25
  182.5 549.5 %all-gather.16.cloned.1.call-start = ((), (), s32[]{:S(2)}) async-start(), calls=%async_computation.9 | async-start | bytes 34603008 | tf_op jit(solution)/shard_map/all_gather | solution.py:27
  183.1 709.6 %reduce-scatter.16.cloned.1.call-start = ((), (), s32[]{:S(2)}) async-start(), calls=%async_computation.13 | async-start | bytes 5242880
  272.2 7.9 copy-start.12
  280.1 2.4 copy-start.2
  280.1 3.2 copy-start.8
  281.1 2.0 copy-start
  283.3 56.9 %copy-start.10 = (bf16[1,128,2048]{2,1,0:T(8,128)(2,1)S(1)}, bf16[1,128,2048]{2,1,0:T(8,128)(2,1)}, u32[]{:S(2)}) copy-start(bf16[1,128,2048]{2,1,0:T(8,128)(2,1)} %param.15) | copy-start | bytes 1572868
  285.0 60.0 %copy-start.15 = (bf16[16,128,128]{2,1,0:T(8,128)(2,1)}, bf16[16,128,128]{2,1,0:T(8,128)(2,1)S(1)}, u32[]{:S(2)}) copy-start(bf16[16,128,128]{2,1,0:T(8,128)(2,1)S(1)} %fusion.25) | copy-start | bytes 1572868
  554.2 193.2 %copy-start.11 = (bf16[1,128,2048]{2,1,0:T(8,128)(2,1)S(1)}, bf16[1,128,2048]{2,1,0:T(8,128)(2,1)}, u32[]{:S(2)}) copy-start(bf16[1,128,2048]{2,1,0:T(8,128)(2,1)} %param.29) | copy-start | bytes 1572868
  769.5 19.1 copy-start.5
  790.9 1.0 copy-start.3
  798.9 5.8 copy-start.9
  801.1 3.6 copy-start.1
  801.1 3.7 copy-start.14
  806.8 1.5 copy-start.13
  817.6 227.4 %all-reduce.18.cloned.1.call-start = ((), (), s32[]{:S(2)}) async-start(), calls=%async_computation.15 | async-start | bytes 196608
  822.5 74.1 %copy-start.4 = (f32[128,2048]{1,0:T(8,128)S(1)}, f32[128,2048]{1,0:T(8,128)}, u32[]{:S(2)}) copy-start(f32[128,2048]{1,0:T(8,128)} %copy-done.3) | copy-start | bytes 3145732
  896.5 314.9 %reduce-scatter.10.cloned.1.call-start = ((), (), s32[]{:S(2)}) async-start(), calls=%async_computation.10 | async-start | bytes 17301504 | tf_op jit(solution)/shard_map/reduce_scatter | solution.py:301
  905.7 746.0 %reduce-scatter.18.cloned.1.call-start = ((), (), s32[]{:S(2)}) async-start(), calls=%async_computation.14 | async-start | bytes 51904512
  975.6 1380.4 %reduce-scatter.12.cloned.1.call-start = ((), (), s32[]{:S(2)}) async-start(), calls=%async_computation.11 | async-start | bytes 69206016 | tf_op jit(solution)/shard_map/reduce_scatter | solution.py:260
  1000.5 1.2 copy-start.6
  1000.5 2068.7 %reduce-scatter.14.cloned.1.call-start = ((), (), s32[]{:S(2)}) async-start(), calls=%async_computation.12 | async-start | bytes 69206016 | tf_op jit(solution)/shard_map/reduce_scatter | solution.py:262
  1027.4 1.0 copy-start.7
Sparse Core Ops, SparseCore 0:
  10.9 157.3 all-gather.7
  181.4 80.0 all-gather.9
  264.3 75.8 all-gather.11
  343.0 193.3 all-gather.13
  539.1 192.9 all-gather.15
  817.8 74.9 reduce-scatter.15
  900.3 124.3 all-reduce.17
  1027.6 183.8 reduce-scatter.9
  1218.5 433.1 reduce-scatter.17
  1654.4 701.5 reduce-scatter.11
  2358.9 710.2 reduce-scatter.13
where the time goes:
time: 3090 us; the launch traced here: 3080 us
  waiting for transfers between devices  2630 us (85%)
  matrix products  204 us (7%)
  blocking collectives  130 us (4%)
  local copies, waits for them, and re-layouts  84.3 us (3%)
    reduce_scatter x1, waiting for transfers between devices, per_device(): lax.psum_scatter(down_w_grad, ('seq', 'dp'), scatter_dimension=0, tiled=T...  713 us
    reduce_scatter x1, waiting for transfers between devices, per_device(): lax.psum_scatter(in_w_grad, ('seq', 'dp'), scatter_dimension=0, tiled=True)  704 us
    unnamed x14, waiting for transfers between devices  513 us
    all_gather x1, waiting for transfers between devices, gather_feed(): lax.all_gather(in_weight, ('seq', 'dp'), axis=0, tiled=True)  191 us
    all_gather x1, waiting for transfers between devices, gather_feed(): lax.all_gather(down_weight, ('seq', 'dp'), axis=0, tiled=True)  178 us
    reduce_scatter x1, waiting for transfers between devices, per_device(): lax.psum_scatter(out_w_grad, ('seq', 'dp'), scatter_dimension=0, tiled=True)  156 us
    all_gather x1, waiting for transfers between devices, gather_attention(): lax.all_gather(qkv_weight, ('seq', 'dp'), axis=0, tiled=True)  117 us
    unnamed x72, local copies, waits for them, and re-layouts  72.8 us
  transfers between devices with their start and end apart: 11, of which 9 were waited for; matrix products, arithmetic and copies ran while one was open for 6% of the time, Pallas kernels for 0%

commit v1 on v0

v1 whole, which is shorter than its diff:
```python
import functools

import jax
import jax.numpy as jnp
from jax import lax
from jax.experimental import pallas as pl
from jax.experimental.pallas import tpu as pltpu
from jax.sharding import PartitionSpec as P

HEAD_DIM = 128
eps_norm = 1e-06
f32 = jnp.float32
bf16 = jnp.bfloat16
ALL = ("seq", "dp")


def shift(value, step):
    n = lax.axis_size("seq")
    return lax.ppermute(value, "seq", [(i, (i + step) % n) for i in range(n)])


def gather_seq(rows):
    n = lax.axis_size("seq")
    return jnp.concatenate([rows] + [shift(rows, k) for k in range(1, n)], axis=0)


def scatter_seq(partial):
    n = lax.axis_size("seq")
    count = partial.shape[0] // n
    total = partial[:count]
    for k in range(1, n):
        block = partial[k * count : (k + 1) * count].astype(bf16)
        total = total + shift(block, -k).astype(f32)
    return total


def normalize(hidden):
    center = hidden - jnp.mean(hidden, axis=-1, keepdims=True)
    spread = jnp.mean(center * center, axis=-1, keepdims=True)
    recip = lax.rsqrt(spread + eps_norm)
    return (center * recip, recip)


def norm_back(grad_out, normed, recip, gain):
    scaled = grad_out * gain
    return recip * (
        scaled
        - jnp.mean(scaled, axis=-1, keepdims=True)
        - normed * jnp.mean(scaled * normed, axis=-1, keepdims=True)
    )


def dot_nn(a, b):
    return lax.dot_general(a, b, (((1,), (0,)), ((), ())), preferred_element_type=f32)


def dot_nt(a, b):
    return lax.dot_general(a, b, (((1,), (1,)), ((), ())), preferred_element_type=f32)


def dot_tn(a, b):
    return lax.dot_general(a, b, (((0,), (0,)), ((), ())), preferred_element_type=f32)


def softmax_of(q, k, seg_col, seg_row):
    scores = dot_nt(q, k) * HEAD_DIM ** (-0.5)
    scores = jnp.where(seg_col == seg_row, scores, -1e30)
    terms = jnp.exp(scores - jnp.max(scores, axis=1, keepdims=True))
    return terms / jnp.sum(terms, axis=1, keepdims=True)


def attend_kernel(seg_col, seg_row, q, k, v, mixed):
    probs = softmax_of(q[...], k[...], seg_col[...], seg_row[...])
    mixed[...] = dot_nn(probs.astype(bf16), v[...]).astype(bf16)


def attend_back_kernel(seg_col, seg_row, q, k, v, gm, grad):
    heads = pl.num_programs(0)
    head = pl.program_id(0)
    probs = softmax_of(q[...], k[...], seg_col[...], seg_row[...])
    grad_probs = dot_nt(gm[...], v[...])
    products = jnp.sum(probs * grad_probs, axis=1, keepdims=True)
    grad_scores = (probs * (grad_probs - products)).astype(bf16)
    scale = HEAD_DIM ** (-0.5)

    def put(part, value):
        start = pl.multiple_of((part * heads + head) * HEAD_DIM, HEAD_DIM)
        grad[:, pl.ds(start, HEAD_DIM)] = value.astype(bf16)

    put(0, dot_nn(grad_scores, k[...]) * scale)
    put(1, dot_tn(grad_scores, q[...]) * scale)
    put(2, dot_tn(probs.astype(bf16), gm[...]))


def head_spec(rows, offset):
    return pl.BlockSpec((rows, HEAD_DIM), lambda h: (0, offset + h))


def attend(qkv, seg):
    rows, width = qkv.shape
    heads = width // (3 * HEAD_DIM)
    return pl.pallas_call(
        attend_kernel,
        grid=(heads,),
        in_specs=[
            pl.BlockSpec((rows, 1), lambda h: (0, 0)),
            pl.BlockSpec((1, rows), lambda h: (0, 0)),
            head_spec(rows, 0),
            head_spec(rows, heads),
            head_spec(rows, 2 * heads),
        ],
        out_specs=head_spec(rows, 0),
        out_shape=jax.ShapeDtypeStruct((rows, width // 3), bf16),
        compiler_params=pltpu.CompilerParams(vmem_limit_bytes=48 << 20),
        name="attend",
    )(seg[:, None], seg[None, :], qkv, qkv, qkv)


def attend_back(qkv, grad_mixed, seg):
    rows, width = qkv.shape
    heads = width // (3 * HEAD_DIM)
    return pl.pallas_call(
        attend_back_kernel,
        grid=(heads,),
        in_specs=[
            pl.BlockSpec((rows, 1), lambda h: (0, 0)),
            pl.BlockSpec((1, rows), lambda h: (0, 0)),
            head_spec(rows, 0),
            head_spec(rows, heads),
            head_spec(rows, 2 * heads),
            head_spec(rows, 0),
        ],
        out_specs=pl.BlockSpec((rows, width), lambda h: (0, 0)),
        out_shape=jax.ShapeDtypeStruct((rows, width), bf16),
        compiler_params=pltpu.CompilerParams(vmem_limit_bytes=48 << 20),
        name="attend_back",
    )(seg[:, None], seg[None, :], qkv, qkv, qkv, grad_mixed)


def columns_to_owner(shard, parts):
    n = lax.axis_size("seq")
    rows, width = shard.shape
    pieces = shard.reshape(rows, parts, n, width // (parts * n))
    pieces = pieces.transpose(2, 0, 1, 3).reshape(n, rows, width // n)
    moved = lax.all_to_all(pieces, "seq", 0, 0)
    full = lax.all_gather(moved, "dp", axis=1, tiled=True)
    return full.reshape(-1, width // n)


def columns_back(grad, parts):
    n = lax.axis_size("seq")
    width = grad.shape[1]
    stacked = grad.astype(bf16).reshape(n, -1, width)
    mine = lax.psum_scatter(stacked, "dp", scatter_dimension=1, tiled=True)
    moved = lax.all_to_all(mine, "seq", 0, 0)
    rows = moved.shape[1]
    moved = moved.reshape(n, rows, parts, width // parts).transpose(1, 2, 0, 3)
    return moved.reshape(rows, n * width).astype(f32)


def rows_back(grad):
    return lax.psum_scatter(grad.astype(bf16), "dp", scatter_dimension=0, tiled=True).astype(f32)


def all_small(vectors):
    count = lax.axis_size("seq") * lax.axis_size("dp")
    packed = jnp.concatenate(vectors)
    table = lax.all_to_all(jnp.broadcast_to(packed[None], (count, packed.shape[0])), ALL, 0, 0)
    out = []
    start = 0
    for vector in vectors:
        size = vector.shape[0]
        out.append(table[:, start : start + size].reshape(-1).astype(f32))
        start += size
    return out


def scatter_small(vectors):
    count = lax.axis_size("seq") * lax.axis_size("dp")
    packed = jnp.concatenate([v.reshape(count, -1) for v in vectors], axis=1)
    mine = jnp.sum(lax.all_to_all(packed, ALL, 0, 0), axis=0)
    out = []
    start = 0
    for vector in vectors:
        size = vector.shape[0] // count
        out.append(mine[start : start + size])
        start += size
    return out


def gelu_parts(v):
    c = 0.7978845608028654
    t = jnp.tanh(c * (v + 0.044715 * v * v * v))
    value = 0.5 * v * (1.0 + t)
    slope = 0.5 * (1.0 + t) + 0.5 * v * (1.0 - t * t) * c * (1.0 + 3 * 0.044715 * v * v)
    return value, slope


def per_device(
    tokens,
    doc_lengths,
    qkv_weight,
    qv_bias,
    out_weight,
    out_bias,
    norm1_gain,
    norm1_bias,
    in_weight,
    in_bias,
    down_weight,
    down_bias,
    norm2_gain,
    norm2_bias,
    cotangent,
):
    n = lax.axis_size("seq")
    s = lax.axis_index("seq")
    rows = tokens.shape[1]
    width = tokens.shape[2]
    part = width // n
    tok_rows = tokens[0]
    ends = jnp.cumsum(doc_lengths[0])
    steps = jnp.arange(n * rows, dtype=jnp.int32)
    places = jnp.remainder(s - steps // rows, n) * rows + steps % rows
    seg = jnp.sum((places[:, None] >= ends[None, :]).astype(jnp.int32), axis=1)

    small = all_small(
        [qv_bias, out_bias, norm1_gain, norm1_bias, in_bias, down_bias, norm2_gain, norm2_bias]
    )
    qv_full, out_b, gain_one, shift_one, in_b, down_b, gain_two, shift_two = small
    qkv_w = columns_to_owner(qkv_weight, 3)
    out_w = lax.all_gather(out_weight, "dp", axis=0, tiled=True)
    in_w = columns_to_owner(in_weight, 1)
    down_w = lax.all_gather(down_weight, "dp", axis=0, tiled=True)

    tok_full = gather_seq(tok_rows)
    q_bias = lax.dynamic_slice_in_dim(qv_full, s * part, part)
    v_bias = lax.dynamic_slice_in_dim(qv_full, width + s * part, part)
    qkv_b = jnp.concatenate([q_bias, jnp.zeros((part,), f32), v_bias])
    qkv = (dot_nn(tok_full, qkv_w) + qkv_b).astype(bf16)
    mixed = attend(qkv, seg)
    attn = scatter_seq(dot_nn(mixed, out_w)) + out_b
    normed_one, recip_one = normalize(tok_rows.astype(f32) + attn)
    first = normed_one * gain_one + shift_one
    first_full = gather_seq(first.astype(bf16))
    hidden = in_w.shape[1]
    pre = dot_nn(first_full, in_w) + lax.dynamic_slice_in_dim(in_b, s * hidden, hidden)
    act_value, act_slope = gelu_parts(pre)
    act = act_value.astype(bf16)
    ffn = scatter_seq(dot_nn(act, down_w)) + down_b
    normed_two, recip_two = normalize(first + ffn)
    result = (normed_two * gain_two + shift_two).astype(bf16)

    grad_out = cotangent[0].astype(f32)
    shift_two_grad = jnp.sum(grad_out, axis=0)
    gain_two_grad = jnp.sum(grad_out * normed_two, axis=0)
    grad_h2 = norm_back(grad_out, normed_two, recip_two, gain_two)
    grad_ffn = grad_h2.astype(bf16)
    down_b_grad = jnp.sum(grad_ffn.astype(f32), axis=0)
    grad_ffn_full = gather_seq(grad_ffn)
    grad_pre = (dot_nt(grad_ffn_full, down_w) * act_slope).astype(bf16)
    grad_first = grad_h2 + scatter_seq(dot_nt(grad_pre, in_w))
    down_w_grad = rows_back(dot_tn(act, grad_ffn_full))
    in_b_grad = jnp.sum(grad_pre.astype(f32), axis=0)
    in_w_grad = columns_back(dot_tn(first_full, grad_pre), 1)

    shift_one_grad = jnp.sum(grad_first, axis=0)
    gain_one_grad = jnp.sum(grad_first * normed_one, axis=0)
    grad_h1 = norm_back(grad_first, normed_one, recip_one, gain_one)
    grad_attn = grad_h1.astype(bf16)
    out_b_grad = jnp.sum(grad_attn.astype(f32), axis=0)
    grad_attn_full = gather_seq(grad_attn)
    grad_mixed = dot_nt(grad_attn_full, out_w).astype(bf16)
    grad_qkv = attend_back(qkv, grad_mixed, seg)
    out_w_grad = rows_back(dot_tn(mixed, grad_attn_full))
    qkv_w_grad = columns_back(dot_tn(tok_full, grad_qkv), 3)
    input_grad = (grad_h1 + scatter_seq(dot_nt(grad_qkv, qkv_w))).astype(bf16)

    sums = jnp.sum(grad_qkv.astype(f32), axis=0)
    qv_grad = jnp.zeros((2 * width,), f32)
    qv_grad = lax.dynamic_update_slice_in_dim(qv_grad, sums[:part], s * part, 0)
    qv_grad = lax.dynamic_update_slice_in_dim(qv_grad, sums[2 * part :], width + s * part, 0)
    in_b_all = jnp.zeros((n * hidden,), f32)
    in_b_all = lax.dynamic_update_slice_in_dim(in_b_all, in_b_grad, s * hidden, 0)
    small_grads = scatter_small(
        [
            qv_grad,
            out_b_grad,
            gain_one_grad,
            shift_one_grad,
            in_b_all,
            down_b_grad,
            gain_two_grad,
            shift_two_grad,
        ]
    )
    return (
        result[None],
        input_grad[None],
        qkv_w_grad,
        small_grads[0],
        out_w_grad,
        small_grads[1],
        small_grads[2],
        small_grads[3],
        in_w_grad,
        small_grads[4],
        down_w_grad,
        small_grads[5],
        small_grads[6],
        small_grads[7],
    )


def solution(mesh):
    rows = P(("seq", "dp"), None)
    flat = P(("seq", "dp"))
    tok = P("dp", "seq", None)
    return jax.shard_map(
        per_device,
        mesh=mesh,
        in_specs=(
            tok,
            P("dp", None),
            rows,
            flat,
            rows,
            flat,
            flat,
            flat,
            rows,
            flat,
            rows,
            flat,
            flat,
            flat,
            tok,
        ),
        out_specs=(tok, tok, rows, flat, rows, flat, flat, flat, rows, flat, rows, flat, flat, flat),
        check_vma=False,
    )
```

time: 3090 us -> 772 us (0.25)
  waiting for transfers between devices: 2630 us -> 427 us
  matrix products: 204 us -> 94.8 us
  starting transfers between devices: 0.44 us -> 79.6 us
  blocking collectives: 130 us -> 63.6 us
  local copies, waits for them, and re-layouts: 84.3 us -> 48.9 us
    reduce_scatter x3 -> x4, waiting for transfers between devices: 1570 us -> 111 us  [the longest x2 68.9 us: columns_back(): mine = lax.psum_scatter(stacked, 'dp', scatter_dimension=1, tiled=True)]
    all_gather x5 -> x4, waiting for transfers between devices: 541 us -> 0.06 us  [the longest x2 0.04 us: columns_to_owner(): full = lax.all_gather(moved, 'dp', axis=1, tiled=True)]
    unnamed x14 -> x8, waiting for transfers between devices: 513 us -> 1.32 us
    ppermute x0 -> x24, waiting for transfers between devices: none -> 265 us  [shift(): return lax.ppermute(value, 'seq', [(i, (i + step) % n) for i in range(n)])]
    dot_general x18 -> x12, matrix products: 204 us -> 94.8 us  [the longest x4 34.3 us: dot_nn(): lax.dot_general(a, b, (((1,), (0,)), ((), ())), preferred_element_type=f32)]
    all_gather x2 -> x0, blocking collectives: 87.8 us -> none  [the longest x1 44.4 us: gather_feed(): lax.all_gather(in_bias, ('seq', 'dp'), axis=0, tiled=True)]
    ppermute x0 -> x24, starting transfers between devices: none -> 64.3 us  [shift(): return lax.ppermute(value, 'seq', [(i, (i + step) % n) for i in range(n)])]
    all_to_all x0 -> x3, blocking collectives: none -> 63.6 us  [the longest x2 54.1 us: columns_to_owner(): moved = lax.all_to_all(pieces, 'seq', 0, 0)]
  transfers between devices with their start and end apart: 11 -> 35, of which waited for: 9 -> 19; matrix products, arithmetic and copies ran while one was open for 6% -> 13% of each run, Pallas kernels for 0% -> 1%
where the time goes in v1:
time: 772 us; the launch traced here: 763 us
  waiting for transfers between devices  427 us (55%)
  matrix products  94.8 us (12%)
  starting transfers between devices  79.6 us (10%)
  blocking collectives  63.6 us (8%)
  local copies, waits for them, and re-layouts  48.9 us (6%)
  other arithmetic  22.1 us (3%)
  between operations  15.3 us (2%)
  Pallas kernels  11.1 us (1%)
    ppermute x24, waiting for transfers between devices, shift(): return lax.ppermute(value, 'seq', [(i, (i + step) % n) for i in range(n)])  265 us
    reduce_scatter x2, waiting for transfers between devices, columns_back(): mine = lax.psum_scatter(stacked, 'dp', scatter_dimension=1, tiled=True)  68.9 us
    ppermute x24, starting transfers between devices, shift(): return lax.ppermute(value, 'seq', [(i, (i + step) % n) for i in range(n)])  64.3 us
    all_to_all x2, blocking collectives, columns_to_owner(): moved = lax.all_to_all(pieces, 'seq', 0, 0)  54.1 us
    reduce_scatter x2, waiting for transfers between devices, rows_back(): lax.psum_scatter(grad.astype(bf16), 'dp', scatter_dimension=0, tiled=True)  42.2 us
    all_to_all x1, waiting for transfers between devices, all_small(): lax.all_to_all(jnp.broadcast_to(packed[None], (count, packed.shape[0])),...  38 us
    dot_general x4, matrix products, dot_nn(): lax.dot_general(a, b, (((1,), (0,)), ((), ())), preferred_element_type=f32)  34.3 us
    dot_general x4, matrix products, dot_tn(): lax.dot_general(a, b, (((0,), (0,)), ((), ())), preferred_element_type=f32)  31.5 us
  transfers between devices with their start and end apart: 35, of which 19 were waited for; matrix products, arithmetic and copies ran while one was open for 13% of the time, Pallas kernels for 1%

profile of v1, /device:TPU:0, one launch (start us, length us, event | category | flops | bytes accessed | tf_op | source)
XLA Modules:
  0.0 762.9 jit_solution(6591343703212171603)
XLA Ops:
  11.2 26.3 %all_to_all.38 = bf16[4,64,1536]{2,1,0:T(8,128)(2,1)} all-to-all(bf16[4,64,1536]{2,1,0:T(8,128)(2,1)S(1)} %reshape.254), channel_id=1, replica_groups=mesh['seq'=4,'dp'=8] {'seq'}, dimensions={0} | all-to-all | bytes 1572864 | tf_op jit(solution)/shard_map/all_to_all | solution.py:145
  39.8 27.8 %all_to_all.39 = bf16[4,64,2048]{2,1,0:T(8,128)(2,1)S(1)} all-to-all(bf16[4,64,2048]{2,1,0:T(8,128)(2,1)S(1)} %copy.51), channel_id=1, replica_groups=mesh['seq'=4,'dp'=8] {'seq'}, dimensions={0} | all-to-all | bytes 2097152 | tf_op jit(solution)/shard_map/all_to_all | solution.py:145
  74.6 5.5 all-to-all-start.1
  80.6 38.0 %all-to-all-done.1 = bf16[32,2,384]{2,1,0:T(2,128)(2,1)S(1)} async-done(((bf16[32,2,384]{2,1,0:T(2,128)(2,1)}), bf16[32,2,384]{2,1,0:T(2,128)(2,1)S(1)}, u32[]{:S(2)}, u32[]{:S(2)}) %all-to-all-start.1) | async-done | bytes 49184 | tf_op jit(solution)/shard_map/all_to_all | solution.py:168
  119.9 7.2 fusion.7.q.k.v
  127.1 4.7 attend.1
  131.8 5.0 fusion.70
  138.1 4.2 collective-permute-start.4
  145.3 9.7 %collective-permute-done.5 = bf16[128,2048]{1,0:T(8,128)(2,1)S(1)} collective-permute-done((bf16[128,2048]{1,0:T(8,128)(2,1)}, bf16[128,2048]{1,0:T(8,128)(2,1)S(1)}, u32[]{:S(2)}, u32[]{:S(2)}) %collective-permute-start.5) | collective-permute-done | bytes 524320 | tf_op jit(solution)/shard_map/ppermute | solution.py:19
  155.0 21.0 %collective-permute-done.4 = bf16[128,2048]{1,0:T(8,128)(2,1)S(1)} collective-permute-done((bf16[128,2048]{1,0:T(8,128)(2,1)}, bf16[128,2048]{1,0:T(8,128)(2,1)S(1)}, u32[]{:S(2)}, u32[]{:S(2)}) %collective-permute-start.4) | collective-permute-done | bytes 524320 | tf_op jit(solution)/shard_map/ppermute | solution.py:19
  179.9 13.2 %collective-permute-start.8 = (bf16[128,2048]{1,0:T(8,128)(2,1)S(1)}, bf16[128,2048]{1,0:T(8,128)(2,1)}, u32[]{:S(2)}, u32[]{:S(2)}) collective-permute-start(bf16[128,2048]{1,0:T(8,128)(2,1)S(1)} %fusion.32), channel_id=1, source_target_pairs={{0,24},{8,0},{16,8},{24,16},{1,25},{9,1},{17,9},{25,17},{2,26},{10... | collective-permute-start | bytes 1572872 | tf_op jit(solution)/shard_map/ppermute | solution.py:19
  194.1 11.3 %copy.53 = bf16[4,512,2048]{2,1,0:T(8,128)(2,1)} copy(bf16[4,512,2048]{2,0,1:T(4,128)(2,1)} %all-gather.9.cloned.1.call-done) | data formatting | bytes 16777216 | tf_op jit(solution)/shard_map/all_gather | solution.py:146
  205.6 32.2 %collective-permute-done.7 = bf16[128,2048]{1,0:T(8,128)(2,1)} collective-permute-done((bf16[128,2048]{1,0:T(8,128)(2,1)S(1)}, bf16[128,2048]{1,0:T(8,128)(2,1)}, u32[]{:S(2)}, u32[]{:S(2)}) %collective-permute-start.7) | collective-permute-done | bytes 524320 | tf_op jit(solution)/shard_map/ppermute | solution.py:19
  237.8 10.4 %fusion.35 = f32[512,2048]{1,0:T(8,128)} fusion(bf16[2048,2048]{1,0:T(8,128)(2,1)} %bitcast.88, bf16[128,2048]{1,0:T(8,128)(2,1)} %collective-permute-done.8, bf16[128,2048]{1,0:T(8,128)(2,1)} %collective-permute-done.7, bf16[128,2048]{1,0:T(8,128)(2,1)} %collective-permute-done.6, bf16[128,2048]{1,0:T(8,128)(2,1)S(1)} %fusion.32), kind=kOutput, calls=%fused_computation.70 | convolution fusion | flops 4303355904 | bytes 14680064 | tf_op jit(solution)/shard_map/dot_general | solution.py:54
  248.2 11.7 %fusion.71 = (bf16[512,2048]{1,0:T(8,128)(2,1)S(1)}, f32[512,2048]{1,0:T(8,128)}) fusion(bf16[2048,2048]{1,0:T(8,128)(2,1)} %all-gather.11.cloned.1.call-done, f32[512,2048]{1,0:T(8,128)} %fusion.35, f32[2048]{0:T(1024)S(1)} %dynamic_slice.11), kind=kOutput, calls=%fused_computation.130 | convolution fusion | flops 4306501632 | bytes 18882560 | tf_op jit(solution)/shard_map/dot_general | solution.py:54
  263.4 3.3 collective-permute-start.9
  266.8 11.3 %collective-permute-done.11 = bf16[128,2048]{1,0:T(8,128)(2,1)} collective-permute-done((bf16[128,2048]{1,0:T(8,128)(2,1)}, bf16[128,2048]{1,0:T(8,128)(2,1)}, u32[]{:S(2)}, u32[]{:S(2)}) %collective-permute-start.11) | collective-permute-done | bytes 524320 | tf_op jit(solution)/shard_map/ppermute | solution.py:19
  278.1 20.7 %collective-permute-done.10 = bf16[128,2048]{1,0:T(8,128)(2,1)} collective-permute-done((bf16[128,2048]{1,0:T(8,128)(2,1)}, bf16[128,2048]{1,0:T(8,128)(2,1)}, u32[]{:S(2)}, u32[]{:S(2)}) %collective-permute-start.10) | collective-permute-done | bytes 524320 | tf_op jit(solution)/shard_map/ppermute | solution.py:19
  302.6 12.5 %collective-permute-start.14 = (bf16[128,2048]{1,0:T(8,128)(2,1)S(1)}, bf16[128,2048]{1,0:T(8,128)(2,1)S(1)}, u32[]{:S(2)}, u32[]{:S(2)}) collective-permute-start(bf16[128,2048]{1,0:T(8,128)(2,1)S(1)} %get-tuple-element.22), channel_id=1, source_target_pairs={{0,24},{8,0},{16,8},{24,16},{1,25},{9,1},{17,9},{25,17},{2,26},{10... | collective-permute-start | bytes 1572872 | tf_op jit(solution)/shard_map/ppermute | solution.py:19
  315.7 11.8 %collective-permute-done.14 = bf16[128,2048]{1,0:T(8,128)(2,1)S(1)} collective-permute-done((bf16[128,2048]{1,0:T(8,128)(2,1)S(1)}, bf16[128,2048]{1,0:T(8,128)(2,1)S(1)}, u32[]{:S(2)}, u32[]{:S(2)}) %collective-permute-start.14) | collective-permute-done | bytes 524320 | tf_op jit(solution)/shard_map/ppermute | solution.py:19
  327.5 31.9 %collective-permute-done.13 = bf16[128,2048]{1,0:T(8,128)(2,1)S(1)} collective-permute-done((bf16[128,2048]{1,0:T(8,128)(2,1)S(1)}, bf16[128,2048]{1,0:T(8,128)(2,1)S(1)}, u32[]{:S(2)}, u32[]{:S(2)}) %collective-permute-start.13) | collective-permute-done | bytes 524320 | tf_op jit(solution)/shard_map/ppermute | solution.py:19
  359.4 13.1 %convert_reduce_fusion = (f32[2048]{0:T(1024)S(1)}, bf16[512,2048]{1,0:T(8,128)(2,1)S(1)}) fusion(f32[512,2048]{1,0:T(8,128)} %fusion.35, f32[2048]{0:T(1024)S(1)} %dynamic_slice.11, bf16[2048,2048]{1,0:T(8,128)(2,1)} %all-gather.11.cloned.1.call-done, bf16[128,2048]{1,0:T(8,128)(2,1)S(1)} %collective-permute-done.14, ...), kind=kOutput, calls=%fused_computation.12 | convolution fusion | flops 4326422528 | bytes 16793600 | tf_op jit(solution)/shard_map/dot_general | solution.py:58
  372.6 6.2 fusion.72
  381.3 2.9 collective-permute-start.15
  384.3 12.8 %collective-permute-done.17 = bf16[128,2048]{1,0:T(8,128)(2,1)} collective-permute-done((bf16[128,2048]{1,0:T(8,128)(2,1)}, bf16[128,2048]{1,0:T(8,128)(2,1)}, u32[]{:S(2)}, u32[]{:S(2)}) %collective-permute-start.17) | collective-permute-done | bytes 524320 | tf_op jit(solution)/shard_map/ppermute | solution.py:19
  397.0 19.7 %collective-permute-done.16 = bf16[128,2048]{1,0:T(8,128)(2,1)} collective-permute-done((bf16[128,2048]{1,0:T(8,128)(2,1)}, bf16[128,2048]{1,0:T(8,128)(2,1)}, u32[]{:S(2)}, u32[]{:S(2)}) %collective-permute-start.16) | collective-permute-done | bytes 524320 | tf_op jit(solution)/shard_map/ppermute | solution.py:19
  416.7 4.0 multiply_reduce_fusion
  422.2 12.4 %collective-permute-start.20 = (bf16[128,2048]{1,0:T(8,128)(2,1)S(1)}, bf16[128,2048]{1,0:T(8,128)(2,1)S(1)}, u32[]{:S(2)}, u32[]{:S(2)}) collective-permute-start(bf16[128,2048]{1,0:T(8,128)(2,1)S(1)} %get-tuple-element.24), channel_id=1, source_target_pairs={{0,24},{8,0},{16,8},{24,16},{1,25},{9,1},{17,9},{25,17},{2,26},{10... | collective-permute-start | bytes 1572872 | tf_op jit(solution)/shard_map/ppermute | solution.py:19
  435.3 11.7 %collective-permute-done.20 = bf16[128,2048]{1,0:T(8,128)(2,1)S(1)} collective-permute-done((bf16[128,2048]{1,0:T(8,128)(2,1)S(1)}, bf16[128,2048]{1,0:T(8,128)(2,1)S(1)}, u32[]{:S(2)}, u32[]{:S(2)}) %collective-permute-start.20) | collective-permute-done | bytes 524320 | tf_op jit(solution)/shard_map/ppermute | solution.py:19
  447.1 32.1 %collective-permute-done.19 = bf16[128,2048]{1,0:T(8,128)(2,1)S(1)} collective-permute-done((bf16[128,2048]{1,0:T(8,128)(2,1)S(1)}, bf16[128,2048]{1,0:T(8,128)(2,1)S(1)}, u32[]{:S(2)}, u32[]{:S(2)}) %collective-permute-start.19) | collective-permute-done | bytes 524320 | tf_op jit(solution)/shard_map/ppermute | solution.py:19
  482.2 6.4 attend_back.1
  488.7 5.4 convolution_convert_fusion.2
  495.2 10.8 %convolution_convert_fusion.1 = bf16[2048,2048]{1,0:T(8,128)(2,1)} fusion(bf16[512,2048]{1,0:T(8,128)(2,1)} %copy-done.40, bf16[128,2048]{1,0:T(8,128)(2,1)} %collective-permute-done.8, bf16[128,2048]{1,0:T(8,128)(2,1)} %collective-permute-done.7, bf16[128,2048]{1,0:T(8,128)(2,1)} %collective-permute-done.6, bf16[128,2048]{1,0:T(8,128)(2,1)S(1)} %copy-done.18), kind=kOutput, calls=%fused_computation.1 | convolution fusion | flops 4307550208 | bytes 12582912 | tf_op jit(solution)/shard_map/dot_general | solution.py:62
  507.2 4.0 convolution_convert_fusion.3
  511.4 11.4 %convolution_convert_fusion = bf16[2048,2048]{1,0:T(8,128)(2,1)} fusion(bf16[128,2048]{1,0:T(8,128)(2,1)} %copy-done.33, bf16[128,2048]{1,0:T(8,128)(2,1)} %copy-done.34, bf16[128,2048]{1,0:T(8,128)(2,1)} %copy-done.35, bf16[128,2048]{1,0:T(8,128)(2,1)S(1)} %copy-done.12, f32[512,2048]{1,0:T(8,128)} %fusion.35, f32[2048]{0:T(1024)S(1)} %dynamic_slice.11), kind=kOutput, calls=%fused_computation | convolution fusion | flops 4318035968 | bytes 14688256 | tf_op jit(solution)/shard_map/dot_general | solution.py:62
  525.3 9.5 %all_to_all.40 = f32[32,1,768]{2,1,0:T(1,128)S(1)} all-to-all(f32[32,1,768]{2,1,0:T(1,128)S(1)} %all_to_all.29), channel_id=1, replica_groups=mesh['seq'=4,'dp'=8] {'seq','dp'}, dimensions={0} | all-to-all | bytes 196608 | tf_op jit(solution)/shard_map/all_to_all | solution.py:181
  534.8 18.6 %reduce-scatter.5.cloned.1.call-done = bf16[4,64,1536]{2,1,0:T(8,128)(2,1)} async-done(((bf16[4,512,1536]{2,1,0:T(8,128)(2,1)}), bf16[4,64,1536]{2,1,0:T(8,128)(2,1)}) %reduce-scatter.5.cloned.1.call-update) | async-done | bytes 786448 | tf_op jit(solution)/shard_map/reduce_scatter | solution.py:154
  553.4 4.6 all-to-all-start.3
  558.0 8.4 %fusion.73 = (bf16[512,2048]{1,0:T(8,128)(2,1)}, f32[512,2048]{1,0:T(8,128)}) fusion(bf16[512,1536]{1,0:T(8,128)(2,1)S(1)} %attend_back.1, bf16[2048,1536]{1,0:T(8,128)(2,1)} %bitcast.109), kind=kOutput, calls=%fused_computation.132 | convolution fusion | flops 3222274048 | bytes 14155776 | tf_op jit(solution)/shard_map/dot_general | solution.py:58
  566.4 11.7 %all-to-all-done.3 = bf16[4,64,1536]{2,1,0:T(8,128)(2,1)S(1)} async-done(((bf16[4,64,1536]{2,1,0:T(8,128)(2,1)}), bf16[4,64,1536]{2,1,0:T(8,128)(2,1)S(1)}, u32[]{:S(2)}, u32[]{:S(2)}) %all-to-all-start.3) | async-done | bytes 786464 | tf_op jit(solution)/shard_map/all_to_all | solution.py:155
  578.2 50.3 %reduce-scatter.9.cloned.1.call-done = bf16[4,64,2048]{2,1,0:T(8,128)(2,1)} async-done(((bf16[4,512,2048]{2,1,0:T(8,128)(2,1)}), bf16[4,64,2048]{2,1,0:T(8,128)(2,1)}) %reduce-scatter.9.cloned.1.call-update) | async-done | bytes 1048592 | tf_op jit(solution)/shard_map/reduce_scatter | solution.py:154
  628.5 4.6 all-to-all-start.5
  643.5 23.5 %collective-permute-done.23 = bf16[128,2048]{1,0:T(8,128)(2,1)} collective-permute-done((bf16[128,2048]{1,0:T(8,128)(2,1)}, bf16[128,2048]{1,0:T(8,128)(2,1)}, u32[]{:S(2)}, u32[]{:S(2)}) %collective-permute-start.23) | collective-permute-done | bytes 524320 | tf_op jit(solution)/shard_map/ppermute | solution.py:19
  667.0 26.7 %collective-permute-done.22 = bf16[128,2048]{1,0:T(8,128)(2,1)} collective-permute-done((bf16[128,2048]{1,0:T(8,128)(2,1)}, bf16[128,2048]{1,0:T(8,128)(2,1)}, u32[]{:S(2)}, u32[]{:S(2)}) %collective-permute-start.22) | collective-permute-done | bytes 524320 | tf_op jit(solution)/shard_map/ppermute | solution.py:19
  693.7 3.0 fusion.34
  703.3 3.2 reshape.277
  706.6 42.2 %reduce-scatter.11.cloned.1.call-done = bf16[256,2048]{1,0:T(8,128)(2,1)} async-done(((bf16[2048,2048]{1,0:T(8,128)(2,1)}), bf16[256,2048]{1,0:T(8,128)(2,1)}) %reduce-scatter.11.cloned.1.call-update) | async-done | bytes 1048592 | tf_op jit(solution)/shard_map/reduce_scatter | solution.py:162
  748.7 2.8 convert_element_type.271
  (215 shorter events, 65.9 us)
Async XLA Ops:
  7.2 111.7 %all-gather.5.cloned.1.call-start = ((), (), s32[]{:S(2)}) async-start(), calls=%async_computation.10 | async-start | bytes 7077888 | tf_op jit(solution)/shard_map/all_gather | solution.py:146
  37.5 94.3 %all-gather.7.cloned.1.call-start = ((), (), s32[]{:S(2)}) async-start(), calls=%async_computation.11 | async-start | bytes 2359296 | tf_op jit(solution)/shard_map/all_gather | solution.py:232
  38.3 155.8 %all-gather.9.cloned.1.call-start = ((), (), s32[]{:S(2)}) async-start(), calls=%async_computation.12 | async-start | bytes 9437184 | tf_op jit(solution)/shard_map/all_gather | solution.py:146
  39.1 33.2 %copy-start.19 = (bf16[128]{0:T(256)(128)(2,1)S(1)}, bf16[128]{0:T(256)(128)(2,1)}, u32[]{:S(2)}) copy-start(bf16[128]{0:T(256)(128)(2,1)} %param.18) | copy-start | bytes 772
  39.2 33.2 %copy-start.20 = (bf16[64]{0:T(256)(128)(2,1)S(1)}, bf16[64]{0:T(256)(128)(2,1)}, u32[]{:S(2)}) copy-start(bf16[64]{0:T(256)(128)(2,1)} %param.20) | copy-start | bytes 388
  39.2 40.9 %copy-start.39 = (s32[1,12]{1,0:T(1,128)S(1)}, s32[1,12]{1,0:T(1,128)}, u32[]{:S(2)}) copy-start(s32[1,12]{1,0:T(1,128)} %param.16) | copy-start | bytes 148
  69.4 178.8 %all-gather.11.cloned.1.call-start = ((), (), s32[]{:S(2)}) async-start(), calls=%async_computation.13 | async-start | bytes 9437184 | tf_op jit(solution)/shard_map/all_gather | solution.py:234
  70.0 48.8 %collective-permute-start.2 = (bf16[128,2048]{1,0:T(8,128)(2,1)S(1)}, bf16[128,2048]{1,0:T(8,128)(2,1)S(1)}, u32[]{:S(2)}, u32[]{:S(2)}) collective-permute-start(bf16[128,2048]{1,0:T(8,128)(2,1)S(1)} %bitcast.97), channel_id=1, source_target_pairs={{0,24},{8,0},{16,8},{24,16},{1,25},{9,1},{17,9},{25,17},{2,26},{10... | collective-permute-start | bytes 1572872 | tf_op jit(solution)/shard_map/ppermute | solution.py:19
  71.5 47.3 %collective-permute-start.1 = (bf16[128,2048]{1,0:T(8,128)(2,1)S(1)}, bf16[128,2048]{1,0:T(8,128)(2,1)S(1)}, u32[]{:S(2)}, u32[]{:S(2)}) collective-permute-start(bf16[128,2048]{1,0:T(8,128)(2,1)S(1)} %bitcast.98), channel_id=1, source_target_pairs={{0,16},{8,24},{16,0},{24,8},{1,17},{9,25},{17,1},{25,9},{2,18},{10... | collective-permute-start | bytes 1572872 | tf_op jit(solution)/shard_map/ppermute | solution.py:19
  71.7 47.1 %collective-permute-start = (bf16[128,2048]{1,0:T(8,128)(2,1)S(1)}, bf16[128,2048]{1,0:T(8,128)(2,1)S(1)}, u32[]{:S(2)}, u32[]{:S(2)}) collective-permute-start(bf16[128,2048]{1,0:T(8,128)(2,1)S(1)} %bitcast.99), channel_id=1, source_target_pairs={{0,8},{8,16},{16,24},{24,0},{1,9},{9,17},{17,25},{25,1},{2,10},{10... | collective-permute-start | bytes 1572872 | tf_op jit(solution)/shard_map/ppermute | solution.py:19
  74.6 44.1 %all-to-all-start.1 = ((bf16[32,2,384]{2,1,0:T(2,128)(2,1)}), bf16[32,2,384]{2,1,0:T(2,128)(2,1)S(1)}, u32[]{:S(2)}, u32[]{:S(2)}) async-start(bf16[32,2,384]{2,1,0:T(2,128)(2,1)} %reshape.281), calls=%async_computation.1 | async-start | bytes 98304 | tf_op jit(solution)/shard_map/all_to_all | solution.py:168
  80.1 473.3 %reduce-scatter.5.cloned.1.call-start = ((), (), s32[]{:S(2)}) async-start(), calls=%async_computation.14 | async-start | bytes 7077888 | tf_op jit(solution)/shard_map/reduce_scatter | solution.py:154
  138.0 17.0 %collective-permute-start.5 = (bf16[128,2048]{1,0:T(8,128)(2,1)}, bf16[128,2048]{1,0:T(8,128)(2,1)S(1)}, u32[]{:S(2)}, u32[]{:S(2)}) collective-permute-start(bf16[128,2048]{1,0:T(8,128)(2,1)} %get-tuple-element.41), channel_id=1, source_target_pairs={{0,8},{8,16},{16,24},{24,0},{1,9},{9,17},{17,25},{25,1},{2,10},{10... | collective-permute-start | bytes 1572872 | tf_op jit(solution)/shard_map/ppermute | solution.py:19
  138.1 38.0 %collective-permute-start.4 = (bf16[128,2048]{1,0:T(8,128)(2,1)}, bf16[128,2048]{1,0:T(8,128)(2,1)S(1)}, u32[]{:S(2)}, u32[]{:S(2)}) collective-permute-start(bf16[128,2048]{1,0:T(8,128)(2,1)} %get-tuple-element.42), channel_id=1, source_target_pairs={{0,16},{8,24},{16,0},{24,8},{1,17},{9,25},{17,1},{25,9},{2,18},{10... | collective-permute-start | bytes 1572872 | tf_op jit(solution)/shard_map/ppermute | solution.py:19
  142.3 33.8 %collective-permute-start.3 = (bf16[128,2048]{1,0:T(8,128)(2,1)}, bf16[128,2048]{1,0:T(8,128)(2,1)}, u32[]{:S(2)}, u32[]{:S(2)}) collective-permute-start(bf16[128,2048]{1,0:T(8,128)(2,1)} %get-tuple-element.40), channel_id=1, source_target_pairs={{0,24},{8,0},{16,8},{24,16},{1,25},{9,1},{17,9},{25,17},{2,26},{10... | collective-permute-start | bytes 1572872 | tf_op jit(solution)/shard_map/ppermute | solution.py:19
  179.9 57.9 %copy-start.17 = (bf16[128,2048]{1,0:T(8,128)(2,1)}, bf16[128,2048]{1,0:T(8,128)(2,1)S(1)}, u32[]{:S(2)}) copy-start(bf16[128,2048]{1,0:T(8,128)(2,1)S(1)} %fusion.32) | copy-start | bytes 1572868
  179.9 25.7 %collective-permute-start.8 = (bf16[128,2048]{1,0:T(8,128)(2,1)S(1)}, bf16[128,2048]{1,0:T(8,128)(2,1)}, u32[]{:S(2)}, u32[]{:S(2)}) collective-permute-start(bf16[128,2048]{1,0:T(8,128)(2,1)S(1)} %fusion.32), channel_id=1, source_target_pairs={{0,24},{8,0},{16,8},{24,16},{1,25},{9,1},{17,9},{25,17},{2,26},{10... | collective-permute-start | bytes 1572872 | tf_op jit(solution)/shard_map/ppermute | solution.py:19
  193.1 44.6 %collective-permute-start.7 = (bf16[128,2048]{1,0:T(8,128)(2,1)S(1)}, bf16[128,2048]{1,0:T(8,128)(2,1)}, u32[]{:S(2)}, u32[]{:S(2)}) collective-permute-start(bf16[128,2048]{1,0:T(8,128)(2,1)S(1)} %fusion.32), channel_id=1, source_target_pairs={{0,16},{8,24},{16,0},{24,8},{1,17},{9,25},{17,1},{25,9},{2,18},{10... | collective-permute-start | bytes 1572872 | tf_op jit(solution)/shard_map/ppermute | solution.py:19
  193.1 44.6 %collective-permute-start.6 = (bf16[128,2048]{1,0:T(8,128)(2,1)S(1)}, bf16[128,2048]{1,0:T(8,128)(2,1)}, u32[]{:S(2)}, u32[]{:S(2)}) collective-permute-start(bf16[128,2048]{1,0:T(8,128)(2,1)S(1)} %fusion.32), channel_id=1, source_target_pairs={{0,8},{8,16},{16,24},{24,0},{1,9},{9,17},{17,25},{25,1},{2,10},{10... | collective-permute-start | bytes 1572872 | tf_op jit(solution)/shard_map/ppermute | solution.py:19
  259.8 41.6 %copy-start.3 = (bf16[1,128,2048]{2,1,0:T(8,128)(2,1)S(1)}, bf16[1,128,2048]{2,1,0:T(8,128)(2,1)}, u32[]{:S(2)}) copy-start(bf16[1,128,2048]{2,1,0:T(8,128)(2,1)} %param.29) | copy-start | bytes 1572868
  261.0 17.1 %collective-permute-start.11 = (bf16[128,2048]{1,0:T(8,128)(2,1)}, bf16[128,2048]{1,0:T(8,128)(2,1)}, u32[]{:S(2)}, u32[]{:S(2)}) collective-permute-start(bf16[128,2048]{1,0:T(8,128)(2,1)} %get-tuple-element.38), channel_id=1, source_target_pairs={{0,8},{8,16},{16,24},{24,0},{1,9},{9,17},{17,25},{25,1},{2,10},{10... | collective-permute-start | bytes 1572872 | tf_op jit(solution)/shard_map/ppermute | solution.py:19
  261.4 37.5 %collective-permute-start.10 = (bf16[128,2048]{1,0:T(8,128)(2,1)}, bf16[128,2048]{1,0:T(8,128)(2,1)}, u32[]{:S(2)}, u32[]{:S(2)}) collective-permute-start(bf16[128,2048]{1,0:T(8,128)(2,1)} %get-tuple-element.39), channel_id=1, source_target_pairs={{0,16},{8,24},{16,0},{24,8},{1,17},{9,25},{17,1},{25,9},{2,18},{10... | collective-permute-start | bytes 1572872 | tf_op jit(solution)/shard_map/ppermute | solution.py:19
  263.4 35.4 %collective-permute-start.9 = (bf16[128,2048]{1,0:T(8,128)(2,1)}, bf16[128,2048]{1,0:T(8,128)(2,1)}, u32[]{:S(2)}, u32[]{:S(2)}) collective-permute-start(bf16[128,2048]{1,0:T(8,128)(2,1)} %get-tuple-element.37), channel_id=1, source_target_pairs={{0,24},{8,0},{16,8},{24,16},{1,25},{9,1},{17,9},{25,17},{2,26},{10... | collective-permute-start | bytes 1572872 | tf_op jit(solution)/shard_map/ppermute | solution.py:19
  302.6 70.0 %copy-start.11 = (bf16[128,2048]{1,0:T(8,128)(2,1)}, bf16[128,2048]{1,0:T(8,128)(2,1)S(1)}, u32[]{:S(2)}) copy-start(bf16[128,2048]{1,0:T(8,128)(2,1)S(1)} %get-tuple-element.22) | copy-start | bytes 1572868
  302.6 70.0 %slice-start = ((s8[8388608]{0:T(1024)(128)(4,1)}), s8[4194304]{0:T(1024)(128)(4,1)S(1)}, s32[]{:S(2)}) async-start(s8[8388608]{0:T(1024)(128)(4,1)} %bitcast.89), calls=%async_computation.18 | async-start | bytes 8388608
  302.6 70.0 %slice-start.1 = ((s8[8388608]{0:T(1024)(128)(4,1)}), s8[4194304]{0:T(1024)(128)(4,1)S(1)}, s32[]{:S(2)}) async-start(s8[8388608]{0:T(1024)(128)(4,1)} %bitcast.89), calls=%async_computation.19 | async-start | bytes 8388608
  302.6 24.9 %collective-permute-start.14 = (bf16[128,2048]{1,0:T(8,128)(2,1)S(1)}, bf16[128,2048]{1,0:T(8,128)(2,1)S(1)}, u32[]{:S(2)}, u32[]{:S(2)}) collective-permute-start(bf16[128,2048]{1,0:T(8,128)(2,1)S(1)} %get-tuple-element.22), channel_id=1, source_target_pairs={{0,24},{8,0},{16,8},{24,16},{1,25},{9,1},{17,9},{25,17},{2,26},{10... | collective-permute-start | bytes 1572872 | tf_op jit(solution)/shard_map/ppermute | solution.py:19
  315.1 44.3 %collective-permute-start.13 = (bf16[128,2048]{1,0:T(8,128)(2,1)S(1)}, bf16[128,2048]{1,0:T(8,128)(2,1)S(1)}, u32[]{:S(2)}, u32[]{:S(2)}) collective-permute-start(bf16[128,2048]{1,0:T(8,128)(2,1)S(1)} %get-tuple-element.22), channel_id=1, source_target_pairs={{0,16},{8,24},{16,0},{24,8},{1,17},{9,25},{17,1},{25,9},{2,18},{10... | collective-permute-start | bytes 1572872 | tf_op jit(solution)/shard_map/ppermute | solution.py:19
  315.1 44.3 %collective-permute-start.12 = (bf16[128,2048]{1,0:T(8,128)(2,1)S(1)}, bf16[128,2048]{1,0:T(8,128)(2,1)S(1)}, u32[]{:S(2)}, u32[]{:S(2)}) collective-permute-start(bf16[128,2048]{1,0:T(8,128)(2,1)S(1)} %get-tuple-element.22), channel_id=1, source_target_pairs={{0,8},{8,16},{16,24},{24,0},{1,9},{9,17},{17,25},{25,1},{2,10},{10... | collective-permute-start | bytes 1572872 | tf_op jit(solution)/shard_map/ppermute | solution.py:19
  327.5 45.0 %copy-start.33 = (bf16[128,2048]{1,0:T(8,128)(2,1)}, bf16[128,2048]{1,0:T(8,128)(2,1)S(1)}, u32[]{:S(2)}) copy-start(bf16[128,2048]{1,0:T(8,128)(2,1)S(1)} %collective-permute-done.14) | copy-start | bytes 1572868
  380.0 17.1 %collective-permute-start.17 = (bf16[128,2048]{1,0:T(8,128)(2,1)}, bf16[128,2048]{1,0:T(8,128)(2,1)}, u32[]{:S(2)}, u32[]{:S(2)}) collective-permute-start(bf16[128,2048]{1,0:T(8,128)(2,1)} %get-tuple-element.35), channel_id=1, source_target_pairs={{0,8},{8,16},{16,24},{24,0},{1,9},{9,17},{17,25},{25,1},{2,10},{10... | collective-permute-start | bytes 1572872 | tf_op jit(solution)/shard_map/ppermute | solution.py:19
  380.0 36.8 %collective-permute-start.16 = (bf16[128,2048]{1,0:T(8,128)(2,1)}, bf16[128,2048]{1,0:T(8,128)(2,1)}, u32[]{:S(2)}, u32[]{:S(2)}) collective-permute-start(bf16[128,2048]{1,0:T(8,128)(2,1)} %get-tuple-element.36), channel_id=1, source_target_pairs={{0,16},{8,24},{16,0},{24,8},{1,17},{9,25},{17,1},{25,9},{2,18},{10... | collective-permute-start | bytes 1572872 | tf_op jit(solution)/shard_map/ppermute | solution.py:19
  381.3 35.4 %collective-permute-start.15 = (bf16[128,2048]{1,0:T(8,128)(2,1)}, bf16[128,2048]{1,0:T(8,128)(2,1)}, u32[]{:S(2)}, u32[]{:S(2)}) collective-permute-start(bf16[128,2048]{1,0:T(8,128)(2,1)} %get-tuple-element.34), channel_id=1, source_target_pairs={{0,24},{8,0},{16,8},{24,16},{1,25},{9,1},{17,9},{25,17},{2,26},{10... | collective-permute-start | bytes 1572872 | tf_op jit(solution)/shard_map/ppermute | solution.py:19
  416.7 64.1 %copy-start.7 = (bf16[512,2048]{1,0:T(8,128)(2,1)S(1)}, bf16[512,2048]{1,0:T(8,128)(2,1)}, u32[]{:S(2)}) copy-start(bf16[512,2048]{1,0:T(8,128)(2,1)} %all-gather.7.cloned.1.call-done) | copy-start | bytes 6291460
  422.2 60.0 %copy-start.13 = (bf16[128,2048]{1,0:T(8,128)(2,1)}, bf16[128,2048]{1,0:T(8,128)(2,1)S(1)}, u32[]{:S(2)}) copy-start(bf16[128,2048]{1,0:T(8,128)(2,1)S(1)} %get-tuple-element.24) | copy-start | bytes 1572868
  422.2 24.9 %collective-permute-start.20 = (bf16[128,2048]{1,0:T(8,128)(2,1)S(1)}, bf16[128,2048]{1,0:T(8,128)(2,1)S(1)}, u32[]{:S(2)}, u32[]{:S(2)}) collective-permute-start(bf16[128,2048]{1,0:T(8,128)(2,1)S(1)} %get-tuple-element.24), channel_id=1, source_target_pairs={{0,24},{8,0},{16,8},{24,16},{1,25},{9,1},{17,9},{25,17},{2,26},{10... | collective-permute-start | bytes 1572872 | tf_op jit(solution)/shard_map/ppermute | solution.py:19
  434.6 44.5 %collective-permute-start.19 = (bf16[128,2048]{1,0:T(8,128)(2,1)S(1)}, bf16[128,2048]{1,0:T(8,128)(2,1)S(1)}, u32[]{:S(2)}, u32[]{:S(2)}) collective-permute-start(bf16[128,2048]{1,0:T(8,128)(2,1)S(1)} %get-tuple-element.24), channel_id=1, source_target_pairs={{0,16},{8,24},{16,0},{24,8},{1,17},{9,25},{17,1},{25,9},{2,18},{10... | collective-permute-start | bytes 1572872 | tf_op jit(solution)/shard_map/ppermute | solution.py:19
  434.6 44.5 %collective-permute-start.18 = (bf16[128,2048]{1,0:T(8,128)(2,1)S(1)}, bf16[128,2048]{1,0:T(8,128)(2,1)S(1)}, u32[]{:S(2)}, u32[]{:S(2)}) collective-permute-start(bf16[128,2048]{1,0:T(8,128)(2,1)S(1)} %get-tuple-element.24), channel_id=1, source_target_pairs={{0,8},{8,16},{16,24},{24,0},{1,9},{9,17},{17,25},{25,1},{2,10},{10... | collective-permute-start | bytes 1572872 | tf_op jit(solution)/shard_map/ppermute | solution.py:19
  494.1 134.3 %reduce-scatter.9.cloned.1.call-start = ((), (), s32[]{:S(2)}) async-start(), calls=%async_computation.16 | async-start | bytes 9437184 | tf_op jit(solution)/shard_map/reduce_scatter | solution.py:154
  506.0 190.7 %reduce-scatter.7.cloned.1.call-start = ((), (), s32[]{:S(2)}) async-start(), calls=%async_computation.15 | async-start | bytes 2359296 | tf_op jit(solution)/shard_map/reduce_scatter | solution.py:162
  511.2 237.6 %reduce-scatter.11.cloned.1.call-start = ((), (), s32[]{:S(2)}) async-start(), calls=%async_computation.17 | async-start | bytes 9437184 | tf_op jit(solution)/shard_map/reduce_scatter | solution.py:162
  553.4 24.7 %all-to-all-start.3 = ((bf16[4,64,1536]{2,1,0:T(8,128)(2,1)}), bf16[4,64,1536]{2,1,0:T(8,128)(2,1)S(1)}, u32[]{:S(2)}, u32[]{:S(2)}) async-start(bf16[4,64,1536]{2,1,0:T(8,128)(2,1)} %reduce-scatter.5.cloned.1.call-done), calls=%async_computation.4 | async-start | bytes 1572864 | tf_op jit(solution)/shard_map/all_to_all | solution.py:155
  566.4 127.3 %copy-start.5 = (f32[128,2048]{1,0:T(8,128)S(1)}, f32[128,2048]{1,0:T(8,128)}, u32[]{:S(2)}) copy-start(f32[128,2048]{1,0:T(8,128)} %get-tuple-element.25) | copy-start | bytes 3145732
  578.2 118.5 %copy-start.6 = (bf16[4,64,1536]{2,1,0:T(8,128)(2,1)}, bf16[4,64,1536]{2,1,0:T(8,128)(2,1)S(1)}, u32[]{:S(2)}) copy-start(bf16[4,64,1536]{2,1,0:T(8,128)(2,1)S(1)} %all-to-all-done.3) | copy-start | bytes 2359300
  628.5 123.1 %all-to-all-start.5 = ((bf16[4,64,2048]{2,1,0:T(8,128)(2,1)}), bf16[4,64,2048]{2,1,0:T(8,128)(2,1)S(1)}, u32[]{:S(2)}, u32[]{:S(2)}) async-start(bf16[4,64,2048]{2,1,0:T(8,128)(2,1)} %reduce-scatter.9.cloned.1.call-done), calls=%async_computation.8 | async-start | bytes 2097152 | tf_op jit(solution)/shard_map/all_to_all | solution.py:155
  635.6 31.4 %collective-permute-start.23 = (bf16[128,2048]{1,0:T(8,128)(2,1)}, bf16[128,2048]{1,0:T(8,128)(2,1)}, u32[]{:S(2)}, u32[]{:S(2)}) collective-permute-start(bf16[128,2048]{1,0:T(8,128)(2,1)} %get-tuple-element.32), channel_id=1, source_target_pairs={{0,8},{8,16},{16,24},{24,0},{1,9},{9,17},{17,25},{25,1},{2,10},{10... | collective-permute-start | bytes 1572872 | tf_op jit(solution)/shard_map/ppermute | solution.py:19
  637.6 56.1 %collective-permute-start.22 = (bf16[128,2048]{1,0:T(8,128)(2,1)}, bf16[128,2048]{1,0:T(8,128)(2,1)}, u32[]{:S(2)}, u32[]{:S(2)}) collective-permute-start(bf16[128,2048]{1,0:T(8,128)(2,1)} %get-tuple-element.33), channel_id=1, source_target_pairs={{0,16},{8,24},{16,0},{24,8},{1,17},{9,25},{17,1},{25,9},{2,18},{10... | collective-permute-start | bytes 1572872 | tf_op jit(solution)/shard_map/ppermute | solution.py:19
  640.0 53.7 %collective-permute-start.21 = (bf16[128,2048]{1,0:T(8,128)(2,1)}, bf16[128,2048]{1,0:T(8,128)(2,1)}, u32[]{:S(2)}, u32[]{:S(2)}) collective-permute-start(bf16[128,2048]{1,0:T(8,128)(2,1)} %get-tuple-element.31), channel_id=1, source_target_pairs={{0,24},{8,0},{16,8},{24,16},{1,25},{9,1},{17,9},{25,17},{2,26},{10... | collective-permute-start | bytes 1572872 | tf_op jit(solution)/shard_map/ppermute | solution.py:19
  (30 other events, 400.8 us)
Sparse Core Ops, SparseCore 0:
  37.6 44.6 all-gather.4
  84.2 28.0 all-gather.6
  114.8 54.4 all-gather.8
  171.0 54.3 all-gather.10
  494.3 59.1 reduce-scatter.4
  557.2 71.2 reduce-scatter.8
  632.3 41.1 reduce-scatter.6
  677.4 71.2 reduce-scatter.10

commit v2 on v1

--- a/solution.py
+++ b/solution.py
@@ -19,19 +19,33 @@
     return lax.ppermute(value, "seq", [(i, (i + step) % n) for i in range(n)])
 
 
+def gather_blocks(rows):
+    n = lax.axis_size("seq")
+    return [rows] + [shift(rows, k) for k in range(1, n)]
+
+
 def gather_seq(rows):
-    n = lax.axis_size("seq")
-    return jnp.concatenate([rows] + [shift(rows, k) for k in range(1, n)], axis=0)
-
-
-def scatter_seq(partial):
+    return jnp.concatenate(gather_blocks(rows), axis=0)
+
+
+def scatter_blocks(partial):
     n = lax.axis_size("seq")
     count = partial.shape[0] // n
-    total = partial[:count]
+    blocks = [partial[:count]]
     for k in range(1, n):
-        block = partial[k * count : (k + 1) * count].astype(bf16)
-        total = total + shift(block, -k).astype(f32)
+        blocks.append(shift(partial[k * count : (k + 1) * count].astype(bf16), -k))
+    return blocks
+
+
+def total_of(blocks):
+    total = blocks[0]
+    for block in blocks[1:]:
+        total = total + block.astype(f32)
     return total
+
+
+def scatter_seq(partial):
+    return total_of(scatter_blocks(partial))
 
 
 def normalize(hidden):
@@ -137,29 +151,175 @@
     )(seg[:, None], seg[None, :], qkv, qkv, qkv, grad_mixed)
 
 
-def columns_to_owner(shard, parts):
+def after(value, *others):
+    return lax.optimization_barrier((value, *others))[0]
+
+
+def whole(kernel, out_shape, name, scalar, *args):
+    spec = pltpu.PrefetchScalarGridSpec(
+        num_scalar_prefetch=1,
+        grid=(1,),
+        in_specs=[pl.BlockSpec(arg.shape, lambda i, sc, r=arg.ndim: (0,) * r) for arg in args],
+        out_specs=jax.tree.map(
+            lambda o: pl.BlockSpec(o.shape, lambda i, sc, r=len(o.shape): (0,) * r), out_shape
+        ),
+    )
+    params = pltpu.CompilerParams(vmem_limit_bytes=40 << 20)
+    call = pl.pallas_call(
+        kernel, grid_spec=spec, out_shape=out_shape, compiler_params=params, name=name
+    )
+    return call(jnp.reshape(scalar, (1,)).astype(jnp.int32), *args)
+
+
+def pack_columns(shard, parts):
     n = lax.axis_size("seq")
     rows, width = shard.shape
-    pieces = shard.reshape(rows, parts, n, width // (parts * n))
-    pieces = pieces.transpose(2, 0, 1, 3).reshape(n, rows, width // n)
-    moved = lax.all_to_all(pieces, "seq", 0, 0)
-    full = lax.all_gather(moved, "dp", axis=1, tiled=True)
-    return full.reshape(-1, width // n)
-
-
-def columns_back(grad, parts):
+    part = width // (parts * n)
+
+    def kernel(s, shard_ref, *outs):
+        for k in range(n):
+            owner = jnp.remainder(s[0] + k, n)
+            for p in range(parts):
+                start = pl.multiple_of((p * n + owner) * part, part)
+                outs[k][:, p * part : (p + 1) * part] = shard_ref[:, pl.ds(start, part)]
+
+    out = [jax.ShapeDtypeStruct((rows, part * parts), shard.dtype)] * n
+    return whole(kernel, out, "pack", lax.axis_index("seq"), shard)
+
+
+def join_rows(blocks):
+    n = len(blocks)
+    shape = blocks[0].shape
+
+    def kernel(s, *refs):
+        for k in range(n):
+            refs[n][jnp.remainder(s[0] - k + n, n)] = refs[k][...]
+
+    out = jax.ShapeDtypeStruct((n, *shape), blocks[0].dtype)
+    return whole(kernel, out, "join_rows", lax.axis_index("seq"), *blocks)
+
+
+def join_columns(blocks, parts):
+    n = len(blocks)
+    rows, width = blocks[0].shape
+    part = width // parts
+
+    def kernel(s, *refs):
+        for k in range(n):
+            source = jnp.remainder(s[0] - k + n, n)
+            for p in range(parts):
+                start = pl.multiple_of((p * n + source) * part, part)
+                piece = refs[k][:, p * part : (p + 1) * part]
+                refs[n][:, pl.ds(start, part)] = piece.astype(f32)
+
+    out = jax.ShapeDtypeStruct((rows, n * width), f32)
+    return whole(kernel, out, "join_columns", lax.axis_index("seq"), *blocks)
+
+
+def exchange(blocks):
+    return [blocks[0]] + [shift(blocks[k], k) for k in range(1, len(blocks))]
+
+
+def exchange_back(pieces):
     n = lax.axis_size("seq")
-    width = grad.shape[1]
-    stacked = grad.astype(bf16).reshape(n, -1, width)
-    mine = lax.psum_scatter(stacked, "dp", scatter_dimension=1, tiled=True)
-    moved = lax.all_to_all(mine, "seq", 0, 0)
-    rows = moved.shape[1]
-    moved = moved.reshape(n, rows, parts, width // parts).transpose(1, 2, 0, 3)
-    return moved.reshape(rows, n * width).astype(f32)
-
-
-def rows_back(grad):
-    return lax.psum_scatter(grad.astype(bf16), "dp", scatter_dimension=0, tiled=True).astype(f32)
+    s = lax.axis_index("seq")
+    blocks = [
+        lax.dynamic_index_in_dim(pieces, jnp.remainder(s + k, n), 0, keepdims=False)
+        for k in range(n)
+    ]
+    return exchange(blocks)
+
+
+def grid_call(kernel, grid, in_specs, out_specs, out_shape, name, args, **more):
+    return pl.pallas_call(
+        kernel,
+        grid=grid,
+        in_specs=in_specs,
+        out_specs=out_specs,
+        out_shape=out_shape,
+        compiler_params=pltpu.CompilerParams(vmem_limit_bytes=48 << 20),
+        name=name,
+        **more,
+    )(*args)
+
+
+def feed_grads(n, groups, act, grad_ffn, first, grad_pre):
+    tokens, hidden = act.shape
+    width = grad_ffn.shape[1]
+    down_rows = hidden // groups
+    shard = down_rows // n
+    shape = jax.ShapeDtypeStruct((2 * n, groups * shard, width), bf16)
+
+    def down_kernel(a, b, out):
+        out[...] = dot_tn(a[...], b[...]).astype(bf16).reshape(n, shard, width)
+
+    part = grid_call(
+        down_kernel,
+        (groups,),
+        [
+            pl.BlockSpec((tokens, down_rows), lambda g: (0, g)),
+            pl.BlockSpec((tokens, width), lambda g: (0, 0)),
+        ],
+        pl.BlockSpec((n, shard, width), lambda g: (0, g, 0)),
+        shape,
+        "down_grad",
+        (act, grad_ffn),
+    )
+    rows = min(256, width // n)
+    per = width // n // rows
+
+    def in_kernel(a, b, before, out):
+        out[0] = dot_tn(a[...], b[...]).astype(bf16)
+
+    return grid_call(
+        in_kernel,
+        (width // rows,),
+        [
+            pl.BlockSpec((tokens, rows), lambda g: (0, g)),
+            pl.BlockSpec((tokens, hidden), lambda g: (0, 0)),
+            pl.BlockSpec(memory_space=pl.ANY),
+        ],
+        pl.BlockSpec((1, rows, hidden), lambda g: (n + g // per, g % per, 0)),
+        shape,
+        "in_grad",
+        (first, grad_pre, part),
+        input_output_aliases={2: 0},
+    )
+
+
+def attn_grads(n, tok, grad_qkv, mixed, grad_attn):
+    tokens, width = tok.shape
+    part = width // n
+    rows = min(256, part)
+    per = part // rows
+
+    def kernel(x, g, m, ga, out):
+        out[0, :, : 3 * part] = dot_tn(x[...], g[...]).astype(bf16)
+        out[0, :, 3 * part :] = dot_tn(m[...], ga[...]).astype(bf16)
+
+    return grid_call(
+        kernel,
+        (n, per),
+        [
+            pl.BlockSpec((tokens, rows), lambda j, h: (0, j * per + h)),
+            pl.BlockSpec((tokens, 3 * part), lambda j, h: (0, 0)),
+            pl.BlockSpec((tokens, rows), lambda j, h: (0, h)),
+            pl.BlockSpec((tokens, part), lambda j, h: (0, j)),
+        ],
+        pl.BlockSpec((1, rows, 4 * part), lambda j, h: (j, h, 0)),
+        jax.ShapeDtypeStruct((n, part, 4 * part), bf16),
+        "attn_grads",
+        (tok, grad_qkv, mixed, grad_attn),
+    )
+
+
+def gather_dp(shard):
+    full = lax.all_gather(shard, "dp", axis=shard.ndim - 2, tiled=True)
+    return full.reshape(-1, full.shape[-1])
+
+
+def scatter_dp(grad):
+    return lax.psum_scatter(grad, "dp", scatter_dimension=grad.ndim - 2, tiled=True)
 
 
 def all_small(vectors):
@@ -214,6 +374,7 @@
     cotangent,
 ):
     n = lax.axis_size("seq")
+    groups = lax.axis_size("dp")
     s = lax.axis_index("seq")
     rows = tokens.shape[1]
     width = tokens.shape[2]
@@ -228,17 +389,23 @@
         [qv_bias, out_bias, norm1_gain, norm1_bias, in_bias, down_bias, norm2_gain, norm2_bias]
     )
     qv_full, out_b, gain_one, shift_one, in_b, down_b, gain_two, shift_two = small
-    qkv_w = columns_to_owner(qkv_weight, 3)
-    out_w = lax.all_gather(out_weight, "dp", axis=0, tiled=True)
-    in_w = columns_to_owner(in_weight, 1)
-    down_w = lax.all_gather(down_weight, "dp", axis=0, tiled=True)
-
-    tok_full = gather_seq(tok_rows)
+    out_w = gather_dp(out_weight)
+    qkv_packed = pack_columns(qkv_weight, 3)
+    qkv_moved = join_rows(exchange(qkv_packed))
+    qkv_w = gather_dp(after(qkv_moved, out_w, small))
+    tok_blocks = gather_blocks(after(tok_rows, qkv_packed))
+    tok_full = jnp.concatenate(tok_blocks, axis=0)
+    down_w = gather_dp(after(down_weight, qkv_moved))
+    in_packed = after(pack_columns(in_weight, 1), tok_blocks)
+    in_blocks = exchange(in_packed)
+
     q_bias = lax.dynamic_slice_in_dim(qv_full, s * part, part)
     v_bias = lax.dynamic_slice_in_dim(qv_full, width + s * part, part)
     qkv_b = jnp.concatenate([q_bias, jnp.zeros((part,), f32), v_bias])
     qkv = (dot_nn(tok_full, qkv_w) + qkv_b).astype(bf16)
     mixed = attend(qkv, seg)
+    in_blocks, mixed = lax.optimization_barrier((in_blocks, mixed))
+    in_w = gather_dp(join_rows(in_blocks))
     attn = scatter_seq(dot_nn(mixed, out_w)) + out_b
     normed_one, recip_one = normalize(tok_rows.astype(f32) + attn)
     first = normed_one * gain_one + shift_one
@@ -246,7 +413,7 @@
     hidden = in_w.shape[1]
     pre = dot_nn(first_full, in_w) + lax.dynamic_slice_in_dim(in_b, s * hidden, hidden)
     act_value, act_slope = gelu_parts(pre)
-    act = act_value.astype(bf16)
+    act, act_slope = lax.optimization_barrier((act_value.astype(bf16), act_slope.astype(bf16)))
     ffn = scatter_seq(dot_nn(act, down_w)) + down_b
     normed_two, recip_two = normalize(first + ffn)
     result = (normed_two * gain_two + shift_two).astype(bf16)
@@ -258,11 +425,24 @@
     grad_ffn = grad_h2.astype(bf16)
     down_b_grad = jnp.sum(grad_ffn.astype(f32), axis=0)
     grad_ffn_full = gather_seq(grad_ffn)
-    grad_pre = (dot_nt(grad_ffn_full, down_w) * act_slope).astype(bf16)
-    grad_first = grad_h2 + scatter_seq(dot_nt(grad_pre, in_w))
-    down_w_grad = rows_back(dot_tn(act, grad_ffn_full))
+    grad_pre = (dot_nt(grad_ffn_full, down_w) * act_slope.astype(f32)).astype(bf16)
+    back_blocks = scatter_blocks(dot_nt(grad_pre, in_w))
     in_b_grad = jnp.sum(grad_pre.astype(f32), axis=0)
-    in_w_grad = columns_back(dot_tn(first_full, grad_pre), 1)
+    merge = down_w.shape[0] == width
+    if merge:
+        low = feed_grads(n, groups, act, grad_ffn_full, first_full, grad_pre)
+    else:
+        down_low = dot_tn(act, grad_ffn_full).astype(bf16)
+        low = (down_low, dot_tn(first_full, grad_pre).astype(bf16).reshape(n, part, -1))
+    back_blocks, low = lax.optimization_barrier((back_blocks, low))
+    grad_first = grad_h2 + total_of(back_blocks)
+    if merge:
+        mine = scatter_dp(low)
+        down_mine = mine[:n].reshape(-1, width)
+        in_mine = mine[n:]
+    else:
+        down_mine = scatter_dp(low[0])
+        in_mine = scatter_dp(low[1])
 
     shift_one_grad = jnp.sum(grad_first, axis=0)
     gain_one_grad = jnp.sum(grad_first * normed_one, axis=0)
@@ -272,9 +452,14 @@
     grad_attn_full = gather_seq(grad_attn)
     grad_mixed = dot_nt(grad_attn_full, out_w).astype(bf16)
     grad_qkv = attend_back(qkv, grad_mixed, seg)
-    out_w_grad = rows_back(dot_tn(mixed, grad_attn_full))
-    qkv_w_grad = columns_back(dot_tn(tok_full, grad_qkv), 3)
-    input_grad = (grad_h1 + scatter_seq(dot_nt(grad_qkv, qkv_w))).astype(bf16)
+    last_blocks = scatter_blocks(dot_nt(grad_qkv, qkv_w))
+    attn_low = attn_grads(n, tok_full, grad_qkv, mixed, grad_attn_full)
+    attn_mine = scatter_dp(after(attn_low, in_mine))
+    input_grad = (grad_h1 + total_of(last_blocks)).astype(bf16)
+    down_w_grad = down_mine.astype(f32)
+    in_w_grad = join_columns(exchange_back(in_mine), 1)
+    out_w_grad = jnp.concatenate([attn_mine[j, :, 3 * part :] for j in range(n)], 1).astype(f32)
+    qkv_w_grad = join_columns(exchange_back(attn_mine[:, :, : 3 * part]), 3)
 
     sums = jnp.sum(grad_qkv.astype(f32), axis=0)
     qv_grad = jnp.zeros((2 * width,), f32)

time: 772 us -> 653 us (0.85)
  blocking collectives: 63.6 us -> 0 us
  waiting for transfers between devices: 427 us -> 371 us
  matrix products: 94.8 us -> 61.5 us
  Pallas kernels: 11.1 us -> 43.2 us
  starting transfers between devices: 79.6 us -> 99.8 us
  local copies, waits for them, and re-layouts: 48.9 us -> 35.2 us
    reduce_scatter x4 -> x2, waiting for transfers between devices: 111 us -> 42.6 us  [scatter_dp(): lax.psum_scatter(grad, 'dp', scatter_dimension=grad.ndim - 2, tiled=True)]
    all_to_all x3 -> x0, blocking collectives: 63.6 us -> none  [the longest x2 54.1 us: columns_to_owner(): moved = lax.all_to_all(pieces, 'seq', 0, 0)]
    all_to_all x1, waiting for transfers between devices: 38 us -> 0.43 us  [all_small(): lax.all_to_all(jnp.broadcast_to(packed[None], (count, packed.shape[0])),...]
    pallas_call x0 -> x9, Pallas kernels: none -> 32.2 us  [the longest x3 26.4 us: grid_call(): pl.pallas_call(kernel, grid=grid, in_specs=in_specs, out_specs=out_specs,...]
    dot_general x4 -> x0, matrix products: 31.5 us -> none  [dot_tn(): lax.dot_general(a, b, (((0,), (0,)), ((), ())), preferred_element_type=f32)]
    all_to_all x2 -> x1, waiting for transfers between devices: 11.7 us -> 42.9 us  [scatter_small(): mine = jnp.sum(lax.all_to_all(packed, ALL, 0, 0), axis=0)]
    ppermute x24 -> x36, starting transfers between devices: 64.3 us -> 89.7 us  [shift(): return lax.ppermute(value, 'seq', [(i, (i + step) % n) for i in range(n)])]
    ppermute x24 -> x36, waiting for transfers between devices: 265 us -> 283 us  [shift(): return lax.ppermute(value, 'seq', [(i, (i + step) % n) for i in range(n)])]
  transfers between devices with their start and end apart: 35 -> 44, of which waited for: 19 -> 22; matrix products, arithmetic and copies ran while one was open for 13% -> 12% of each run, Pallas kernels for 1% -> 6%
where the time goes in v2:
time: 653 us; the launch traced here: 649 us
  waiting for transfers between devices  371 us (57%)
  starting transfers between devices  99.8 us (15%)
  matrix products  61.5 us (9%)
  Pallas kernels  43.2 us (7%)
  local copies, waits for them, and re-layouts  35.2 us (5%)
  other arithmetic  24.1 us (4%)
  between operations  14.6 us (2%)
    ppermute x36, waiting for transfers between devices, shift(): return lax.ppermute(value, 'seq', [(i, (i + step) % n) for i in range(n)])  283 us
    ppermute x36, starting transfers between devices, shift(): return lax.ppermute(value, 'seq', [(i, (i + step) % n) for i in range(n)])  89.7 us
    all_to_all x1, waiting for transfers between devices, scatter_small(): mine = jnp.sum(lax.all_to_all(packed, ALL, 0, 0), axis=0)  42.9 us
    reduce_scatter x2, waiting for transfers between devices, scatter_dp(): lax.psum_scatter(grad, 'dp', scatter_dimension=grad.ndim - 2, tiled=True)  42.6 us
    dot_general x4, matrix products, dot_nn(): lax.dot_general(a, b, (((1,), (0,)), ((), ())), preferred_element_type=f32)  35.1 us
    pallas_call x3, Pallas kernels, grid_call(): pl.pallas_call(kernel, grid=grid, in_specs=in_specs, out_specs=out_specs,...  26.4 us
    dot_general x4, matrix products, dot_nt(): lax.dot_general(a, b, (((1,), (1,)), ((), ())), preferred_element_type=f32)  26.4 us
  transfers between devices with their start and end apart: 44, of which 22 were waited for; matrix products, arithmetic and copies ran while one was open for 12% of the time, Pallas kernels for 6%

profile of v2, /device:TPU:0, one launch (start us, length us, event | category | flops | bytes accessed | tf_op | source)
XLA Modules:
  0.0 649.2 jit_solution(11574264052518491305)
XLA Ops:
  7.9 5.4 concatenate.25
  15.5 7.3 %all-to-all-start = ((bf16[32,2,384]{2,1,0:T(2,128)(2,1)}), bf16[32,2,384]{2,1,0:T(2,128)(2,1)S(1)}, u32[]{:S(2)}, u32[]{:S(2)}) async-start(bf16[32,2,384]{2,1,0:T(2,128)(2,1)} %reshape.254), calls=%async_computation | async-start | bytes 98304 | tf_op jit(solution)/shard_map/all_to_all | solution.py:328
  25.9 2.4 collective-permute-start.7
  30.9 2.9 collective-permute-done.6.refs_1_
  33.8 7.7 %collective-permute-done.7.refs_2_ = bf16[64,1536]{1,0:T(8,128)(2,1)S(1)} collective-permute-done((bf16[64,1536]{1,0:T(8,128)(2,1)S(1)}, bf16[64,1536]{1,0:T(8,128)(2,1)S(1)}, u32[]{:S(2)}, u32[]{:S(2)}) %collective-permute-start.7) | collective-permute-done | bytes 196640 | tf_op jit(solution)/shard_map/ppermute | solution.py:19
  42.5 4.7 collective-permute-start
  52.0 9.5 %collective-permute-done = bf16[128,2048]{1,0:T(8,128)(2,1)S(1)} collective-permute-done((bf16[128,2048]{1,0:T(8,128)(2,1)}, bf16[128,2048]{1,0:T(8,128)(2,1)S(1)}, u32[]{:S(2)}, u32[]{:S(2)}) %collective-permute-start) | collective-permute-done | bytes 524320 | tf_op jit(solution)/shard_map/ppermute | solution.py:19
  61.5 21.2 %collective-permute-done.1 = bf16[128,2048]{1,0:T(8,128)(2,1)} collective-permute-done((bf16[128,2048]{1,0:T(8,128)(2,1)}, bf16[128,2048]{1,0:T(8,128)(2,1)}, u32[]{:S(2)}, u32[]{:S(2)}) %collective-permute-start.1) | collective-permute-done | bytes 524320 | tf_op jit(solution)/shard_map/ppermute | solution.py:19
  82.7 11.7 %collective-permute-start.3 = (bf16[64,2048]{1,0:T(8,128)(2,1)}, bf16[64,2048]{1,0:T(8,128)(2,1)S(1)}, u32[]{:S(2)}, u32[]{:S(2)}) collective-permute-start(bf16[64,2048]{1,0:T(8,128)(2,1)} %get-tuple-element.52), channel_id=1, source_target_pairs={{0,8},{8,16},{16,24},{24,0},{1,9},{9,17},{17,25},{25,1},{2,10},{10... | collective-permute-start | bytes 786440 | tf_op jit(solution)/shard_map/ppermute | solution.py:19
  102.4 6.8 %fusion.6.q.k.v = bf16[512,1536]{1,0:T(8,128)(2,1)S(1)} fusion(bf16[512,2048]{1,0:T(8,128)(2,1)} %constant_dynamic-update-slice_fusion.x, bf16[2048,1536]{1,0:T(8,128)(2,1)} %bitcast.107, f32[1536]{0:T(1024)S(1)} %pad_maximum_fusion.3), kind=kOutput, calls=%fused_computation.13 | convolution fusion | flops 3222798336 | bytes 9967616 | tf_op jit(solution)/shard_map/dot_general | solution.py:68
  109.2 4.7 attend.1.m
  115.7 4.9 fusion.57
  121.8 5.4 collective-permute-start.11
  131.1 10.1 %collective-permute-done.11 = bf16[128,2048]{1,0:T(8,128)(2,1)S(1)} collective-permute-done((bf16[128,2048]{1,0:T(8,128)(2,1)}, bf16[128,2048]{1,0:T(8,128)(2,1)S(1)}, u32[]{:S(2)}, u32[]{:S(2)}) %collective-permute-start.11) | collective-permute-done | bytes 524320 | tf_op jit(solution)/shard_map/ppermute | solution.py:19
  141.2 21.2 %collective-permute-done.10 = bf16[128,2048]{1,0:T(8,128)(2,1)S(1)} collective-permute-done((bf16[128,2048]{1,0:T(8,128)(2,1)}, bf16[128,2048]{1,0:T(8,128)(2,1)S(1)}, u32[]{:S(2)}, u32[]{:S(2)}) %collective-permute-start.10) | collective-permute-done | bytes 524320 | tf_op jit(solution)/shard_map/ppermute | solution.py:19
  166.1 13.1 %collective-permute-start.14 = (bf16[128,2048]{1,0:T(8,128)(2,1)S(1)}, bf16[128,2048]{1,0:T(8,128)(2,1)}, u32[]{:S(2)}, u32[]{:S(2)}) collective-permute-start(bf16[128,2048]{1,0:T(8,128)(2,1)S(1)} %fusion.28), channel_id=1, source_target_pairs={{0,24},{8,0},{16,8},{24,16},{1,25},{9,1},{17,9},{25,17},{2,26},{10... | collective-permute-start | bytes 1572872 | tf_op jit(solution)/shard_map/ppermute | solution.py:19
  180.5 11.1 %collective-permute-done.14 = bf16[128,2048]{1,0:T(8,128)(2,1)} collective-permute-done((bf16[128,2048]{1,0:T(8,128)(2,1)S(1)}, bf16[128,2048]{1,0:T(8,128)(2,1)}, u32[]{:S(2)}, u32[]{:S(2)}) %collective-permute-start.14) | collective-permute-done | bytes 524320 | tf_op jit(solution)/shard_map/ppermute | solution.py:19
  191.6 32.6 %collective-permute-done.13 = bf16[128,2048]{1,0:T(8,128)(2,1)} collective-permute-done((bf16[128,2048]{1,0:T(8,128)(2,1)S(1)}, bf16[128,2048]{1,0:T(8,128)(2,1)}, u32[]{:S(2)}, u32[]{:S(2)}) %collective-permute-start.13) | collective-permute-done | bytes 524320 | tf_op jit(solution)/shard_map/ppermute | solution.py:19
  224.2 12.9 %fusion.5 = (bf16[512,2048]{1,0:T(8,128)(2,1)}, bf16[512,2048]{1,0:T(8,128)(2,1)}) fusion(f32[2048]{0:T(1024)S(1)} %dynamic_slice.37, bf16[2048,2048]{1,0:T(8,128)(2,1)} %bitcast.105, bf16[128,2048]{1,0:T(8,128)(2,1)} %collective-permute-done.14, bf16[128,2048]{1,0:T(8,128)(2,1)} %collective-permute-done.13, bf16[128,2048]{1,0:T(8,128)(2,1)} %collective-permute-done.12, ...), kind=kOutput, calls=%fused_computation.7 | convolution fusion | flops 4325376000 | bytes 14688256 | tf_op jit(solution)/shard_map/dot_general | solution.py:68
  237.1 10.5 %fusion.58 = (bf16[512,2048]{1,0:T(8,128)(2,1)S(1)}, f32[512,2048]{1,0:T(8,128)}) fusion(bf16[512,2048]{1,0:T(8,128)(2,1)} %get-tuple-element.61.a, bf16[2048,2048]{1,0:T(8,128)(2,1)} %all-gather.11.cloned.1.call-done), kind=kOutput, calls=%fused_computation.130 | convolution fusion | flops 4296015872 | bytes 16777216 | tf_op jit(solution)/shard_map/dot_general | solution.py:68
  251.0 2.9 collective-permute-start.15
  254.1 11.8 %collective-permute-done.17 = bf16[128,2048]{1,0:T(8,128)(2,1)} collective-permute-done((bf16[128,2048]{1,0:T(8,128)(2,1)}, bf16[128,2048]{1,0:T(8,128)(2,1)}, u32[]{:S(2)}, u32[]{:S(2)}) %collective-permute-start.17) | collective-permute-done | bytes 524320 | tf_op jit(solution)/shard_map/ppermute | solution.py:19
  265.9 20.7 %collective-permute-done.16 = bf16[128,2048]{1,0:T(8,128)(2,1)} collective-permute-done((bf16[128,2048]{1,0:T(8,128)(2,1)}, bf16[128,2048]{1,0:T(8,128)(2,1)}, u32[]{:S(2)}, u32[]{:S(2)}) %collective-permute-start.16) | collective-permute-done | bytes 524320 | tf_op jit(solution)/shard_map/ppermute | solution.py:19
  286.6 2.5 fusion.46
  290.3 12.3 %collective-permute-start.20 = (bf16[128,2048]{1,0:T(8,128)(2,1)S(1)}, bf16[128,2048]{1,0:T(8,128)(2,1)S(1)}, u32[]{:S(2)}, u32[]{:S(2)}) collective-permute-start(bf16[128,2048]{1,0:T(8,128)(2,1)S(1)} %get-tuple-element.78), channel_id=1, source_target_pairs={{0,24},{8,0},{16,8},{24,16},{1,25},{9,1},{17,9},{25,17},{2,26},{10... | collective-permute-start | bytes 1572872 | tf_op jit(solution)/shard_map/ppermute | solution.py:19
  303.3 11.8 %collective-permute-done.20 = bf16[128,2048]{1,0:T(8,128)(2,1)S(1)} collective-permute-done((bf16[128,2048]{1,0:T(8,128)(2,1)S(1)}, bf16[128,2048]{1,0:T(8,128)(2,1)S(1)}, u32[]{:S(2)}, u32[]{:S(2)}) %collective-permute-start.20) | collective-permute-done | bytes 524320 | tf_op jit(solution)/shard_map/ppermute | solution.py:19
  315.0 32.1 %collective-permute-done.19 = bf16[128,2048]{1,0:T(8,128)(2,1)S(1)} collective-permute-done((bf16[128,2048]{1,0:T(8,128)(2,1)S(1)}, bf16[128,2048]{1,0:T(8,128)(2,1)S(1)}, u32[]{:S(2)}, u32[]{:S(2)}) %collective-permute-start.19) | collective-permute-done | bytes 524320 | tf_op jit(solution)/shard_map/ppermute | solution.py:19
  347.1 10.0 %convert_reduce_fusion = (f32[2048]{0:T(1024)S(1)}, bf16[512,2048]{1,0:T(8,128)(2,1)S(1)}) fusion(bf16[512,2048]{1,0:T(8,128)(2,1)S(1)} %copy-done.20, bf16[2048,2048]{1,0:T(8,128)(2,1)} %all-gather.11.cloned.1.call-done, bf16[128,2048]{1,0:T(8,128)(2,1)S(1)} %collective-permute-done.20, bf16[128,2048]{1,0:T(8,128)(2,1)S(1)} %collective-permute-done.19, ...), kind=kOutput, calls=%fused_computation.8 | convolution fusion | flops 4308596736 | bytes 14688256 | tf_op jit(solution)/shard_map/dot_general | solution.py:72
  357.2 7.2 %fusion.59 = (bf16[512,2048]{1,0:T(8,128)(2,1)S(1)}, f32[512,2048]{1,0:T(8,128)S(1)}) fusion(bf16[512,2048]{1,0:T(8,128)(2,1)S(1)} %get-tuple-element.139.b, bf16[2048,2048]{1,0:T(8,128)(2,1)} %bitcast.106), kind=kOutput, calls=%fused_computation.131 | convolution fusion | flops 4296015872 | bytes 16777216 | tf_op jit(solution)/shard_map/dot_general | solution.py:72
  372.6 7.9 %down_grad.1.before = bf16[8,512,2048]{2,1,0:T(8,128)(2,1)} custom-call(bf16[512,2048]{1,0:T(8,128)(2,1)S(1)} %copy-done.2, bf16[512,2048]{1,0:T(8,128)(2,1)S(1)} %pad_maximum_fusion.1.b), custom_call_target="tpu_custom_call" | custom-call | tf_op jit(solution)/shard_map/down_grad/pallas_call | solution.py:234
  380.4 7.9 %in_grad.1 = bf16[8,512,2048]{2,1,0:T(8,128)(2,1)} custom-call(bf16[512,2048]{1,0:T(8,128)(2,1)S(1)} %pad_maximum_fusion.a, bf16[512,2048]{1,0:T(8,128)(2,1)S(1)} %get-tuple-element.139.b, bf16[8,512,2048]{2,1,0:T(8,128)(2,1)} %down_grad.1.before), custom_call_target="tpu_custom_call", output_to_operand_aliasing={{}: (2, {})} | custom-call | tf_op jit(solution)/shard_map/in_grad/pallas_call | solution.py:234
  388.3 23.9 %collective-permute-done.22 = bf16[128,2048]{1,0:T(8,128)(2,1)} collective-permute-done((bf16[128,2048]{1,0:T(8,128)(2,1)}, bf16[128,2048]{1,0:T(8,128)(2,1)}, u32[]{:S(2)}, u32[]{:S(2)}) %collective-permute-start.22) | collective-permute-done | bytes 524320 | tf_op jit(solution)/shard_map/ppermute | solution.py:19
  412.3 4.0 multiply_reduce_fusion
  420.4 9.9 %collective-permute-done.26 = bf16[128,2048]{1,0:T(8,128)(2,1)S(1)} collective-permute-done((bf16[128,2048]{1,0:T(8,128)(2,1)S(1)}, bf16[128,2048]{1,0:T(8,128)(2,1)S(1)}, u32[]{:S(2)}, u32[]{:S(2)}) %collective-permute-start.26) | collective-permute-done | bytes 524320 | tf_op jit(solution)/shard_map/ppermute | solution.py:19
  430.3 33.9 %collective-permute-done.25 = bf16[128,2048]{1,0:T(8,128)(2,1)S(1)} collective-permute-done((bf16[128,2048]{1,0:T(8,128)(2,1)S(1)}, bf16[128,2048]{1,0:T(8,128)(2,1)S(1)}, u32[]{:S(2)}, u32[]{:S(2)}) %collective-permute-start.25) | collective-permute-done | bytes 524320 | tf_op jit(solution)/shard_map/ppermute | solution.py:19
  465.5 6.4 attend_back.1.g
  473.5 10.6 %attn_grads.1 = bf16[4,512,2048]{2,1,0:T(8,128)(2,1)} custom-call(bf16[512,2048]{1,0:T(8,128)(2,1)} %constant_dynamic-update-slice_fusion.x, bf16[512,1536]{1,0:T(8,128)(2,1)S(1)} %attend_back.1.g, bf16[512,512]{1,0:T(8,128)(2,1)S(1)} %copy-done.1, bf16[512,2048]{1,0:T(8,128)(2,1)} %pad_maximum_fusion.2.ga), custom_call_target="tpu_custom_call" | custom-call | tf_op jit(solution)/shard_map/attn_grads/pallas_call | solution.py:234
  484.2 42.6 %reduce-scatter.3.cloned.1.call-done = bf16[8,64,2048]{2,1,0:T(8,128)(2,1)} async-done(((bf16[8,512,2048]{2,1,0:T(8,128)(2,1)}), bf16[8,64,2048]{2,1,0:T(8,128)(2,1)}) %reduce-scatter.3.cloned.1.call-update) | async-done | bytes 2097168 | tf_op jit(solution)/shard_map/reduce_scatter | solution.py:322
  526.7 3.1 fusion.50
  531.7 7.9 %fusion.60 = (bf16[512,2048]{1,0:T(8,128)(2,1)S(1)}, f32[512,2048]{1,0:T(8,128)}) fusion(bf16[512,1536]{1,0:T(8,128)(2,1)S(1)} %attend_back.1.g, bf16[2048,1536]{1,0:T(8,128)(2,1)} %bitcast.108), kind=kOutput, calls=%fused_computation.132 | convolution fusion | flops 3222274048 | bytes 14155776 | tf_op jit(solution)/shard_map/dot_general | solution.py:72
  547.3 2.6 all-to-all-start.1
  549.9 42.9 %all-to-all-done.1 = f32[32,1,768]{2,1,0:T(1,128)S(1)} async-done(((f32[32,1,768]{2,1,0:T(1,128)}), f32[32,1,768]{2,1,0:T(1,128)S(1)}, u32[]{:S(2)}, u32[]{:S(2)}) %all-to-all-start.1) | async-done | bytes 98336 | tf_op jit(solution)/shard_map/all_to_all | solution.py:341
  594.7 2.8 fusion.30
  602.7 2.8 bitcast_convert_fusion
  605.5 4.5 collective-permute-done.33.refs_1_
  609.9 10.5 %collective-permute-done.34.refs_2_ = bf16[64,2048]{1,0:T(8,128)(2,1)S(1)} collective-permute-done((bf16[64,2048]{1,0:T(8,128)(2,1)S(1)}, bf16[64,2048]{1,0:T(8,128)(2,1)S(1)}, u32[]{:S(2)}, u32[]{:S(2)}) %collective-permute-start.34) | collective-permute-done | bytes 262176 | tf_op jit(solution)/shard_map/ppermute | solution.py:19
  623.1 5.6 collective-permute-start.30
  634.1 7.0 %collective-permute-done.31.refs_2_ = bf16[64,1536]{1,0:T(8,128)(2,1)S(1)} collective-permute-done((bf16[64,1536]{1,0:T(8,128)(2,1)S(1)}, bf16[64,1536]{1,0:T(8,128)(2,1)S(1)}, u32[]{:S(2)}, u32[]{:S(2)}) %collective-permute-start.31) | collective-permute-done | bytes 196640 | tf_op jit(solution)/shard_map/ppermute | solution.py:19
  (188 shorter events, 80.4 us)
Async XLA Ops:
  7.2 35.3 %all-gather.5.cloned.1.call-start = ((), (), s32[]{:S(2)}) async-start(), calls=%async_computation.4 | async-start | bytes 2359296 | tf_op jit(solution)/shard_map/all_gather | solution.py:317
  15.5 14.6 %all-to-all-start = ((bf16[32,2,384]{2,1,0:T(2,128)(2,1)}), bf16[32,2,384]{2,1,0:T(2,128)(2,1)S(1)}, u32[]{:S(2)}, u32[]{:S(2)}) async-start(bf16[32,2,384]{2,1,0:T(2,128)(2,1)} %reshape.254), calls=%async_computation | async-start | bytes 98304 | tf_op jit(solution)/shard_map/all_to_all | solution.py:328
  22.8 79.6 %all-gather.7.cloned.1.call-start = ((), (), s32[]{:S(2)}) async-start(), calls=%async_computation.5 | async-start | bytes 7077888 | tf_op jit(solution)/shard_map/all_gather | solution.py:317
  24.0 9.7 %collective-permute-start.6 = (bf16[64,1536]{1,0:T(8,128)(2,1)S(1)}, bf16[64,1536]{1,0:T(8,128)(2,1)S(1)}, u32[]{:S(2)}, u32[]{:S(2)}) collective-permute-start(bf16[64,1536]{1,0:T(8,128)(2,1)S(1)} %get-tuple-element.47), channel_id=1, source_target_pairs={{0,8},{8,16},{16,24},{24,0},{1,9},{9,17},{17,25},{25,1},{2,10},{10... | collective-permute-start | bytes 589832 | tf_op jit(solution)/shard_map/ppermute | solution.py:19
  25.9 15.6 %collective-permute-start.7 = (bf16[64,1536]{1,0:T(8,128)(2,1)S(1)}, bf16[64,1536]{1,0:T(8,128)(2,1)S(1)}, u32[]{:S(2)}, u32[]{:S(2)}) collective-permute-start(bf16[64,1536]{1,0:T(8,128)(2,1)S(1)} %get-tuple-element.48), channel_id=1, source_target_pairs={{0,16},{8,24},{16,0},{24,8},{1,17},{9,25},{17,1},{25,9},{2,18},{10... | collective-permute-start | bytes 589832 | tf_op jit(solution)/shard_map/ppermute | solution.py:19
  28.3 13.2 %collective-permute-start.8 = (bf16[64,1536]{1,0:T(8,128)(2,1)S(1)}, bf16[64,1536]{1,0:T(8,128)(2,1)S(1)}, u32[]{:S(2)}, u32[]{:S(2)}) collective-permute-start(bf16[64,1536]{1,0:T(8,128)(2,1)S(1)} %get-tuple-element.49), channel_id=1, source_target_pairs={{0,24},{8,0},{16,8},{24,16},{1,25},{9,1},{17,9},{25,17},{2,26},{10... | collective-permute-start | bytes 589832 | tf_op jit(solution)/shard_map/ppermute | solution.py:19
  42.5 181.7 %all-gather.9.cloned.1.call-start = ((), (), s32[]{:S(2)}) async-start(), calls=%async_computation.6 | async-start | bytes 9437184 | tf_op jit(solution)/shard_map/all_gather | solution.py:317
  42.5 19.0 %collective-permute-start = (bf16[128,2048]{1,0:T(8,128)(2,1)}, bf16[128,2048]{1,0:T(8,128)(2,1)S(1)}, u32[]{:S(2)}, u32[]{:S(2)}) collective-permute-start(bf16[128,2048]{1,0:T(8,128)(2,1)} %bitcast.95), channel_id=1, source_target_pairs={{0,8},{8,16},{16,24},{24,0},{1,9},{9,17},{17,25},{25,1},{2,10},{10... | collective-permute-start | bytes 1572872 | tf_op jit(solution)/shard_map/ppermute | solution.py:19
  47.3 35.4 %collective-permute-start.1 = (bf16[128,2048]{1,0:T(8,128)(2,1)}, bf16[128,2048]{1,0:T(8,128)(2,1)}, u32[]{:S(2)}, u32[]{:S(2)}) collective-permute-start(bf16[128,2048]{1,0:T(8,128)(2,1)} %bitcast.96), channel_id=1, source_target_pairs={{0,16},{8,24},{16,0},{24,8},{1,17},{9,25},{17,1},{25,9},{2,18},{10... | collective-permute-start | bytes 1572872 | tf_op jit(solution)/shard_map/ppermute | solution.py:19
  48.9 33.8 %collective-permute-start.2 = (bf16[128,2048]{1,0:T(8,128)(2,1)}, bf16[128,2048]{1,0:T(8,128)(2,1)}, u32[]{:S(2)}, u32[]{:S(2)}) collective-permute-start(bf16[128,2048]{1,0:T(8,128)(2,1)} %bitcast.97), channel_id=1, source_target_pairs={{0,24},{8,0},{16,8},{24,16},{1,25},{9,1},{17,9},{25,17},{2,26},{10... | collective-permute-start | bytes 1572872 | tf_op jit(solution)/shard_map/ppermute | solution.py:19
  82.7 31.2 %collective-permute-start.3 = (bf16[64,2048]{1,0:T(8,128)(2,1)}, bf16[64,2048]{1,0:T(8,128)(2,1)S(1)}, u32[]{:S(2)}, u32[]{:S(2)}) collective-permute-start(bf16[64,2048]{1,0:T(8,128)(2,1)} %get-tuple-element.52), channel_id=1, source_target_pairs={{0,8},{8,16},{16,24},{24,0},{1,9},{9,17},{17,25},{25,1},{2,10},{10... | collective-permute-start | bytes 786440 | tf_op jit(solution)/shard_map/ppermute | solution.py:19
  94.4 19.5 %collective-permute-start.4 = (bf16[64,2048]{1,0:T(8,128)(2,1)}, bf16[64,2048]{1,0:T(8,128)(2,1)S(1)}, u32[]{:S(2)}, u32[]{:S(2)}) collective-permute-start(bf16[64,2048]{1,0:T(8,128)(2,1)} %get-tuple-element.53), channel_id=1, source_target_pairs={{0,16},{8,24},{16,0},{24,8},{1,17},{9,25},{17,1},{25,9},{2,18},{10... | collective-permute-start | bytes 786440 | tf_op jit(solution)/shard_map/ppermute | solution.py:19
  96.3 17.6 %collective-permute-start.5 = (bf16[64,2048]{1,0:T(8,128)(2,1)}, bf16[64,2048]{1,0:T(8,128)(2,1)S(1)}, u32[]{:S(2)}, u32[]{:S(2)}) collective-permute-start(bf16[64,2048]{1,0:T(8,128)(2,1)} %get-tuple-element.54), channel_id=1, source_target_pairs={{0,24},{8,0},{16,8},{24,16},{1,25},{9,1},{17,9},{25,17},{2,26},{10... | collective-permute-start | bytes 786440 | tf_op jit(solution)/shard_map/ppermute | solution.py:19
  115.0 122.1 %all-gather.11.cloned.1.call-start = ((), (), s32[]{:S(2)}) async-start(), calls=%async_computation.7 | async-start | bytes 9437184 | tf_op jit(solution)/shard_map/all_gather | solution.py:317
  115.6 411.1 %reduce-scatter.3.cloned.1.call-start = ((), (), s32[]{:S(2)}) async-start(), calls=%async_computation.8 | async-start | bytes 18874368 | tf_op jit(solution)/shard_map/reduce_scatter | solution.py:322
  121.8 19.5 %collective-permute-start.11 = (bf16[128,2048]{1,0:T(8,128)(2,1)}, bf16[128,2048]{1,0:T(8,128)(2,1)S(1)}, u32[]{:S(2)}, u32[]{:S(2)}) collective-permute-start(bf16[128,2048]{1,0:T(8,128)(2,1)} %get-tuple-element.101), channel_id=1, source_target_pairs={{0,8},{8,16},{16,24},{24,0},{1,9},{9,17},{17,25},{25,1},{2,10},{10... | collective-permute-start | bytes 1572872 | tf_op jit(solution)/shard_map/ppermute | solution.py:19
  127.2 35.3 %collective-permute-start.10 = (bf16[128,2048]{1,0:T(8,128)(2,1)}, bf16[128,2048]{1,0:T(8,128)(2,1)S(1)}, u32[]{:S(2)}, u32[]{:S(2)}) collective-permute-start(bf16[128,2048]{1,0:T(8,128)(2,1)} %get-tuple-element.102), channel_id=1, source_target_pairs={{0,16},{8,24},{16,0},{24,8},{1,17},{9,25},{17,1},{25,9},{2,18},{10... | collective-permute-start | bytes 1572872 | tf_op jit(solution)/shard_map/ppermute | solution.py:19
  128.6 33.8 %collective-permute-start.9 = (bf16[128,2048]{1,0:T(8,128)(2,1)}, bf16[128,2048]{1,0:T(8,128)(2,1)}, u32[]{:S(2)}, u32[]{:S(2)}) collective-permute-start(bf16[128,2048]{1,0:T(8,128)(2,1)} %get-tuple-element.100), channel_id=1, source_target_pairs={{0,24},{8,0},{16,8},{24,16},{1,25},{9,1},{17,9},{25,17},{2,26},{10... | collective-permute-start | bytes 1572872 | tf_op jit(solution)/shard_map/ppermute | solution.py:19
  166.1 71.0 %copy-start.12 = (bf16[128,2048]{1,0:T(8,128)(2,1)}, bf16[128,2048]{1,0:T(8,128)(2,1)S(1)}, u32[]{:S(2)}) copy-start(bf16[128,2048]{1,0:T(8,128)(2,1)S(1)} %fusion.28) | copy-start | bytes 1572868
  166.1 25.5 %collective-permute-start.14 = (bf16[128,2048]{1,0:T(8,128)(2,1)S(1)}, bf16[128,2048]{1,0:T(8,128)(2,1)}, u32[]{:S(2)}, u32[]{:S(2)}) collective-permute-start(bf16[128,2048]{1,0:T(8,128)(2,1)S(1)} %fusion.28), channel_id=1, source_target_pairs={{0,24},{8,0},{16,8},{24,16},{1,25},{9,1},{17,9},{25,17},{2,26},{10... | collective-permute-start | bytes 1572872 | tf_op jit(solution)/shard_map/ppermute | solution.py:19
  179.2 45.0 %collective-permute-start.13 = (bf16[128,2048]{1,0:T(8,128)(2,1)S(1)}, bf16[128,2048]{1,0:T(8,128)(2,1)}, u32[]{:S(2)}, u32[]{:S(2)}) collective-permute-start(bf16[128,2048]{1,0:T(8,128)(2,1)S(1)} %fusion.28), channel_id=1, source_target_pairs={{0,16},{8,24},{16,0},{24,8},{1,17},{9,25},{17,1},{25,9},{2,18},{10... | collective-permute-start | bytes 1572872 | tf_op jit(solution)/shard_map/ppermute | solution.py:19
  179.2 45.0 %collective-permute-start.12 = (bf16[128,2048]{1,0:T(8,128)(2,1)S(1)}, bf16[128,2048]{1,0:T(8,128)(2,1)}, u32[]{:S(2)}, u32[]{:S(2)}) collective-permute-start(bf16[128,2048]{1,0:T(8,128)(2,1)S(1)} %fusion.28), channel_id=1, source_target_pairs={{0,8},{8,16},{16,24},{24,0},{1,9},{9,17},{17,25},{25,1},{2,10},{10... | collective-permute-start | bytes 1572872 | tf_op jit(solution)/shard_map/ppermute | solution.py:19
  248.8 17.1 %collective-permute-start.17 = (bf16[128,2048]{1,0:T(8,128)(2,1)}, bf16[128,2048]{1,0:T(8,128)(2,1)}, u32[]{:S(2)}, u32[]{:S(2)}) collective-permute-start(bf16[128,2048]{1,0:T(8,128)(2,1)} %get-tuple-element.98), channel_id=1, source_target_pairs={{0,8},{8,16},{16,24},{24,0},{1,9},{9,17},{17,25},{25,1},{2,10},{10... | collective-permute-start | bytes 1572872 | tf_op jit(solution)/shard_map/ppermute | solution.py:19
  248.9 37.7 %collective-permute-start.16 = (bf16[128,2048]{1,0:T(8,128)(2,1)}, bf16[128,2048]{1,0:T(8,128)(2,1)}, u32[]{:S(2)}, u32[]{:S(2)}) collective-permute-start(bf16[128,2048]{1,0:T(8,128)(2,1)} %get-tuple-element.99), channel_id=1, source_target_pairs={{0,16},{8,24},{16,0},{24,8},{1,17},{9,25},{17,1},{25,9},{2,18},{10... | collective-permute-start | bytes 1572872 | tf_op jit(solution)/shard_map/ppermute | solution.py:19
  251.0 35.6 %collective-permute-start.15 = (bf16[128,2048]{1,0:T(8,128)(2,1)}, bf16[128,2048]{1,0:T(8,128)(2,1)}, u32[]{:S(2)}, u32[]{:S(2)}) collective-permute-start(bf16[128,2048]{1,0:T(8,128)(2,1)} %get-tuple-element.97), channel_id=1, source_target_pairs={{0,24},{8,0},{16,8},{24,16},{1,25},{9,1},{17,9},{25,17},{2,26},{10... | collective-permute-start | bytes 1572872 | tf_op jit(solution)/shard_map/ppermute | solution.py:19
  286.6 60.5 %copy-start.20 = (bf16[512,2048]{1,0:T(8,128)(2,1)S(1)}, bf16[512,2048]{1,0:T(8,128)(2,1)}, u32[]{:S(2)}) copy-start(bf16[512,2048]{1,0:T(8,128)(2,1)} %get-tuple-element.63) | copy-start | bytes 6291460
  289.1 58.0 %copy-start.5 = (f32[128,2048]{1,0:T(8,128)}, f32[128,2048]{1,0:T(8,128)S(1)}, u32[]{:S(2)}) copy-start(f32[128,2048]{1,0:T(8,128)S(1)} %get-tuple-element.84) | copy-start | bytes 3145732
  290.3 24.7 %collective-permute-start.20 = (bf16[128,2048]{1,0:T(8,128)(2,1)S(1)}, bf16[128,2048]{1,0:T(8,128)(2,1)S(1)}, u32[]{:S(2)}, u32[]{:S(2)}) collective-permute-start(bf16[128,2048]{1,0:T(8,128)(2,1)S(1)} %get-tuple-element.78), channel_id=1, source_target_pairs={{0,24},{8,0},{16,8},{24,16},{1,25},{9,1},{17,9},{25,17},{2,26},{10... | collective-permute-start | bytes 1572872 | tf_op jit(solution)/shard_map/ppermute | solution.py:19
  302.6 44.5 %collective-permute-start.19 = (bf16[128,2048]{1,0:T(8,128)(2,1)S(1)}, bf16[128,2048]{1,0:T(8,128)(2,1)S(1)}, u32[]{:S(2)}, u32[]{:S(2)}) collective-permute-start(bf16[128,2048]{1,0:T(8,128)(2,1)S(1)} %get-tuple-element.78), channel_id=1, source_target_pairs={{0,16},{8,24},{16,0},{24,8},{1,17},{9,25},{17,1},{25,9},{2,18},{10... | collective-permute-start | bytes 1572872 | tf_op jit(solution)/shard_map/ppermute | solution.py:19
  302.6 44.5 %collective-permute-start.18 = (bf16[128,2048]{1,0:T(8,128)(2,1)S(1)}, bf16[128,2048]{1,0:T(8,128)(2,1)S(1)}, u32[]{:S(2)}, u32[]{:S(2)}) collective-permute-start(bf16[128,2048]{1,0:T(8,128)(2,1)S(1)} %get-tuple-element.78), channel_id=1, source_target_pairs={{0,8},{8,16},{16,24},{24,0},{1,9},{9,17},{17,25},{25,1},{2,10},{10... | collective-permute-start | bytes 1572872 | tf_op jit(solution)/shard_map/ppermute | solution.py:19
  365.6 22.7 %collective-permute-start.21 = (bf16[128,2048]{1,0:T(8,128)(2,1)}, bf16[128,2048]{1,0:T(8,128)(2,1)}, u32[]{:S(2)}, u32[]{:S(2)}) collective-permute-start(bf16[128,2048]{1,0:T(8,128)(2,1)} %get-tuple-element.96), channel_id=1, source_target_pairs={{0,24},{8,0},{16,8},{24,16},{1,25},{9,1},{17,9},{25,17},{2,26},{10... | collective-permute-start | bytes 1572872 | tf_op jit(solution)/shard_map/ppermute | solution.py:19
  365.6 46.6 %collective-permute-start.22 = (bf16[128,2048]{1,0:T(8,128)(2,1)}, bf16[128,2048]{1,0:T(8,128)(2,1)}, u32[]{:S(2)}, u32[]{:S(2)}) collective-permute-start(bf16[128,2048]{1,0:T(8,128)(2,1)} %get-tuple-element.95), channel_id=1, source_target_pairs={{0,16},{8,24},{16,0},{24,8},{1,17},{9,25},{17,1},{25,9},{2,18},{10... | collective-permute-start | bytes 1572872 | tf_op jit(solution)/shard_map/ppermute | solution.py:19
  367.0 45.2 %collective-permute-start.23 = (bf16[128,2048]{1,0:T(8,128)(2,1)}, bf16[128,2048]{1,0:T(8,128)(2,1)}, u32[]{:S(2)}, u32[]{:S(2)}) collective-permute-start(bf16[128,2048]{1,0:T(8,128)(2,1)} %get-tuple-element.94), channel_id=1, source_target_pairs={{0,8},{8,16},{16,24},{24,0},{1,9},{9,17},{17,25},{25,1},{2,10},{10... | collective-permute-start | bytes 1572872 | tf_op jit(solution)/shard_map/ppermute | solution.py:19
  412.2 209.7 %reduce-scatter.5.cloned.1.call-start = ((), (), s32[]{:S(2)}) async-start(), calls=%async_computation.9 | async-start | bytes 9437184 | tf_op jit(solution)/shard_map/reduce_scatter | solution.py:322
  417.8 12.5 %collective-permute-start.26 = (bf16[128,2048]{1,0:T(8,128)(2,1)S(1)}, bf16[128,2048]{1,0:T(8,128)(2,1)S(1)}, u32[]{:S(2)}, u32[]{:S(2)}) collective-permute-start(bf16[128,2048]{1,0:T(8,128)(2,1)S(1)} %get-tuple-element.80), channel_id=1, source_target_pairs={{0,24},{8,0},{16,8},{24,16},{1,25},{9,1},{17,9},{25,17},{2,26},{10... | collective-permute-start | bytes 1572872 | tf_op jit(solution)/shard_map/ppermute | solution.py:19
  417.8 46.4 %collective-permute-start.25 = (bf16[128,2048]{1,0:T(8,128)(2,1)S(1)}, bf16[128,2048]{1,0:T(8,128)(2,1)S(1)}, u32[]{:S(2)}, u32[]{:S(2)}) collective-permute-start(bf16[128,2048]{1,0:T(8,128)(2,1)S(1)} %get-tuple-element.80), channel_id=1, source_target_pairs={{0,16},{8,24},{16,0},{24,8},{1,17},{9,25},{17,1},{25,9},{2,18},{10... | collective-permute-start | bytes 1572872 | tf_op jit(solution)/shard_map/ppermute | solution.py:19
  418.4 45.8 %collective-permute-start.24 = (bf16[128,2048]{1,0:T(8,128)(2,1)S(1)}, bf16[128,2048]{1,0:T(8,128)(2,1)S(1)}, u32[]{:S(2)}, u32[]{:S(2)}) collective-permute-start(bf16[128,2048]{1,0:T(8,128)(2,1)S(1)} %get-tuple-element.80), channel_id=1, source_target_pairs={{0,8},{8,16},{16,24},{24,0},{1,9},{9,17},{17,25},{25,1},{2,10},{10... | collective-permute-start | bytes 1572872 | tf_op jit(solution)/shard_map/ppermute | solution.py:19
  539.5 55.1 %copy-start.8 = (f32[128,2048]{1,0:T(8,128)S(1)}, f32[128,2048]{1,0:T(8,128)}, u32[]{:S(2)}) copy-start(f32[128,2048]{1,0:T(8,128)} %get-tuple-element.81) | copy-start | bytes 3145732
  540.6 54.0 %collective-permute-start.29 = (bf16[128,2048]{1,0:T(8,128)(2,1)}, bf16[128,2048]{1,0:T(8,128)(2,1)}, u32[]{:S(2)}, u32[]{:S(2)}) collective-permute-start(bf16[128,2048]{1,0:T(8,128)(2,1)} %get-tuple-element.92), channel_id=1, source_target_pairs={{0,8},{8,16},{16,24},{24,0},{1,9},{9,17},{17,25},{25,1},{2,10},{10... | collective-permute-start | bytes 1572872 | tf_op jit(solution)/shard_map/ppermute | solution.py:19
  542.1 52.5 %collective-permute-start.28 = (bf16[128,2048]{1,0:T(8,128)(2,1)}, bf16[128,2048]{1,0:T(8,128)(2,1)}, u32[]{:S(2)}, u32[]{:S(2)}) collective-permute-start(bf16[128,2048]{1,0:T(8,128)(2,1)} %get-tuple-element.93), channel_id=1, source_target_pairs={{0,16},{8,24},{16,0},{24,8},{1,17},{9,25},{17,1},{25,9},{2,18},{10... | collective-permute-start | bytes 1572872 | tf_op jit(solution)/shard_map/ppermute | solution.py:19
  544.5 50.2 %collective-permute-start.27 = (bf16[128,2048]{1,0:T(8,128)(2,1)S(1)}, bf16[128,2048]{1,0:T(8,128)(2,1)}, u32[]{:S(2)}, u32[]{:S(2)}) collective-permute-start(bf16[128,2048]{1,0:T(8,128)(2,1)S(1)} %get-tuple-element.91), channel_id=1, source_target_pairs={{0,24},{8,0},{16,8},{24,16},{1,25},{9,1},{17,9},{25,17},{2,26},{10... | collective-permute-start | bytes 1572872 | tf_op jit(solution)/shard_map/ppermute | solution.py:19
  547.3 45.6 %all-to-all-start.1 = ((f32[32,1,768]{2,1,0:T(1,128)}), f32[32,1,768]{2,1,0:T(1,128)S(1)}, u32[]{:S(2)}, u32[]{:S(2)}) async-start(f32[32,1,768]{2,1,0:T(1,128)} %all_to_all.14), calls=%async_computation.3 | async-start | bytes 196608 | tf_op jit(solution)/shard_map/all_to_all | solution.py:341
  598.8 11.1 %collective-permute-start.33 = (bf16[64,2048]{1,0:T(8,128)(2,1)S(1)}, bf16[64,2048]{1,0:T(8,128)(2,1)S(1)}, u32[]{:S(2)}, u32[]{:S(2)}) collective-permute-start(bf16[64,2048]{1,0:T(8,128)(2,1)S(1)} %get-tuple-element.106), channel_id=1, source_target_pairs={{0,8},{8,16},{16,24},{24,0},{1,9},{9,17},{17,25},{25,1},{2,10},{10... | collective-permute-start | bytes 786440 | tf_op jit(solution)/shard_map/ppermute | solution.py:19
  599.5 20.9 %collective-permute-start.34 = (bf16[64,2048]{1,0:T(8,128)(2,1)S(1)}, bf16[64,2048]{1,0:T(8,128)(2,1)S(1)}, u32[]{:S(2)}, u32[]{:S(2)}) collective-permute-start(bf16[64,2048]{1,0:T(8,128)(2,1)S(1)} %get-tuple-element.105), channel_id=1, source_target_pairs={{0,16},{8,24},{16,0},{24,8},{1,17},{9,25},{17,1},{25,9},{2,18},{10... | collective-permute-start | bytes 786440 | tf_op jit(solution)/shard_map/ppermute | solution.py:19
  601.0 19.4 %collective-permute-start.35 = (bf16[64,2048]{1,0:T(8,128)(2,1)S(1)}, bf16[64,2048]{1,0:T(8,128)(2,1)S(1)}, u32[]{:S(2)}, u32[]{:S(2)}) collective-permute-start(bf16[64,2048]{1,0:T(8,128)(2,1)S(1)} %get-tuple-element.104), channel_id=1, source_target_pairs={{0,24},{8,0},{16,8},{24,16},{1,25},{9,1},{17,9},{25,17},{2,26},{10... | collective-permute-start | bytes 786440 | tf_op jit(solution)/shard_map/ppermute | solution.py:19
  623.1 10.9 %collective-permute-start.30 = (bf16[64,1536]{1,0:T(8,128)(2,1)S(1)}, bf16[64,1536]{1,0:T(8,128)(2,1)S(1)}, u32[]{:S(2)}, u32[]{:S(2)}) collective-permute-start(bf16[64,1536]{1,0:T(8,128)(2,1)S(1)} %get-tuple-element.114), channel_id=1, source_target_pairs={{0,8},{8,16},{16,24},{24,0},{1,9},{9,17},{17,25},{25,1},{2,10},{10... | collective-permute-start | bytes 589832 | tf_op jit(solution)/shard_map/ppermute | solution.py:19
  628.7 12.3 %collective-permute-start.31 = (bf16[64,1536]{1,0:T(8,128)(2,1)S(1)}, bf16[64,1536]{1,0:T(8,128)(2,1)S(1)}, u32[]{:S(2)}, u32[]{:S(2)}) collective-permute-start(bf16[64,1536]{1,0:T(8,128)(2,1)S(1)} %get-tuple-element.113), channel_id=1, source_target_pairs={{0,16},{8,24},{16,0},{24,8},{1,17},{9,25},{17,1},{25,9},{2,18},{10... | collective-permute-start | bytes 589832 | tf_op jit(solution)/shard_map/ppermute | solution.py:19
  628.8 12.2 %collective-permute-start.32 = (bf16[64,1536]{1,0:T(8,128)(2,1)S(1)}, bf16[64,1536]{1,0:T(8,128)(2,1)S(1)}, u32[]{:S(2)}, u32[]{:S(2)}) collective-permute-start(bf16[64,1536]{1,0:T(8,128)(2,1)S(1)} %get-tuple-element.112), channel_id=1, source_target_pairs={{0,24},{8,0},{16,8},{24,16},{1,25},{9,1},{17,9},{25,17},{2,26},{10... | collective-permute-start | bytes 589832 | tf_op jit(solution)/shard_map/ppermute | solution.py:19
  (17 other events, 328.7 us)
Sparse Core Ops, SparseCore 0:
  9.9 30.8 all-gather.4
  43.2 48.2 all-gather.6
  115.2 58.2 all-gather.8
  175.2 54.3 all-gather.10
  412.3 114.3 reduce-scatter.2
  530.0 71.8 reduce-scatter.4

commit v3 on v1

v3 whole, which is shorter than its diff:
```python
import jax
import jax.numpy as jnp
from jax import lax
from jax.experimental import pallas as pl
from jax.experimental.pallas import tpu as pltpu
from jax.sharding import PartitionSpec as P

HEAD_DIM = 128
eps_norm = 1e-06
f32 = jnp.float32
bf16 = jnp.bfloat16
DP = ("chip", "core")
ALL = ("seq", "chip", "core")


def after(value, *others):
    return lax.optimization_barrier((value, *others))[0]


def shift(value, step):
    n = lax.axis_size("seq")
    return lax.ppermute(value, "seq", [(i, (i + step) % n) for i in range(n)])


def gather_blocks(rows):
    n = lax.axis_size("seq")
    return [rows] + [shift(rows, k) for k in range(1, n)]


def gather_seq(rows):
    return jnp.concatenate(gather_blocks(rows), axis=0)


def split_blocks(partial, part=0, parts=1):
    n = lax.axis_size("seq")
    size = partial.shape[0] // (n * parts)
    starts = [(k * parts + part) * size for k in range(n)]
    blocks = [partial[start : start + size] for start in starts]
    return [blocks[0]] + [block.astype(bf16) for block in blocks[1:]]


def send_blocks(blocks):
    return [blocks[0]] + [shift(blocks[k], -k) for k in range(1, len(blocks))]


def total_of(blocks):
    total = blocks[0]
    for block in blocks[1:]:
        total = total + block.astype(f32)
    return total


def scatter_seq(partial):
    return total_of(send_blocks(split_blocks(partial)))


def normalize(hidden):
    center = hidden - jnp.mean(hidden, axis=-1, keepdims=True)
    spread = jnp.mean(center * center, axis=-1, keepdims=True)
    recip = lax.rsqrt(spread + eps_norm)
    return (center * recip, recip)


def norm_back(grad_out, normed, recip, gain):
    scaled = grad_out * gain
    return recip * (
        scaled
        - jnp.mean(scaled, axis=-1, keepdims=True)
        - normed * jnp.mean(scaled * normed, axis=-1, keepdims=True)
    )


def dot_nn(a, b):
    return lax.dot_general(a, b, (((1,), (0,)), ((), ())), preferred_element_type=f32)


def dot_nt(a, b):
    return lax.dot_general(a, b, (((1,), (1,)), ((), ())), preferred_element_type=f32)


def dot_tn(a, b):
    return lax.dot_general(a, b, (((0,), (0,)), ((), ())), preferred_element_type=f32)


def grid_call(kernel, scalar, grid, in_specs, out_specs, out_shape, name, args, flops=None):
    grid_spec = pltpu.PrefetchScalarGridSpec(
        num_scalar_prefetch=1, grid=grid, in_specs=in_specs, out_specs=out_specs
    )
    return pl.pallas_call(
        kernel,
        grid_spec=grid_spec,
        out_shape=out_shape,
        compiler_params=pltpu.CompilerParams(vmem_limit_bytes=56 << 20),
        cost_estimate=flops and pl.CostEstimate(flops=flops, transcendentals=0, bytes_accessed=1),
        name=name,
    )(jnp.reshape(scalar, (1,)).astype(jnp.int32), *args)


def fixed(shape):
    return pl.BlockSpec(shape, lambda g, sc: (0,) * len(shape))


def softmax_of(q, k, seg_col, seg_row):
    scores = dot_nt(q, k) * HEAD_DIM ** (-0.5)
    scores = jnp.where(seg_col == seg_row, scores, -1e30)
    terms = jnp.exp(scores - jnp.max(scores, axis=1, keepdims=True))
    return terms / jnp.sum(terms, axis=1, keepdims=True)


def attend_kernel(core, seg_col, seg_row, q, k, v, mixed):
    probs = softmax_of(q[...], k[...], seg_col[...], seg_row[...])
    mixed[...] = dot_nn(probs.astype(bf16), v[...]).astype(bf16)


def attend_back_kernel(core, seg_col, seg_row, q, k, v, gm, grad, sent):
    heads = pl.num_programs(0)
    head = pl.program_id(0)
    probs = softmax_of(q[...], k[...], seg_col[...], seg_row[...])
    grad_probs = dot_nt(gm[...], v[...])
    products = jnp.sum(probs * grad_probs, axis=1, keepdims=True)
    grad_scores = (probs * (grad_probs - products)).astype(bf16)
    scale = HEAD_DIM ** (-0.5)
    half = heads // 2

    def put(part, value):
        value = value.astype(bf16)
        start = pl.multiple_of((part * heads + head) * HEAD_DIM, HEAD_DIM)
        grad[:, pl.ds(start, HEAD_DIM)] = value

        @pl.when(head // half != core[0])
        def _():
            into = pl.multiple_of((part * half + head % half) * HEAD_DIM, HEAD_DIM)
            sent[:, pl.ds(into, HEAD_DIM)] = value

    put(0, dot_nn(grad_scores, k[...]) * scale)
    put(1, dot_tn(grad_scores, q[...]) * scale)
    put(2, dot_tn(probs.astype(bf16), gm[...]))


def head_spec(rows, offset):
    return pl.BlockSpec((rows, HEAD_DIM), lambda h, sc: (0, offset + h))


def qkv_specs(rows, heads):
    return [
        fixed((rows, 1)),
        fixed((1, rows)),
        head_spec(rows, 0),
        head_spec(rows, heads),
        head_spec(rows, 2 * heads),
    ]


def attend(qkv, seg, core):
    rows, width = qkv.shape
    heads = width // (3 * HEAD_DIM)
    return grid_call(
        attend_kernel,
        core,
        (heads,),
        qkv_specs(rows, heads),
        head_spec(rows, 0),
        jax.ShapeDtypeStruct((rows, width // 3), bf16),
        "attend",
        (seg[:, None], seg[None, :], qkv, qkv, qkv),
    )


def attend_back(qkv, grad_mixed, seg, core):
    rows, width = qkv.shape
    heads = width // (3 * HEAD_DIM)
    return grid_call(
        attend_back_kernel,
        core,
        (heads,),
        qkv_specs(rows, heads) + [head_spec(rows, 0)],
        [fixed((rows, width)), fixed((rows, width // 2))],
        [
            jax.ShapeDtypeStruct((rows, width), bf16),
            jax.ShapeDtypeStruct((rows, width // 2), bf16),
        ],
        "attend_back",
        (seg[:, None], seg[None, :], qkv, qkv, qkv, grad_mixed),
        flops=400_000_000_000,
    )


def pack_columns(shard, parts, core):
    n = lax.axis_size("seq")
    rows, width = shard.shape
    part = width // (parts * n)

    def kernel(sc, shard_ref, out):
        for j in range(n):
            for p in range(parts):
                start = (p * n + j) * part
                out[j, :, p * part : (p + 1) * part] = shard_ref[:, start : start + part]

    out = (n, rows, part * parts)
    return grid_call(
        kernel,
        core,
        (1,),
        [fixed(shard.shape)],
        fixed(out),
        jax.ShapeDtypeStruct(out, shard.dtype),
        "pack",
        (shard,),
    )


def join_columns(pieces, parts, halves, core):
    n, rows, width = pieces.shape
    piece = width // (parts * halves)

    def kernel(sc, pieces_ref, out):
        for h in range(halves):
            for j in range(n):
                for p in range(parts):
                    start = (p * n + j) * halves * piece
                    if halves > 1:
                        side = jnp.bitwise_xor(sc[0], h)
                        start = pl.multiple_of(start + side * piece, piece)
                    at = (h * parts + p) * piece
                    value = pieces_ref[j, :, at : at + piece].astype(f32)
                    out[:, pl.ds(start, piece)] = value

    out = (rows, n * width)
    return grid_call(
        kernel,
        core,
        (1,),
        [fixed(pieces.shape)],
        fixed(out),
        jax.ShapeDtypeStruct(out, f32),
        "join_columns",
        (pieces,),
    )


def exchange(pieces):
    return lax.all_to_all(pieces, "seq", 0, 0)


def gather_dp(shard):
    full = lax.all_gather(shard, DP, axis=shard.ndim - 2, tiled=True)
    return full.reshape(-1, full.shape[-1])


def sum_over(value, axes):
    return lax.psum_scatter(value, axes, scatter_dimension=value.ndim - 2, tiled=True)


def to_partner(value):
    return lax.ppermute(value, "core", [(0, 1), (1, 0)])


def column_half(value, index):
    width = value.shape[1] // 2
    return lax.dynamic_slice_in_dim(value, index * width, width, axis=1)


def feed_grad(core, own, far, grad_own, grad_far, name):
    tokens, height = own.shape
    width = grad_far.shape[1]
    rows = 256

    def kernel(sc, a, b, go, gf, out):
        out[...] = (dot_tn(a[...], go[...]) + dot_tn(b[...], gf[...])).astype(bf16)

    rows_spec = pl.BlockSpec((tokens, rows), lambda g, sc: (0, g))
    return grid_call(
        kernel,
        core,
        (height // rows,),
        [
            rows_spec,
            rows_spec,
            pl.BlockSpec((tokens, width), lambda g, sc: (0, sc[0])),
            fixed((tokens, width)),
        ],
        pl.BlockSpec((rows, width), lambda g, sc: (g, 0)),
        jax.ShapeDtypeStruct((height, width), bf16),
        name,
        (own, far, grad_own, grad_far),
        flops=1,
    )


def attn_grad(core, tok, tok_far, mixed, mixed_far, grad_qkv, qkv_far, grad_attn, attn_far):
    n = lax.axis_size("seq")
    chips = lax.axis_size("chip")
    tokens = tok.shape[0]
    half = qkv_far.shape[1] // 3
    out_cols = attn_far.shape[1]
    cols = out_cols // n
    rows = mixed.shape[1] // chips

    def kernel(sc, *refs):
        own_refs, far_refs = refs[:n], refs[n : 2 * n]
        mo, mf, qo, ko, vo, qkv_f, ao, af, out = refs[2 * n :]
        side = (dot_tn(mo[...], ao[...]) + dot_tn(mf[...], af[...])).astype(bf16)
        own = jnp.concatenate([qo[...], ko[...], vo[...]], axis=1)
        for j in range(n):
            total = dot_tn(own_refs[j][...], own) + dot_tn(far_refs[j][...], qkv_f[...])
            out[j, :, : 3 * half] = total.astype(bf16)
            out[j, :, 3 * half :] = side[:, j * cols : (j + 1) * cols]

    def rows_spec(j):
        return pl.BlockSpec((tokens, rows), lambda o, sc: (0, j * chips + o))

    def part_spec(p):
        return pl.BlockSpec((tokens, half), lambda o, sc: (0, 2 * p + sc[0]))

    width = 3 * half + cols
    return grid_call(
        kernel,
        core,
        (chips,),
        [rows_spec(j) for j in range(n)] * 2
        + [rows_spec(0)] * 2
        + [part_spec(p) for p in range(3)]
        + [
            fixed((tokens, 3 * half)),
            pl.BlockSpec((tokens, out_cols), lambda o, sc: (0, sc[0])),
            fixed((tokens, out_cols)),
        ],
        pl.BlockSpec((n, rows, width), lambda o, sc: (0, o, 0)),
        jax.ShapeDtypeStruct((n, chips * rows, width), bf16),
        "attn_grad",
        (
            *[tok] * n,
            *[tok_far] * n,
            mixed,
            mixed_far,
            *[grad_qkv] * 3,
            qkv_far,
            grad_attn,
            attn_far,
        ),
    )


def pick(value, axis, index):
    return lax.dynamic_index_in_dim(value, index, axis, keepdims=False)


def swap_rows(total, split, axis, core):
    value = total.reshape(split)
    return pick(value, axis, core), to_partner(pick(value, axis, 1 - core).astype(bf16))


def join_halves(own, far, core):
    return jnp.where(
        core == 0, jnp.concatenate([own, far], axis=-1), jnp.concatenate([far, own], axis=-1)
    )


def device_count():
    return lax.axis_size("seq") * lax.axis_size("chip") * lax.axis_size("core")


def all_small(vectors):
    count = device_count()
    packed = jnp.concatenate(vectors)
    table = lax.all_to_all(jnp.broadcast_to(packed[None], (count, packed.shape[0])), ALL, 0, 0)
    out = []
    start = 0
    for vector in vectors:
        size = vector.shape[0]
        out.append(table[:, start : start + size].reshape(-1).astype(f32))
        start += size
    return out


def scatter_small(vectors):
    count = device_count()
    packed = jnp.concatenate([v.reshape(count, -1) for v in vectors], axis=1)
    mine = jnp.sum(lax.all_to_all(packed, ALL, 0, 0), axis=0)
    out = []
    start = 0
    for vector in vectors:
        size = vector.shape[0] // count
        out.append(mine[start : start + size])
        start += size
    return out


def gelu_parts(v):
    c = 0.7978845608028654
    t = jnp.tanh(c * (v + 0.044715 * v * v * v))
    value = 0.5 * v * (1.0 + t)
    slope = 0.5 * (1.0 + t) + 0.5 * v * (1.0 - t * t) * c * (1.0 + 3 * 0.044715 * v * v)
    return value, slope


def per_device(
    tokens,
    doc_lengths,
    qkv_weight,
    qv_bias,
    out_weight,
    out_bias,
    norm1_gain,
    norm1_bias,
    in_weight,
    in_bias,
    down_weight,
    down_bias,
    norm2_gain,
    norm2_bias,
    cotangent,
):
    n = lax.axis_size("seq")
    chips = lax.axis_size("chip")
    s = lax.axis_index("seq")
    c = lax.axis_index("core")
    rows = tokens.shape[1]
    width = tokens.shape[2]
    part = width // n
    half = width // 2
    paired = part // chips % 128 == 0
    tok_rows = tokens[0]

    tok_blocks = gather_blocks(tok_rows)
    tok_full = jnp.concatenate(tok_blocks, axis=0)
    out_w = gather_dp(out_weight)
    qkv_moved = exchange(pack_columns(qkv_weight, 3, c))
    vectors = [qv_bias, out_bias, norm1_gain, norm1_bias]
    vectors += [in_bias, down_bias, norm2_gain, norm2_bias]
    small = all_small(after(vectors, qkv_moved))
    qv_full, out_b, gain_one, shift_one, in_b, down_b, gain_two, shift_two = small
    qkv_w = gather_dp(after(qkv_moved, out_w, tok_blocks[1]))
    in_moved = exchange(after(pack_columns(in_weight, 1, c), tok_blocks))
    down_w = gather_dp(after(down_weight, qkv_moved))

    ends = jnp.cumsum(doc_lengths[0])
    steps = jnp.arange(n * rows, dtype=jnp.int32)
    places = jnp.remainder(s - steps // rows, n) * rows + steps % rows
    seg = jnp.sum((places[:, None] >= ends[None, :]).astype(jnp.int32), axis=1)

    q_bias = lax.dynamic_slice_in_dim(qv_full, s * part, part)
    v_bias = lax.dynamic_slice_in_dim(qv_full, width + s * part, part)
    qkv_b = jnp.concatenate([q_bias, jnp.zeros((part,), f32), v_bias])
    qkv = (dot_nn(tok_full, qkv_w) + qkv_b).astype(bf16)
    mixed = attend(qkv, seg, c)
    size = rows // 2
    halves = range(2)
    cut = [slice(h * size, (h + 1) * size) for h in halves]
    attn_partial = dot_nn(mixed, out_w)
    attn_blocks = [send_blocks(split_blocks(attn_partial, h, 2)) for h in halves]
    in_w = gather_dp(after(in_moved, attn_blocks[0], down_w))
    hidden = in_w.shape[1]
    in_bias_own = lax.dynamic_slice_in_dim(in_b, s * hidden, hidden)

    first, normed_one, recip_one, first_blocks = [], [], [], []
    for h in halves:
        if h:
            attn_blocks[h] = after(attn_blocks[h], first[0])
        attn = total_of(attn_blocks[h]) + out_b
        normed, recip = normalize(tok_rows[cut[h]].astype(f32) + attn)
        normed_one.append(normed)
        recip_one.append(recip)
        first.append(normed * gain_one + shift_one)
        first_blocks.append(gather_blocks(first[h].astype(bf16)))

    first_blocks[0] = after(first_blocks[0], first[1])
    act, act_slope, first_full, ffn_blocks, ffn_split = [], [], [], [], []
    for h in halves:
        if h:
            first_blocks[h] = after(first_blocks[h], ffn_split[0])
        first_full.append(jnp.concatenate(first_blocks[h], axis=0))
        act_value, slope = gelu_parts(dot_nn(first_full[h], in_w) + in_bias_own)
        pair = lax.optimization_barrier((act_value.astype(bf16), slope.astype(bf16)))
        act.append(pair[0])
        act_slope.append(pair[1])
        ffn_split.append(split_blocks(dot_nn(act[h], down_w)))
        ffn_blocks.append(send_blocks(ffn_split[h]))

    ffn_blocks[0] = after(ffn_blocks[0], ffn_split[1])
    result, normed_two, grad_h2, grad_ffn, grad_blocks = [], [], [], [], []
    grad_out = cotangent[0].astype(f32)
    for h in halves:
        if h:
            ffn_blocks[h] = after(ffn_blocks[h], grad_ffn[0])
        ffn = total_of(ffn_blocks[h]) + down_b
        normed, recip = normalize(first[h] + ffn)
        normed_two.append(normed)
        result.append((normed * gain_two + shift_two).astype(bf16))
        grad_h2.append(norm_back(grad_out[cut[h]], normed, recip, gain_two))
        grad_ffn.append(grad_h2[h].astype(bf16))
        grad_blocks.append(gather_blocks(grad_ffn[h]))
    result = jnp.concatenate(result, axis=0)
    shift_two_grad = jnp.sum(grad_out, axis=0)
    gain_two_grad = sum(jnp.sum(grad_out[cut[h]] * normed_two[h], axis=0) for h in halves)
    down_b_grad = sum(jnp.sum(grad_ffn[h].astype(f32), axis=0) for h in halves)

    grad_blocks[0] = after(grad_blocks[0], grad_ffn[1])
    grad_ffn_full, grad_pre, back_split, back_blocks = [], [], [], []
    for h in halves:
        if h:
            grad_blocks[h] = after(grad_blocks[h], back_split[0])
        grad_ffn_full.append(jnp.concatenate(grad_blocks[h], axis=0))
        grad_act = dot_nt(grad_ffn_full[h], down_w)
        grad_pre.append((grad_act * act_slope[h].astype(f32)).astype(bf16))
        back_split.append(split_blocks(dot_nt(grad_pre[h], in_w)))
        back_blocks.append(send_blocks(back_split[h]))
    act, first_full, grad_ffn_full, grad_pre = (
        jnp.concatenate(v, axis=0) for v in (act, first_full, grad_ffn_full, grad_pre)
    )
    in_b_grad = jnp.sum(grad_pre.astype(f32), axis=0)
    back_blocks[0] = after(back_blocks[0], back_split[1])
    if paired:
        tok_far, mixed_far, first_far, act_far = (
            to_partner(v) for v in (tok_full, mixed, first_full, act)
        )
        ffn_far = to_partner(column_half(grad_ffn_full, 1 - c))
        pre_far = to_partner(column_half(grad_pre, 1 - c))
        at = after(c, back_split[1])
        in_low = feed_grad(at, first_full, first_far, grad_pre, pre_far, "in_grad")
        back_blocks[1], in_low = lax.optimization_barrier((back_blocks[1], in_low))
        in_sum = sum_over(in_low.reshape(n, part, -1), "chip")
    else:
        down_low = dot_tn(act, grad_ffn_full).astype(bf16)
        in_low = dot_tn(first_full, grad_pre).astype(bf16).reshape(n, part, -1)
        down_w_grad = sum_over(down_low, DP).astype(f32)
        in_w_grad = join_columns(exchange(sum_over(in_low, DP)), 1, 1, c)
    grad_first, grad_h1, grad_attn, attn_blocks = [], [], [], []
    for h in halves:
        if h:
            back_blocks[h] = after(back_blocks[h], grad_attn[0])
        grad_first.append(grad_h2[h] + total_of(back_blocks[h]))
        grad_h1.append(norm_back(grad_first[h], normed_one[h], recip_one[h], gain_one))
        grad_attn.append(grad_h1[h].astype(bf16))
        attn_blocks.append(gather_blocks(grad_attn[h]))
    if paired:
        at = after(c, grad_attn[1])
        down_low = feed_grad(at, act, act_far, grad_ffn_full, ffn_far, "down_grad")
        down_got = lax.all_to_all(down_low.reshape(chips, -1, half), "chip", 0, 0)
    attn_blocks = after(attn_blocks, down_low)
    shift_one_grad = sum(jnp.sum(grad_first[h], axis=0) for h in halves)
    gain_one_grad = sum(jnp.sum(grad_first[h] * normed_one[h], axis=0) for h in halves)
    out_b_grad = sum(jnp.sum(grad_attn[h].astype(f32), axis=0) for h in halves)
    grad_h1 = jnp.concatenate(grad_h1, axis=0)
    grad_attn_full = jnp.concatenate([attn_blocks[h][k] for k in range(n) for h in halves], axis=0)
    grad_mixed = dot_nt(grad_attn_full, out_w).astype(bf16)
    grad_qkv, qkv_sent = attend_back(qkv, grad_mixed, seg, c)
    if paired:
        attn_far = to_partner(column_half(grad_attn_full, 1 - c))
        in_own, in_far = swap_rows(after(in_sum, qkv_sent), (n, 2, -1, half), 1, c)
        in_pieces = exchange(jnp.concatenate([in_own, in_far], axis=2))
        args = (tok_full, tok_far, mixed, mixed_far)
        qkv_far = to_partner(qkv_sent)
        attn_low = attn_grad(c, *args, grad_qkv, qkv_far, grad_attn_full, attn_far)
        attn_sum = sum_over(attn_low, "chip")
        last_split = split_blocks(dot_nt(after(grad_qkv, attn_low), qkv_w))
        last_blocks = send_blocks(last_split)
        down_sum = jnp.sum(after(down_got, last_split).astype(f32), axis=0)
        down_own, down_far = swap_rows(down_sum, (2, -1, half), 0, c)
        down_w_grad = join_halves(down_own, down_far.astype(f32), c)
        in_w_grad = join_columns(in_pieces, 1, 2, c)
        attn_sum = after(attn_sum, last_blocks)
        attn_own, attn_far = swap_rows(attn_sum, (n, 2, -1, half), 1, c)
        split = 3 * part // 2
        pieces = jnp.concatenate([attn_own[:, :, :split], attn_far[:, :, :split]], 2)
        qkv_w_grad = join_columns(exchange(pieces), 3, 2, c)
        out_own, out_far = (
            jnp.concatenate([v[j, :, split:] for j in range(n)], axis=1).astype(f32)
            for v in (attn_own, attn_far)
        )
        out_w_grad = join_halves(out_own, out_far, c)
    else:
        last_split = split_blocks(dot_nt(grad_qkv, qkv_w))
        last_blocks = send_blocks(last_split)
        attn_low = after(dot_tn(tok_full, grad_qkv).astype(bf16), last_split)
        out_w_grad = sum_over(dot_tn(mixed, grad_attn_full).astype(bf16), DP).astype(f32)
        pieces = exchange(sum_over(attn_low.reshape(n, part, -1), DP))
        qkv_w_grad = join_columns(pieces, 3, 1, c)
    sums = jnp.sum(grad_qkv.astype(f32), axis=0)
    qv_grad = jnp.zeros((2 * width,), f32)
    qv_grad = lax.dynamic_update_slice_in_dim(qv_grad, sums[:part], s * part, 0)
    qv_grad = lax.dynamic_update_slice_in_dim(qv_grad, sums[2 * part :], width + s * part, 0)
    in_b_all = jnp.zeros((n * hidden,), f32)
    in_b_all = lax.dynamic_update_slice_in_dim(in_b_all, in_b_grad, s * hidden, 0)
    small_grads = scatter_small(
        [
            qv_grad,
            out_b_grad,
            gain_one_grad,
            shift_one_grad,
            in_b_all,
            down_b_grad,
            gain_two_grad,
            shift_two_grad,
        ]
    )
    last_blocks = after(last_blocks, small_grads)
    input_grad = (grad_h1 + total_of(last_blocks)).astype(bf16)
    return (
        result[None],
        input_grad[None],
        qkv_w_grad,
        small_grads[0],
        out_w_grad,
        small_grads[1],
        small_grads[2],
        small_grads[3],
        in_w_grad,
        small_grads[4],
        down_w_grad,
        small_grads[5],
        small_grads[6],
        small_grads[7],
    )


def solution(mesh):
    devices = mesh.devices
    split = jax.sharding.Mesh(devices.reshape(devices.shape[0], -1, 2), ALL)
    rows = P(ALL, None)
    flat = P(ALL)
    tok = P(DP, "seq", None)
    ins = (tok, P(DP, None), rows, flat, rows, *[flat] * 3, rows, flat, rows, *[flat] * 3, tok)
    outs = (tok, tok, rows, flat, rows, *[flat] * 3, rows, flat, rows, *[flat] * 3)
    return jax.shard_map(per_device, mesh=split, in_specs=ins, out_specs=outs, check_vma=False)
```

time: 772 us -> 604 us (0.78)
  waiting for transfers between devices: 427 us -> 238 us
  starting transfers between devices: 79.6 us -> 133 us
  blocking collectives: 63.6 us -> 14.5 us
  Pallas kernels: 11.1 us -> 57 us
  matrix products: 94.8 us -> 67.9 us
  local copies, waits for them, and re-layouts: 48.9 us -> 35.1 us
  other arithmetic: 22.1 us -> 35 us
    ppermute x24 -> x42, waiting for transfers between devices: 265 us -> 147 us  [shift(): return lax.ppermute(value, 'seq', [(i, (i + step) % n) for i in range(n)])]
    reduce_scatter x4 -> x2, waiting for transfers between devices: 111 us -> 0.01 us  [sum_over(): lax.psum_scatter(value, axes, scatter_dimension=value.ndim - 2, tiled=True)]
    all_to_all x2 -> x5, waiting for transfers between devices: 11.7 us -> 67.9 us  [the longest x1 42.8 us: per_device(): down_got = lax.all_to_all(down_low.reshape(chips, -1, half), 'chip', 0, 0)]
    all_to_all x2 -> x0, blocking collectives: 54.1 us -> none  [columns_to_owner(): moved = lax.all_to_all(pieces, 'seq', 0, 0)]
    pallas_call x2 -> x9, Pallas kernels: 11.1 us -> 57 us  [grid_call(): pl.pallas_call(kernel, grid_spec=grid_spec, out_shape=out_shape, compiler...]
    ppermute x24 -> x42, starting transfers between devices: 64.3 us -> 101 us  [shift(): return lax.ppermute(value, 'seq', [(i, (i + step) % n) for i in range(n)])]
    all_to_all x1, waiting for transfers between devices: 38 us -> 2.07 us  [all_small(): lax.all_to_all(jnp.broadcast_to(packed[None], (count, packed.shape[0])),...]
    dot_general x4 -> x0, matrix products: 31.5 us -> none  [dot_tn(): lax.dot_general(a, b, (((0,), (0,)), ((), ())), preferred_element_type=f32)]
  transfers between devices with their start and end apart: 35 -> 65, of which waited for: 19 -> 20; matrix products, arithmetic and copies ran while one was open for 13% -> 22% of each run, Pallas kernels for 1% -> 9%
where the time goes in v3:
time: 604 us; the launch traced here: 596 us
  waiting for transfers between devices  238 us (39%)
  starting transfers between devices  133 us (22%)
  matrix products  67.9 us (11%)
  Pallas kernels  57 us (9%)
  local copies, waits for them, and re-layouts  35.1 us (6%)
  other arithmetic  35 us (6%)
  between operations  15.7 us (3%)
  blocking collectives  14.5 us (2%)
    ppermute x42, waiting for transfers between devices, shift(): return lax.ppermute(value, 'seq', [(i, (i + step) % n) for i in range(n)])  147 us
    ppermute x42, starting transfers between devices, shift(): return lax.ppermute(value, 'seq', [(i, (i + step) % n) for i in range(n)])  101 us
    pallas_call x9, Pallas kernels, grid_call(): pl.pallas_call(kernel, grid_spec=grid_spec, out_shape=out_shape, compiler...  57 us
    all_to_all x1, waiting for transfers between devices, per_device(): down_got = lax.all_to_all(down_low.reshape(chips, -1, half), 'chip', 0, 0)  42.8 us
    dot_general x6, matrix products, dot_nt(): lax.dot_general(a, b, (((1,), (1,)), ((), ())), preferred_element_type=f32)  34.3 us
    dot_general x6, matrix products, dot_nn(): lax.dot_general(a, b, (((1,), (0,)), ((), ())), preferred_element_type=f32)  33.6 us
    all_to_all x4, waiting for transfers between devices, exchange(): return lax.all_to_all(pieces, 'seq', 0, 0)  25.2 us
    all_to_all x4, starting transfers between devices, exchange(): return lax.all_to_all(pieces, 'seq', 0, 0)  19.8 us
  transfers between devices with their start and end apart: 65, of which 20 were waited for; matrix products, arithmetic and copies ran while one was open for 22% of the time, Pallas kernels for 9%

profile of v3, /device:TPU:0, one launch (start us, length us, event | category | flops | bytes accessed | tf_op | source)
XLA Modules:
  0.0 595.9 jit_solution(966463101435417868)
XLA Ops:
  10.1 6.5 %all-to-all-start = ((bf16[4,64,1536]{2,1,0:T(8,128)(2,1)}), bf16[4,64,1536]{2,1,0:T(8,128)(2,1)S(1)}, u32[]{:S(2)}, u32[]{:S(2)}) async-start(bf16[4,64,1536]{2,1,0:T(8,128)(2,1)} %pack.2), calls=%async_computation | async-start | bytes 1572864 | tf_op jit(solution)/shard_map/all_to_all | solution.py:242
  18.6 26.1 %collective-permute-done = bf16[128,2048]{1,0:T(8,128)(2,1)S(1)} collective-permute-done((bf16[128,2048]{1,0:T(8,128)(2,1)S(1)}, bf16[128,2048]{1,0:T(8,128)(2,1)S(1)}, u32[]{:S(2)}, u32[]{:S(2)}) %collective-permute-start) | collective-permute-done | bytes 524320 | tf_op jit(solution)/shard_map/ppermute | solution.py:22
  44.7 3.2 all-to-all-done
  52.8 5.9 all-to-all-start.1
  64.1 20.1 %collective-permute-done.1 = bf16[128,2048]{1,0:T(8,128)(2,1)S(1)} collective-permute-done((bf16[128,2048]{1,0:T(8,128)(2,1)S(1)}, bf16[128,2048]{1,0:T(8,128)(2,1)S(1)}, u32[]{:S(2)}, u32[]{:S(2)}) %collective-permute-start.1) | collective-permute-done | bytes 524320 | tf_op jit(solution)/shard_map/ppermute | solution.py:22
  86.3 5.0 all-to-all-start.2
  93.2 7.5 %fusion.q.k.v = bf16[512,1536]{1,0:T(8,128)(2,1)} fusion(bf16[2048,1536]{1,0:T(8,128)(2,1)} %bitcast.144, f32[1536]{0:T(1024)S(1)} %pad_maximum_fusion.4, bf16[128,2048]{1,0:T(8,128)(2,1)S(1)} %collective-permute-done.2, bf16[128,2048]{1,0:T(8,128)(2,1)} %copy-done.35, bf16[128,2048]{1,0:T(8,128)(2,1)S(1)} %collective-permute-done, ...), kind=kOutput, calls=%fused_computation.8 | convolution fusion | flops 3231186944 | bytes 9967616 | tf_op jit(solution)/shard_map/dot_general | solution.py:74
  100.8 6.5 %attend.1.refs_8_ = bf16[512,512]{1,0:T(8,128)(2,1)} custom-call(s32[1]{0:T(128)} %bitcast.1.sc.core, s32[512,1]{1,0:T(8,128)} %copy.39.seg_col, s32[1,512]{1,0:T(1,128)} %bitcast.133, bf16[512,1536]{1,0:T(8,128)(2,1)} %fusion.q.k.v, bf16[512,1536]{1,0:T(8,128)(2,1)} %fusion.q.k.v, bf16[512,1536]{1,0:T(8,128)(2,1)} %fusion.q.k.v), custom_call_target="tpu_custom_call" | custom-call | tf_op jit(solution)/shard_map/attend/pallas_call | solution.py:89
  107.3 4.3 fusion.81
  117.9 5.7 collective-permute-done.5
  123.6 10.6 %collective-permute-done.4 = bf16[64,2048]{1,0:T(8,128)(2,1)S(1)} collective-permute-done((bf16[64,2048]{1,0:T(8,128)(2,1)S(1)}, bf16[64,2048]{1,0:T(8,128)(2,1)S(1)}, u32[]{:S(2)}, u32[]{:S(2)}) %collective-permute-start.4) | collective-permute-done | bytes 262176 | tf_op jit(solution)/shard_map/ppermute | solution.py:22
  134.2 15.3 %all-gather.9.cloned.1.call-done = bf16[2048,2048]{1,0:T(8,128)(2,1)} async-done(((bf16[256,2048]{1,0:T(8,128)(2,1)}), bf16[2048,2048]{1,0:T(8,128)(2,1)}) %all-gather.9.cloned.1.call-update) | async-done | bytes 8388624 | tf_op jit(solution)/shard_map/all_gather | solution.py:246
  150.3 3.3 collective-permute-start.9
  160.7 4.2 collective-permute-start.8
  165.0 23.8 %collective-permute-done.10 = bf16[64,2048]{1,0:T(8,128)(2,1)S(1)} collective-permute-done((bf16[64,2048]{1,0:T(8,128)(2,1)}, bf16[64,2048]{1,0:T(8,128)(2,1)S(1)}, u32[]{:S(2)}, u32[]{:S(2)}) %collective-permute-start.10) | collective-permute-done | bytes 262176 | tf_op jit(solution)/shard_map/ppermute | solution.py:22
  189.6 3.9 collective-permute-start.17
  193.6 11.4 %collective-permute-done.7 = bf16[64,2048]{1,0:T(8,128)(2,1)S(1)} collective-permute-done((bf16[64,2048]{1,0:T(8,128)(2,1)S(1)}, bf16[64,2048]{1,0:T(8,128)(2,1)S(1)}, u32[]{:S(2)}, u32[]{:S(2)}) %collective-permute-start.7) | collective-permute-done | bytes 262176 | tf_op jit(solution)/shard_map/ppermute | solution.py:22
  208.0 7.4 %fusion.8 = (bf16[256,2048]{1,0:T(8,128)(2,1)S(1)}, bf16[256,2048]{1,0:T(8,128)(2,1)S(1)}) fusion(f32[2048]{0:T(1024)S(1)} %dynamic_slice.40, bf16[2048,2048]{1,0:T(8,128)(2,1)} %bitcast.138, bf16[64,2048]{1,0:T(8,128)(2,1)} %copy-done.44, bf16[64,2048]{1,0:T(8,128)(2,1)} %copy-done.43, bf16[64,2048]{1,0:T(8,128)(2,1)} %copy-done.42, ...), kind=kOutput, calls=%fused_computation.23 | convolution fusion | flops 2162688000 | bytes 11542528 | tf_op jit(solution)/shard_map/dot_general | solution.py:74
  215.4 5.9 fusion.82
  221.3 9.9 %collective-permute-start.12 = (bf16[64,2048]{1,0:T(8,128)(2,1)S(1)}, bf16[64,2048]{1,0:T(8,128)(2,1)S(1)}, u32[]{:S(2)}, u32[]{:S(2)}) collective-permute-start(bf16[64,2048]{1,0:T(8,128)(2,1)S(1)} %get-tuple-element.237), channel_id=1, source_target_pairs={{0,24},{8,0},{16,8},{24,16},{1,25},{9,1},{17,9},{25,17},{2,26},{10... | collective-permute-start | bytes 786440 | tf_op jit(solution)/shard_map/ppermute | solution.py:22
  232.1 6.2 %fusion.14 = (bf16[256,2048]{1,0:T(8,128)(2,1)}, bf16[256,2048]{1,0:T(8,128)(2,1)S(1)}) fusion(f32[2048]{0:T(1024)S(1)} %dynamic_slice.40, bf16[2048,2048]{1,0:T(8,128)(2,1)S(1)} %bitcast.143, bf16[64,2048]{1,0:T(8,128)(2,1)} %collective-permute-done.17, bf16[64,2048]{1,0:T(8,128)(2,1)} %collective-permute-done.16, ...), kind=kOutput, calls=%fused_computation.29 | convolution fusion | flops 2162688000 | bytes 11542528 | tf_op jit(solution)/shard_map/dot_general | solution.py:74
  250.8 4.4 collective-permute-done.13
  258.2 10.2 %collective-permute-start.21 = (bf16[64,2048]{1,0:T(8,128)(2,1)S(1)}, bf16[64,2048]{1,0:T(8,128)(2,1)S(1)}, u32[]{:S(2)}, u32[]{:S(2)}) collective-permute-start(bf16[64,2048]{1,0:T(8,128)(2,1)S(1)} %get-tuple-element.125), channel_id=1, source_target_pairs={{0,8},{8,16},{16,24},{24,0},{1,9},{9,17},{17,25},{25,1},{2,10},{10... | collective-permute-start | bytes 786440 | tf_op jit(solution)/shard_map/ppermute | solution.py:22
  268.3 6.9 %collective-permute-start.22 = (bf16[64,2048]{1,0:T(8,128)(2,1)S(1)}, bf16[64,2048]{1,0:T(8,128)(2,1)S(1)}, u32[]{:S(2)}, u32[]{:S(2)}) collective-permute-start(bf16[64,2048]{1,0:T(8,128)(2,1)S(1)} %get-tuple-element.125), channel_id=1, source_target_pairs={{0,16},{8,24},{16,0},{24,8},{1,17},{9,25},{17,1},{25,9},{2,18},{10... | collective-permute-start | bytes 786440 | tf_op jit(solution)/shard_map/ppermute | solution.py:22
  275.2 11.7 %collective-permute-done.19 = bf16[64,2048]{1,0:T(8,128)(2,1)S(1)} collective-permute-done((bf16[64,2048]{1,0:T(8,128)(2,1)S(1)}, bf16[64,2048]{1,0:T(8,128)(2,1)S(1)}, u32[]{:S(2)}, u32[]{:S(2)}) %collective-permute-start.19) | collective-permute-done | bytes 262176 | tf_op jit(solution)/shard_map/ppermute | solution.py:22
  294.2 16.2 %collective-permute-start.29 = (bf16[64,2048]{1,0:T(8,128)(2,1)S(1)}, bf16[64,2048]{1,0:T(8,128)(2,1)S(1)}, u32[]{:S(2)}, u32[]{:S(2)}) collective-permute-start(bf16[64,2048]{1,0:T(8,128)(2,1)S(1)} %get-tuple-element.130), channel_id=1, source_target_pairs={{0,24},{8,0},{16,8},{24,16},{1,25},{9,1},{17,9},{25,17},{2,26},{10... | collective-permute-start | bytes 786440 | tf_op jit(solution)/shard_map/ppermute | solution.py:22
  310.3 5.8 fusion.1
  316.2 6.1 %fusion.84 = (bf16[256,2048]{1,0:T(8,128)(2,1)S(1)}, f32[256,2048]{1,0:T(8,128)S(1)}) fusion(bf16[256,2048]{1,0:T(8,128)(2,1)S(1)} %fusion.1, bf16[2048,2048]{1,0:T(8,128)(2,1)} %bitcast.139), kind=kOutput, calls=%fused_computation.228 | convolution fusion | flops 2148007936 | bytes 12582912 | tf_op jit(solution)/shard_map/dot_general | solution.py:78
  323.7 7.0 %collective-permute-start.26 = (bf16[64,2048]{1,0:T(8,128)(2,1)S(1)}, bf16[64,2048]{1,0:T(8,128)(2,1)S(1)}, u32[]{:S(2)}, u32[]{:S(2)}) collective-permute-start(bf16[64,2048]{1,0:T(8,128)(2,1)S(1)} %get-tuple-element.229), channel_id=1, source_target_pairs={{0,8},{8,16},{16,24},{24,0},{1,9},{9,17},{17,25},{25,1},{2,10},{10... | collective-permute-start | bytes 786440 | tf_op jit(solution)/shard_map/ppermute | solution.py:22
  330.7 5.8 fusion.2
  336.5 6.1 %fusion.85 = (bf16[256,2048]{1,0:T(8,128)(2,1)S(1)}, f32[256,2048]{1,0:T(8,128)S(1)}) fusion(bf16[256,2048]{1,0:T(8,128)(2,1)S(1)} %fusion.2, bf16[2048,2048]{1,0:T(8,128)(2,1)} %bitcast.140), kind=kOutput, calls=%fused_computation.229 | convolution fusion | flops 2148007936 | bytes 12582912 | tf_op jit(solution)/shard_map/dot_general | solution.py:78
  347.3 3.4 collective-permute-start.30
  356.5 10.0 %in_grad.1 = bf16[2048,1024]{1,0:T(8,128)(2,1)} custom-call(s32[1]{0:T(128)} %bitcast.15.sc, bf16[512,2048]{1,0:T(8,128)(2,1)} %constant_dynamic-update-slice_fusion.a, bf16[512,2048]{1,0:T(8,128)(2,1)} %copy-done.16, bf16[512,2048]{1,0:T(8,128)(2,1)} %pad_maximum_fusion.go, bf16[512,1024]{1,0:T(8,128)(2,1)} %copy-done.24), custom_call_target="tpu_custom_call" | custom-call | flops 1 | bytes 1 | tf_op jit(solution)/shard_map/in_grad/pallas_call | solution.py:89
  367.5 18.8 %collective-permute-done.31 = bf16[64,2048]{1,0:T(8,128)(2,1)} collective-permute-done((bf16[64,2048]{1,0:T(8,128)(2,1)}, bf16[64,2048]{1,0:T(8,128)(2,1)}, u32[]{:S(2)}, u32[]{:S(2)}) %collective-permute-start.31) | collective-permute-done | bytes 262176 | tf_op jit(solution)/shard_map/ppermute | solution.py:22
  392.1 2.9 collective-permute-start.39
  397.6 10.1 %down_grad.1 = bf16[2048,1024]{1,0:T(8,128)(2,1)} custom-call(s32[1]{0:T(128)} %bitcast.16.sc, bf16[512,2048]{1,0:T(8,128)(2,1)} %copy-done.7, bf16[512,2048]{1,0:T(8,128)(2,1)} %collective-permute-done.41.b, bf16[512,2048]{1,0:T(8,128)(2,1)} %copy-done.6, bf16[512,1024]{1,0:T(8,128)(2,1)} %copy-done.23), custom_call_target="tpu_custom_call" | custom-call | flops 1 | bytes 1 | tf_op jit(solution)/shard_map/down_grad/pallas_call | solution.py:89
  407.7 11.2 %collective-permute-done.39 = bf16[64,2048]{1,0:T(8,128)(2,1)S(1)} collective-permute-done((bf16[64,2048]{1,0:T(8,128)(2,1)S(1)}, bf16[64,2048]{1,0:T(8,128)(2,1)S(1)}, u32[]{:S(2)}, u32[]{:S(2)}) %collective-permute-start.39) | collective-permute-done | bytes 262176 | tf_op jit(solution)/shard_map/ppermute | solution.py:22
  423.8 11.3 %attend_back.1 = (bf16[512,1536]{1,0:T(8,128)(2,1)}, bf16[512,768]{1,0:T(8,128)(2,1)}) custom-call(s32[1]{0:T(128)} %bitcast.1.sc.core, s32[512,1]{1,0:T(8,128)} %copy.39.seg_col, s32[1,512]{1,0:T(1,128)} %bitcast.134, bf16[512,1536]{1,0:T(8,128)(2,1)} %fusion.q.k.v, bf16[512,1536]{1,0:T(8,128)(2,1)} %fusion.q.k.v, bf16[512,1536]{1,0:T(8,128)(2,1)} %fusion.q.k.v, ...), custom_call_target="tpu_custom_call" | custom-call | flops 399999991808 | bytes 1 | tf_op jit(solution)/shard_map/attend_back/pallas_call | solution.py:89
  439.2 9.6 %attn_grad.1 = bf16[4,512,1024]{2,1,0:T(8,128)(2,1)} custom-call(s32[1]{0:T(128)} %bitcast.1.sc.core, bf16[512,2048]{1,0:T(8,128)(2,1)} %pad_maximum_fusion.1.refs_0_.refs_1_.refs_2_.refs_3_, bf16[512,2048]{1,0:T(8,128)(2,1)} %pad_maximum_fusion.1.refs_0_.refs_1_.refs_2_.refs_3_, bf16[512,2048]{1,0:T(8,128)(2,1)} %pad_maximum_fusion.1.refs_0_.refs_1_.refs_2_.refs_3_, ...), custom_call_target="tpu_custom_call" | custom-call | tf_op jit(solution)/shard_map/attn_grad/pallas_call | solution.py:89
  453.3 14.5 %all_to_all.43 = f32[32,1,768]{2,1,0:T(1,128)S(1)} all-to-all(f32[32,1,768]{2,1,0:T(1,128)S(1)} %all_to_all.31), channel_id=1, replica_groups=mesh['seq'=4,'chip'=4,'core'=2] {'seq','chip','core'}, dimensions={0} | all-to-all | bytes 196608 | tf_op jit(solution)/shard_map/all_to_all | solution.py:379
  467.8 4.8 all-to-all-start.6
  472.7 8.4 %fusion.86 = (bf16[512,2048]{1,0:T(8,128)(2,1)}, f32[512,2048]{1,0:T(8,128)}) fusion(bf16[512,1536]{1,0:T(8,128)(2,1)S(1)} %copy-done, bf16[2048,1536]{1,0:T(8,128)(2,1)} %bitcast.145), kind=kOutput, calls=%fused_computation.230 | convolution fusion | flops 3222274048 | bytes 14155776 | tf_op jit(solution)/shard_map/dot_general | solution.py:78
  489.8 42.8 %all-to-all-done.6 = bf16[4,512,1024]{2,1,0:T(8,128)(2,1)} async-done(((bf16[4,512,1024]{2,1,0:T(8,128)(2,1)}), bf16[4,512,1024]{2,1,0:T(8,128)(2,1)}, u32[]{:S(2)}, u32[]{:S(2)}) %all-to-all-start.6) | async-done | bytes 4194336 | tf_op jit(solution)/shard_map/all_to_all | solution.py:539
  532.6 4.9 all-to-all-start.5
  541.7 3.3 convert_reduce_fusion
  553.3 9.2 %all-to-all-done.5.pieces_ref = bf16[4,64,2048]{2,1,0:T(8,128)(2,1)} async-done(((bf16[4,64,2048]{2,1,0:T(8,128)(2,1)}), bf16[4,64,2048]{2,1,0:T(8,128)(2,1)}, u32[]{:S(2)}, u32[]{:S(2)}) %all-to-all-start.5) | async-done | bytes 1048608 | tf_op jit(solution)/shard_map/all_to_all | solution.py:242
  562.5 3.5 all-to-all-start.4
  572.8 12.8 %all-to-all-done.4.pieces_ref = bf16[4,64,1536]{2,1,0:T(8,128)(2,1)S(1)} async-done(((bf16[4,64,1536]{2,1,0:T(8,128)(2,1)}), bf16[4,64,1536]{2,1,0:T(8,128)(2,1)S(1)}, u32[]{:S(2)}, u32[]{:S(2)}) %all-to-all-start.4) | async-done | bytes 786464 | tf_op jit(solution)/shard_map/all_to_all | solution.py:242
  (405 shorter events, 125.9 us)
Async XLA Ops:
  7.2 40.7 %all-gather.5.cloned.1.call-start = ((), (), s32[]{:S(2)}) async-start(), calls=%async_computation.9 | async-start | bytes 2359296 | tf_op jit(solution)/shard_map/all_gather | solution.py:246
  10.1 37.8 %all-to-all-start = ((bf16[4,64,1536]{2,1,0:T(8,128)(2,1)}), bf16[4,64,1536]{2,1,0:T(8,128)(2,1)S(1)}, u32[]{:S(2)}, u32[]{:S(2)}) async-start(bf16[4,64,1536]{2,1,0:T(8,128)(2,1)} %pack.2), calls=%async_computation | async-start | bytes 1572864 | tf_op jit(solution)/shard_map/all_to_all | solution.py:242
  16.5 76.7 %all-gather.7.cloned.1.call-start = ((), (), s32[]{:S(2)}) async-start(), calls=%async_computation.10 | async-start | bytes 7077888 | tf_op jit(solution)/shard_map/all_gather | solution.py:246
  16.5 28.2 %collective-permute-start = (bf16[128,2048]{1,0:T(8,128)(2,1)S(1)}, bf16[128,2048]{1,0:T(8,128)(2,1)S(1)}, u32[]{:S(2)}, u32[]{:S(2)}) collective-permute-start(bf16[128,2048]{1,0:T(8,128)(2,1)S(1)} %bitcast.120), channel_id=1, source_target_pairs={{0,8},{8,16},{16,24},{24,0},{1,9},{9,17},{17,25},{25,1},{2,10},{10... | collective-permute-start | bytes 1572872 | tf_op jit(solution)/shard_map/ppermute | solution.py:22
  48.8 100.7 %all-gather.9.cloned.1.call-start = ((), (), s32[]{:S(2)}) async-start(), calls=%async_computation.11 | async-start | bytes 9437184 | tf_op jit(solution)/shard_map/all_gather | solution.py:246
  49.6 34.6 %collective-permute-start.1 = (bf16[128,2048]{1,0:T(8,128)(2,1)S(1)}, bf16[128,2048]{1,0:T(8,128)(2,1)S(1)}, u32[]{:S(2)}, u32[]{:S(2)}) collective-permute-start(bf16[128,2048]{1,0:T(8,128)(2,1)S(1)} %bitcast.122), channel_id=1, source_target_pairs={{0,16},{8,24},{16,0},{24,8},{1,17},{9,25},{17,1},{25,9},{2,18},{10... | collective-permute-start | bytes 1572872 | tf_op jit(solution)/shard_map/ppermute | solution.py:22
  52.8 33.5 %all-to-all-start.1 = ((bf16[32,2,384]{2,1,0:T(2,128)(2,1)}), bf16[32,2,384]{2,1,0:T(2,128)(2,1)S(1)}, u32[]{:S(2)}, u32[]{:S(2)}) async-start(bf16[32,2,384]{2,1,0:T(2,128)(2,1)} %reshape.330), calls=%async_computation.1 | async-start | bytes 98304 | tf_op jit(solution)/shard_map/all_to_all | solution.py:366
  86.3 31.6 %all-to-all-start.2 = ((bf16[4,64,2048]{2,1,0:T(8,128)(2,1)}), bf16[4,64,2048]{2,1,0:T(8,128)(2,1)S(1)}, u32[]{:S(2)}, u32[]{:S(2)}) async-start(bf16[4,64,2048]{2,1,0:T(8,128)(2,1)} %pack.3), calls=%async_computation.2 | async-start | bytes 2097152 | tf_op jit(solution)/shard_map/all_to_all | solution.py:242
  91.2 116.7 %all-gather.11.cloned.1.call-start = ((), (), s32[]{:S(2)}) async-start(), calls=%async_computation.12 | async-start | bytes 9437184 | tf_op jit(solution)/shard_map/all_gather | solution.py:246
  149.5 331.6 %reduce-scatter.5.cloned.1.call-start = ((), (), s32[]{:S(2)}) async-start(), calls=%async_computation.14 | async-start | bytes 5242880 | tf_op jit(solution)/shard_map/reduce_scatter | solution.py:251
  153.7 35.1 %collective-permute-start.10 = (bf16[64,2048]{1,0:T(8,128)(2,1)}, bf16[64,2048]{1,0:T(8,128)(2,1)S(1)}, u32[]{:S(2)}, u32[]{:S(2)}) collective-permute-start(bf16[64,2048]{1,0:T(8,128)(2,1)} %get-tuple-element.218), channel_id=1, source_target_pairs={{0,16},{8,24},{16,0},{24,8},{1,17},{9,25},{17,1},{25,9},{2,18},{10... | collective-permute-start | bytes 786440 | tf_op jit(solution)/shard_map/ppermute | solution.py:22
  153.7 35.1 %collective-permute-start.11 = (bf16[64,2048]{1,0:T(8,128)(2,1)S(1)}, bf16[64,2048]{1,0:T(8,128)(2,1)S(1)}, u32[]{:S(2)}, u32[]{:S(2)}) collective-permute-start(bf16[64,2048]{1,0:T(8,128)(2,1)S(1)} %get-tuple-element.217), channel_id=1, source_target_pairs={{0,8},{8,16},{16,24},{24,0},{1,9},{9,17},{17,25},{25,1},{2,10},{10... | collective-permute-start | bytes 786440 | tf_op jit(solution)/shard_map/ppermute | solution.py:22
  156.9 32.7 %collective-permute-start.6 = (bf16[64,2048]{1,0:T(8,128)(2,1)S(1)}, bf16[64,2048]{1,0:T(8,128)(2,1)S(1)}, u32[]{:S(2)}, u32[]{:S(2)}) collective-permute-start(bf16[64,2048]{1,0:T(8,128)(2,1)S(1)} %get-tuple-element.104), channel_id=1, source_target_pairs={{0,8},{8,16},{16,24},{24,0},{1,9},{9,17},{17,25},{25,1},{2,10},{10... | collective-permute-start | bytes 786440 | tf_op jit(solution)/shard_map/ppermute | solution.py:22
  159.3 45.7 %collective-permute-start.7 = (bf16[64,2048]{1,0:T(8,128)(2,1)S(1)}, bf16[64,2048]{1,0:T(8,128)(2,1)S(1)}, u32[]{:S(2)}, u32[]{:S(2)}) collective-permute-start(bf16[64,2048]{1,0:T(8,128)(2,1)S(1)} %get-tuple-element.104), channel_id=1, source_target_pairs={{0,16},{8,24},{16,0},{24,8},{1,17},{9,25},{17,1},{25,9},{2,18},{10... | collective-permute-start | bytes 786440 | tf_op jit(solution)/shard_map/ppermute | solution.py:22
  160.7 44.3 %collective-permute-start.8 = (bf16[64,2048]{1,0:T(8,128)(2,1)S(1)}, bf16[64,2048]{1,0:T(8,128)(2,1)S(1)}, u32[]{:S(2)}, u32[]{:S(2)}) collective-permute-start(bf16[64,2048]{1,0:T(8,128)(2,1)S(1)} %get-tuple-element.104), channel_id=1, source_target_pairs={{0,24},{8,0},{16,8},{24,16},{1,25},{9,1},{17,9},{25,17},{2,26},{10... | collective-permute-start | bytes 786440 | tf_op jit(solution)/shard_map/ppermute | solution.py:22
  189.4 41.9 %collective-permute-start.15 = (bf16[64,2048]{1,0:T(8,128)(2,1)S(1)}, bf16[64,2048]{1,0:T(8,128)(2,1)}, u32[]{:S(2)}, u32[]{:S(2)}) collective-permute-start(bf16[64,2048]{1,0:T(8,128)(2,1)S(1)} %get-tuple-element.112), channel_id=1, source_target_pairs={{0,8},{8,16},{16,24},{24,0},{1,9},{9,17},{17,25},{25,1},{2,10},{10... | collective-permute-start | bytes 786440 | tf_op jit(solution)/shard_map/ppermute | solution.py:22
  189.5 42.6 %collective-permute-start.16 = (bf16[64,2048]{1,0:T(8,128)(2,1)S(1)}, bf16[64,2048]{1,0:T(8,128)(2,1)}, u32[]{:S(2)}, u32[]{:S(2)}) collective-permute-start(bf16[64,2048]{1,0:T(8,128)(2,1)S(1)} %get-tuple-element.112), channel_id=1, source_target_pairs={{0,16},{8,24},{16,0},{24,8},{1,17},{9,25},{17,1},{25,9},{2,18},{10... | collective-permute-start | bytes 786440 | tf_op jit(solution)/shard_map/ppermute | solution.py:22
  189.6 42.5 %collective-permute-start.17 = (bf16[64,2048]{1,0:T(8,128)(2,1)S(1)}, bf16[64,2048]{1,0:T(8,128)(2,1)}, u32[]{:S(2)}, u32[]{:S(2)}) collective-permute-start(bf16[64,2048]{1,0:T(8,128)(2,1)S(1)} %get-tuple-element.112), channel_id=1, source_target_pairs={{0,24},{8,0},{16,8},{24,16},{1,25},{9,1},{17,9},{25,17},{2,26},{10... | collective-permute-start | bytes 786440 | tf_op jit(solution)/shard_map/ppermute | solution.py:22
  221.3 29.2 %collective-permute-start.12 = (bf16[64,2048]{1,0:T(8,128)(2,1)S(1)}, bf16[64,2048]{1,0:T(8,128)(2,1)S(1)}, u32[]{:S(2)}, u32[]{:S(2)}) collective-permute-start(bf16[64,2048]{1,0:T(8,128)(2,1)S(1)} %get-tuple-element.237), channel_id=1, source_target_pairs={{0,24},{8,0},{16,8},{24,16},{1,25},{9,1},{17,9},{25,17},{2,26},{10... | collective-permute-start | bytes 786440 | tf_op jit(solution)/shard_map/ppermute | solution.py:22
  231.3 24.0 %collective-permute-start.13 = (bf16[64,2048]{1,0:T(8,128)(2,1)S(1)}, bf16[64,2048]{1,0:T(8,128)(2,1)S(1)}, u32[]{:S(2)}, u32[]{:S(2)}) collective-permute-start(bf16[64,2048]{1,0:T(8,128)(2,1)S(1)} %get-tuple-element.236), channel_id=1, source_target_pairs={{0,16},{8,24},{16,0},{24,8},{1,17},{9,25},{17,1},{25,9},{2,18},{10... | collective-permute-start | bytes 786440 | tf_op jit(solution)/shard_map/ppermute | solution.py:22
  231.4 23.8 %collective-permute-start.14 = (bf16[64,2048]{1,0:T(8,128)(2,1)S(1)}, bf16[64,2048]{1,0:T(8,128)(2,1)S(1)}, u32[]{:S(2)}, u32[]{:S(2)}) collective-permute-start(bf16[64,2048]{1,0:T(8,128)(2,1)S(1)} %get-tuple-element.235), channel_id=1, source_target_pairs={{0,8},{8,16},{16,24},{24,0},{1,9},{9,17},{17,25},{25,1},{2,10},{10... | collective-permute-start | bytes 786440 | tf_op jit(solution)/shard_map/ppermute | solution.py:22
  240.7 27.6 %collective-permute-start.18 = (bf16[64,2048]{1,0:T(8,128)(2,1)S(1)}, bf16[64,2048]{1,0:T(8,128)(2,1)S(1)}, u32[]{:S(2)}, u32[]{:S(2)}) collective-permute-start(bf16[64,2048]{1,0:T(8,128)(2,1)S(1)} %get-tuple-element.234), channel_id=1, source_target_pairs={{0,24},{8,0},{16,8},{24,16},{1,25},{9,1},{17,9},{25,17},{2,26},{10... | collective-permute-start | bytes 786440 | tf_op jit(solution)/shard_map/ppermute | solution.py:22
  243.6 43.3 %collective-permute-start.19 = (bf16[64,2048]{1,0:T(8,128)(2,1)S(1)}, bf16[64,2048]{1,0:T(8,128)(2,1)S(1)}, u32[]{:S(2)}, u32[]{:S(2)}) collective-permute-start(bf16[64,2048]{1,0:T(8,128)(2,1)S(1)} %get-tuple-element.233), channel_id=1, source_target_pairs={{0,16},{8,24},{16,0},{24,8},{1,17},{9,25},{17,1},{25,9},{2,18},{10... | collective-permute-start | bytes 786440 | tf_op jit(solution)/shard_map/ppermute | solution.py:22
  250.6 36.6 %collective-permute-start.20 = (bf16[64,2048]{1,0:T(8,128)(2,1)S(1)}, bf16[64,2048]{1,0:T(8,128)(2,1)S(1)}, u32[]{:S(2)}, u32[]{:S(2)}) collective-permute-start(bf16[64,2048]{1,0:T(8,128)(2,1)S(1)} %get-tuple-element.232), channel_id=1, source_target_pairs={{0,8},{8,16},{16,24},{24,0},{1,9},{9,17},{17,25},{25,1},{2,10},{10... | collective-permute-start | bytes 786440 | tf_op jit(solution)/shard_map/ppermute | solution.py:22
  255.2 99.5 %collective-permute-start.33 = (bf16[512,2048]{1,0:T(8,128)(2,1)}, bf16[512,2048]{1,0:T(8,128)(2,1)S(1)}, u32[]{:S(2)}, u32[]{:S(2)}) collective-permute-start(bf16[512,2048]{1,0:T(8,128)(2,1)} %constant_dynamic-update-slice_fusion.a), channel_id=1, source_target_pairs={{0,1},{1,0},{2,3},{3,2},{4,5},{5,4},{6,7},{7,6},{8,9},{9,8},{10,11... | collective-permute-start | bytes 6291464 | tf_op jit(solution)/shard_map/ppermute | solution.py:255
  258.2 33.9 %collective-permute-start.21 = (bf16[64,2048]{1,0:T(8,128)(2,1)S(1)}, bf16[64,2048]{1,0:T(8,128)(2,1)S(1)}, u32[]{:S(2)}, u32[]{:S(2)}) collective-permute-start(bf16[64,2048]{1,0:T(8,128)(2,1)S(1)} %get-tuple-element.125), channel_id=1, source_target_pairs={{0,8},{8,16},{16,24},{24,0},{1,9},{9,17},{17,25},{25,1},{2,10},{10... | collective-permute-start | bytes 786440 | tf_op jit(solution)/shard_map/ppermute | solution.py:22
  268.3 25.8 %collective-permute-start.22 = (bf16[64,2048]{1,0:T(8,128)(2,1)S(1)}, bf16[64,2048]{1,0:T(8,128)(2,1)S(1)}, u32[]{:S(2)}, u32[]{:S(2)}) collective-permute-start(bf16[64,2048]{1,0:T(8,128)(2,1)S(1)} %get-tuple-element.125), channel_id=1, source_target_pairs={{0,16},{8,24},{16,0},{24,8},{1,17},{9,25},{17,1},{25,9},{2,18},{10... | collective-permute-start | bytes 786440 | tf_op jit(solution)/shard_map/ppermute | solution.py:22
  286.9 23.4 %collective-permute-start.23 = (bf16[64,2048]{1,0:T(8,128)(2,1)S(1)}, bf16[64,2048]{1,0:T(8,128)(2,1)S(1)}, u32[]{:S(2)}, u32[]{:S(2)}) collective-permute-start(bf16[64,2048]{1,0:T(8,128)(2,1)S(1)} %get-tuple-element.125), channel_id=1, source_target_pairs={{0,24},{8,0},{16,8},{24,16},{1,25},{9,1},{17,9},{25,17},{2,26},{10... | collective-permute-start | bytes 786440 | tf_op jit(solution)/shard_map/ppermute | solution.py:22
  290.0 32.5 %collective-permute-start.27 = (bf16[64,2048]{1,0:T(8,128)(2,1)S(1)}, bf16[64,2048]{1,0:T(8,128)(2,1)S(1)}, u32[]{:S(2)}, u32[]{:S(2)}) collective-permute-start(bf16[64,2048]{1,0:T(8,128)(2,1)S(1)} %get-tuple-element.130), channel_id=1, source_target_pairs={{0,8},{8,16},{16,24},{24,0},{1,9},{9,17},{17,25},{25,1},{2,10},{10... | collective-permute-start | bytes 786440 | tf_op jit(solution)/shard_map/ppermute | solution.py:22
  292.1 31.6 %collective-permute-start.28 = (bf16[64,2048]{1,0:T(8,128)(2,1)S(1)}, bf16[64,2048]{1,0:T(8,128)(2,1)S(1)}, u32[]{:S(2)}, u32[]{:S(2)}) collective-permute-start(bf16[64,2048]{1,0:T(8,128)(2,1)S(1)} %get-tuple-element.130), channel_id=1, source_target_pairs={{0,16},{8,24},{16,0},{24,8},{1,17},{9,25},{17,1},{25,9},{2,18},{10... | collective-permute-start | bytes 786440 | tf_op jit(solution)/shard_map/ppermute | solution.py:22
  294.2 36.5 %collective-permute-start.29 = (bf16[64,2048]{1,0:T(8,128)(2,1)S(1)}, bf16[64,2048]{1,0:T(8,128)(2,1)S(1)}, u32[]{:S(2)}, u32[]{:S(2)}) collective-permute-start(bf16[64,2048]{1,0:T(8,128)(2,1)S(1)} %get-tuple-element.130), channel_id=1, source_target_pairs={{0,24},{8,0},{16,8},{24,16},{1,25},{9,1},{17,9},{25,17},{2,26},{10... | collective-permute-start | bytes 786440 | tf_op jit(solution)/shard_map/ppermute | solution.py:22
  322.4 23.1 %collective-permute-start.24 = (bf16[64,2048]{1,0:T(8,128)(2,1)S(1)}, bf16[64,2048]{1,0:T(8,128)(2,1)S(1)}, u32[]{:S(2)}, u32[]{:S(2)}) collective-permute-start(bf16[64,2048]{1,0:T(8,128)(2,1)S(1)} %get-tuple-element.231), channel_id=1, source_target_pairs={{0,24},{8,0},{16,8},{24,16},{1,25},{9,1},{17,9},{25,17},{2,26},{10... | collective-permute-start | bytes 786440 | tf_op jit(solution)/shard_map/ppermute | solution.py:22
  322.5 24.8 %collective-permute-start.25 = (bf16[64,2048]{1,0:T(8,128)(2,1)S(1)}, bf16[64,2048]{1,0:T(8,128)(2,1)S(1)}, u32[]{:S(2)}, u32[]{:S(2)}) collective-permute-start(bf16[64,2048]{1,0:T(8,128)(2,1)S(1)} %get-tuple-element.230), channel_id=1, source_target_pairs={{0,16},{8,24},{16,0},{24,8},{1,17},{9,25},{17,1},{25,9},{2,18},{10... | collective-permute-start | bytes 786440 | tf_op jit(solution)/shard_map/ppermute | solution.py:22
  323.7 27.0 %collective-permute-start.26 = (bf16[64,2048]{1,0:T(8,128)(2,1)S(1)}, bf16[64,2048]{1,0:T(8,128)(2,1)S(1)}, u32[]{:S(2)}, u32[]{:S(2)}) collective-permute-start(bf16[64,2048]{1,0:T(8,128)(2,1)S(1)} %get-tuple-element.229), channel_id=1, source_target_pairs={{0,8},{8,16},{16,24},{24,0},{1,9},{9,17},{17,25},{25,1},{2,10},{10... | collective-permute-start | bytes 786440 | tf_op jit(solution)/shard_map/ppermute | solution.py:22
  345.5 49.5 %collective-permute-start.41 = (bf16[512,2048]{1,0:T(8,128)(2,1)S(1)}, bf16[512,2048]{1,0:T(8,128)(2,1)}, u32[]{:S(2)}, u32[]{:S(2)}) collective-permute-start(bf16[512,2048]{1,0:T(8,128)(2,1)S(1)} %constant_dynamic-update-slice_fusion.8.a), channel_id=1, source_target_pairs={{0,1},{1,0},{2,3},{3,2},{4,5},{5,4},{6,7},{7,6},{8,9},{9,8},{10,11... | collective-permute-start | bytes 6291464 | tf_op jit(solution)/shard_map/ppermute | solution.py:255
  350.7 35.6 %collective-permute-start.31 = (bf16[64,2048]{1,0:T(8,128)(2,1)}, bf16[64,2048]{1,0:T(8,128)(2,1)}, u32[]{:S(2)}, u32[]{:S(2)}) collective-permute-start(bf16[64,2048]{1,0:T(8,128)(2,1)} %get-tuple-element.227), channel_id=1, source_target_pairs={{0,16},{8,24},{16,0},{24,8},{1,17},{9,25},{17,1},{25,9},{2,18},{10... | collective-permute-start | bytes 786440 | tf_op jit(solution)/shard_map/ppermute | solution.py:22
  352.3 34.0 %collective-permute-start.32 = (bf16[64,2048]{1,0:T(8,128)(2,1)}, bf16[64,2048]{1,0:T(8,128)(2,1)S(1)}, u32[]{:S(2)}, u32[]{:S(2)}) collective-permute-start(bf16[64,2048]{1,0:T(8,128)(2,1)} %get-tuple-element.226), channel_id=1, source_target_pairs={{0,8},{8,16},{16,24},{24,0},{1,9},{9,17},{17,25},{25,1},{2,10},{10... | collective-permute-start | bytes 786440 | tf_op jit(solution)/shard_map/ppermute | solution.py:22
  354.7 37.4 %collective-permute-start.42 = (bf16[512,1024]{1,0:T(8,128)(2,1)}, bf16[512,1024]{1,0:T(8,128)(2,1)S(1)}, u32[]{:S(2)}, u32[]{:S(2)}) collective-permute-start(bf16[512,1024]{1,0:T(8,128)(2,1)} %constant_dynamic-slice_fusion.1), channel_id=1, source_target_pairs={{0,1},{1,0},{2,3},{3,2},{4,5},{5,4},{6,7},{7,6},{8,9},{9,8},{10,11... | collective-permute-start | bytes 3145736 | tf_op jit(solution)/shard_map/ppermute | solution.py:255
  366.6 23.5 %collective-permute-start.35 = (bf16[64,2048]{1,0:T(8,128)(2,1)S(1)}, bf16[64,2048]{1,0:T(8,128)(2,1)S(1)}, u32[]{:S(2)}, u32[]{:S(2)}) collective-permute-start(bf16[64,2048]{1,0:T(8,128)(2,1)S(1)} %get-tuple-element.149), channel_id=1, source_target_pairs={{0,8},{8,16},{16,24},{24,0},{1,9},{9,17},{17,25},{25,1},{2,10},{10... | collective-permute-start | bytes 786440 | tf_op jit(solution)/shard_map/ppermute | solution.py:22
  392.1 26.8 %collective-permute-start.39 = (bf16[64,2048]{1,0:T(8,128)(2,1)S(1)}, bf16[64,2048]{1,0:T(8,128)(2,1)S(1)}, u32[]{:S(2)}, u32[]{:S(2)}) collective-permute-start(bf16[64,2048]{1,0:T(8,128)(2,1)S(1)} %get-tuple-element.150), channel_id=1, source_target_pairs={{0,16},{8,24},{16,0},{24,8},{1,17},{9,25},{17,1},{25,9},{2,18},{10... | collective-permute-start | bytes 786440 | tf_op jit(solution)/shard_map/ppermute | solution.py:22
  395.0 23.9 %collective-permute-start.40 = (bf16[64,2048]{1,0:T(8,128)(2,1)S(1)}, bf16[64,2048]{1,0:T(8,128)(2,1)S(1)}, u32[]{:S(2)}, u32[]{:S(2)}) collective-permute-start(bf16[64,2048]{1,0:T(8,128)(2,1)S(1)} %get-tuple-element.150), channel_id=1, source_target_pairs={{0,24},{8,0},{16,8},{24,16},{1,25},{9,1},{17,9},{25,17},{2,26},{10... | collective-permute-start | bytes 786440 | tf_op jit(solution)/shard_map/ppermute | solution.py:22
  397.5 148.4 %reduce-scatter.3.cloned.1.call-start = ((), (), s32[]{:S(2)}) async-start(), calls=%async_computation.13 | async-start | bytes 5242880 | tf_op jit(solution)/shard_map/reduce_scatter | solution.py:251
  407.7 27.9 %collective-permute-start.43 = (bf16[512,2048]{1,0:T(8,128)(2,1)}, bf16[512,2048]{1,0:T(8,128)(2,1)}, u32[]{:S(2)}, u32[]{:S(2)}) collective-permute-start(bf16[512,2048]{1,0:T(8,128)(2,1)} %pad_maximum_fusion.1.refs_0_.refs_1_.refs_2_.refs_3_), channel_id=1, source_target_pairs={{0,1},{1,0},{2,3},{3,2},{4,5},{5,4},{6,7},{7,6},{8,9},{9,8},{10,11... | collective-permute-start | bytes 6291464 | tf_op jit(solution)/shard_map/ppermute | solution.py:255
  467.8 64.7 %all-to-all-start.6 = ((bf16[4,512,1024]{2,1,0:T(8,128)(2,1)}), bf16[4,512,1024]{2,1,0:T(8,128)(2,1)}, u32[]{:S(2)}, u32[]{:S(2)}) async-start(bf16[4,512,1024]{2,1,0:T(8,128)(2,1)} %bitcast.117), calls=%async_computation.8 | async-start | bytes 8388608 | tf_op jit(solution)/shard_map/all_to_all | solution.py:539
  484.2 56.4 %collective-permute-start.47 = (bf16[128,2048]{1,0:T(8,128)(2,1)}, bf16[128,2048]{1,0:T(8,128)(2,1)S(1)}, u32[]{:S(2)}, u32[]{:S(2)}) collective-permute-start(bf16[128,2048]{1,0:T(8,128)(2,1)} %get-tuple-element.211), channel_id=1, source_target_pairs={{0,24},{8,0},{16,8},{24,16},{1,25},{9,1},{17,9},{25,17},{2,26},{10... | collective-permute-start | bytes 1572872 | tf_op jit(solution)/shard_map/ppermute | solution.py:22
  485.2 55.3 %collective-permute-start.48 = (bf16[128,2048]{1,0:T(8,128)(2,1)}, bf16[128,2048]{1,0:T(8,128)(2,1)S(1)}, u32[]{:S(2)}, u32[]{:S(2)}) collective-permute-start(bf16[128,2048]{1,0:T(8,128)(2,1)} %get-tuple-element.210), channel_id=1, source_target_pairs={{0,16},{8,24},{16,0},{24,8},{1,17},{9,25},{17,1},{25,9},{2,18},{10... | collective-permute-start | bytes 1572872 | tf_op jit(solution)/shard_map/ppermute | solution.py:22
  486.3 54.3 %collective-permute-start.49 = (bf16[128,2048]{1,0:T(8,128)(2,1)}, bf16[128,2048]{1,0:T(8,128)(2,1)S(1)}, u32[]{:S(2)}, u32[]{:S(2)}) collective-permute-start(bf16[128,2048]{1,0:T(8,128)(2,1)} %get-tuple-element.209), channel_id=1, source_target_pairs={{0,8},{8,16},{16,24},{24,0},{1,9},{9,17},{17,25},{25,1},{2,10},{10... | collective-permute-start | bytes 1572872 | tf_op jit(solution)/shard_map/ppermute | solution.py:22
  532.6 29.9 %all-to-all-start.5 = ((bf16[4,64,2048]{2,1,0:T(8,128)(2,1)}), bf16[4,64,2048]{2,1,0:T(8,128)(2,1)}, u32[]{:S(2)}, u32[]{:S(2)}) async-start(bf16[4,64,2048]{2,1,0:T(8,128)(2,1)} %pad_maximum_fusion.2), calls=%async_computation.7 | async-start | bytes 2097152 | tf_op jit(solution)/shard_map/all_to_all | solution.py:242
  (91 other events, 1263.7 us)
Sparse Core Ops, SparseCore 0:
  9.9 30.5 all-gather.4
  48.9 44.2 all-gather.6
  95.1 54.3 all-gather.8
  151.8 54.3 all-gather.10
  397.6 50.4 reduce-scatter.4
  451.3 89.7 reduce-scatter.2

commit v4 on v3

--- a/solution.py
+++ b/solution.py
@@ -260,30 +260,37 @@
     return lax.dynamic_slice_in_dim(value, index * width, width, axis=1)
 
 
-def feed_grad(core, own, far, grad_own, grad_far, name):
-    tokens, height = own.shape
-    width = grad_far.shape[1]
-    rows = 256
-
-    def kernel(sc, a, b, go, gf, out):
-        out[...] = (dot_tn(a[...], go[...]) + dot_tn(b[...], gf[...])).astype(bf16)
-
-    rows_spec = pl.BlockSpec((tokens, rows), lambda g, sc: (0, g))
+def feed_grads(core, first, first_far, pre, pre_far, act, act_far, ffn, ffn_far):
+    n = lax.axis_size("seq")
+    chips = lax.axis_size("chip")
+    tokens, height = first.shape
+    width = ffn_far.shape[1]
+    rows = height // (n * chips)
+
+    def kernel(sc, *refs):
+        (ao, af, po, pf, go, gf, out) = refs[2 * n :]
+        for j in range(n):
+            total = dot_tn(refs[j][...], po[...]) + dot_tn(refs[n + j][...], pf[...])
+            out[j] = total.astype(bf16)
+        total = dot_tn(ao[...], go[...]) + dot_tn(af[...], gf[...])
+        out[n:] = total.astype(bf16).reshape(n, rows, width)
+
+    def rows_spec(j):
+        return pl.BlockSpec((tokens, rows), lambda o, sc: (0, j * chips + o))
+
+    own_half = pl.BlockSpec((tokens, width), lambda o, sc: (0, sc[0]))
+    act_spec = pl.BlockSpec((tokens, n * rows), lambda o, sc: (0, o))
     return grid_call(
         kernel,
         core,
-        (height // rows,),
-        [
-            rows_spec,
-            rows_spec,
-            pl.BlockSpec((tokens, width), lambda g, sc: (0, sc[0])),
-            fixed((tokens, width)),
-        ],
-        pl.BlockSpec((rows, width), lambda g, sc: (g, 0)),
-        jax.ShapeDtypeStruct((height, width), bf16),
-        name,
-        (own, far, grad_own, grad_far),
-        flops=1,
+        (chips,),
+        [rows_spec(j) for j in range(n)] * 2
+        + [act_spec] * 2
+        + [own_half, fixed((tokens, width))] * 2,
+        pl.BlockSpec((2 * n, rows, width), lambda o, sc: (0, o, 0)),
+        jax.ShapeDtypeStruct((2 * n, chips * rows, width), bf16),
+        "feed_grads",
+        (*[first] * n, *[first_far] * n, act, act_far, pre, pre_far, ffn, ffn_far),
     )
 
 
@@ -516,10 +523,10 @@
         )
         ffn_far = to_partner(column_half(grad_ffn_full, 1 - c))
         pre_far = to_partner(column_half(grad_pre, 1 - c))
-        at = after(c, back_split[1])
-        in_low = feed_grad(at, first_full, first_far, grad_pre, pre_far, "in_grad")
-        back_blocks[1], in_low = lax.optimization_barrier((back_blocks[1], in_low))
-        in_sum = sum_over(in_low.reshape(n, part, -1), "chip")
+        feed = (first_full, first_far, grad_pre, pre_far, act, act_far, grad_ffn_full, ffn_far)
+        feed_low = feed_grads(after(c, back_split[1]), *feed)
+        back_blocks[1], feed_low = lax.optimization_barrier((back_blocks[1], feed_low))
+        feed_sum = sum_over(feed_low, "chip")
     else:
         down_low = dot_tn(act, grad_ffn_full).astype(bf16)
         in_low = dot_tn(first_full, grad_pre).astype(bf16).reshape(n, part, -1)
@@ -533,11 +540,6 @@
         grad_h1.append(norm_back(grad_first[h], normed_one[h], recip_one[h], gain_one))
         grad_attn.append(grad_h1[h].astype(bf16))
         attn_blocks.append(gather_blocks(grad_attn[h]))
-    if paired:
-        at = after(c, grad_attn[1])
-        down_low = feed_grad(at, act, act_far, grad_ffn_full, ffn_far, "down_grad")
-        down_got = lax.all_to_all(down_low.reshape(chips, -1, half), "chip", 0, 0)
-    attn_blocks = after(attn_blocks, down_low)
     shift_one_grad = sum(jnp.sum(grad_first[h], axis=0) for h in halves)
     gain_one_grad = sum(jnp.sum(grad_first[h] * normed_one[h], axis=0) for h in halves)
     out_b_grad = sum(jnp.sum(grad_attn[h].astype(f32), axis=0) for h in halves)
@@ -545,21 +547,44 @@
     grad_attn_full = jnp.concatenate([attn_blocks[h][k] for k in range(n) for h in halves], axis=0)
     grad_mixed = dot_nt(grad_attn_full, out_w).astype(bf16)
     grad_qkv, qkv_sent = attend_back(qkv, grad_mixed, seg, c)
+
+    def small_sums(grad_qkv):
+        sums = jnp.sum(grad_qkv.astype(f32), axis=0)
+        qv_grad = jnp.zeros((2 * width,), f32)
+        qv_grad = lax.dynamic_update_slice_in_dim(qv_grad, sums[:part], s * part, 0)
+        qv_grad = lax.dynamic_update_slice_in_dim(qv_grad, sums[2 * part :], width + s * part, 0)
+        in_b_all = jnp.zeros((n * hidden,), f32)
+        in_b_all = lax.dynamic_update_slice_in_dim(in_b_all, in_b_grad, s * hidden, 0)
+        return scatter_small(
+            [
+                qv_grad,
+                out_b_grad,
+                gain_one_grad,
+                shift_one_grad,
+                in_b_all,
+                down_b_grad,
+                gain_two_grad,
+                shift_two_grad,
+            ]
+        )
+
     if paired:
         attn_far = to_partner(column_half(grad_attn_full, 1 - c))
-        in_own, in_far = swap_rows(after(in_sum, qkv_sent), (n, 2, -1, half), 1, c)
-        in_pieces = exchange(jnp.concatenate([in_own, in_far], axis=2))
         args = (tok_full, tok_far, mixed, mixed_far)
         qkv_far = to_partner(qkv_sent)
         attn_low = attn_grad(c, *args, grad_qkv, qkv_far, grad_attn_full, attn_far)
         attn_sum = sum_over(attn_low, "chip")
         last_split = split_blocks(dot_nt(after(grad_qkv, attn_low), qkv_w))
         last_blocks = send_blocks(last_split)
-        down_sum = jnp.sum(after(down_got, last_split).astype(f32), axis=0)
-        down_own, down_far = swap_rows(down_sum, (2, -1, half), 0, c)
-        down_w_grad = join_halves(down_own, down_far.astype(f32), c)
+        small_grads = small_sums(after(grad_qkv, last_blocks[1]))
+        last_blocks[-1] = after(last_blocks[-1], small_grads)
+        feed_sum = after(feed_sum, last_blocks)
+        in_own, in_far = swap_rows(feed_sum[:n], (n, 2, -1, half), 1, c)
+        in_pieces = exchange(jnp.concatenate([in_own, in_far], axis=2))
         in_w_grad = join_columns(in_pieces, 1, 2, c)
-        attn_sum = after(attn_sum, last_blocks)
+        down_own, down_far = swap_rows(feed_sum[n:], (2, -1, half), 0, c)
+        down_w_grad = join_halves(down_own.astype(f32), down_far.astype(f32), c)
+        attn_sum = after(attn_sum, in_far, down_own)
         attn_own, attn_far = swap_rows(attn_sum, (n, 2, -1, half), 1, c)
         split = 3 * part // 2
         pieces = jnp.concatenate([attn_own[:, :, :split], attn_far[:, :, :split]], 2)
@@ -572,28 +597,11 @@
     else:
         last_split = split_blocks(dot_nt(grad_qkv, qkv_w))
         last_blocks = send_blocks(last_split)
+        small_grads = small_sums(after(grad_qkv, last_split))
         attn_low = after(dot_tn(tok_full, grad_qkv).astype(bf16), last_split)
         out_w_grad = sum_over(dot_tn(mixed, grad_attn_full).astype(bf16), DP).astype(f32)
         pieces = exchange(sum_over(attn_low.reshape(n, part, -1), DP))
         qkv_w_grad = join_columns(pieces, 3, 1, c)
-    sums = jnp.sum(grad_qkv.astype(f32), axis=0)
-    qv_grad = jnp.zeros((2 * width,), f32)
-    qv_grad = lax.dynamic_update_slice_in_dim(qv_grad, sums[:part], s * part, 0)
-    qv_grad = lax.dynamic_update_slice_in_dim(qv_grad, sums[2 * part :], width + s * part, 0)
-    in_b_all = jnp.zeros((n * hidden,), f32)
-    in_b_all = lax.dynamic_update_slice_in_dim(in_b_all, in_b_grad, s * hidden, 0)
-    small_grads = scatter_small(
-        [
-            qv_grad,
-            out_b_grad,
-            gain_one_grad,
-            shift_one_grad,
-            in_b_all,
-            down_b_grad,
-            gain_two_grad,
-            shift_two_grad,
-        ]
-    )
     last_blocks = after(last_blocks, small_grads)
     input_grad = (grad_h1 + total_of(last_blocks)).astype(bf16)
     return (

time: 604 us -> 595 us (0.985)
  waiting for transfers between devices: 238 us -> 261 us
  blocking collectives: 14.5 us -> 0 us
  starting transfers between devices: 133 us -> 120 us
    ppermute x42, waiting for transfers between devices: 147 us -> 176 us  [shift(): return lax.ppermute(value, 'seq', [(i, (i + step) % n) for i in range(n)])]
    all_to_all x1, waiting for transfers between devices: 42.8 us -> 27.8 us  [scatter_small(): mine = jnp.sum(lax.all_to_all(packed, ALL, 0, 0), axis=0)]
    all_to_all x1 -> x0, blocking collectives: 14.5 us -> none  [scatter_small(): mine = jnp.sum(lax.all_to_all(packed, ALL, 0, 0), axis=0)]
    ppermute x42, starting transfers between devices: 101 us -> 86.4 us  [shift(): return lax.ppermute(value, 'seq', [(i, (i + step) % n) for i in range(n)])]
    reduce_scatter x2, waiting for transfers between devices: 0.01 us -> 12.2 us  [sum_over(): lax.psum_scatter(value, axes, scatter_dimension=value.ndim - 2, tiled=True)]
    pallas_call x9 -> x8, Pallas kernels: 57 us -> 51.3 us  [grid_call(): pl.pallas_call(kernel, grid_spec=grid_spec, out_shape=out_shape, compiler...]
    unnamed x174 -> x168, local copies, waits for them, and re-layouts: 15.8 us -> 14.1 us
  transfers between devices with their start and end apart: 65 -> 65, of which waited for: 20 -> 26; matrix products, arithmetic and copies ran while one was open for 22% -> 22% of each run, Pallas kernels for 9% -> 8%
where the time goes in v4:
time: 595 us; the launch traced here: 587 us
  waiting for transfers between devices  261 us (44%)
  starting transfers between devices  120 us (20%)
  matrix products  69.5 us (12%)
  Pallas kernels  51.3 us (9%)
  other arithmetic  35.9 us (6%)
  local copies, waits for them, and re-layouts  33.5 us (6%)
  between operations  15.5 us (3%)
    ppermute x42, waiting for transfers between devices, shift(): return lax.ppermute(value, 'seq', [(i, (i + step) % n) for i in range(n)])  176 us
    ppermute x42, starting transfers between devices, shift(): return lax.ppermute(value, 'seq', [(i, (i + step) % n) for i in range(n)])  86.4 us
    pallas_call x8, Pallas kernels, grid_call(): pl.pallas_call(kernel, grid_spec=grid_spec, out_shape=out_shape, compiler...  51.3 us
    dot_general x6, matrix products, dot_nn(): lax.dot_general(a, b, (((1,), (0,)), ((), ())), preferred_element_type=f32)  35.9 us
    dot_general x6, matrix products, dot_nt(): lax.dot_general(a, b, (((1,), (1,)), ((), ())), preferred_element_type=f32)  33.6 us
    all_to_all x1, waiting for transfers between devices, scatter_small(): mine = jnp.sum(lax.all_to_all(packed, ALL, 0, 0), axis=0)  27.8 us
    all_to_all x4, waiting for transfers between devices, exchange(): return lax.all_to_all(pieces, 'seq', 0, 0)  21.1 us
    all_to_all x4, starting transfers between devices, exchange(): return lax.all_to_all(pieces, 'seq', 0, 0)  20 us
  transfers between devices with their start and end apart: 65, of which 26 were waited for; matrix products, arithmetic and copies ran while one was open for 22% of the time, Pallas kernels for 8%

profile of v4, /device:TPU:0, one launch (start us, length us, event | category | flops | bytes accessed | tf_op | source)
XLA Modules:
  0.0 586.8 jit_solution(10850674774097867752)
XLA Ops:
  10.1 6.5 %all-to-all-start = ((bf16[4,64,1536]{2,1,0:T(8,128)(2,1)}), bf16[4,64,1536]{2,1,0:T(8,128)(2,1)S(1)}, u32[]{:S(2)}, u32[]{:S(2)}) async-start(bf16[4,64,1536]{2,1,0:T(8,128)(2,1)} %pack.2), calls=%async_computation | async-start | bytes 1572864 | tf_op jit(solution)/shard_map/all_to_all | solution.py:242
  18.6 26.1 %collective-permute-done = bf16[128,2048]{1,0:T(8,128)(2,1)S(1)} collective-permute-done((bf16[128,2048]{1,0:T(8,128)(2,1)S(1)}, bf16[128,2048]{1,0:T(8,128)(2,1)S(1)}, u32[]{:S(2)}, u32[]{:S(2)}) %collective-permute-start) | collective-permute-done | bytes 524320 | tf_op jit(solution)/shard_map/ppermute | solution.py:22
  44.7 3.2 all-to-all-done
  52.8 5.9 %all-to-all-start.1 = ((bf16[32,2,384]{2,1,0:T(2,128)(2,1)}), bf16[32,2,384]{2,1,0:T(2,128)(2,1)S(1)}, u32[]{:S(2)}, u32[]{:S(2)}) async-start(bf16[32,2,384]{2,1,0:T(2,128)(2,1)} %reshape.317), calls=%async_computation.1 | async-start | bytes 98304 | tf_op jit(solution)/shard_map/all_to_all | solution.py:373
  64.1 20.0 %collective-permute-done.1 = bf16[128,2048]{1,0:T(8,128)(2,1)S(1)} collective-permute-done((bf16[128,2048]{1,0:T(8,128)(2,1)S(1)}, bf16[128,2048]{1,0:T(8,128)(2,1)S(1)}, u32[]{:S(2)}, u32[]{:S(2)}) %collective-permute-start.1) | collective-permute-done | bytes 524320 | tf_op jit(solution)/shard_map/ppermute | solution.py:22
  86.2 5.0 all-to-all-start.2
  93.2 8.8 %fusion.q.k.v = bf16[512,1536]{1,0:T(8,128)(2,1)} fusion(bf16[2048,1536]{1,0:T(8,128)(2,1)} %bitcast.143, f32[1536]{0:T(1024)S(1)} %pad_maximum_fusion.4, bf16[128,2048]{1,0:T(8,128)(2,1)S(1)} %collective-permute-done.2, bf16[128,2048]{1,0:T(8,128)(2,1)S(1)} %collective-permute-done.1, bf16[128,2048]{1,0:T(8,128)(2,1)S(1)} %collective-permute-done, ...), kind=kOutput, calls=%fused_computation.7 | convolution fusion | flops 3231186944 | bytes 9967616 | tf_op jit(solution)/shard_map/dot_general | solution.py:74
  102.0 6.5 %attend.1.refs_8_ = bf16[512,512]{1,0:T(8,128)(2,1)} custom-call(s32[1]{0:T(128)} %bitcast.1.sc.core, s32[512,1]{1,0:T(8,128)} %copy.45.seg_col, s32[1,512]{1,0:T(1,128)} %bitcast.132, bf16[512,1536]{1,0:T(8,128)(2,1)} %fusion.q.k.v, bf16[512,1536]{1,0:T(8,128)(2,1)} %fusion.q.k.v, bf16[512,1536]{1,0:T(8,128)(2,1)} %fusion.q.k.v), custom_call_target="tpu_custom_call" | custom-call | tf_op jit(solution)/shard_map/attend/pallas_call | solution.py:89
  108.5 4.3 fusion.82
  119.3 6.1 %collective-permute-done.5 = bf16[64,2048]{1,0:T(8,128)(2,1)} collective-permute-done((bf16[64,2048]{1,0:T(8,128)(2,1)}, bf16[64,2048]{1,0:T(8,128)(2,1)}, u32[]{:S(2)}, u32[]{:S(2)}) %collective-permute-start.5) | collective-permute-done | bytes 262176 | tf_op jit(solution)/shard_map/ppermute | solution.py:22
  125.4 10.6 %collective-permute-done.4 = bf16[64,2048]{1,0:T(8,128)(2,1)} collective-permute-done((bf16[64,2048]{1,0:T(8,128)(2,1)}, bf16[64,2048]{1,0:T(8,128)(2,1)}, u32[]{:S(2)}, u32[]{:S(2)}) %collective-permute-start.4) | collective-permute-done | bytes 262176 | tf_op jit(solution)/shard_map/ppermute | solution.py:22
  136.0 13.5 %all-gather.9.cloned.1.call-done = bf16[2048,2048]{1,0:T(8,128)(2,1)} async-done(((bf16[256,2048]{1,0:T(8,128)(2,1)}), bf16[2048,2048]{1,0:T(8,128)(2,1)}) %all-gather.9.cloned.1.call-update) | async-done | bytes 8388624 | tf_op jit(solution)/shard_map/all_gather | solution.py:246
  153.8 3.3 collective-permute-start.9
  164.8 3.5 collective-permute-start.8
  168.2 23.8 %collective-permute-done.10 = bf16[64,2048]{1,0:T(8,128)(2,1)S(1)} collective-permute-done((bf16[64,2048]{1,0:T(8,128)(2,1)S(1)}, bf16[64,2048]{1,0:T(8,128)(2,1)S(1)}, u32[]{:S(2)}, u32[]{:S(2)}) %collective-permute-start.10) | collective-permute-done | bytes 262176 | tf_op jit(solution)/shard_map/ppermute | solution.py:22
  193.5 4.0 collective-permute-start.17
  197.6 10.0 %collective-permute-done.7 = bf16[64,2048]{1,0:T(8,128)(2,1)S(1)} collective-permute-done((bf16[64,2048]{1,0:T(8,128)(2,1)S(1)}, bf16[64,2048]{1,0:T(8,128)(2,1)S(1)}, u32[]{:S(2)}, u32[]{:S(2)}) %collective-permute-start.7) | collective-permute-done | bytes 262176 | tf_op jit(solution)/shard_map/ppermute | solution.py:22
  208.5 8.3 %fusion.8 = (bf16[256,2048]{1,0:T(8,128)(2,1)}, bf16[256,2048]{1,0:T(8,128)(2,1)S(1)}) fusion(f32[2048]{0:T(1024)S(1)} %dynamic_slice.40, bf16[2048,2048]{1,0:T(8,128)(2,1)} %bitcast.137, bf16[64,2048]{1,0:T(8,128)(2,1)} %copy-done.44, bf16[64,2048]{1,0:T(8,128)(2,1)} %copy-done.43, bf16[64,2048]{1,0:T(8,128)(2,1)} %copy-done.42, ...), kind=kOutput, calls=%fused_computation.22 | convolution fusion | flops 2162688000 | bytes 11542528 | tf_op jit(solution)/shard_map/dot_general | solution.py:74
  216.8 5.9 fusion.83
  222.8 10.6 %collective-permute-start.12 = (bf16[64,2048]{1,0:T(8,128)(2,1)S(1)}, bf16[64,2048]{1,0:T(8,128)(2,1)S(1)}, u32[]{:S(2)}, u32[]{:S(2)}) collective-permute-start(bf16[64,2048]{1,0:T(8,128)(2,1)S(1)} %get-tuple-element.226), channel_id=1, source_target_pairs={{0,24},{8,0},{16,8},{24,16},{1,25},{9,1},{17,9},{25,17},{2,26},{10... | collective-permute-start | bytes 786440 | tf_op jit(solution)/shard_map/ppermute | solution.py:22
  234.2 6.1 %fusion.14 = (bf16[256,2048]{1,0:T(8,128)(2,1)}, bf16[256,2048]{1,0:T(8,128)(2,1)S(1)}) fusion(f32[2048]{0:T(1024)S(1)} %dynamic_slice.40, bf16[2048,2048]{1,0:T(8,128)(2,1)S(1)} %bitcast.142, bf16[64,2048]{1,0:T(8,128)(2,1)} %collective-permute-done.17, bf16[64,2048]{1,0:T(8,128)(2,1)} %collective-permute-done.16, ...), kind=kOutput, calls=%fused_computation.28 | convolution fusion | flops 2162688000 | bytes 11542528 | tf_op jit(solution)/shard_map/dot_general | solution.py:74
  250.2 7.1 %collective-permute-done.13 = bf16[64,2048]{1,0:T(8,128)(2,1)S(1)} collective-permute-done((bf16[64,2048]{1,0:T(8,128)(2,1)S(1)}, bf16[64,2048]{1,0:T(8,128)(2,1)S(1)}, u32[]{:S(2)}, u32[]{:S(2)}) %collective-permute-start.13) | collective-permute-done | bytes 262176 | tf_op jit(solution)/shard_map/ppermute | solution.py:22
  260.8 17.7 %collective-permute-start.21 = (bf16[64,2048]{1,0:T(8,128)(2,1)S(1)}, bf16[64,2048]{1,0:T(8,128)(2,1)S(1)}, u32[]{:S(2)}, u32[]{:S(2)}) collective-permute-start(bf16[64,2048]{1,0:T(8,128)(2,1)S(1)} %get-tuple-element.117), channel_id=1, source_target_pairs={{0,8},{8,16},{16,24},{24,0},{1,9},{9,17},{17,25},{25,1},{2,10},{10... | collective-permute-start | bytes 786440 | tf_op jit(solution)/shard_map/ppermute | solution.py:22
  278.6 8.9 %collective-permute-done.19 = bf16[64,2048]{1,0:T(8,128)(2,1)S(1)} collective-permute-done((bf16[64,2048]{1,0:T(8,128)(2,1)S(1)}, bf16[64,2048]{1,0:T(8,128)(2,1)S(1)}, u32[]{:S(2)}, u32[]{:S(2)}) %collective-permute-start.19) | collective-permute-done | bytes 262176 | tf_op jit(solution)/shard_map/ppermute | solution.py:22
  292.6 16.3 %collective-permute-done.22 = bf16[64,2048]{1,0:T(8,128)(2,1)S(1)} collective-permute-done((bf16[64,2048]{1,0:T(8,128)(2,1)S(1)}, bf16[64,2048]{1,0:T(8,128)(2,1)S(1)}, u32[]{:S(2)}, u32[]{:S(2)}) %collective-permute-start.22) | collective-permute-done | bytes 262176 | tf_op jit(solution)/shard_map/ppermute | solution.py:22
  308.9 5.8 fusion.1
  314.7 6.1 %fusion.85 = (bf16[256,2048]{1,0:T(8,128)(2,1)S(1)}, f32[256,2048]{1,0:T(8,128)S(1)}) fusion(bf16[256,2048]{1,0:T(8,128)(2,1)S(1)} %fusion.1, bf16[2048,2048]{1,0:T(8,128)(2,1)} %bitcast.138), kind=kOutput, calls=%fused_computation.228 | convolution fusion | flops 2148007936 | bytes 12582912 | tf_op jit(solution)/shard_map/dot_general | solution.py:78
  321.0 6.7 %collective-permute-start.24 = (bf16[64,2048]{1,0:T(8,128)(2,1)S(1)}, bf16[64,2048]{1,0:T(8,128)(2,1)S(1)}, u32[]{:S(2)}, u32[]{:S(2)}) collective-permute-start(bf16[64,2048]{1,0:T(8,128)(2,1)S(1)} %get-tuple-element.220), channel_id=1, source_target_pairs={{0,24},{8,0},{16,8},{24,16},{1,25},{9,1},{17,9},{25,17},{2,26},{10... | collective-permute-start | bytes 786440 | tf_op jit(solution)/shard_map/ppermute | solution.py:22
  328.7 5.8 fusion.2
  334.5 6.1 %fusion.86 = (bf16[256,2048]{1,0:T(8,128)(2,1)S(1)}, f32[256,2048]{1,0:T(8,128)S(1)}) fusion(bf16[256,2048]{1,0:T(8,128)(2,1)S(1)} %fusion.2, bf16[2048,2048]{1,0:T(8,128)(2,1)} %bitcast.139), kind=kOutput, calls=%fused_computation.229 | convolution fusion | flops 2148007936 | bytes 12582912 | tf_op jit(solution)/shard_map/dot_general | solution.py:78
  347.0 6.7 %collective-permute-done.26 = bf16[64,2048]{1,0:T(8,128)(2,1)S(1)} collective-permute-done((bf16[64,2048]{1,0:T(8,128)(2,1)S(1)}, bf16[64,2048]{1,0:T(8,128)(2,1)S(1)}, u32[]{:S(2)}, u32[]{:S(2)}) %collective-permute-start.26) | collective-permute-done | bytes 262176 | tf_op jit(solution)/shard_map/ppermute | solution.py:22
  362.4 14.4 %feed_grads.1 = bf16[8,512,1024]{2,1,0:T(8,128)(2,1)} custom-call(s32[1]{0:T(128)} %bitcast.15.sc, bf16[512,2048]{1,0:T(8,128)(2,1)} %copy-done, bf16[512,2048]{1,0:T(8,128)(2,1)} %copy-done, bf16[512,2048]{1,0:T(8,128)(2,1)} %copy-done, bf16[512,2048]{1,0:T(8,128)(2,1)} %copy-done, bf16[512,2048]{1,0:T(8,128)(2,1)} %copy-done.1, ...), custom_call_target="tpu_custom_call" | custom-call | tf_op jit(solution)/shard_map/feed_grads/pallas_call | solution.py:89
  379.3 14.4 %collective-permute-done.31 = bf16[64,2048]{1,0:T(8,128)(2,1)} collective-permute-done((bf16[64,2048]{1,0:T(8,128)(2,1)}, bf16[64,2048]{1,0:T(8,128)(2,1)}, u32[]{:S(2)}, u32[]{:S(2)}) %collective-permute-start.31) | collective-permute-done | bytes 262176 | tf_op jit(solution)/shard_map/ppermute | solution.py:22
  400.9 5.1 collective-permute-done.38
  406.0 3.7 collective-permute-start.42
  410.8 6.5 %collective-permute-done.40 = bf16[64,2048]{1,0:T(8,128)(2,1)S(1)} collective-permute-done((bf16[64,2048]{1,0:T(8,128)(2,1)S(1)}, bf16[64,2048]{1,0:T(8,128)(2,1)S(1)}, u32[]{:S(2)}, u32[]{:S(2)}) %collective-permute-start.40) | collective-permute-done | bytes 262176 | tf_op jit(solution)/shard_map/ppermute | solution.py:22
  418.3 5.3 collective-permute-done.42
  426.9 11.3 %attend_back.1 = (bf16[512,1536]{1,0:T(8,128)(2,1)}, bf16[512,768]{1,0:T(8,128)(2,1)}) custom-call(s32[1]{0:T(128)} %bitcast.1.sc.core, s32[512,1]{1,0:T(8,128)} %copy.45.seg_col, s32[1,512]{1,0:T(1,128)} %bitcast.133, bf16[512,1536]{1,0:T(8,128)(2,1)} %fusion.q.k.v, bf16[512,1536]{1,0:T(8,128)(2,1)} %fusion.q.k.v, bf16[512,1536]{1,0:T(8,128)(2,1)} %fusion.q.k.v, ...), custom_call_target="tpu_custom_call" | custom-call | flops 399999991808 | bytes 1 | tf_op jit(solution)/shard_map/attend_back/pallas_call | solution.py:89
  442.6 9.7 %attn_grad.1 = bf16[4,512,1024]{2,1,0:T(8,128)(2,1)} custom-call(s32[1]{0:T(128)} %bitcast.1.sc.core, bf16[512,2048]{1,0:T(8,128)(2,1)} %pad_maximum_fusion.1.refs_0_.refs_1_.refs_2_.refs_3_, bf16[512,2048]{1,0:T(8,128)(2,1)} %pad_maximum_fusion.1.refs_0_.refs_1_.refs_2_.refs_3_, bf16[512,2048]{1,0:T(8,128)(2,1)} %pad_maximum_fusion.1.refs_0_.refs_1_.refs_2_.refs_3_, ...), custom_call_target="tpu_custom_call" | custom-call | tf_op jit(solution)/shard_map/attn_grad/pallas_call | solution.py:89
  453.7 7.8 %fusion.87 = (bf16[512,2048]{1,0:T(8,128)(2,1)S(1)}, f32[512,2048]{1,0:T(8,128)}) fusion(bf16[512,1536]{1,0:T(8,128)(2,1)S(1)} %copy-done.2, bf16[2048,1536]{1,0:T(8,128)(2,1)} %bitcast.144), kind=kOutput, calls=%fused_computation.230 | convolution fusion | flops 3222274048 | bytes 14155776 | tf_op jit(solution)/shard_map/dot_general | solution.py:78
  471.0 7.3 %collective-permute-done.47 = bf16[128,2048]{1,0:T(8,128)(2,1)} collective-permute-done((bf16[128,2048]{1,0:T(8,128)(2,1)}, bf16[128,2048]{1,0:T(8,128)(2,1)}, u32[]{:S(2)}, u32[]{:S(2)}) %collective-permute-start.47) | collective-permute-done | bytes 524320 | tf_op jit(solution)/shard_map/ppermute | solution.py:22
  479.6 5.8 all-to-all-start.3
  487.7 27.8 %all-to-all-done.3 = f32[32,1,768]{2,1,0:T(1,128)S(1)} async-done(((f32[32,1,768]{2,1,0:T(1,128)}), f32[32,1,768]{2,1,0:T(1,128)S(1)}, u32[]{:S(2)}, u32[]{:S(2)}) %all-to-all-start.3) | async-done | bytes 98336 | tf_op jit(solution)/shard_map/all_to_all | solution.py:386
  523.0 4.4 all-to-all-start.5
  529.2 12.2 %reduce-scatter.3.cloned.1.call-done = bf16[4,128,1024]{2,1,0:T(8,128)(2,1)} async-done(((bf16[4,512,1024]{2,1,0:T(8,128)(2,1)}), bf16[4,128,1024]{2,1,0:T(8,128)(2,1)}) %reduce-scatter.3.cloned.1.call-update) | async-done | bytes 1048592 | tf_op jit(solution)/shard_map/reduce_scatter | solution.py:251
  548.4 5.0 all-to-all-done.5.pieces_ref
  553.4 4.2 all-to-all-start.4
  564.4 12.9 %all-to-all-done.4.pieces_ref = bf16[4,64,1536]{2,1,0:T(8,128)(2,1)} async-done(((bf16[4,64,1536]{2,1,0:T(8,128)(2,1)}), bf16[4,64,1536]{2,1,0:T(8,128)(2,1)}, u32[]{:S(2)}, u32[]{:S(2)}) %all-to-all-start.4) | async-done | bytes 786464 | tf_op jit(solution)/shard_map/all_to_all | solution.py:242
  (396 shorter events, 134.4 us)
Async XLA Ops:
  7.2 40.7 %all-gather.5.cloned.1.call-start = ((), (), s32[]{:S(2)}) async-start(), calls=%async_computation.8 | async-start | bytes 2359296 | tf_op jit(solution)/shard_map/all_gather | solution.py:246
  10.1 37.8 %all-to-all-start = ((bf16[4,64,1536]{2,1,0:T(8,128)(2,1)}), bf16[4,64,1536]{2,1,0:T(8,128)(2,1)S(1)}, u32[]{:S(2)}, u32[]{:S(2)}) async-start(bf16[4,64,1536]{2,1,0:T(8,128)(2,1)} %pack.2), calls=%async_computation | async-start | bytes 1572864 | tf_op jit(solution)/shard_map/all_to_all | solution.py:242
  16.5 76.6 %all-gather.7.cloned.1.call-start = ((), (), s32[]{:S(2)}) async-start(), calls=%async_computation.9 | async-start | bytes 7077888 | tf_op jit(solution)/shard_map/all_gather | solution.py:246
  16.5 28.2 %collective-permute-start = (bf16[128,2048]{1,0:T(8,128)(2,1)S(1)}, bf16[128,2048]{1,0:T(8,128)(2,1)S(1)}, u32[]{:S(2)}, u32[]{:S(2)}) collective-permute-start(bf16[128,2048]{1,0:T(8,128)(2,1)S(1)} %bitcast.120), channel_id=1, source_target_pairs={{0,8},{8,16},{16,24},{24,0},{1,9},{9,17},{17,25},{25,1},{2,10},{10... | collective-permute-start | bytes 1572872 | tf_op jit(solution)/shard_map/ppermute | solution.py:22
  48.8 100.7 %all-gather.9.cloned.1.call-start = ((), (), s32[]{:S(2)}) async-start(), calls=%async_computation.10 | async-start | bytes 9437184 | tf_op jit(solution)/shard_map/all_gather | solution.py:246
  49.6 34.6 %collective-permute-start.1 = (bf16[128,2048]{1,0:T(8,128)(2,1)S(1)}, bf16[128,2048]{1,0:T(8,128)(2,1)S(1)}, u32[]{:S(2)}, u32[]{:S(2)}) collective-permute-start(bf16[128,2048]{1,0:T(8,128)(2,1)S(1)} %bitcast.122), channel_id=1, source_target_pairs={{0,16},{8,24},{16,0},{24,8},{1,17},{9,25},{17,1},{25,9},{2,18},{10... | collective-permute-start | bytes 1572872 | tf_op jit(solution)/shard_map/ppermute | solution.py:22
  52.8 33.5 %all-to-all-start.1 = ((bf16[32,2,384]{2,1,0:T(2,128)(2,1)}), bf16[32,2,384]{2,1,0:T(2,128)(2,1)S(1)}, u32[]{:S(2)}, u32[]{:S(2)}) async-start(bf16[32,2,384]{2,1,0:T(2,128)(2,1)} %reshape.317), calls=%async_computation.1 | async-start | bytes 98304 | tf_op jit(solution)/shard_map/all_to_all | solution.py:373
  86.2 33.1 %all-to-all-start.2 = ((bf16[4,64,2048]{2,1,0:T(8,128)(2,1)}), bf16[4,64,2048]{2,1,0:T(8,128)(2,1)S(1)}, u32[]{:S(2)}, u32[]{:S(2)}) async-start(bf16[4,64,2048]{2,1,0:T(8,128)(2,1)} %pack.3), calls=%async_computation.2 | async-start | bytes 2097152 | tf_op jit(solution)/shard_map/all_to_all | solution.py:242
  91.2 117.2 %all-gather.11.cloned.1.call-start = ((), (), s32[]{:S(2)}) async-start(), calls=%async_computation.11 | async-start | bytes 9437184 | tf_op jit(solution)/shard_map/all_gather | solution.py:246
  115.5 20.4 %collective-permute-start.4 = (bf16[64,2048]{1,0:T(8,128)(2,1)}, bf16[64,2048]{1,0:T(8,128)(2,1)}, u32[]{:S(2)}, u32[]{:S(2)}) collective-permute-start(bf16[64,2048]{1,0:T(8,128)(2,1)} %get-tuple-element.209), channel_id=1, source_target_pairs={{0,16},{8,24},{16,0},{24,8},{1,17},{9,25},{17,1},{25,9},{2,18},{10... | collective-permute-start | bytes 786440 | tf_op jit(solution)/shard_map/ppermute | solution.py:22
  117.9 18.1 %collective-permute-start.3 = (bf16[64,2048]{1,0:T(8,128)(2,1)}, bf16[64,2048]{1,0:T(8,128)(2,1)}, u32[]{:S(2)}, u32[]{:S(2)}) collective-permute-start(bf16[64,2048]{1,0:T(8,128)(2,1)} %get-tuple-element.204), channel_id=1, source_target_pairs={{0,24},{8,0},{16,8},{24,16},{1,25},{9,1},{17,9},{25,17},{2,26},{10... | collective-permute-start | bytes 786440 | tf_op jit(solution)/shard_map/ppermute | solution.py:22
  149.5 368.7 %reduce-scatter.5.cloned.1.call-start = ((), (), s32[]{:S(2)}) async-start(), calls=%async_computation.13 | async-start | bytes 10485760 | tf_op jit(solution)/shard_map/reduce_scatter | solution.py:251
  157.1 34.9 %collective-permute-start.10 = (bf16[64,2048]{1,0:T(8,128)(2,1)S(1)}, bf16[64,2048]{1,0:T(8,128)(2,1)S(1)}, u32[]{:S(2)}, u32[]{:S(2)}) collective-permute-start(bf16[64,2048]{1,0:T(8,128)(2,1)S(1)} %copy-done.40), channel_id=1, source_target_pairs={{0,16},{8,24},{16,0},{24,8},{1,17},{9,25},{17,1},{25,9},{2,18},{10... | collective-permute-start | bytes 786440 | tf_op jit(solution)/shard_map/ppermute | solution.py:22
  157.2 34.9 %collective-permute-start.11 = (bf16[64,2048]{1,0:T(8,128)(2,1)S(1)}, bf16[64,2048]{1,0:T(8,128)(2,1)S(1)}, u32[]{:S(2)}, u32[]{:S(2)}) collective-permute-start(bf16[64,2048]{1,0:T(8,128)(2,1)S(1)} %copy-done.39), channel_id=1, source_target_pairs={{0,8},{8,16},{16,24},{24,0},{1,9},{9,17},{17,25},{25,1},{2,10},{10... | collective-permute-start | bytes 786440 | tf_op jit(solution)/shard_map/ppermute | solution.py:22
  161.4 32.1 %collective-permute-start.6 = (bf16[64,2048]{1,0:T(8,128)(2,1)S(1)}, bf16[64,2048]{1,0:T(8,128)(2,1)S(1)}, u32[]{:S(2)}, u32[]{:S(2)}) collective-permute-start(bf16[64,2048]{1,0:T(8,128)(2,1)S(1)} %get-tuple-element.96), channel_id=1, source_target_pairs={{0,8},{8,16},{16,24},{24,0},{1,9},{9,17},{17,25},{25,1},{2,10},{10... | collective-permute-start | bytes 786440 | tf_op jit(solution)/shard_map/ppermute | solution.py:22
  163.7 43.9 %collective-permute-start.7 = (bf16[64,2048]{1,0:T(8,128)(2,1)S(1)}, bf16[64,2048]{1,0:T(8,128)(2,1)S(1)}, u32[]{:S(2)}, u32[]{:S(2)}) collective-permute-start(bf16[64,2048]{1,0:T(8,128)(2,1)S(1)} %get-tuple-element.96), channel_id=1, source_target_pairs={{0,16},{8,24},{16,0},{24,8},{1,17},{9,25},{17,1},{25,9},{2,18},{10... | collective-permute-start | bytes 786440 | tf_op jit(solution)/shard_map/ppermute | solution.py:22
  164.8 42.8 %collective-permute-start.8 = (bf16[64,2048]{1,0:T(8,128)(2,1)S(1)}, bf16[64,2048]{1,0:T(8,128)(2,1)S(1)}, u32[]{:S(2)}, u32[]{:S(2)}) collective-permute-start(bf16[64,2048]{1,0:T(8,128)(2,1)S(1)} %get-tuple-element.96), channel_id=1, source_target_pairs={{0,24},{8,0},{16,8},{24,16},{1,25},{9,1},{17,9},{25,17},{2,26},{10... | collective-permute-start | bytes 786440 | tf_op jit(solution)/shard_map/ppermute | solution.py:22
  193.5 40.0 %collective-permute-start.15 = (bf16[64,2048]{1,0:T(8,128)(2,1)S(1)}, bf16[64,2048]{1,0:T(8,128)(2,1)}, u32[]{:S(2)}, u32[]{:S(2)}) collective-permute-start(bf16[64,2048]{1,0:T(8,128)(2,1)S(1)} %get-tuple-element.104), channel_id=1, source_target_pairs={{0,8},{8,16},{16,24},{24,0},{1,9},{9,17},{17,25},{25,1},{2,10},{10... | collective-permute-start | bytes 786440 | tf_op jit(solution)/shard_map/ppermute | solution.py:22
  193.5 40.7 %collective-permute-start.16 = (bf16[64,2048]{1,0:T(8,128)(2,1)S(1)}, bf16[64,2048]{1,0:T(8,128)(2,1)}, u32[]{:S(2)}, u32[]{:S(2)}) collective-permute-start(bf16[64,2048]{1,0:T(8,128)(2,1)S(1)} %get-tuple-element.104), channel_id=1, source_target_pairs={{0,16},{8,24},{16,0},{24,8},{1,17},{9,25},{17,1},{25,9},{2,18},{10... | collective-permute-start | bytes 786440 | tf_op jit(solution)/shard_map/ppermute | solution.py:22
  193.5 40.7 %collective-permute-start.17 = (bf16[64,2048]{1,0:T(8,128)(2,1)S(1)}, bf16[64,2048]{1,0:T(8,128)(2,1)}, u32[]{:S(2)}, u32[]{:S(2)}) collective-permute-start(bf16[64,2048]{1,0:T(8,128)(2,1)S(1)} %get-tuple-element.104), channel_id=1, source_target_pairs={{0,24},{8,0},{16,8},{24,16},{1,25},{9,1},{17,9},{25,17},{2,26},{10... | collective-permute-start | bytes 786440 | tf_op jit(solution)/shard_map/ppermute | solution.py:22
  222.8 27.2 %collective-permute-start.12 = (bf16[64,2048]{1,0:T(8,128)(2,1)S(1)}, bf16[64,2048]{1,0:T(8,128)(2,1)S(1)}, u32[]{:S(2)}, u32[]{:S(2)}) collective-permute-start(bf16[64,2048]{1,0:T(8,128)(2,1)S(1)} %get-tuple-element.226), channel_id=1, source_target_pairs={{0,24},{8,0},{16,8},{24,16},{1,25},{9,1},{17,9},{25,17},{2,26},{10... | collective-permute-start | bytes 786440 | tf_op jit(solution)/shard_map/ppermute | solution.py:22
  233.4 23.9 %collective-permute-start.13 = (bf16[64,2048]{1,0:T(8,128)(2,1)S(1)}, bf16[64,2048]{1,0:T(8,128)(2,1)S(1)}, u32[]{:S(2)}, u32[]{:S(2)}) collective-permute-start(bf16[64,2048]{1,0:T(8,128)(2,1)S(1)} %get-tuple-element.225), channel_id=1, source_target_pairs={{0,16},{8,24},{16,0},{24,8},{1,17},{9,25},{17,1},{25,9},{2,18},{10... | collective-permute-start | bytes 786440 | tf_op jit(solution)/shard_map/ppermute | solution.py:22
  233.5 23.8 %collective-permute-start.14 = (bf16[64,2048]{1,0:T(8,128)(2,1)S(1)}, bf16[64,2048]{1,0:T(8,128)(2,1)S(1)}, u32[]{:S(2)}, u32[]{:S(2)}) collective-permute-start(bf16[64,2048]{1,0:T(8,128)(2,1)S(1)} %get-tuple-element.224), channel_id=1, source_target_pairs={{0,8},{8,16},{16,24},{24,0},{1,9},{9,17},{17,25},{25,1},{2,10},{10... | collective-permute-start | bytes 786440 | tf_op jit(solution)/shard_map/ppermute | solution.py:22
  242.9 17.9 %collective-permute-start.18 = (bf16[64,2048]{1,0:T(8,128)(2,1)S(1)}, bf16[64,2048]{1,0:T(8,128)(2,1)S(1)}, u32[]{:S(2)}, u32[]{:S(2)}) collective-permute-start(bf16[64,2048]{1,0:T(8,128)(2,1)S(1)} %get-tuple-element.223), channel_id=1, source_target_pairs={{0,24},{8,0},{16,8},{24,16},{1,25},{9,1},{17,9},{25,17},{2,26},{10... | collective-permute-start | bytes 786440 | tf_op jit(solution)/shard_map/ppermute | solution.py:22
  245.8 41.7 %collective-permute-start.19 = (bf16[64,2048]{1,0:T(8,128)(2,1)S(1)}, bf16[64,2048]{1,0:T(8,128)(2,1)S(1)}, u32[]{:S(2)}, u32[]{:S(2)}) collective-permute-start(bf16[64,2048]{1,0:T(8,128)(2,1)S(1)} %get-tuple-element.222), channel_id=1, source_target_pairs={{0,16},{8,24},{16,0},{24,8},{1,17},{9,25},{17,1},{25,9},{2,18},{10... | collective-permute-start | bytes 786440 | tf_op jit(solution)/shard_map/ppermute | solution.py:22
  250.0 37.5 %collective-permute-start.20 = (bf16[64,2048]{1,0:T(8,128)(2,1)S(1)}, bf16[64,2048]{1,0:T(8,128)(2,1)S(1)}, u32[]{:S(2)}, u32[]{:S(2)}) collective-permute-start(bf16[64,2048]{1,0:T(8,128)(2,1)S(1)} %get-tuple-element.221), channel_id=1, source_target_pairs={{0,8},{8,16},{16,24},{24,0},{1,9},{9,17},{17,25},{25,1},{2,10},{10... | collective-permute-start | bytes 786440 | tf_op jit(solution)/shard_map/ppermute | solution.py:22
  257.3 102.3 %collective-permute-start.33 = (bf16[512,2048]{1,0:T(8,128)(2,1)S(1)}, bf16[512,2048]{1,0:T(8,128)(2,1)S(1)}, u32[]{:S(2)}, u32[]{:S(2)}) collective-permute-start(bf16[512,2048]{1,0:T(8,128)(2,1)S(1)} %constant_dynamic-update-slice_fusion.refs_0_.refs_1_.refs_2_.refs_3_), channel_id=1, source_target_pairs={{0,1},{1,0},{2,3},{3,2},{4,5},{5,4},{6,7},{7,6},{8,9},{9,8},{10,11... | collective-permute-start | bytes 6291464 | tf_op jit(solution)/shard_map/ppermute | solution.py:255
  257.3 102.3 %collective-permute-start.34 = (bf16[512,2048]{1,0:T(8,128)(2,1)S(1)}, bf16[512,2048]{1,0:T(8,128)(2,1)S(1)}, u32[]{:S(2)}, u32[]{:S(2)}) collective-permute-start(bf16[512,2048]{1,0:T(8,128)(2,1)S(1)} %constant_dynamic-update-slice_fusion.8.refs_8_), channel_id=1, source_target_pairs={{0,1},{1,0},{2,3},{3,2},{4,5},{5,4},{6,7},{7,6},{8,9},{9,8},{10,11... | collective-permute-start | bytes 6291464 | tf_op jit(solution)/shard_map/ppermute | solution.py:255
  260.8 29.8 %collective-permute-start.21 = (bf16[64,2048]{1,0:T(8,128)(2,1)S(1)}, bf16[64,2048]{1,0:T(8,128)(2,1)S(1)}, u32[]{:S(2)}, u32[]{:S(2)}) collective-permute-start(bf16[64,2048]{1,0:T(8,128)(2,1)S(1)} %get-tuple-element.117), channel_id=1, source_target_pairs={{0,8},{8,16},{16,24},{24,0},{1,9},{9,17},{17,25},{25,1},{2,10},{10... | collective-permute-start | bytes 786440 | tf_op jit(solution)/shard_map/ppermute | solution.py:22
  287.5 21.4 %collective-permute-start.22 = (bf16[64,2048]{1,0:T(8,128)(2,1)S(1)}, bf16[64,2048]{1,0:T(8,128)(2,1)S(1)}, u32[]{:S(2)}, u32[]{:S(2)}) collective-permute-start(bf16[64,2048]{1,0:T(8,128)(2,1)S(1)} %get-tuple-element.117), channel_id=1, source_target_pairs={{0,16},{8,24},{16,0},{24,8},{1,17},{9,25},{17,1},{25,9},{2,18},{10... | collective-permute-start | bytes 786440 | tf_op jit(solution)/shard_map/ppermute | solution.py:22
  287.5 21.4 %collective-permute-start.23 = (bf16[64,2048]{1,0:T(8,128)(2,1)S(1)}, bf16[64,2048]{1,0:T(8,128)(2,1)S(1)}, u32[]{:S(2)}, u32[]{:S(2)}) collective-permute-start(bf16[64,2048]{1,0:T(8,128)(2,1)S(1)} %get-tuple-element.117), channel_id=1, source_target_pairs={{0,24},{8,0},{16,8},{24,16},{1,25},{9,1},{17,9},{25,17},{2,26},{10... | collective-permute-start | bytes 786440 | tf_op jit(solution)/shard_map/ppermute | solution.py:22
  290.6 30.4 %collective-permute-start.27 = (bf16[64,2048]{1,0:T(8,128)(2,1)S(1)}, bf16[64,2048]{1,0:T(8,128)(2,1)S(1)}, u32[]{:S(2)}, u32[]{:S(2)}) collective-permute-start(bf16[64,2048]{1,0:T(8,128)(2,1)S(1)} %get-tuple-element.122), channel_id=1, source_target_pairs={{0,8},{8,16},{16,24},{24,0},{1,9},{9,17},{17,25},{25,1},{2,10},{10... | collective-permute-start | bytes 786440 | tf_op jit(solution)/shard_map/ppermute | solution.py:22
  308.9 18.8 %collective-permute-start.28 = (bf16[64,2048]{1,0:T(8,128)(2,1)S(1)}, bf16[64,2048]{1,0:T(8,128)(2,1)S(1)}, u32[]{:S(2)}, u32[]{:S(2)}) collective-permute-start(bf16[64,2048]{1,0:T(8,128)(2,1)S(1)} %get-tuple-element.122), channel_id=1, source_target_pairs={{0,16},{8,24},{16,0},{24,8},{1,17},{9,25},{17,1},{25,9},{2,18},{10... | collective-permute-start | bytes 786440 | tf_op jit(solution)/shard_map/ppermute | solution.py:22
  308.9 19.9 %collective-permute-start.29 = (bf16[64,2048]{1,0:T(8,128)(2,1)S(1)}, bf16[64,2048]{1,0:T(8,128)(2,1)S(1)}, u32[]{:S(2)}, u32[]{:S(2)}) collective-permute-start(bf16[64,2048]{1,0:T(8,128)(2,1)S(1)} %get-tuple-element.122), channel_id=1, source_target_pairs={{0,24},{8,0},{16,8},{24,16},{1,25},{9,1},{17,9},{25,17},{2,26},{10... | collective-permute-start | bytes 786440 | tf_op jit(solution)/shard_map/ppermute | solution.py:22
  321.0 20.2 %collective-permute-start.24 = (bf16[64,2048]{1,0:T(8,128)(2,1)S(1)}, bf16[64,2048]{1,0:T(8,128)(2,1)S(1)}, u32[]{:S(2)}, u32[]{:S(2)}) collective-permute-start(bf16[64,2048]{1,0:T(8,128)(2,1)S(1)} %get-tuple-element.220), channel_id=1, source_target_pairs={{0,24},{8,0},{16,8},{24,16},{1,25},{9,1},{17,9},{25,17},{2,26},{10... | collective-permute-start | bytes 786440 | tf_op jit(solution)/shard_map/ppermute | solution.py:22
  353.7 23.1 %collective-permute-start.30 = (bf16[64,2048]{1,0:T(8,128)(2,1)}, bf16[64,2048]{1,0:T(8,128)(2,1)}, u32[]{:S(2)}, u32[]{:S(2)}) collective-permute-start(bf16[64,2048]{1,0:T(8,128)(2,1)} %get-tuple-element.217), channel_id=1, source_target_pairs={{0,24},{8,0},{16,8},{24,16},{1,25},{9,1},{17,9},{25,17},{2,26},{10... | collective-permute-start | bytes 786440 | tf_op jit(solution)/shard_map/ppermute | solution.py:22
  354.7 39.1 %collective-permute-start.31 = (bf16[64,2048]{1,0:T(8,128)(2,1)}, bf16[64,2048]{1,0:T(8,128)(2,1)}, u32[]{:S(2)}, u32[]{:S(2)}) collective-permute-start(bf16[64,2048]{1,0:T(8,128)(2,1)} %get-tuple-element.216), channel_id=1, source_target_pairs={{0,16},{8,24},{16,0},{24,8},{1,17},{9,25},{17,1},{25,9},{2,18},{10... | collective-permute-start | bytes 786440 | tf_op jit(solution)/shard_map/ppermute | solution.py:22
  356.3 37.4 %collective-permute-start.32 = (bf16[64,2048]{1,0:T(8,128)(2,1)}, bf16[64,2048]{1,0:T(8,128)(2,1)}, u32[]{:S(2)}, u32[]{:S(2)}) collective-permute-start(bf16[64,2048]{1,0:T(8,128)(2,1)} %get-tuple-element.215), channel_id=1, source_target_pairs={{0,8},{8,16},{16,24},{24,0},{1,9},{9,17},{17,25},{25,1},{2,10},{10... | collective-permute-start | bytes 786440 | tf_op jit(solution)/shard_map/ppermute | solution.py:22
  359.6 79.3 %collective-permute-start.43 = (bf16[512,2048]{1,0:T(8,128)(2,1)}, bf16[512,2048]{1,0:T(8,128)(2,1)}, u32[]{:S(2)}, u32[]{:S(2)}) collective-permute-start(bf16[512,2048]{1,0:T(8,128)(2,1)} %pad_maximum_fusion.1.refs_0_.refs_1_.refs_2_.refs_3_), channel_id=1, source_target_pairs={{0,1},{1,0},{2,3},{3,2},{4,5},{5,4},{6,7},{7,6},{8,9},{9,8},{10,11... | collective-permute-start | bytes 6291464 | tf_op jit(solution)/shard_map/ppermute | solution.py:255
  361.0 38.8 %collective-permute-start.37 = (bf16[64,2048]{1,0:T(8,128)(2,1)S(1)}, bf16[64,2048]{1,0:T(8,128)(2,1)}, u32[]{:S(2)}, u32[]{:S(2)}) collective-permute-start(bf16[64,2048]{1,0:T(8,128)(2,1)S(1)} %get-tuple-element.178), channel_id=1, source_target_pairs={{0,8},{8,16},{16,24},{24,0},{1,9},{9,17},{17,25},{25,1},{2,10},{10... | collective-permute-start | bytes 786440 | tf_op jit(solution)/shard_map/ppermute | solution.py:22
  376.8 32.9 %collective-permute-start.39 = (bf16[64,2048]{1,0:T(8,128)(2,1)S(1)}, bf16[64,2048]{1,0:T(8,128)(2,1)}, u32[]{:S(2)}, u32[]{:S(2)}) collective-permute-start(bf16[64,2048]{1,0:T(8,128)(2,1)S(1)} %get-tuple-element.178), channel_id=1, source_target_pairs={{0,16},{8,24},{16,0},{24,8},{1,17},{9,25},{17,1},{25,9},{2,18},{10... | collective-permute-start | bytes 786440 | tf_op jit(solution)/shard_map/ppermute | solution.py:22
  393.7 23.6 %collective-permute-start.41 = (bf16[64,2048]{1,0:T(8,128)(2,1)S(1)}, bf16[64,2048]{1,0:T(8,128)(2,1)}, u32[]{:S(2)}, u32[]{:S(2)}) collective-permute-start(bf16[64,2048]{1,0:T(8,128)(2,1)S(1)} %get-tuple-element.178), channel_id=1, source_target_pairs={{0,24},{8,0},{16,8},{24,16},{1,25},{9,1},{17,9},{25,17},{2,26},{10... | collective-permute-start | bytes 786440 | tf_op jit(solution)/shard_map/ppermute | solution.py:22
  399.8 141.6 %reduce-scatter.3.cloned.1.call-start = ((), (), s32[]{:S(2)}) async-start(), calls=%async_computation.12 | async-start | bytes 5242880 | tf_op jit(solution)/shard_map/reduce_scatter | solution.py:251
  468.2 49.1 %collective-permute-start.48 = (bf16[128,2048]{1,0:T(8,128)(2,1)S(1)}, bf16[128,2048]{1,0:T(8,128)(2,1)S(1)}, u32[]{:S(2)}, u32[]{:S(2)}) collective-permute-start(bf16[128,2048]{1,0:T(8,128)(2,1)S(1)} %get-tuple-element.198), channel_id=1, source_target_pairs={{0,16},{8,24},{16,0},{24,8},{1,17},{9,25},{17,1},{25,9},{2,18},{10... | collective-permute-start | bytes 1572872 | tf_op jit(solution)/shard_map/ppermute | solution.py:22
  469.3 48.0 %collective-permute-start.49 = (bf16[128,2048]{1,0:T(8,128)(2,1)}, bf16[128,2048]{1,0:T(8,128)(2,1)S(1)}, u32[]{:S(2)}, u32[]{:S(2)}) collective-permute-start(bf16[128,2048]{1,0:T(8,128)(2,1)} %get-tuple-element.197), channel_id=1, source_target_pairs={{0,8},{8,16},{16,24},{24,0},{1,9},{9,17},{17,25},{25,1},{2,10},{10... | collective-permute-start | bytes 1572872 | tf_op jit(solution)/shard_map/ppermute | solution.py:22
  479.6 35.9 %all-to-all-start.3 = ((f32[32,1,768]{2,1,0:T(1,128)}), f32[32,1,768]{2,1,0:T(1,128)S(1)}, u32[]{:S(2)}, u32[]{:S(2)}) async-start(f32[32,1,768]{2,1,0:T(1,128)} %all_to_all.28), calls=%async_computation.3 | async-start | bytes 196608 | tf_op jit(solution)/shard_map/all_to_all | solution.py:386
  523.0 30.4 %all-to-all-start.5 = ((bf16[4,64,2048]{2,1,0:T(8,128)(2,1)}), bf16[4,64,2048]{2,1,0:T(8,128)(2,1)S(1)}, u32[]{:S(2)}, u32[]{:S(2)}) async-start(bf16[4,64,2048]{2,1,0:T(8,128)(2,1)} %pad_maximum_fusion.2), calls=%async_computation.7 | async-start | bytes 2097152 | tf_op jit(solution)/shard_map/all_to_all | solution.py:242
  553.4 23.9 %all-to-all-start.4 = ((bf16[4,64,1536]{2,1,0:T(8,128)(2,1)}), bf16[4,64,1536]{2,1,0:T(8,128)(2,1)}, u32[]{:S(2)}, u32[]{:S(2)}) async-start(bf16[4,64,1536]{2,1,0:T(8,128)(2,1)} %pad_maximum_fusion.3), calls=%async_computation.6 | async-start | bytes 1572864 | tf_op jit(solution)/shard_map/all_to_all | solution.py:242
  (88 other events, 1148.8 us)
Sparse Core Ops, SparseCore 0:
  9.9 30.5 all-gather.4
  48.9 44.2 all-gather.6
  95.1 54.3 all-gather.8
  151.2 54.3 all-gather.10
  399.9 84.8 reduce-scatter.4
  487.9 53.3 reduce-scatter.2

commit v5 on v4

--- a/solution.py
+++ b/solution.py
@@ -27,18 +27,6 @@
     return [rows] + [shift(rows, k) for k in range(1, n)]
 
 
-def gather_seq(rows):
-    return jnp.concatenate(gather_blocks(rows), axis=0)
-
-
-def split_blocks(partial, part=0, parts=1):
-    n = lax.axis_size("seq")
-    size = partial.shape[0] // (n * parts)
-    starts = [(k * parts + part) * size for k in range(n)]
-    blocks = [partial[start : start + size] for start in starts]
-    return [blocks[0]] + [block.astype(bf16) for block in blocks[1:]]
-
-
 def send_blocks(blocks):
     return [blocks[0]] + [shift(blocks[k], -k) for k in range(1, len(blocks))]
 
@@ -48,10 +36,6 @@
     for block in blocks[1:]:
         total = total + block.astype(f32)
     return total
-
-
-def scatter_seq(partial):
-    return total_of(send_blocks(split_blocks(partial)))
 
 
 def normalize(hidden):
@@ -82,7 +66,7 @@
     return lax.dot_general(a, b, (((0,), (0,)), ((), ())), preferred_element_type=f32)
 
 
-def grid_call(kernel, scalar, grid, in_specs, out_specs, out_shape, name, args, flops=None):
+def grid_call(kernel, scalar, grid, in_specs, out_specs, out_shape, name, args, cost=None):
     grid_spec = pltpu.PrefetchScalarGridSpec(
         num_scalar_prefetch=1, grid=grid, in_specs=in_specs, out_specs=out_specs
     )
@@ -91,13 +75,92 @@
         grid_spec=grid_spec,
         out_shape=out_shape,
         compiler_params=pltpu.CompilerParams(vmem_limit_bytes=56 << 20),
-        cost_estimate=flops and pl.CostEstimate(flops=flops, transcendentals=0, bytes_accessed=1),
+        cost_estimate=cost
+        and pl.CostEstimate(flops=cost[0], transcendentals=0, bytes_accessed=cost[1]),
         name=name,
     )(jnp.reshape(scalar, (1,)).astype(jnp.int32), *args)
 
 
 def fixed(shape):
     return pl.BlockSpec(shape, lambda g, sc: (0,) * len(shape))
+
+
+def tile_of(width, most):
+    return next(t for t in range(most, 0, -128) if width % t == 0)
+
+
+def product(
+    core, blocks, w, finish, outs, name, nt=False, extra=(), more=(), keep=False, send=False, at=None,
+    most=1024,
+):
+    depth = blocks[0].shape[1]
+    sizes = [at[0]] if at else [block.shape[0] for block in blocks]
+    rows = sum(sizes)
+    width = w.shape[0] if nt else w.shape[1]
+    tile = tile_of(width, most)
+    count = len(blocks)
+
+    def kernel(sc, *refs):
+        block_refs, w_ref = refs[:count], refs[count]
+        extra_refs = refs[count + 1 : count + 1 + len(extra)]
+        out_refs = refs[count + 1 + len(extra) :]
+        step = pl.program_id(0)
+        if keep:
+            full_ref = out_refs[-1]
+
+            @pl.when(step == 0)
+            def _():
+                start = 0
+                for ref, size in zip(block_refs, sizes):
+                    full_ref[start : start + size] = ref[...]
+                    start += size
+                if send:
+                    side = pl.multiple_of((1 - sc[0]) * (depth // 2), 128)
+                    out_refs[-2][:rows] = full_ref[:rows, pl.ds(side, depth // 2)]
+
+            value = full_ref[:rows]
+        else:
+            value = block_refs[0][...]
+        dot = dot_nt if nt else dot_nn
+        finish(dot(value, w_ref[...]), extra_refs, out_refs, step, sc[0])
+
+    w_spec = (
+        pl.BlockSpec((tile, depth), lambda i, sc: (i, 0))
+        if nt
+        else pl.BlockSpec((depth, tile), lambda i, sc: (0, i))
+    )
+    tiled = lambda size: pl.BlockSpec((size, tile), lambda i, sc: (0, i))
+    index = at[1] if at else 0
+    return grid_call(
+        kernel,
+        core,
+        (width // tile,),
+        [pl.BlockSpec((size, depth), lambda i, sc: (index, 0)) for size in sizes]
+        + [w_spec]
+        + [tiled(array.shape[0]) for array in extra],
+        [tiled(size) for size, _ in outs] + [fixed(shape) for shape in more],
+        [jax.ShapeDtypeStruct((size, width), kind) for size, kind in outs]
+        + [jax.ShapeDtypeStruct(shape, bf16) for shape in more],
+        name,
+        (*blocks, w, *extra),
+        cost=(2 * rows * depth * width, 2 * (rows * depth + width * depth + rows * width)),
+    )
+
+
+def split_product(core, value, w, name, nt=False, parts=1, at=None):
+    n = lax.axis_size("seq")
+    size = (at[0] if at else value.shape[0]) // (n * parts)
+
+    def finish(total, extra, outs, step, core):
+        for p in range(parts):
+            for k in range(n):
+                start = (k * parts + p) * size
+                ref = outs[p * n + k]
+                ref[...] = total[start : start + size].astype(ref.dtype)
+
+    outs = [(size, f32 if k == 0 else bf16) for p in range(parts) for k in range(n)]
+    got = product(core, [value], w, finish, outs, name, nt=nt, at=at)
+    return [list(got[p * n : (p + 1) * n]) for p in range(parts)]
 
 
 def softmax_of(q, k, seg_col, seg_row):
@@ -181,7 +244,7 @@
         ],
         "attend_back",
         (seg[:, None], seg[None, :], qkv, qkv, qkv, grad_mixed),
-        flops=400_000_000_000,
+        cost=(400_000_000_000, 1),
     )
 
 
@@ -255,42 +318,47 @@
     return lax.ppermute(value, "core", [(0, 1), (1, 0)])
 
 
-def column_half(value, index):
-    width = value.shape[1] // 2
-    return lax.dynamic_slice_in_dim(value, index * width, width, axis=1)
-
-
-def feed_grads(core, first, first_far, pre, pre_far, act, act_far, ffn, ffn_far):
+def feed_grads(core, pairs, pre, ffn, far):
     n = lax.axis_size("seq")
     chips = lax.axis_size("chip")
-    tokens, height = first.shape
-    width = ffn_far.shape[1]
+    tokens = pre[0].shape[0]
+    height = pairs[0].shape[1]
+    width = far[0].shape[1]
     rows = height // (n * chips)
+    parts = len(pairs)
 
     def kernel(sc, *refs):
-        (ao, af, po, pf, go, gf, out) = refs[2 * n :]
+        act_refs = refs[n * parts : (n + 1) * parts]
+        pre_refs = refs[(n + 1) * parts : (n + 2) * parts]
+        ffn_refs = refs[(n + 2) * parts : (n + 3) * parts]
+        out = refs[-1]
         for j in range(n):
-            total = dot_tn(refs[j][...], po[...]) + dot_tn(refs[n + j][...], pf[...])
-            out[j] = total.astype(bf16)
-        total = dot_tn(ao[...], go[...]) + dot_tn(af[...], gf[...])
+            joined = zip(refs[j * parts : (j + 1) * parts], pre_refs)
+            out[j] = sum(dot_tn(a[...], b[...]) for a, b in joined).astype(bf16)
+        total = sum(dot_tn(a[...], b[...]) for a, b in zip(act_refs, ffn_refs))
         out[n:] = total.astype(bf16).reshape(n, rows, width)
 
     def rows_spec(j):
         return pl.BlockSpec((tokens, rows), lambda o, sc: (0, j * chips + o))
 
-    own_half = pl.BlockSpec((tokens, width), lambda o, sc: (0, sc[0]))
-    act_spec = pl.BlockSpec((tokens, n * rows), lambda o, sc: (0, o))
+    own_half = [pl.BlockSpec((tokens, width), lambda o, sc: (0, sc[0]))] * len(pre)
+    far_top = [pl.BlockSpec((tokens, width), lambda o, sc: (0, 0))] * len(far)
+    far_low = [pl.BlockSpec((tokens, width), lambda o, sc: (1, 0))] * len(far)
+    act_spec = pl.BlockSpec((tokens, n * rows), lambda o, sc: (1, o))
     return grid_call(
         kernel,
         core,
         (chips,),
-        [rows_spec(j) for j in range(n)] * 2
-        + [act_spec] * 2
-        + [own_half, fixed((tokens, width))] * 2,
+        [rows_spec(j) for j in range(n) for _ in range(parts)]
+        + [act_spec] * parts
+        + own_half
+        + far_low
+        + own_half
+        + far_top,
         pl.BlockSpec((2 * n, rows, width), lambda o, sc: (0, o, 0)),
         jax.ShapeDtypeStruct((2 * n, chips * rows, width), bf16),
         "feed_grads",
-        (*[first] * n, *[first_far] * n, act, act_far, pre, pre_far, ffn, ffn_far),
+        (*[pair for _ in range(n) for pair in pairs], *pairs, *pre, *far, *ffn, *far),
     )
 
 
@@ -301,7 +369,8 @@
     half = qkv_far.shape[1] // 3
     out_cols = attn_far.shape[1]
     cols = out_cols // n
-    rows = mixed.shape[1] // chips
+    rows = mixed.shape[1] // chips * 2
+    steps = chips // 2
 
     def kernel(sc, *refs):
         own_refs, far_refs = refs[:n], refs[n : 2 * n]
@@ -314,7 +383,7 @@
             out[j, :, 3 * half :] = side[:, j * cols : (j + 1) * cols]
 
     def rows_spec(j):
-        return pl.BlockSpec((tokens, rows), lambda o, sc: (0, j * chips + o))
+        return pl.BlockSpec((tokens, rows), lambda o, sc: (0, j * steps + o))
 
     def part_spec(p):
         return pl.BlockSpec((tokens, half), lambda o, sc: (0, 2 * p + sc[0]))
@@ -323,7 +392,7 @@
     return grid_call(
         kernel,
         core,
-        (chips,),
+        (steps,),
         [rows_spec(j) for j in range(n)] * 2
         + [rows_spec(0)] * 2
         + [part_spec(p) for p in range(3)]
@@ -333,7 +402,7 @@
             fixed((tokens, out_cols)),
         ],
         pl.BlockSpec((n, rows, width), lambda o, sc: (0, o, 0)),
-        jax.ShapeDtypeStruct((n, chips * rows, width), bf16),
+        jax.ShapeDtypeStruct((n, steps * rows, width), bf16),
         "attn_grad",
         (
             *[tok] * n,
@@ -426,11 +495,10 @@
     width = tokens.shape[2]
     part = width // n
     half = width // 2
-    paired = part // chips % 128 == 0
+    paired = part // chips % 128 == 0 and in_weight.shape[1] == n * width
     tok_rows = tokens[0]
 
     tok_blocks = gather_blocks(tok_rows)
-    tok_full = jnp.concatenate(tok_blocks, axis=0)
     out_w = gather_dp(out_weight)
     qkv_moved = exchange(pack_columns(qkv_weight, 3, c))
     vectors = [qv_bias, out_bias, norm1_gain, norm1_bias]
@@ -449,21 +517,36 @@
     q_bias = lax.dynamic_slice_in_dim(qv_full, s * part, part)
     v_bias = lax.dynamic_slice_in_dim(qv_full, width + s * part, part)
     qkv_b = jnp.concatenate([q_bias, jnp.zeros((part,), f32), v_bias])
-    qkv = (dot_nn(tok_full, qkv_w) + qkv_b).astype(bf16)
+
+    def finish_qkv(total, extra, outs, step, core):
+        outs[0][...] = (total + extra[0][...]).astype(bf16)
+
+    total_rows = n * rows
+    qkv, tok_full = product(
+        c,
+        tok_blocks,
+        qkv_w,
+        finish_qkv,
+        [(total_rows, bf16)],
+        "qkv",
+        extra=(qkv_b[None],),
+        more=[(total_rows, width)],
+        keep=True,
+    )
     mixed = attend(qkv, seg, c)
     size = rows // 2
     halves = range(2)
     cut = [slice(h * size, (h + 1) * size) for h in halves]
-    attn_partial = dot_nn(mixed, out_w)
-    attn_blocks = [send_blocks(split_blocks(attn_partial, h, 2)) for h in halves]
-    in_w = gather_dp(after(in_moved, attn_blocks[0], down_w))
+    attn_split = split_product(c, mixed, out_w, "out", parts=2)
+    attn_blocks = [send_blocks(blocks) for blocks in attn_split]
+    in_w = gather_dp(after(in_moved, attn_blocks[0]))
     hidden = in_w.shape[1]
     in_bias_own = lax.dynamic_slice_in_dim(in_b, s * hidden, hidden)
 
     first, normed_one, recip_one, first_blocks = [], [], [], []
     for h in halves:
         if h:
-            attn_blocks[h] = after(attn_blocks[h], first[0])
+            attn_blocks[h] = after(attn_blocks[h], first[0], down_w)
         attn = total_of(attn_blocks[h]) + out_b
         normed, recip = normalize(tok_rows[cut[h]].astype(f32) + attn)
         normed_one.append(normed)
@@ -472,16 +555,41 @@
         first_blocks.append(gather_blocks(first[h].astype(bf16)))
 
     first_blocks[0] = after(first_blocks[0], first[1])
-    act, act_slope, first_full, ffn_blocks, ffn_split = [], [], [], [], []
+
+    def finish_in(total, extra, outs, step, core):
+        value, slope = gelu_parts(total + extra[0][...])
+        outs[0][...] = slope.astype(bf16)
+        tile = value.shape[1]
+        start = pl.multiple_of(step * tile, tile)
+        outs[1][:, pl.ds(start, tile)] = value.astype(bf16)
+
+    def finish_pair(total, extra, outs, step, core):
+        value, slope = gelu_parts(total + extra[0][...])
+        outs[0][...] = slope.astype(bf16)
+        tile = value.shape[1]
+        start = pl.multiple_of(step * tile, tile)
+        outs[1][rows_half:, pl.ds(start, tile)] = value.astype(bf16)
+
+    rows_half = n * size
+    act_slope, pairs, ffn_blocks, ffn_split = [], [], [], []
     for h in halves:
         if h:
             first_blocks[h] = after(first_blocks[h], ffn_split[0])
-        first_full.append(jnp.concatenate(first_blocks[h], axis=0))
-        act_value, slope = gelu_parts(dot_nn(first_full[h], in_w) + in_bias_own)
-        pair = lax.optimization_barrier((act_value.astype(bf16), slope.astype(bf16)))
-        act.append(pair[0])
-        act_slope.append(pair[1])
-        ffn_split.append(split_blocks(dot_nn(act[h], down_w)))
+        args = (c, first_blocks[h], in_w)
+        outs = [(rows_half, bf16)]
+        bias = (in_bias_own[None],)
+        if paired:
+            more = [(2 * rows_half, width)]
+            slope, pair = product(
+                *args, finish_pair, outs, "in", extra=bias, more=more, keep=True, most=512
+            )
+            ffn_split += split_product(c, pair, down_w, "down", at=(rows_half, 1))
+        else:
+            more = [(rows_half, hidden), (rows_half, width)]
+            slope, *pair = product(*args, finish_in, outs, "in", extra=bias, more=more, keep=True)
+            ffn_split += split_product(c, pair[0], down_w, "down")
+        act_slope.append(slope)
+        pairs.append(pair)
         ffn_blocks.append(send_blocks(ffn_split[h]))
 
     ffn_blocks[0] = after(ffn_blocks[0], ffn_split[1])
@@ -503,31 +611,57 @@
     down_b_grad = sum(jnp.sum(grad_ffn[h].astype(f32), axis=0) for h in halves)
 
     grad_blocks[0] = after(grad_blocks[0], grad_ffn[1])
-    grad_ffn_full, grad_pre, back_split, back_blocks = [], [], [], []
+    if paired:
+        pairs_far = [to_partner(v) for v in pairs]
+        grad_blocks = [after(grad_blocks[0], pairs_far), grad_blocks[1]]
+
+    def finish_pre(total, extra, outs, step, core):
+        value = (total * extra[0][...].astype(f32)).astype(bf16)
+        outs[0][...] = value
+        if paired:
+            tile = value.shape[1]
+            steps = hidden // (2 * tile)
+
+            @pl.when(step // steps != core)
+            def _():
+                start = pl.multiple_of(step % steps * tile, tile)
+                outs[1][rows_half:, pl.ds(start, tile)] = value
+
+    grad_ffn_full, grad_pre, grad_sent, back_split, back_blocks = [], [], [], [], []
     for h in halves:
         if h:
             grad_blocks[h] = after(grad_blocks[h], back_split[0])
-        grad_ffn_full.append(jnp.concatenate(grad_blocks[h], axis=0))
-        grad_act = dot_nt(grad_ffn_full[h], down_w)
-        grad_pre.append((grad_act * act_slope[h].astype(f32)).astype(bf16))
-        back_split.append(split_blocks(dot_nt(grad_pre[h], in_w)))
+        sent = [(2 * rows_half, half)] if paired else []
+        got = product(
+            c,
+            grad_blocks[h],
+            down_w,
+            finish_pre,
+            [(rows_half, bf16)],
+            "pre_grad",
+            nt=True,
+            extra=(act_slope[h],),
+            more=sent + [(rows_half, width)],
+            keep=True,
+            send=paired,
+        )
+        grad_pre.append(got[0])
+        grad_sent.append(got[1])
+        grad_ffn_full.append(got[-1])
+        back_split += split_product(c, grad_pre[h], in_w, "back", nt=True)
         back_blocks.append(send_blocks(back_split[h]))
-    act, first_full, grad_ffn_full, grad_pre = (
-        jnp.concatenate(v, axis=0) for v in (act, first_full, grad_ffn_full, grad_pre)
-    )
-    in_b_grad = jnp.sum(grad_pre.astype(f32), axis=0)
+    in_b_grad = sum(jnp.sum(v.astype(f32), axis=0) for v in grad_pre)
     back_blocks[0] = after(back_blocks[0], back_split[1])
     if paired:
-        tok_far, mixed_far, first_far, act_far = (
-            to_partner(v) for v in (tok_full, mixed, first_full, act)
-        )
-        ffn_far = to_partner(column_half(grad_ffn_full, 1 - c))
-        pre_far = to_partner(column_half(grad_pre, 1 - c))
-        feed = (first_full, first_far, grad_pre, pre_far, act, act_far, grad_ffn_full, ffn_far)
+        tok_far, mixed_far = to_partner(tok_full), to_partner(mixed)
+        grad_far = [to_partner(v) for v in grad_sent]
+        feed = (pairs + pairs_far, grad_pre, grad_ffn_full, grad_far)
         feed_low = feed_grads(after(c, back_split[1]), *feed)
         back_blocks[1], feed_low = lax.optimization_barrier((back_blocks[1], feed_low))
         feed_sum = sum_over(feed_low, "chip")
     else:
+        act, first_full = (jnp.concatenate([p[i] for p in pairs], axis=0) for i in range(2))
+        grad_ffn_full, grad_pre = (jnp.concatenate(v, axis=0) for v in (grad_ffn_full, grad_pre))
         down_low = dot_tn(act, grad_ffn_full).astype(bf16)
         in_low = dot_tn(first_full, grad_pre).astype(bf16).reshape(n, part, -1)
         down_w_grad = sum_over(down_low, DP).astype(f32)
@@ -544,8 +678,23 @@
     gain_one_grad = sum(jnp.sum(grad_first[h] * normed_one[h], axis=0) for h in halves)
     out_b_grad = sum(jnp.sum(grad_attn[h].astype(f32), axis=0) for h in halves)
     grad_h1 = jnp.concatenate(grad_h1, axis=0)
-    grad_attn_full = jnp.concatenate([attn_blocks[h][k] for k in range(n) for h in halves], axis=0)
-    grad_mixed = dot_nt(grad_attn_full, out_w).astype(bf16)
+
+    def finish_mixed(total, extra, outs, step, core):
+        outs[0][...] = total.astype(bf16)
+
+    blocks = [attn_blocks[h][k] for k in range(n) for h in halves]
+    grad_mixed, attn_sent, grad_attn_full = product(
+        c,
+        blocks,
+        out_w,
+        finish_mixed,
+        [(total_rows, bf16)],
+        "mixed_grad",
+        nt=True,
+        more=[(total_rows, half), (total_rows, width)],
+        keep=True,
+        send=True,
+    )
     grad_qkv, qkv_sent = attend_back(qkv, grad_mixed, seg, c)
 
     def small_sums(grad_qkv):
@@ -569,12 +718,12 @@
         )
 
     if paired:
-        attn_far = to_partner(column_half(grad_attn_full, 1 - c))
+        attn_far = to_partner(attn_sent)
         args = (tok_full, tok_far, mixed, mixed_far)
         qkv_far = to_partner(qkv_sent)
         attn_low = attn_grad(c, *args, grad_qkv, qkv_far, grad_attn_full, attn_far)
         attn_sum = sum_over(attn_low, "chip")
-        last_split = split_blocks(dot_nt(after(grad_qkv, attn_low), qkv_w))
+        last_split = split_product(c, after(grad_qkv, attn_low), qkv_w, "last", nt=True)[0]
         last_blocks = send_blocks(last_split)
         small_grads = small_sums(after(grad_qkv, last_blocks[1]))
         last_blocks[-1] = after(last_blocks[-1], small_grads)
@@ -595,7 +744,7 @@
         )
         out_w_grad = join_halves(out_own, out_far, c)
     else:
-        last_split = split_blocks(dot_nt(grad_qkv, qkv_w))
+        last_split = split_product(c, grad_qkv, qkv_w, "last", nt=True)[0]
         last_blocks = send_blocks(last_split)
         small_grads = small_sums(after(grad_qkv, last_split))
         attn_low = after(dot_tn(tok_full, grad_qkv).astype(bf16), last_split)

time: 595 us -> 576 us (0.968); the launches traced: 587 us -> 574 us
  Pallas kernels: 51.3 us -> 129 us
  matrix products: 69.5 us -> 0 us
  local copies, waits for them, and re-layouts: 33.5 us -> 22.1 us
  other arithmetic: 35.9 us -> 29.7 us
    pallas_call x8 -> x20, Pallas kernels: 51.3 us -> 129 us  [grid_call(): pl.pallas_call(kernel, grid_spec=grid_spec, out_shape=out_shape, compiler...]
    dot_general x12 -> x0, matrix products: 69.5 us -> none  [the longest x6 35.9 us: dot_nn(): lax.dot_general(a, b, (((1,), (0,)), ((), ())), preferred_element_type=f32)]
    ppermute x42, waiting for transfers between devices: 176 us -> 163 us  [shift(): return lax.ppermute(value, 'seq', [(i, (i + step) % n) for i in range(n)])]
    all_to_all x1, waiting for transfers between devices: 2.07 us -> 12.4 us  [all_small(): lax.all_to_all(jnp.broadcast_to(packed[None], (count, packed.shape[0])),...]
    slice x11 -> x0, local copies, waits for them, and re-layouts: 6.56 us -> none  [split_blocks(): blocks = [partial[start:start + size] for start in starts]]
    unnamed x168 -> x156, local copies, waits for them, and re-layouts: 14.1 us -> 10.8 us
  transfers between devices with their start and end apart: 65 -> 65, of which waited for: 26 -> 28; matrix products, arithmetic and copies ran while one was open for 22% -> 7% of each run, Pallas kernels for 8% -> 22%
where the time goes in v5:
time: 576 us; the launch traced here: 574 us
  waiting for transfers between devices  259 us (45%)
  Pallas kernels  129 us (22%)
  starting transfers between devices  119 us (21%)
  other arithmetic  29.7 us (5%)
  local copies, waits for them, and re-layouts  22.1 us (4%)
  between operations  15.1 us (3%)
    ppermute x42, waiting for transfers between devices, shift(): return lax.ppermute(value, 'seq', [(i, (i + step) % n) for i in range(n)])  163 us
    pallas_call x20, Pallas kernels, grid_call(): pl.pallas_call(kernel, grid_spec=grid_spec, out_shape=out_shape, compiler...  129 us
    ppermute x42, starting transfers between devices, shift(): return lax.ppermute(value, 'seq', [(i, (i + step) % n) for i in range(n)])  87.2 us
    all_to_all x1, waiting for transfers between devices, scatter_small(): mine = jnp.sum(lax.all_to_all(packed, ALL, 0, 0), axis=0)  28.1 us
    all_to_all x4, waiting for transfers between devices, exchange(): return lax.all_to_all(pieces, 'seq', 0, 0)  23.7 us
    all_to_all x4, starting transfers between devices, exchange(): return lax.all_to_all(pieces, 'seq', 0, 0)  18.8 us
    all_gather x4, waiting for transfers between devices, gather_dp(): full = lax.all_gather(shard, DP, axis=shard.ndim - 2, tiled=True)  14.2 us
    all_to_all x1, waiting for transfers between devices, all_small(): lax.all_to_all(jnp.broadcast_to(packed[None], (count, packed.shape[0])),...  12.4 us
  transfers between devices with their start and end apart: 65, of which 28 were waited for; matrix products, arithmetic and copies ran while one was open for 7% of the time, Pallas kernels for 22%

profile of v5, /device:TPU:0, one launch (start us, length us, event | category | flops | bytes accessed | tf_op | source)
XLA Modules:
  0.0 574.5 jit_solution(9572625915334716858)
XLA Ops:
  10.1 6.5 %all-to-all-start = ((bf16[4,64,1536]{2,1,0:T(8,128)(2,1)}), bf16[4,64,1536]{2,1,0:T(8,128)(2,1)S(1)}, u32[]{:S(2)}, u32[]{:S(2)}) async-start(bf16[4,64,1536]{2,1,0:T(8,128)(2,1)} %pack.2), calls=%async_computation | async-start | bytes 1572864 | tf_op jit(solution)/shard_map/all_to_all | solution.py:305
  18.5 26.1 %collective-permute-done.refs_1_ = bf16[128,2048]{1,0:T(8,128)(2,1)S(1)} collective-permute-done((bf16[128,2048]{1,0:T(8,128)(2,1)S(1)}, bf16[128,2048]{1,0:T(8,128)(2,1)S(1)}, u32[]{:S(2)}, u32[]{:S(2)}) %collective-permute-start) | collective-permute-done | bytes 524320 | tf_op jit(solution)/shard_map/ppermute | solution.py:22
  52.9 5.6 all-to-all-start.1
  60.8 12.0 %collective-permute-done.1.refs_2_ = bf16[128,2048]{1,0:T(8,128)(2,1)S(1)} collective-permute-done((bf16[128,2048]{1,0:T(8,128)(2,1)S(1)}, bf16[128,2048]{1,0:T(8,128)(2,1)S(1)}, u32[]{:S(2)}, u32[]{:S(2)}) %collective-permute-start.1) | collective-permute-done | bytes 524320 | tf_op jit(solution)/shard_map/ppermute | solution.py:22
  74.2 12.4 %all-to-all-done.1 = bf16[32,2,384]{2,1,0:T(2,128)(2,1)S(1)} async-done(((bf16[32,2,384]{2,1,0:T(2,128)(2,1)}), bf16[32,2,384]{2,1,0:T(2,128)(2,1)S(1)}, u32[]{:S(2)}, u32[]{:S(2)}) %all-to-all-start.1) | async-done | bytes 49184 | tf_op jit(solution)/shard_map/all_to_all | solution.py:442
  86.6 3.5 all-to-all-start.2
  93.2 7.1 %qkv.1 = (bf16[512,1536]{1,0:T(8,128)(2,1)}, bf16[512,2048]{1,0:T(8,128)(2,1)}) custom-call(s32[1]{0:T(128)} %bitcast.1.sc.core, bf16[128,2048]{1,0:T(8,128)(2,1)} %bitcast.107, bf16[128,2048]{1,0:T(8,128)(2,1)} %copy-done.72, bf16[128,2048]{1,0:T(8,128)(2,1)} %copy-done.73, bf16[128,2048]{1,0:T(8,128)(2,1)} %copy-done.74, bf16[2048,1536]{1,0:T(8,128)(2,1)} %bitcast.122, ...), custom_call_target="tpu_custom_call" | custom-call | flops 3221225472 | bytes 9961472 | tf_op jit(solution)/shard_map/qkv/pallas_call | solution.py:73
  100.4 6.4 %attend.1.refs_0_.refs_8_ = bf16[512,512]{1,0:T(8,128)(2,1)} custom-call(s32[1]{0:T(128)} %bitcast.1.sc.core, s32[512,1]{1,0:T(8,128)} %copy.45.seg_col, s32[1,512]{1,0:T(1,128)} %bitcast.119, bf16[512,1536]{1,0:T(8,128)(2,1)} %get-tuple-element.135.q.k.v, bf16[512,1536]{1,0:T(8,128)(2,1)} %get-tuple-element.135.q.k.v, ...), custom_call_target="tpu_custom_call" | custom-call | tf_op jit(solution)/shard_map/attend/pallas_call | solution.py:73
  106.8 3.8 out.1
  116.9 4.9 collective-permute-done.3
  121.8 16.5 %collective-permute-done.4 = bf16[64,2048]{1,0:T(8,128)(2,1)S(1)} collective-permute-done((bf16[64,2048]{1,0:T(8,128)(2,1)}, bf16[64,2048]{1,0:T(8,128)(2,1)S(1)}, u32[]{:S(2)}, u32[]{:S(2)}) %collective-permute-start.4) | collective-permute-done | bytes 262176 | tf_op jit(solution)/shard_map/ppermute | solution.py:22
  141.7 3.8 collective-permute-start.9
  148.0 13.2 %collective-permute-done.10 = bf16[64,2048]{1,0:T(8,128)(2,1)} collective-permute-done((bf16[64,2048]{1,0:T(8,128)(2,1)}, bf16[64,2048]{1,0:T(8,128)(2,1)}, u32[]{:S(2)}, u32[]{:S(2)}) %collective-permute-start.10) | collective-permute-done | bytes 262176 | tf_op jit(solution)/shard_map/ppermute | solution.py:22
  161.2 6.0 %collective-permute-done.9 = bf16[64,2048]{1,0:T(8,128)(2,1)} collective-permute-done((bf16[64,2048]{1,0:T(8,128)(2,1)}, bf16[64,2048]{1,0:T(8,128)(2,1)}, u32[]{:S(2)}, u32[]{:S(2)}) %collective-permute-start.9) | collective-permute-done | bytes 262176 | tf_op jit(solution)/shard_map/ppermute | solution.py:22
  169.8 11.4 %collective-permute-start.15 = (bf16[64,2048]{1,0:T(8,128)(2,1)}, bf16[64,2048]{1,0:T(8,128)(2,1)}, u32[]{:S(2)}, u32[]{:S(2)}) collective-permute-start(bf16[64,2048]{1,0:T(8,128)(2,1)} %get-tuple-element.160.refs_0_), channel_id=1, source_target_pairs={{0,8},{8,16},{16,24},{24,0},{1,9},{9,17},{17,25},{25,1},{2,10},{10... | collective-permute-start | bytes 786440 | tf_op jit(solution)/shard_map/ppermute | solution.py:22
  183.6 9.6 %collective-permute-done.7.refs_2_ = bf16[64,2048]{1,0:T(8,128)(2,1)} collective-permute-done((bf16[64,2048]{1,0:T(8,128)(2,1)S(1)}, bf16[64,2048]{1,0:T(8,128)(2,1)}, u32[]{:S(2)}, u32[]{:S(2)}) %collective-permute-start.7) | collective-permute-done | bytes 262176 | tf_op jit(solution)/shard_map/ppermute | solution.py:22
  193.2 13.1 %all-gather.11.cloned.1.call-done = bf16[4,512,2048]{2,1,0:T(8,128)(2,1)} async-done(((bf16[4,64,2048]{2,1,0:T(8,128)(2,1)}), bf16[4,512,2048]{2,1,0:T(8,128)(2,1)}) %all-gather.11.cloned.1.call-update) | async-done | bytes 8388624 | tf_op jit(solution)/shard_map/all_gather | solution.py:309
  206.3 8.3 %in.2 = (bf16[256,2048]{1,0:T(8,128)(2,1)}, bf16[512,2048]{1,0:T(8,128)(2,1)}) custom-call(s32[1]{0:T(128)} %bitcast.1.sc.core, bf16[64,2048]{1,0:T(8,128)(2,1)} %copy-done.19, bf16[64,2048]{1,0:T(8,128)(2,1)} %collective-permute-done.6.refs_1_, bf16[64,2048]{1,0:T(8,128)(2,1)} %collective-permute-done.7.refs_2_, ...), custom_call_target="tpu_custom_call" | custom-call | flops 2147483648 | bytes 10485760 | tf_op jit(solution)/shard_map/in/pallas_call | solution.py:73
  214.8 5.8 %down.2 = (f32[64,2048]{1,0:T(8,128)}, bf16[64,2048]{1,0:T(8,128)(2,1)}, bf16[64,2048]{1,0:T(8,128)(2,1)}, bf16[64,2048]{1,0:T(8,128)(2,1)}) custom-call(s32[1]{0:T(128)} %bitcast.1.sc.core, bf16[512,2048]{1,0:T(8,128)(2,1)} %get-tuple-element.155.refs_0_.refs_4_.refs_8_.refs_12_.refs_16_, bf16[2048,2048]{1,0:T(8,128)(2,1)} %all-gather.9.cloned.1.call-done.refs_1_.refs_4_), custom_call_target="tpu_custom_call" | custom-call | flops 2147483648 | bytes 10485760 | tf_op jit(solution)/shard_map/down/pallas_call | solution.py:73
  225.0 8.3 %in.3 = (bf16[256,2048]{1,0:T(8,128)(2,1)}, bf16[512,2048]{1,0:T(8,128)(2,1)}) custom-call(s32[1]{0:T(128)} %bitcast.1.sc.core, bf16[64,2048]{1,0:T(8,128)(2,1)} %get-tuple-element.160.refs_0_, bf16[64,2048]{1,0:T(8,128)(2,1)} %collective-permute-done.15.refs_1_, bf16[64,2048]{1,0:T(8,128)(2,1)} %collective-permute-done.16.refs_2_, ...), custom_call_target="tpu_custom_call" | custom-call | flops 2147483648 | bytes 10485760 | tf_op jit(solution)/shard_map/in/pallas_call | solution.py:73
  233.4 5.9 %down.3 = (f32[64,2048]{1,0:T(8,128)}, bf16[64,2048]{1,0:T(8,128)(2,1)}, bf16[64,2048]{1,0:T(8,128)(2,1)}, bf16[64,2048]{1,0:T(8,128)(2,1)}) custom-call(s32[1]{0:T(128)} %bitcast.1.sc.core, bf16[512,2048]{1,0:T(8,128)(2,1)} %get-tuple-element.164.refs_0_.refs_1_.refs_5_.refs_9_.refs_13_.refs_17_, bf16[2048,2048]{1,0:T(8,128)(2,1)} %all-gather.9.cloned.1.call-done.refs_1_.refs_4_), custom_call_target="tpu_custom_call" | custom-call | flops 2147483648 | bytes 10485760 | tf_op jit(solution)/shard_map/down/pallas_call | solution.py:73
  242.7 5.1 collective-permute-done.13
  247.9 12.0 %collective-permute-start.20 = (bf16[64,2048]{1,0:T(8,128)(2,1)}, bf16[64,2048]{1,0:T(8,128)(2,1)S(1)}, u32[]{:S(2)}, u32[]{:S(2)}) collective-permute-start(bf16[64,2048]{1,0:T(8,128)(2,1)} %get-tuple-element.168), channel_id=1, source_target_pairs={{0,8},{8,16},{16,24},{24,0},{1,9},{9,17},{17,25},{25,1},{2,10},{10... | collective-permute-start | bytes 786440 | tf_op jit(solution)/shard_map/ppermute | solution.py:22
  266.4 14.4 %collective-permute-done.19 = bf16[64,2048]{1,0:T(8,128)(2,1)S(1)} collective-permute-done((bf16[64,2048]{1,0:T(8,128)(2,1)}, bf16[64,2048]{1,0:T(8,128)(2,1)S(1)}, u32[]{:S(2)}, u32[]{:S(2)}) %collective-permute-start.19) | collective-permute-done | bytes 262176 | tf_op jit(solution)/shard_map/ppermute | solution.py:22
  285.8 16.4 %collective-permute-done.22.refs_2_ = bf16[64,2048]{1,0:T(8,128)(2,1)S(1)} collective-permute-done((bf16[64,2048]{1,0:T(8,128)(2,1)S(1)}, bf16[64,2048]{1,0:T(8,128)(2,1)S(1)}, u32[]{:S(2)}, u32[]{:S(2)}) %collective-permute-start.22) | collective-permute-done | bytes 262176 | tf_op jit(solution)/shard_map/ppermute | solution.py:22
  303.0 7.7 %pre_grad.2 = (bf16[256,2048]{1,0:T(8,128)(2,1)}, bf16[512,1024]{1,0:T(8,128)(2,1)}, bf16[256,2048]{1,0:T(8,128)(2,1)}) custom-call(s32[1]{0:T(128)} %bitcast.1.sc.core, bf16[64,2048]{1,0:T(8,128)(2,1)} %copy-done.23, bf16[64,2048]{1,0:T(8,128)(2,1)} %copy-done.46, bf16[64,2048]{1,0:T(8,128)(2,1)} %copy-done.47, bf16[64,2048]{1,0:T(8,128)(2,1)} %copy-done.48, ...), custom_call_target="tpu_custom_call" | custom-call | flops 2147483648 | bytes 10485760 | tf_op jit(solution)/shard_map/pre_grad/pallas_call | solution.py:73
  310.7 5.9 %back.2 = (f32[64,2048]{1,0:T(8,128)}, bf16[64,2048]{1,0:T(8,128)(2,1)}, bf16[64,2048]{1,0:T(8,128)(2,1)}, bf16[64,2048]{1,0:T(8,128)(2,1)}) custom-call(s32[1]{0:T(128)} %bitcast.1.sc.core, bf16[256,2048]{1,0:T(8,128)(2,1)} %get-tuple-element.186.refs_0_.refs_20_, bf16[2048,2048]{1,0:T(8,128)(2,1)} %bitcast.102), custom_call_target="tpu_custom_call" | custom-call | flops 2147483648 | bytes 10485760 | tf_op jit(solution)/shard_map/back/pallas_call | solution.py:73
  316.6 6.5 %collective-permute-start.26 = (bf16[64,2048]{1,0:T(8,128)(2,1)}, bf16[64,2048]{1,0:T(8,128)(2,1)S(1)}, u32[]{:S(2)}, u32[]{:S(2)}) collective-permute-start(bf16[64,2048]{1,0:T(8,128)(2,1)} %get-tuple-element.188), channel_id=1, source_target_pairs={{0,24},{8,0},{16,8},{24,16},{1,25},{9,1},{17,9},{25,17},{2,26},{10... | collective-permute-start | bytes 786440 | tf_op jit(solution)/shard_map/ppermute | solution.py:22
  327.0 7.0 %pre_grad.3 = (bf16[256,2048]{1,0:T(8,128)(2,1)}, bf16[512,1024]{1,0:T(8,128)(2,1)}, bf16[256,2048]{1,0:T(8,128)(2,1)}) custom-call(s32[1]{0:T(128)} %bitcast.1.sc.core, bf16[64,2048]{1,0:T(8,128)(2,1)} %copy-done.22, bf16[64,2048]{1,0:T(8,128)(2,1)} %copy-done.49, bf16[64,2048]{1,0:T(8,128)(2,1)} %copy-done.50, bf16[64,2048]{1,0:T(8,128)(2,1)} %copy-done.51, ...), custom_call_target="tpu_custom_call" | custom-call | flops 2147483648 | bytes 10485760 | tf_op jit(solution)/shard_map/pre_grad/pallas_call | solution.py:73
  334.4 5.9 %back.3 = (f32[64,2048]{1,0:T(8,128)}, bf16[64,2048]{1,0:T(8,128)(2,1)}, bf16[64,2048]{1,0:T(8,128)(2,1)}, bf16[64,2048]{1,0:T(8,128)(2,1)}) custom-call(s32[1]{0:T(128)} %bitcast.1.sc.core, bf16[256,2048]{1,0:T(8,128)(2,1)} %get-tuple-element.196.refs_0_.refs_21_, bf16[2048,2048]{1,0:T(8,128)(2,1)} %bitcast.103), custom_call_target="tpu_custom_call" | custom-call | flops 2147483648 | bytes 10485760 | tf_op jit(solution)/shard_map/back/pallas_call | solution.py:73
  348.2 11.6 %collective-permute-start.37 = (bf16[64,2048]{1,0:T(8,128)(2,1)S(1)}, bf16[64,2048]{1,0:T(8,128)(2,1)}, u32[]{:S(2)}, u32[]{:S(2)}) collective-permute-start(bf16[64,2048]{1,0:T(8,128)(2,1)S(1)} %get-tuple-element.264.refs_0_), channel_id=1, source_target_pairs={{0,8},{8,16},{16,24},{24,0},{1,9},{9,17},{17,25},{25,1},{2,10},{10... | collective-permute-start | bytes 786440 | tf_op jit(solution)/shard_map/ppermute | solution.py:22
  360.8 14.3 %feed_grads.1 = bf16[8,512,1024]{2,1,0:T(8,128)(2,1)} custom-call(s32[1]{0:T(128)} %bitcast.16.sc, bf16[512,2048]{1,0:T(8,128)(2,1)} %get-tuple-element.155.refs_0_.refs_4_.refs_8_.refs_12_.refs_16_, bf16[512,2048]{1,0:T(8,128)(2,1)} %get-tuple-element.164.refs_0_.refs_1_.refs_5_.refs_9_.refs_13_.refs_17_, bf16[512,2048]{1,0:T(8,128)(2,1)} %copy-done, ...), custom_call_target="tpu_custom_call" | custom-call | tf_op jit(solution)/shard_map/feed_grads/pallas_call | solution.py:73
  383.2 3.8 collective-permute-start.42
  387.4 5.0 collective-permute-done.41.refs_6_
  394.3 13.2 %collective-permute-done.40.refs_5_ = bf16[64,2048]{1,0:T(8,128)(2,1)S(1)} collective-permute-done((bf16[64,2048]{1,0:T(8,128)(2,1)S(1)}, bf16[64,2048]{1,0:T(8,128)(2,1)S(1)}, u32[]{:S(2)}, u32[]{:S(2)}) %collective-permute-start.40) | collective-permute-done | bytes 262176 | tf_op jit(solution)/shard_map/ppermute | solution.py:22
  408.9 5.6 mixed_grad.1
  414.5 11.4 %attend_back.1 = (bf16[512,1536]{1,0:T(8,128)(2,1)}, bf16[512,768]{1,0:T(8,128)(2,1)}) custom-call(s32[1]{0:T(128)} %bitcast.1.sc.core, s32[512,1]{1,0:T(8,128)} %copy.45.seg_col, s32[1,512]{1,0:T(1,128)} %bitcast.120, bf16[512,1536]{1,0:T(8,128)(2,1)} %get-tuple-element.135.q.k.v, bf16[512,1536]{1,0:T(8,128)(2,1)} %get-tuple-element.135.q.k.v, ...), custom_call_target="tpu_custom_call" | custom-call | flops 399999991808 | bytes 1 | tf_op jit(solution)/shard_map/attend_back/pallas_call | solution.py:73
  430.2 9.5 %attn_grad.1 = bf16[4,512,1024]{2,1,0:T(8,128)(2,1)} custom-call(s32[1]{0:T(128)} %bitcast.1.sc.core, bf16[512,2048]{1,0:T(8,128)(2,1)} %get-tuple-element.220.refs_0_.refs_1_.refs_2_.refs_3_, bf16[512,2048]{1,0:T(8,128)(2,1)} %get-tuple-element.220.refs_0_.refs_1_.refs_2_.refs_3_, bf16[512,2048]{1,0:T(8,128)(2,1)} %get-tuple-element.220.refs_0_.refs_1_.refs_2_.refs_3_, ...), custom_call_target="tpu_custom_call" | custom-call | tf_op jit(solution)/shard_map/attn_grad/pallas_call | solution.py:73
  441.1 7.2 %last.1 = (f32[128,2048]{1,0:T(8,128)}, bf16[128,2048]{1,0:T(8,128)(2,1)}, bf16[128,2048]{1,0:T(8,128)(2,1)}, bf16[128,2048]{1,0:T(8,128)(2,1)}) custom-call(s32[1]{0:T(128)} %bitcast.1.sc.core, bf16[512,1536]{1,0:T(8,128)(2,1)} %get-tuple-element.229.refs_10_.refs_11_.refs_12_.refs_0_, bf16[2048,1536]{1,0:T(8,128)(2,1)} %bitcast.123), custom_call_target="tpu_custom_call" | custom-call | flops 3221225472 | bytes 9961472 | tf_op jit(solution)/shard_map/last/pallas_call | solution.py:73
  448.3 7.4 %collective-permute-start.47 = (bf16[128,2048]{1,0:T(8,128)(2,1)}, bf16[128,2048]{1,0:T(8,128)(2,1)S(1)}, u32[]{:S(2)}, u32[]{:S(2)}) collective-permute-start(bf16[128,2048]{1,0:T(8,128)(2,1)} %get-tuple-element.226), channel_id=1, source_target_pairs={{0,24},{8,0},{16,8},{24,16},{1,25},{9,1},{17,9},{25,17},{2,26},{10... | collective-permute-start | bytes 1572872 | tf_op jit(solution)/shard_map/ppermute | solution.py:22
  457.1 11.2 %collective-permute-done.47 = bf16[128,2048]{1,0:T(8,128)(2,1)S(1)} collective-permute-done((bf16[128,2048]{1,0:T(8,128)(2,1)}, bf16[128,2048]{1,0:T(8,128)(2,1)S(1)}, u32[]{:S(2)}, u32[]{:S(2)}) %collective-permute-start.47) | collective-permute-done | bytes 524320 | tf_op jit(solution)/shard_map/ppermute | solution.py:22
  469.6 5.3 all-to-all-start.3
  474.9 28.1 %all-to-all-done.3 = f32[32,1,768]{2,1,0:T(1,128)S(1)} async-done(((f32[32,1,768]{2,1,0:T(1,128)}), f32[32,1,768]{2,1,0:T(1,128)S(1)}, u32[]{:S(2)}, u32[]{:S(2)}) %all-to-all-start.3) | async-done | bytes 98336 | tf_op jit(solution)/shard_map/all_to_all | solution.py:455
  510.7 4.6 all-to-all-start.5
  517.1 11.6 %reduce-scatter.3.cloned.1.call-done = bf16[4,128,1024]{2,1,0:T(8,128)(2,1)} async-done(((bf16[4,512,1024]{2,1,0:T(8,128)(2,1)}), bf16[4,128,1024]{2,1,0:T(8,128)(2,1)}) %reduce-scatter.3.cloned.1.call-update) | async-done | bytes 1048592 | tf_op jit(solution)/shard_map/reduce_scatter | solution.py:314
  535.7 5.6 all-to-all-done.5.pieces_ref
  541.3 4.2 all-to-all-start.4
  552.3 12.9 %all-to-all-done.4.pieces_ref = bf16[4,64,1536]{2,1,0:T(8,128)(2,1)} async-done(((bf16[4,64,1536]{2,1,0:T(8,128)(2,1)}), bf16[4,64,1536]{2,1,0:T(8,128)(2,1)}, u32[]{:S(2)}, u32[]{:S(2)}) %all-to-all-start.4) | async-done | bytes 786464 | tf_op jit(solution)/shard_map/all_to_all | solution.py:305
  (364 shorter events, 115.8 us)
Async XLA Ops:
  7.2 40.7 %all-gather.5.cloned.1.call-start = ((), (), s32[]{:S(2)}) async-start(), calls=%async_computation.8 | async-start | bytes 2359296 | tf_op jit(solution)/shard_map/all_gather | solution.py:309
  10.1 37.8 %all-to-all-start = ((bf16[4,64,1536]{2,1,0:T(8,128)(2,1)}), bf16[4,64,1536]{2,1,0:T(8,128)(2,1)S(1)}, u32[]{:S(2)}, u32[]{:S(2)}) async-start(bf16[4,64,1536]{2,1,0:T(8,128)(2,1)} %pack.2), calls=%async_computation | async-start | bytes 1572864 | tf_op jit(solution)/shard_map/all_to_all | solution.py:305
  16.5 76.7 %all-gather.7.cloned.1.call-start = ((), (), s32[]{:S(2)}) async-start(), calls=%async_computation.9 | async-start | bytes 7077888 | tf_op jit(solution)/shard_map/all_gather | solution.py:309
  16.5 28.2 %collective-permute-start = (bf16[128,2048]{1,0:T(8,128)(2,1)S(1)}, bf16[128,2048]{1,0:T(8,128)(2,1)S(1)}, u32[]{:S(2)}, u32[]{:S(2)}) collective-permute-start(bf16[128,2048]{1,0:T(8,128)(2,1)S(1)} %bitcast.108), channel_id=1, source_target_pairs={{0,8},{8,16},{16,24},{24,0},{1,9},{9,17},{17,25},{25,1},{2,10},{10... | collective-permute-start | bytes 1572872 | tf_op jit(solution)/shard_map/ppermute | solution.py:22
  48.8 118.4 %all-gather.9.cloned.1.call-start = ((), (), s32[]{:S(2)}) async-start(), calls=%async_computation.10 | async-start | bytes 9437184 | tf_op jit(solution)/shard_map/all_gather | solution.py:309
  49.5 23.2 %collective-permute-start.1 = (bf16[128,2048]{1,0:T(8,128)(2,1)S(1)}, bf16[128,2048]{1,0:T(8,128)(2,1)S(1)}, u32[]{:S(2)}, u32[]{:S(2)}) collective-permute-start(bf16[128,2048]{1,0:T(8,128)(2,1)S(1)} %bitcast.109), channel_id=1, source_target_pairs={{0,16},{8,24},{16,0},{24,8},{1,17},{9,25},{17,1},{25,9},{2,18},{10... | collective-permute-start | bytes 1572872 | tf_op jit(solution)/shard_map/ppermute | solution.py:22
  50.2 24.0 %collective-permute-start.2 = (bf16[128,2048]{1,0:T(8,128)(2,1)S(1)}, bf16[128,2048]{1,0:T(8,128)(2,1)S(1)}, u32[]{:S(2)}, u32[]{:S(2)}) collective-permute-start(bf16[128,2048]{1,0:T(8,128)(2,1)S(1)} %bitcast.110), channel_id=1, source_target_pairs={{0,24},{8,0},{16,8},{24,16},{1,25},{9,1},{17,9},{25,17},{2,26},{10... | collective-permute-start | bytes 1572872 | tf_op jit(solution)/shard_map/ppermute | solution.py:22
  52.9 33.6 %all-to-all-start.1 = ((bf16[32,2,384]{2,1,0:T(2,128)(2,1)}), bf16[32,2,384]{2,1,0:T(2,128)(2,1)S(1)}, u32[]{:S(2)}, u32[]{:S(2)}) async-start(bf16[32,2,384]{2,1,0:T(2,128)(2,1)} %reshape.327), calls=%async_computation.1 | async-start | bytes 98304 | tf_op jit(solution)/shard_map/all_to_all | solution.py:442
  86.6 30.3 %all-to-all-start.2 = ((bf16[4,64,2048]{2,1,0:T(8,128)(2,1)}), bf16[4,64,2048]{2,1,0:T(8,128)(2,1)S(1)}, u32[]{:S(2)}, u32[]{:S(2)}) async-start(bf16[4,64,2048]{2,1,0:T(8,128)(2,1)} %pack.3), calls=%async_computation.2 | async-start | bytes 2097152 | tf_op jit(solution)/shard_map/all_to_all | solution.py:305
  90.1 116.2 %all-gather.11.cloned.1.call-start = ((), (), s32[]{:S(2)}) async-start(), calls=%async_computation.11 | async-start | bytes 9437184 | tf_op jit(solution)/shard_map/all_gather | solution.py:309
  113.8 24.5 %collective-permute-start.4 = (bf16[64,2048]{1,0:T(8,128)(2,1)}, bf16[64,2048]{1,0:T(8,128)(2,1)S(1)}, u32[]{:S(2)}, u32[]{:S(2)}) collective-permute-start(bf16[64,2048]{1,0:T(8,128)(2,1)} %get-tuple-element.138), channel_id=1, source_target_pairs={{0,16},{8,24},{16,0},{24,8},{1,17},{9,25},{17,1},{25,9},{2,18},{10... | collective-permute-start | bytes 786440 | tf_op jit(solution)/shard_map/ppermute | solution.py:22
  113.8 24.5 %collective-permute-start.5 = (bf16[64,2048]{1,0:T(8,128)(2,1)}, bf16[64,2048]{1,0:T(8,128)(2,1)S(1)}, u32[]{:S(2)}, u32[]{:S(2)}) collective-permute-start(bf16[64,2048]{1,0:T(8,128)(2,1)} %get-tuple-element.139), channel_id=1, source_target_pairs={{0,8},{8,16},{16,24},{24,0},{1,9},{9,17},{17,25},{25,1},{2,10},{10... | collective-permute-start | bytes 786440 | tf_op jit(solution)/shard_map/ppermute | solution.py:22
  138.4 366.5 %reduce-scatter.5.cloned.1.call-start = ((), (), s32[]{:S(2)}) async-start(), calls=%async_computation.13 | async-start | bytes 10485760 | tf_op jit(solution)/shard_map/reduce_scatter | solution.py:314
  141.7 25.5 %collective-permute-start.9 = (bf16[64,2048]{1,0:T(8,128)(2,1)}, bf16[64,2048]{1,0:T(8,128)(2,1)}, u32[]{:S(2)}, u32[]{:S(2)}) collective-permute-start(bf16[64,2048]{1,0:T(8,128)(2,1)} %get-tuple-element.141), channel_id=1, source_target_pairs={{0,24},{8,0},{16,8},{24,16},{1,25},{9,1},{17,9},{25,17},{2,26},{10... | collective-permute-start | bytes 786440 | tf_op jit(solution)/shard_map/ppermute | solution.py:22
  147.3 33.9 %collective-permute-start.6 = (bf16[64,2048]{1,0:T(8,128)(2,1)S(1)}, bf16[64,2048]{1,0:T(8,128)(2,1)}, u32[]{:S(2)}, u32[]{:S(2)}) collective-permute-start(bf16[64,2048]{1,0:T(8,128)(2,1)S(1)} %get-tuple-element.149.refs_0_), channel_id=1, source_target_pairs={{0,8},{8,16},{16,24},{24,0},{1,9},{9,17},{17,25},{25,1},{2,10},{10... | collective-permute-start | bytes 786440 | tf_op jit(solution)/shard_map/ppermute | solution.py:22
  147.4 45.8 %collective-permute-start.7 = (bf16[64,2048]{1,0:T(8,128)(2,1)S(1)}, bf16[64,2048]{1,0:T(8,128)(2,1)}, u32[]{:S(2)}, u32[]{:S(2)}) collective-permute-start(bf16[64,2048]{1,0:T(8,128)(2,1)S(1)} %get-tuple-element.149.refs_0_), channel_id=1, source_target_pairs={{0,16},{8,24},{16,0},{24,8},{1,17},{9,25},{17,1},{25,9},{2,18},{10... | collective-permute-start | bytes 786440 | tf_op jit(solution)/shard_map/ppermute | solution.py:22
  161.2 32.0 %collective-permute-start.8 = (bf16[64,2048]{1,0:T(8,128)(2,1)S(1)}, bf16[64,2048]{1,0:T(8,128)(2,1)}, u32[]{:S(2)}, u32[]{:S(2)}) collective-permute-start(bf16[64,2048]{1,0:T(8,128)(2,1)S(1)} %get-tuple-element.149.refs_0_), channel_id=1, source_target_pairs={{0,24},{8,0},{16,8},{24,16},{1,25},{9,1},{17,9},{25,17},{2,26},{10... | collective-permute-start | bytes 786440 | tf_op jit(solution)/shard_map/ppermute | solution.py:22
  169.8 54.1 %collective-permute-start.15 = (bf16[64,2048]{1,0:T(8,128)(2,1)}, bf16[64,2048]{1,0:T(8,128)(2,1)}, u32[]{:S(2)}, u32[]{:S(2)}) collective-permute-start(bf16[64,2048]{1,0:T(8,128)(2,1)} %get-tuple-element.160.refs_0_), channel_id=1, source_target_pairs={{0,8},{8,16},{16,24},{24,0},{1,9},{9,17},{17,25},{25,1},{2,10},{10... | collective-permute-start | bytes 786440 | tf_op jit(solution)/shard_map/ppermute | solution.py:22
  181.2 42.7 %collective-permute-start.16 = (bf16[64,2048]{1,0:T(8,128)(2,1)}, bf16[64,2048]{1,0:T(8,128)(2,1)}, u32[]{:S(2)}, u32[]{:S(2)}) collective-permute-start(bf16[64,2048]{1,0:T(8,128)(2,1)} %get-tuple-element.160.refs_0_), channel_id=1, source_target_pairs={{0,16},{8,24},{16,0},{24,8},{1,17},{9,25},{17,1},{25,9},{2,18},{10... | collective-permute-start | bytes 786440 | tf_op jit(solution)/shard_map/ppermute | solution.py:22
  181.2 43.8 %collective-permute-start.17 = (bf16[64,2048]{1,0:T(8,128)(2,1)}, bf16[64,2048]{1,0:T(8,128)(2,1)}, u32[]{:S(2)}, u32[]{:S(2)}) collective-permute-start(bf16[64,2048]{1,0:T(8,128)(2,1)} %get-tuple-element.160.refs_0_), channel_id=1, source_target_pairs={{0,24},{8,0},{16,8},{24,16},{1,25},{9,1},{17,9},{25,17},{2,26},{10... | collective-permute-start | bytes 786440 | tf_op jit(solution)/shard_map/ppermute | solution.py:22
  214.5 87.8 %collective-permute-start.24 = (bf16[512,2048]{1,0:T(8,128)(2,1)}, bf16[512,2048]{1,0:T(8,128)(2,1)S(1)}, u32[]{:S(2)}, u32[]{:S(2)}) collective-permute-start(bf16[512,2048]{1,0:T(8,128)(2,1)} %get-tuple-element.155.refs_0_.refs_4_.refs_8_.refs_12_.refs_16_), channel_id=1, source_target_pairs={{0,1},{1,0},{2,3},{3,2},{4,5},{5,4},{6,7},{7,6},{8,9},{9,8},{10,11... | collective-permute-start | bytes 6291464 | tf_op jit(solution)/shard_map/ppermute | solution.py:318
  223.9 23.9 %collective-permute-start.13 = (bf16[64,2048]{1,0:T(8,128)(2,1)}, bf16[64,2048]{1,0:T(8,128)(2,1)}, u32[]{:S(2)}, u32[]{:S(2)}) collective-permute-start(bf16[64,2048]{1,0:T(8,128)(2,1)} %get-tuple-element.158), channel_id=1, source_target_pairs={{0,16},{8,24},{16,0},{24,8},{1,17},{9,25},{17,1},{25,9},{2,18},{10... | collective-permute-start | bytes 786440 | tf_op jit(solution)/shard_map/ppermute | solution.py:22
  223.9 23.9 %collective-permute-start.14 = (bf16[64,2048]{1,0:T(8,128)(2,1)}, bf16[64,2048]{1,0:T(8,128)(2,1)}, u32[]{:S(2)}, u32[]{:S(2)}) collective-permute-start(bf16[64,2048]{1,0:T(8,128)(2,1)} %get-tuple-element.159), channel_id=1, source_target_pairs={{0,8},{8,16},{16,24},{24,0},{1,9},{9,17},{17,25},{25,1},{2,10},{10... | collective-permute-start | bytes 786440 | tf_op jit(solution)/shard_map/ppermute | solution.py:22
  233.3 68.9 %collective-permute-start.25 = (bf16[512,2048]{1,0:T(8,128)(2,1)}, bf16[512,2048]{1,0:T(8,128)(2,1)S(1)}, u32[]{:S(2)}, u32[]{:S(2)}) collective-permute-start(bf16[512,2048]{1,0:T(8,128)(2,1)} %get-tuple-element.164.refs_0_.refs_1_.refs_5_.refs_9_.refs_13_.refs_17_), channel_id=1, source_target_pairs={{0,1},{1,0},{2,3},{3,2},{4,5},{5,4},{6,7},{7,6},{8,9},{9,8},{10,11... | collective-permute-start | bytes 6291464 | tf_op jit(solution)/shard_map/ppermute | solution.py:318
  240.0 24.0 %collective-permute-start.18 = (bf16[64,2048]{1,0:T(8,128)(2,1)}, bf16[64,2048]{1,0:T(8,128)(2,1)S(1)}, u32[]{:S(2)}, u32[]{:S(2)}) collective-permute-start(bf16[64,2048]{1,0:T(8,128)(2,1)} %get-tuple-element.166), channel_id=1, source_target_pairs={{0,24},{8,0},{16,8},{24,16},{1,25},{9,1},{17,9},{25,17},{2,26},{10... | collective-permute-start | bytes 786440 | tf_op jit(solution)/shard_map/ppermute | solution.py:22
  247.9 32.9 %collective-permute-start.19 = (bf16[64,2048]{1,0:T(8,128)(2,1)}, bf16[64,2048]{1,0:T(8,128)(2,1)S(1)}, u32[]{:S(2)}, u32[]{:S(2)}) collective-permute-start(bf16[64,2048]{1,0:T(8,128)(2,1)} %get-tuple-element.167), channel_id=1, source_target_pairs={{0,16},{8,24},{16,0},{24,8},{1,17},{9,25},{17,1},{25,9},{2,18},{10... | collective-permute-start | bytes 786440 | tf_op jit(solution)/shard_map/ppermute | solution.py:22
  247.9 32.9 %collective-permute-start.20 = (bf16[64,2048]{1,0:T(8,128)(2,1)}, bf16[64,2048]{1,0:T(8,128)(2,1)S(1)}, u32[]{:S(2)}, u32[]{:S(2)}) collective-permute-start(bf16[64,2048]{1,0:T(8,128)(2,1)} %get-tuple-element.168), channel_id=1, source_target_pairs={{0,8},{8,16},{16,24},{24,0},{1,9},{9,17},{17,25},{25,1},{2,10},{10... | collective-permute-start | bytes 786440 | tf_op jit(solution)/shard_map/ppermute | solution.py:22
  283.7 40.5 %collective-permute-start.29 = (bf16[64,2048]{1,0:T(8,128)(2,1)S(1)}, bf16[64,2048]{1,0:T(8,128)(2,1)S(1)}, u32[]{:S(2)}, u32[]{:S(2)}) collective-permute-start(bf16[64,2048]{1,0:T(8,128)(2,1)S(1)} %get-tuple-element.191.refs_0_), channel_id=1, source_target_pairs={{0,8},{8,16},{16,24},{24,0},{1,9},{9,17},{17,25},{25,1},{2,10},{10... | collective-permute-start | bytes 786440 | tf_op jit(solution)/shard_map/ppermute | solution.py:22
  302.2 24.0 %collective-permute-start.30 = (bf16[64,2048]{1,0:T(8,128)(2,1)S(1)}, bf16[64,2048]{1,0:T(8,128)(2,1)S(1)}, u32[]{:S(2)}, u32[]{:S(2)}) collective-permute-start(bf16[64,2048]{1,0:T(8,128)(2,1)S(1)} %get-tuple-element.191.refs_0_), channel_id=1, source_target_pairs={{0,16},{8,24},{16,0},{24,8},{1,17},{9,25},{17,1},{25,9},{2,18},{10... | collective-permute-start | bytes 786440 | tf_op jit(solution)/shard_map/ppermute | solution.py:22
  302.2 24.0 %collective-permute-start.31 = (bf16[64,2048]{1,0:T(8,128)(2,1)S(1)}, bf16[64,2048]{1,0:T(8,128)(2,1)S(1)}, u32[]{:S(2)}, u32[]{:S(2)}) collective-permute-start(bf16[64,2048]{1,0:T(8,128)(2,1)S(1)} %get-tuple-element.191.refs_0_), channel_id=1, source_target_pairs={{0,24},{8,0},{16,8},{24,16},{1,25},{9,1},{17,9},{25,17},{2,26},{10... | collective-permute-start | bytes 786440 | tf_op jit(solution)/shard_map/ppermute | solution.py:22
  316.6 23.8 %collective-permute-start.26 = (bf16[64,2048]{1,0:T(8,128)(2,1)}, bf16[64,2048]{1,0:T(8,128)(2,1)S(1)}, u32[]{:S(2)}, u32[]{:S(2)}) collective-permute-start(bf16[64,2048]{1,0:T(8,128)(2,1)} %get-tuple-element.188), channel_id=1, source_target_pairs={{0,24},{8,0},{16,8},{24,16},{1,25},{9,1},{17,9},{25,17},{2,26},{10... | collective-permute-start | bytes 786440 | tf_op jit(solution)/shard_map/ppermute | solution.py:22
  323.1 22.6 %collective-permute-start.27 = (bf16[64,2048]{1,0:T(8,128)(2,1)}, bf16[64,2048]{1,0:T(8,128)(2,1)S(1)}, u32[]{:S(2)}, u32[]{:S(2)}) collective-permute-start(bf16[64,2048]{1,0:T(8,128)(2,1)} %get-tuple-element.189), channel_id=1, source_target_pairs={{0,16},{8,24},{16,0},{24,8},{1,17},{9,25},{17,1},{25,9},{2,18},{10... | collective-permute-start | bytes 786440 | tf_op jit(solution)/shard_map/ppermute | solution.py:22
  324.2 21.5 %collective-permute-start.28 = (bf16[64,2048]{1,0:T(8,128)(2,1)}, bf16[64,2048]{1,0:T(8,128)(2,1)S(1)}, u32[]{:S(2)}, u32[]{:S(2)}) collective-permute-start(bf16[64,2048]{1,0:T(8,128)(2,1)} %get-tuple-element.190), channel_id=1, source_target_pairs={{0,8},{8,16},{16,24},{24,0},{1,9},{9,17},{17,25},{25,1},{2,10},{10... | collective-permute-start | bytes 786440 | tf_op jit(solution)/shard_map/ppermute | solution.py:22
  333.9 25.8 %collective-permute-start.35 = (bf16[512,1024]{1,0:T(8,128)(2,1)S(1)}, bf16[512,1024]{1,0:T(8,128)(2,1)S(1)}, u32[]{:S(2)}, u32[]{:S(2)}) collective-permute-start(bf16[512,1024]{1,0:T(8,128)(2,1)S(1)} %copy-done.71), channel_id=1, source_target_pairs={{0,1},{1,0},{2,3},{3,2},{4,5},{5,4},{6,7},{7,6},{8,9},{9,8},{10,11... | collective-permute-start | bytes 3145736 | tf_op jit(solution)/shard_map/ppermute | solution.py:318
  340.4 34.7 %collective-permute-start.32 = (bf16[64,2048]{1,0:T(8,128)(2,1)}, bf16[64,2048]{1,0:T(8,128)(2,1)}, u32[]{:S(2)}, u32[]{:S(2)}) collective-permute-start(bf16[64,2048]{1,0:T(8,128)(2,1)} %get-tuple-element.198), channel_id=1, source_target_pairs={{0,24},{8,0},{16,8},{24,16},{1,25},{9,1},{17,9},{25,17},{2,26},{10... | collective-permute-start | bytes 786440 | tf_op jit(solution)/shard_map/ppermute | solution.py:22
  345.7 33.9 %collective-permute-start.33 = (bf16[64,2048]{1,0:T(8,128)(2,1)}, bf16[64,2048]{1,0:T(8,128)(2,1)}, u32[]{:S(2)}, u32[]{:S(2)}) collective-permute-start(bf16[64,2048]{1,0:T(8,128)(2,1)} %get-tuple-element.199), channel_id=1, source_target_pairs={{0,16},{8,24},{16,0},{24,8},{1,17},{9,25},{17,1},{25,9},{2,18},{10... | collective-permute-start | bytes 786440 | tf_op jit(solution)/shard_map/ppermute | solution.py:22
  345.7 33.9 %collective-permute-start.34 = (bf16[64,2048]{1,0:T(8,128)(2,1)}, bf16[64,2048]{1,0:T(8,128)(2,1)}, u32[]{:S(2)}, u32[]{:S(2)}) collective-permute-start(bf16[64,2048]{1,0:T(8,128)(2,1)} %get-tuple-element.200), channel_id=1, source_target_pairs={{0,8},{8,16},{16,24},{24,0},{1,9},{9,17},{17,25},{25,1},{2,10},{10... | collective-permute-start | bytes 786440 | tf_op jit(solution)/shard_map/ppermute | solution.py:22
  348.2 35.0 %collective-permute-start.37 = (bf16[64,2048]{1,0:T(8,128)(2,1)S(1)}, bf16[64,2048]{1,0:T(8,128)(2,1)}, u32[]{:S(2)}, u32[]{:S(2)}) collective-permute-start(bf16[64,2048]{1,0:T(8,128)(2,1)S(1)} %get-tuple-element.264.refs_0_), channel_id=1, source_target_pairs={{0,8},{8,16},{16,24},{24,0},{1,9},{9,17},{17,25},{25,1},{2,10},{10... | collective-permute-start | bytes 786440 | tf_op jit(solution)/shard_map/ppermute | solution.py:22
  359.8 27.6 %collective-permute-start.39 = (bf16[64,2048]{1,0:T(8,128)(2,1)S(1)}, bf16[64,2048]{1,0:T(8,128)(2,1)}, u32[]{:S(2)}, u32[]{:S(2)}) collective-permute-start(bf16[64,2048]{1,0:T(8,128)(2,1)S(1)} %get-tuple-element.264.refs_0_), channel_id=1, source_target_pairs={{0,16},{8,24},{16,0},{24,8},{1,17},{9,25},{17,1},{25,9},{2,18},{10... | collective-permute-start | bytes 786440 | tf_op jit(solution)/shard_map/ppermute | solution.py:22
  383.2 24.3 %collective-permute-start.40 = (bf16[64,2048]{1,0:T(8,128)(2,1)S(1)}, bf16[64,2048]{1,0:T(8,128)(2,1)S(1)}, u32[]{:S(2)}, u32[]{:S(2)}) collective-permute-start(bf16[64,2048]{1,0:T(8,128)(2,1)S(1)} %get-tuple-element.261.refs_1_), channel_id=1, source_target_pairs={{0,16},{8,24},{16,0},{24,8},{1,17},{9,25},{17,1},{25,9},{2,18},{10... | collective-permute-start | bytes 786440 | tf_op jit(solution)/shard_map/ppermute | solution.py:22
  383.2 24.3 %collective-permute-start.42 = (bf16[64,2048]{1,0:T(8,128)(2,1)S(1)}, bf16[64,2048]{1,0:T(8,128)(2,1)S(1)}, u32[]{:S(2)}, u32[]{:S(2)}) collective-permute-start(bf16[64,2048]{1,0:T(8,128)(2,1)S(1)} %get-tuple-element.261.refs_1_), channel_id=1, source_target_pairs={{0,24},{8,0},{16,8},{24,16},{1,25},{9,1},{17,9},{25,17},{2,26},{10... | collective-permute-start | bytes 786440 | tf_op jit(solution)/shard_map/ppermute | solution.py:22
  387.1 141.6 %reduce-scatter.3.cloned.1.call-start = ((), (), s32[]{:S(2)}) async-start(), calls=%async_computation.12 | async-start | bytes 5242880 | tf_op jit(solution)/shard_map/reduce_scatter | solution.py:314
  387.4 41.8 %collective-permute-start.43 = (bf16[512,2048]{1,0:T(8,128)(2,1)}, bf16[512,2048]{1,0:T(8,128)(2,1)}, u32[]{:S(2)}, u32[]{:S(2)}) collective-permute-start(bf16[512,2048]{1,0:T(8,128)(2,1)} %get-tuple-element.220.refs_0_.refs_1_.refs_2_.refs_3_), channel_id=1, source_target_pairs={{0,1},{1,0},{2,3},{3,2},{4,5},{5,4},{6,7},{7,6},{8,9},{9,8},{10,11... | collective-permute-start | bytes 6291464 | tf_op jit(solution)/shard_map/ppermute | solution.py:318
  456.4 48.5 %collective-permute-start.49 = (bf16[128,2048]{1,0:T(8,128)(2,1)}, bf16[128,2048]{1,0:T(8,128)(2,1)S(1)}, u32[]{:S(2)}, u32[]{:S(2)}) collective-permute-start(bf16[128,2048]{1,0:T(8,128)(2,1)} %get-tuple-element.228), channel_id=1, source_target_pairs={{0,8},{8,16},{16,24},{24,0},{1,9},{9,17},{17,25},{25,1},{2,10},{10... | collective-permute-start | bytes 1572872 | tf_op jit(solution)/shard_map/ppermute | solution.py:22
  456.4 48.5 %collective-permute-start.48 = (bf16[128,2048]{1,0:T(8,128)(2,1)}, bf16[128,2048]{1,0:T(8,128)(2,1)S(1)}, u32[]{:S(2)}, u32[]{:S(2)}) collective-permute-start(bf16[128,2048]{1,0:T(8,128)(2,1)} %get-tuple-element.227), channel_id=1, source_target_pairs={{0,16},{8,24},{16,0},{24,8},{1,17},{9,25},{17,1},{25,9},{2,18},{10... | collective-permute-start | bytes 1572872 | tf_op jit(solution)/shard_map/ppermute | solution.py:22
  469.6 33.5 %all-to-all-start.3 = ((f32[32,1,768]{2,1,0:T(1,128)}), f32[32,1,768]{2,1,0:T(1,128)S(1)}, u32[]{:S(2)}, u32[]{:S(2)}) async-start(f32[32,1,768]{2,1,0:T(1,128)} %all_to_all.28), calls=%async_computation.3 | async-start | bytes 196608 | tf_op jit(solution)/shard_map/all_to_all | solution.py:455
  510.7 30.6 %all-to-all-start.5 = ((bf16[4,64,2048]{2,1,0:T(8,128)(2,1)}), bf16[4,64,2048]{2,1,0:T(8,128)(2,1)S(1)}, u32[]{:S(2)}, u32[]{:S(2)}) async-start(bf16[4,64,2048]{2,1,0:T(8,128)(2,1)} %pad_maximum_fusion), calls=%async_computation.7 | async-start | bytes 2097152 | tf_op jit(solution)/shard_map/all_to_all | solution.py:305
  541.3 23.9 %all-to-all-start.4 = ((bf16[4,64,1536]{2,1,0:T(8,128)(2,1)}), bf16[4,64,1536]{2,1,0:T(8,128)(2,1)}, u32[]{:S(2)}, u32[]{:S(2)}) async-start(bf16[4,64,1536]{2,1,0:T(8,128)(2,1)} %pad_maximum_fusion.1), calls=%async_computation.6 | async-start | bytes 1572864 | tf_op jit(solution)/shard_map/all_to_all | solution.py:305
  (93 other events, 1346.1 us)
Sparse Core Ops, SparseCore 0:
  9.9 30.5 all-gather.4
  48.9 44.2 all-gather.6
  95.1 54.3 all-gather.8
  151.8 54.3 all-gather.10
  387.2 85.0 reduce-scatter.4
  475.4 53.1 reduce-scatter.2

commit v6 on v5

--- a/solution.py
+++ b/solution.py
@@ -167,41 +167,52 @@
     scores = dot_nt(q, k) * HEAD_DIM ** (-0.5)
     scores = jnp.where(seg_col == seg_row, scores, -1e30)
     terms = jnp.exp(scores - jnp.max(scores, axis=1, keepdims=True))
-    return terms / jnp.sum(terms, axis=1, keepdims=True)
+    return terms * (1.0 / jnp.sum(terms, axis=1, keepdims=True))
+
+
+PAIR = 2
+
+
+def head_of(ref, i):
+    return ref[:, i * HEAD_DIM : (i + 1) * HEAD_DIM]
 
 
 def attend_kernel(core, seg_col, seg_row, q, k, v, mixed):
-    probs = softmax_of(q[...], k[...], seg_col[...], seg_row[...])
-    mixed[...] = dot_nn(probs.astype(bf16), v[...]).astype(bf16)
+    for i in range(PAIR):
+        probs = softmax_of(head_of(q, i), head_of(k, i), seg_col[...], seg_row[...])
+        result = dot_nn(probs.astype(bf16), head_of(v, i))
+        mixed[:, i * HEAD_DIM : (i + 1) * HEAD_DIM] = result.astype(bf16)
 
 
 def attend_back_kernel(core, seg_col, seg_row, q, k, v, gm, grad, sent):
-    heads = pl.num_programs(0)
-    head = pl.program_id(0)
-    probs = softmax_of(q[...], k[...], seg_col[...], seg_row[...])
-    grad_probs = dot_nt(gm[...], v[...])
-    products = jnp.sum(probs * grad_probs, axis=1, keepdims=True)
-    grad_scores = (probs * (grad_probs - products)).astype(bf16)
+    heads = pl.num_programs(0) * PAIR
+    half = heads // 2
     scale = HEAD_DIM ** (-0.5)
-    half = heads // 2
-
-    def put(part, value):
-        value = value.astype(bf16)
-        start = pl.multiple_of((part * heads + head) * HEAD_DIM, HEAD_DIM)
-        grad[:, pl.ds(start, HEAD_DIM)] = value
+    for i in range(PAIR):
+        head = pl.program_id(0) * PAIR + i
+        qi, ki, vi, gi = (head_of(ref, i) for ref in (q, k, v, gm))
+        probs = softmax_of(qi, ki, seg_col[...], seg_row[...])
+        grad_probs = dot_nt(gi, vi)
+        products = jnp.sum(probs * grad_probs, axis=1, keepdims=True)
+        grad_scores = (probs * (grad_probs - products)).astype(bf16)
+        values = (
+            dot_nn(grad_scores, ki) * scale,
+            dot_tn(grad_scores, qi) * scale,
+            dot_tn(probs.astype(bf16), gi),
+        )
+        for part, value in enumerate(values):
+            start = pl.multiple_of((part * heads + head) * HEAD_DIM, HEAD_DIM)
+            grad[:, pl.ds(start, HEAD_DIM)] = value.astype(bf16)
 
         @pl.when(head // half != core[0])
         def _():
-            into = pl.multiple_of((part * half + head % half) * HEAD_DIM, HEAD_DIM)
-            sent[:, pl.ds(into, HEAD_DIM)] = value
-
-    put(0, dot_nn(grad_scores, k[...]) * scale)
-    put(1, dot_tn(grad_scores, q[...]) * scale)
-    put(2, dot_tn(probs.astype(bf16), gm[...]))
+            for part, value in enumerate(values):
+                into = pl.multiple_of((part * half + head % half) * HEAD_DIM, HEAD_DIM)
+                sent[:, pl.ds(into, HEAD_DIM)] = value.astype(bf16)
 
 
 def head_spec(rows, offset):
-    return pl.BlockSpec((rows, HEAD_DIM), lambda h, sc: (0, offset + h))
+    return pl.BlockSpec((rows, PAIR * HEAD_DIM), lambda h, sc: (0, offset // PAIR + h))
 
 
 def qkv_specs(rows, heads):
@@ -220,7 +231,7 @@
     return grid_call(
         attend_kernel,
         core,
-        (heads,),
+        (heads // PAIR,),
         qkv_specs(rows, heads),
         head_spec(rows, 0),
         jax.ShapeDtypeStruct((rows, width // 3), bf16),
@@ -235,7 +246,7 @@
     return grid_call(
         attend_back_kernel,
         core,
-        (heads,),
+        (heads // PAIR,),
         qkv_specs(rows, heads) + [head_spec(rows, 0)],
         [fixed((rows, width)), fixed((rows, width // 2))],
         [
@@ -464,9 +475,10 @@
 
 def gelu_parts(v):
     c = 0.7978845608028654
-    t = jnp.tanh(c * (v + 0.044715 * v * v * v))
-    value = 0.5 * v * (1.0 + t)
-    slope = 0.5 * (1.0 + t) + 0.5 * v * (1.0 - t * t) * c * (1.0 + 3 * 0.044715 * v * v)
+    square = v * v
+    share = 0.5 + 0.5 * jnp.tanh(v * (c + 0.044715 * c * square))
+    value = v * share
+    slope = share + value * (1.0 - share) * (2 * c + 6 * 0.044715 * c * square)
     return value, slope
 
 
@@ -505,7 +517,7 @@
     vectors += [in_bias, down_bias, norm2_gain, norm2_bias]
     small = all_small(after(vectors, qkv_moved))
     qv_full, out_b, gain_one, shift_one, in_b, down_b, gain_two, shift_two = small
-    qkv_w = gather_dp(after(qkv_moved, out_w, tok_blocks[1]))
+    qkv_w = gather_dp(after(qkv_moved, out_w))
     in_moved = exchange(after(pack_columns(in_weight, 1, c), tok_blocks))
     down_w = gather_dp(after(down_weight, qkv_moved))
 

time: 576 us -> 571 us (level)
  blocking collectives: 0 us -> 26.7 us
  waiting for transfers between devices: 259 us -> 241 us
  starting transfers between devices: 119 us -> 109 us
    all_to_all x0 -> x1, blocking collectives: none -> 26.7 us  [exchange(): return lax.all_to_all(pieces, 'seq', 0, 0)]
    ppermute x42, waiting for transfers between devices: 163 us -> 155 us  [shift(): return lax.ppermute(value, 'seq', [(i, (i + step) % n) for i in range(n)])]
    all_gather x4, waiting for transfers between devices: 14.2 us -> 6.05 us  [gather_dp(): full = lax.all_gather(shard, DP, axis=shard.ndim - 2, tiled=True)]
    all_to_all x4 -> x3, starting transfers between devices: 18.8 us -> 12.3 us  [exchange(): return lax.all_to_all(pieces, 'seq', 0, 0)]
    all_to_all x4 -> x3, waiting for transfers between devices: 23.7 us -> 18.9 us  [exchange(): return lax.all_to_all(pieces, 'seq', 0, 0)]
  transfers between devices with their start and end apart: 65 -> 64, of which waited for: 28 -> 26; matrix products, arithmetic and copies ran while one was open for 7% -> 7% of each run, Pallas kernels for 22% -> 22%
where the time goes in v6:
time: 571 us; the launch traced here: 570 us
  waiting for transfers between devices  241 us (42%)
  Pallas kernels  126 us (22%)
  starting transfers between devices  109 us (19%)
  other arithmetic  30.1 us (5%)
  blocking collectives  26.7 us (5%)
  local copies, waits for them, and re-layouts  21.3 us (4%)
  between operations  15.1 us (3%)
    ppermute x42, waiting for transfers between devices, shift(): return lax.ppermute(value, 'seq', [(i, (i + step) % n) for i in range(n)])  155 us
    pallas_call x20, Pallas kernels, grid_call(): pl.pallas_call(kernel, grid_spec=grid_spec, out_shape=out_shape, compiler...  126 us
    ppermute x42, starting transfers between devices, shift(): return lax.ppermute(value, 'seq', [(i, (i + step) % n) for i in range(n)])  86.9 us
    all_to_all x1, waiting for transfers between devices, scatter_small(): mine = jnp.sum(lax.all_to_all(packed, ALL, 0, 0), axis=0)  28.1 us
    all_to_all x1, blocking collectives, exchange(): return lax.all_to_all(pieces, 'seq', 0, 0)  26.7 us
    all_to_all x3, waiting for transfers between devices, exchange(): return lax.all_to_all(pieces, 'seq', 0, 0)  18.9 us
    reduce_scatter x2, waiting for transfers between devices, sum_over(): lax.psum_scatter(value, axes, scatter_dimension=value.ndim - 2, tiled=True)  14.8 us
    all_to_all x1, waiting for transfers between devices, all_small(): lax.all_to_all(jnp.broadcast_to(packed[None], (count, packed.shape[0])),...  12.7 us
  transfers between devices with their start and end apart: 64, of which 26 were waited for; matrix products, arithmetic and copies ran while one was open for 7% of the time, Pallas kernels for 22%

profile of v6, /device:TPU:0, one launch (start us, length us, event | category | flops | bytes accessed | tf_op | source)
XLA Modules:
  0.0 569.8 jit_solution(8159050588991790411)
XLA Ops:
  10.1 26.7 %all_to_all.38 = bf16[4,64,1536]{2,1,0:T(8,128)(2,1)} all-to-all(bf16[4,64,1536]{2,1,0:T(8,128)(2,1)} %pack.2), channel_id=1, replica_groups=mesh['seq'=4,'chip'=4,'core'=2] {'seq'}, dimensions={0} | all-to-all | bytes 1572864 | tf_op jit(solution)/shard_map/all_to_all | solution.py:316
  36.8 3.7 all-gather.5.cloned.1.call-done.refs_1_.refs_8_
  53.8 4.2 collective-permute-done.refs_1_
  58.0 22.1 %collective-permute-done.1.refs_2_ = bf16[128,2048]{1,0:T(8,128)(2,1)S(1)} collective-permute-done((bf16[128,2048]{1,0:T(8,128)(2,1)S(1)}, bf16[128,2048]{1,0:T(8,128)(2,1)S(1)}, u32[]{:S(2)}, u32[]{:S(2)}) %collective-permute-start.1) | collective-permute-done | bytes 524320 | tf_op jit(solution)/shard_map/ppermute | solution.py:22
  80.2 12.7 %all-to-all-done.1 = bf16[32,2,384]{2,1,0:T(2,128)(2,1)S(1)} async-done(((bf16[32,2,384]{2,1,0:T(2,128)(2,1)}), bf16[32,2,384]{2,1,0:T(2,128)(2,1)S(1)}, u32[]{:S(2)}, u32[]{:S(2)}) %all-to-all-start.1) | async-done | bytes 49184 | tf_op jit(solution)/shard_map/all_to_all | solution.py:453
  98.4 7.5 %qkv.1 = (bf16[512,1536]{1,0:T(8,128)(2,1)}, bf16[512,2048]{1,0:T(8,128)(2,1)}) custom-call(s32[1]{0:T(128)} %bitcast.1.sc.core, bf16[128,2048]{1,0:T(8,128)(2,1)} %bitcast.107, bf16[128,2048]{1,0:T(8,128)(2,1)} %copy-done.71, bf16[128,2048]{1,0:T(8,128)(2,1)} %copy-done.72, bf16[128,2048]{1,0:T(8,128)(2,1)} %copy-done.73, bf16[2048,1536]{1,0:T(8,128)(2,1)} %bitcast.122, ...), custom_call_target="tpu_custom_call" | custom-call | flops 3221225472 | bytes 9961472 | tf_op jit(solution)/shard_map/qkv/pallas_call | solution.py:73
  105.9 5.4 attend.1.refs_0_.refs_8_
  111.3 3.9 out.1
  115.2 3.8 collective-permute-start.3
  123.6 4.7 collective-permute-done.3
  128.3 16.9 %collective-permute-done.4 = bf16[64,2048]{1,0:T(8,128)(2,1)S(1)} collective-permute-done((bf16[64,2048]{1,0:T(8,128)(2,1)}, bf16[64,2048]{1,0:T(8,128)(2,1)S(1)}, u32[]{:S(2)}, u32[]{:S(2)}) %collective-permute-start.4) | collective-permute-done | bytes 262176 | tf_op jit(solution)/shard_map/ppermute | solution.py:22
  147.8 3.8 collective-permute-start.9
  154.2 13.0 %collective-permute-done.10 = bf16[64,2048]{1,0:T(8,128)(2,1)} collective-permute-done((bf16[64,2048]{1,0:T(8,128)(2,1)}, bf16[64,2048]{1,0:T(8,128)(2,1)}, u32[]{:S(2)}, u32[]{:S(2)}) %collective-permute-start.10) | collective-permute-done | bytes 262176 | tf_op jit(solution)/shard_map/ppermute | solution.py:22
  167.2 7.7 %collective-permute-done.9 = bf16[64,2048]{1,0:T(8,128)(2,1)} collective-permute-done((bf16[64,2048]{1,0:T(8,128)(2,1)}, bf16[64,2048]{1,0:T(8,128)(2,1)}, u32[]{:S(2)}, u32[]{:S(2)}) %collective-permute-start.9) | collective-permute-done | bytes 262176 | tf_op jit(solution)/shard_map/ppermute | solution.py:22
  178.0 9.5 %collective-permute-start.15 = (bf16[64,2048]{1,0:T(8,128)(2,1)}, bf16[64,2048]{1,0:T(8,128)(2,1)}, u32[]{:S(2)}, u32[]{:S(2)}) collective-permute-start(bf16[64,2048]{1,0:T(8,128)(2,1)} %get-tuple-element.160.refs_0_), channel_id=1, source_target_pairs={{0,8},{8,16},{16,24},{24,0},{1,9},{9,17},{17,25},{25,1},{2,10},{10... | collective-permute-start | bytes 786440 | tf_op jit(solution)/shard_map/ppermute | solution.py:22
  189.8 9.3 %collective-permute-done.7.refs_2_ = bf16[64,2048]{1,0:T(8,128)(2,1)} collective-permute-done((bf16[64,2048]{1,0:T(8,128)(2,1)S(1)}, bf16[64,2048]{1,0:T(8,128)(2,1)}, u32[]{:S(2)}, u32[]{:S(2)}) %collective-permute-start.7) | collective-permute-done | bytes 262176 | tf_op jit(solution)/shard_map/ppermute | solution.py:22
  201.5 8.0 %in.2 = (bf16[256,2048]{1,0:T(8,128)(2,1)}, bf16[512,2048]{1,0:T(8,128)(2,1)}) custom-call(s32[1]{0:T(128)} %bitcast.1.sc.core, bf16[64,2048]{1,0:T(8,128)(2,1)} %copy-done.18, bf16[64,2048]{1,0:T(8,128)(2,1)} %collective-permute-done.6.refs_1_, bf16[64,2048]{1,0:T(8,128)(2,1)} %collective-permute-done.7.refs_2_, ...), custom_call_target="tpu_custom_call" | custom-call | flops 2147483648 | bytes 10485760 | tf_op jit(solution)/shard_map/in/pallas_call | solution.py:73
  209.7 5.8 %down.2 = (f32[64,2048]{1,0:T(8,128)}, bf16[64,2048]{1,0:T(8,128)(2,1)}, bf16[64,2048]{1,0:T(8,128)(2,1)}, bf16[64,2048]{1,0:T(8,128)(2,1)}) custom-call(s32[1]{0:T(128)} %bitcast.1.sc.core, bf16[512,2048]{1,0:T(8,128)(2,1)} %get-tuple-element.155.refs_0_.refs_4_.refs_8_.refs_12_.refs_16_, bf16[2048,2048]{1,0:T(8,128)(2,1)} %all-gather.9.cloned.1.call-done.refs_1_.refs_4_), custom_call_target="tpu_custom_call" | custom-call | flops 2147483648 | bytes 10485760 | tf_op jit(solution)/shard_map/down/pallas_call | solution.py:73
  220.6 8.0 %in.3 = (bf16[256,2048]{1,0:T(8,128)(2,1)}, bf16[512,2048]{1,0:T(8,128)(2,1)}) custom-call(s32[1]{0:T(128)} %bitcast.1.sc.core, bf16[64,2048]{1,0:T(8,128)(2,1)} %get-tuple-element.160.refs_0_, bf16[64,2048]{1,0:T(8,128)(2,1)} %collective-permute-done.15.refs_1_, bf16[64,2048]{1,0:T(8,128)(2,1)} %collective-permute-done.16.refs_2_, ...), custom_call_target="tpu_custom_call" | custom-call | flops 2147483648 | bytes 10485760 | tf_op jit(solution)/shard_map/in/pallas_call | solution.py:73
  228.7 5.9 %down.3 = (f32[64,2048]{1,0:T(8,128)}, bf16[64,2048]{1,0:T(8,128)(2,1)}, bf16[64,2048]{1,0:T(8,128)(2,1)}, bf16[64,2048]{1,0:T(8,128)(2,1)}) custom-call(s32[1]{0:T(128)} %bitcast.1.sc.core, bf16[512,2048]{1,0:T(8,128)(2,1)} %get-tuple-element.164.refs_0_.refs_1_.refs_5_.refs_9_.refs_13_.refs_17_, bf16[2048,2048]{1,0:T(8,128)(2,1)} %all-gather.9.cloned.1.call-done.refs_1_.refs_4_), custom_call_target="tpu_custom_call" | custom-call | flops 2147483648 | bytes 10485760 | tf_op jit(solution)/shard_map/down/pallas_call | solution.py:73
  235.3 3.8 collective-permute-start.18
  239.1 6.0 %collective-permute-done.13 = bf16[64,2048]{1,0:T(8,128)(2,1)} collective-permute-done((bf16[64,2048]{1,0:T(8,128)(2,1)}, bf16[64,2048]{1,0:T(8,128)(2,1)}, u32[]{:S(2)}, u32[]{:S(2)}) %collective-permute-start.13) | collective-permute-done | bytes 262176 | tf_op jit(solution)/shard_map/ppermute | solution.py:22
  245.1 9.7 %collective-permute-start.20 = (bf16[64,2048]{1,0:T(8,128)(2,1)}, bf16[64,2048]{1,0:T(8,128)(2,1)S(1)}, u32[]{:S(2)}, u32[]{:S(2)}) collective-permute-start(bf16[64,2048]{1,0:T(8,128)(2,1)} %get-tuple-element.168), channel_id=1, source_target_pairs={{0,8},{8,16},{16,24},{24,0},{1,9},{9,17},{17,25},{25,1},{2,10},{10... | collective-permute-start | bytes 786440 | tf_op jit(solution)/shard_map/ppermute | solution.py:22
  262.2 15.9 %collective-permute-done.19 = bf16[64,2048]{1,0:T(8,128)(2,1)S(1)} collective-permute-done((bf16[64,2048]{1,0:T(8,128)(2,1)}, bf16[64,2048]{1,0:T(8,128)(2,1)S(1)}, u32[]{:S(2)}, u32[]{:S(2)}) %collective-permute-start.19) | collective-permute-done | bytes 262176 | tf_op jit(solution)/shard_map/ppermute | solution.py:22
  283.1 16.4 %collective-permute-done.22.refs_2_ = bf16[64,2048]{1,0:T(8,128)(2,1)S(1)} collective-permute-done((bf16[64,2048]{1,0:T(8,128)(2,1)S(1)}, bf16[64,2048]{1,0:T(8,128)(2,1)S(1)}, u32[]{:S(2)}, u32[]{:S(2)}) %collective-permute-start.22) | collective-permute-done | bytes 262176 | tf_op jit(solution)/shard_map/ppermute | solution.py:22
  300.3 7.6 %pre_grad.2 = (bf16[256,2048]{1,0:T(8,128)(2,1)}, bf16[512,1024]{1,0:T(8,128)(2,1)}, bf16[256,2048]{1,0:T(8,128)(2,1)}) custom-call(s32[1]{0:T(128)} %bitcast.1.sc.core, bf16[64,2048]{1,0:T(8,128)(2,1)} %copy-done.22, bf16[64,2048]{1,0:T(8,128)(2,1)} %copy-done.45, bf16[64,2048]{1,0:T(8,128)(2,1)} %copy-done.46, bf16[64,2048]{1,0:T(8,128)(2,1)} %copy-done.47, ...), custom_call_target="tpu_custom_call" | custom-call | flops 2147483648 | bytes 10485760 | tf_op jit(solution)/shard_map/pre_grad/pallas_call | solution.py:73
  308.0 5.9 %back.2 = (f32[64,2048]{1,0:T(8,128)}, bf16[64,2048]{1,0:T(8,128)(2,1)}, bf16[64,2048]{1,0:T(8,128)(2,1)}, bf16[64,2048]{1,0:T(8,128)(2,1)}) custom-call(s32[1]{0:T(128)} %bitcast.1.sc.core, bf16[256,2048]{1,0:T(8,128)(2,1)} %get-tuple-element.186.refs_0_.refs_20_, bf16[2048,2048]{1,0:T(8,128)(2,1)} %bitcast.102), custom_call_target="tpu_custom_call" | custom-call | flops 2147483648 | bytes 10485760 | tf_op jit(solution)/shard_map/back/pallas_call | solution.py:73
  313.8 6.5 %collective-permute-start.26 = (bf16[64,2048]{1,0:T(8,128)(2,1)}, bf16[64,2048]{1,0:T(8,128)(2,1)S(1)}, u32[]{:S(2)}, u32[]{:S(2)}) collective-permute-start(bf16[64,2048]{1,0:T(8,128)(2,1)} %get-tuple-element.188), channel_id=1, source_target_pairs={{0,24},{8,0},{16,8},{24,16},{1,25},{9,1},{17,9},{25,17},{2,26},{10... | collective-permute-start | bytes 786440 | tf_op jit(solution)/shard_map/ppermute | solution.py:22
  324.2 7.0 %pre_grad.3 = (bf16[256,2048]{1,0:T(8,128)(2,1)}, bf16[512,1024]{1,0:T(8,128)(2,1)}, bf16[256,2048]{1,0:T(8,128)(2,1)}) custom-call(s32[1]{0:T(128)} %bitcast.1.sc.core, bf16[64,2048]{1,0:T(8,128)(2,1)} %copy-done.21, bf16[64,2048]{1,0:T(8,128)(2,1)} %copy-done.48, bf16[64,2048]{1,0:T(8,128)(2,1)} %copy-done.49, bf16[64,2048]{1,0:T(8,128)(2,1)} %copy-done.50, ...), custom_call_target="tpu_custom_call" | custom-call | flops 2147483648 | bytes 10485760 | tf_op jit(solution)/shard_map/pre_grad/pallas_call | solution.py:73
  331.7 5.9 %back.3 = (f32[64,2048]{1,0:T(8,128)}, bf16[64,2048]{1,0:T(8,128)(2,1)}, bf16[64,2048]{1,0:T(8,128)(2,1)}, bf16[64,2048]{1,0:T(8,128)(2,1)}) custom-call(s32[1]{0:T(128)} %bitcast.1.sc.core, bf16[256,2048]{1,0:T(8,128)(2,1)} %get-tuple-element.196.refs_0_.refs_21_, bf16[2048,2048]{1,0:T(8,128)(2,1)} %bitcast.103), custom_call_target="tpu_custom_call" | custom-call | flops 2147483648 | bytes 10485760 | tf_op jit(solution)/shard_map/back/pallas_call | solution.py:73
  339.5 4.5 collective-permute-done.27
  344.1 9.4 %collective-permute-start.34 = (bf16[64,2048]{1,0:T(8,128)(2,1)}, bf16[64,2048]{1,0:T(8,128)(2,1)}, u32[]{:S(2)}, u32[]{:S(2)}) collective-permute-start(bf16[64,2048]{1,0:T(8,128)(2,1)} %get-tuple-element.200), channel_id=1, source_target_pairs={{0,8},{8,16},{16,24},{24,0},{1,9},{9,17},{17,25},{25,1},{2,10},{10... | collective-permute-start | bytes 786440 | tf_op jit(solution)/shard_map/ppermute | solution.py:22
  359.4 14.3 %feed_grads.1 = bf16[8,512,1024]{2,1,0:T(8,128)(2,1)} custom-call(s32[1]{0:T(128)} %bitcast.16.sc, bf16[512,2048]{1,0:T(8,128)(2,1)} %get-tuple-element.155.refs_0_.refs_4_.refs_8_.refs_12_.refs_16_, bf16[512,2048]{1,0:T(8,128)(2,1)} %get-tuple-element.164.refs_0_.refs_1_.refs_5_.refs_9_.refs_13_.refs_17_, bf16[512,2048]{1,0:T(8,128)(2,1)} %copy-done, ...), custom_call_target="tpu_custom_call" | custom-call | tf_op jit(solution)/shard_map/feed_grads/pallas_call | solution.py:73
  381.6 3.8 collective-permute-start.42
  385.8 5.4 collective-permute-done.39.refs_4_
  392.9 13.0 %collective-permute-done.40.refs_5_ = bf16[64,2048]{1,0:T(8,128)(2,1)S(1)} collective-permute-done((bf16[64,2048]{1,0:T(8,128)(2,1)S(1)}, bf16[64,2048]{1,0:T(8,128)(2,1)S(1)}, u32[]{:S(2)}, u32[]{:S(2)}) %collective-permute-start.40) | collective-permute-done | bytes 262176 | tf_op jit(solution)/shard_map/ppermute | solution.py:22
  407.3 5.6 mixed_grad.1
  412.9 9.0 %attend_back.1 = (bf16[512,1536]{1,0:T(8,128)(2,1)}, bf16[512,768]{1,0:T(8,128)(2,1)}) custom-call(s32[1]{0:T(128)} %bitcast.1.sc.core, s32[512,1]{1,0:T(8,128)} %copy.45.seg_col, s32[1,512]{1,0:T(1,128)} %bitcast.120, bf16[512,1536]{1,0:T(8,128)(2,1)} %get-tuple-element.135.q.k.v, bf16[512,1536]{1,0:T(8,128)(2,1)} %get-tuple-element.135.q.k.v, ...), custom_call_target="tpu_custom_call" | custom-call | flops 399999991808 | bytes 1 | tf_op jit(solution)/shard_map/attend_back/pallas_call | solution.py:73
  426.2 9.7 %attn_grad.1 = bf16[4,512,1024]{2,1,0:T(8,128)(2,1)} custom-call(s32[1]{0:T(128)} %bitcast.1.sc.core, bf16[512,2048]{1,0:T(8,128)(2,1)} %get-tuple-element.220.refs_0_.refs_1_.refs_2_.refs_3_, bf16[512,2048]{1,0:T(8,128)(2,1)} %get-tuple-element.220.refs_0_.refs_1_.refs_2_.refs_3_, bf16[512,2048]{1,0:T(8,128)(2,1)} %get-tuple-element.220.refs_0_.refs_1_.refs_2_.refs_3_, ...), custom_call_target="tpu_custom_call" | custom-call | tf_op jit(solution)/shard_map/attn_grad/pallas_call | solution.py:73
  437.3 7.2 %last.1 = (f32[128,2048]{1,0:T(8,128)}, bf16[128,2048]{1,0:T(8,128)(2,1)}, bf16[128,2048]{1,0:T(8,128)(2,1)}, bf16[128,2048]{1,0:T(8,128)(2,1)}) custom-call(s32[1]{0:T(128)} %bitcast.1.sc.core, bf16[512,1536]{1,0:T(8,128)(2,1)} %get-tuple-element.229.refs_10_.refs_11_.refs_12_.refs_0_, bf16[2048,1536]{1,0:T(8,128)(2,1)} %bitcast.123), custom_call_target="tpu_custom_call" | custom-call | flops 3221225472 | bytes 9961472 | tf_op jit(solution)/shard_map/last/pallas_call | solution.py:73
  444.6 6.2 %collective-permute-start.47 = (bf16[128,2048]{1,0:T(8,128)(2,1)}, bf16[128,2048]{1,0:T(8,128)(2,1)S(1)}, u32[]{:S(2)}, u32[]{:S(2)}) collective-permute-start(bf16[128,2048]{1,0:T(8,128)(2,1)} %get-tuple-element.226), channel_id=1, source_target_pairs={{0,24},{8,0},{16,8},{24,16},{1,25},{9,1},{17,9},{25,17},{2,26},{10... | collective-permute-start | bytes 1572872 | tf_op jit(solution)/shard_map/ppermute | solution.py:22
  452.3 11.2 %collective-permute-done.47 = bf16[128,2048]{1,0:T(8,128)(2,1)S(1)} collective-permute-done((bf16[128,2048]{1,0:T(8,128)(2,1)}, bf16[128,2048]{1,0:T(8,128)(2,1)S(1)}, u32[]{:S(2)}, u32[]{:S(2)}) %collective-permute-start.47) | collective-permute-done | bytes 524320 | tf_op jit(solution)/shard_map/ppermute | solution.py:22
  464.8 5.4 all-to-all-start.3
  470.2 28.1 %all-to-all-done.3 = f32[32,1,768]{2,1,0:T(1,128)S(1)} async-done(((f32[32,1,768]{2,1,0:T(1,128)}), f32[32,1,768]{2,1,0:T(1,128)S(1)}, u32[]{:S(2)}, u32[]{:S(2)}) %all-to-all-start.3) | async-done | bytes 98336 | tf_op jit(solution)/shard_map/all_to_all | solution.py:466
  506.0 4.6 all-to-all-start.5
  512.4 14.7 %reduce-scatter.3.cloned.1.call-done = bf16[4,128,1024]{2,1,0:T(8,128)(2,1)} async-done(((bf16[4,512,1024]{2,1,0:T(8,128)(2,1)}), bf16[4,128,1024]{2,1,0:T(8,128)(2,1)}) %reduce-scatter.3.cloned.1.call-update) | async-done | bytes 1048592 | tf_op jit(solution)/shard_map/reduce_scatter | solution.py:325
  536.6 4.2 all-to-all-start.4
  547.6 12.9 %all-to-all-done.4.pieces_ref = bf16[4,64,1536]{2,1,0:T(8,128)(2,1)} async-done(((bf16[4,64,1536]{2,1,0:T(8,128)(2,1)}), bf16[4,64,1536]{2,1,0:T(8,128)(2,1)}, u32[]{:S(2)}, u32[]{:S(2)}) %all-to-all-start.4) | async-done | bytes 786464 | tf_op jit(solution)/shard_map/all_to_all | solution.py:316
  (361 shorter events, 118.1 us)
Async XLA Ops:
  7.2 33.4 %all-gather.5.cloned.1.call-start = ((), (), s32[]{:S(2)}) async-start(), calls=%async_computation.8 | async-start | bytes 2359296 | tf_op jit(solution)/shard_map/all_gather | solution.py:320
  7.9 90.5 %all-gather.7.cloned.1.call-start = ((), (), s32[]{:S(2)}) async-start(), calls=%async_computation.9 | async-start | bytes 7077888 | tf_op jit(solution)/shard_map/all_gather | solution.py:320
  40.6 134.3 %all-gather.9.cloned.1.call-start = ((), (), s32[]{:S(2)}) async-start(), calls=%async_computation.10 | async-start | bytes 9437184 | tf_op jit(solution)/shard_map/all_gather | solution.py:320
  42.8 37.3 %collective-permute-start.1 = (bf16[128,2048]{1,0:T(8,128)(2,1)S(1)}, bf16[128,2048]{1,0:T(8,128)(2,1)S(1)}, u32[]{:S(2)}, u32[]{:S(2)}) collective-permute-start(bf16[128,2048]{1,0:T(8,128)(2,1)S(1)} %bitcast.109), channel_id=1, source_target_pairs={{0,16},{8,24},{16,0},{24,8},{1,17},{9,25},{17,1},{25,9},{2,18},{10... | collective-permute-start | bytes 1572872 | tf_op jit(solution)/shard_map/ppermute | solution.py:22
  45.2 34.9 %collective-permute-start.2 = (bf16[128,2048]{1,0:T(8,128)(2,1)S(1)}, bf16[128,2048]{1,0:T(8,128)(2,1)S(1)}, u32[]{:S(2)}, u32[]{:S(2)}) collective-permute-start(bf16[128,2048]{1,0:T(8,128)(2,1)S(1)} %bitcast.110), channel_id=1, source_target_pairs={{0,24},{8,0},{16,8},{24,16},{1,25},{9,1},{17,9},{25,17},{2,26},{10... | collective-permute-start | bytes 1572872 | tf_op jit(solution)/shard_map/ppermute | solution.py:22
  49.0 43.9 %all-to-all-start.1 = ((bf16[32,2,384]{2,1,0:T(2,128)(2,1)}), bf16[32,2,384]{2,1,0:T(2,128)(2,1)S(1)}, u32[]{:S(2)}, u32[]{:S(2)}) async-start(bf16[32,2,384]{2,1,0:T(2,128)(2,1)} %reshape.327), calls=%async_computation.1 | async-start | bytes 98304 | tf_op jit(solution)/shard_map/all_to_all | solution.py:453
  92.9 30.7 %all-to-all-start.2 = ((bf16[4,64,2048]{2,1,0:T(8,128)(2,1)}), bf16[4,64,2048]{2,1,0:T(8,128)(2,1)S(1)}, u32[]{:S(2)}, u32[]{:S(2)}) async-start(bf16[4,64,2048]{2,1,0:T(8,128)(2,1)} %pack.3), calls=%async_computation.2 | async-start | bytes 2097152 | tf_op jit(solution)/shard_map/all_to_all | solution.py:316
  96.4 105.0 %all-gather.11.cloned.1.call-start = ((), (), s32[]{:S(2)}) async-start(), calls=%async_computation.11 | async-start | bytes 9437184 | tf_op jit(solution)/shard_map/all_gather | solution.py:320
  118.9 26.2 %collective-permute-start.4 = (bf16[64,2048]{1,0:T(8,128)(2,1)}, bf16[64,2048]{1,0:T(8,128)(2,1)S(1)}, u32[]{:S(2)}, u32[]{:S(2)}) collective-permute-start(bf16[64,2048]{1,0:T(8,128)(2,1)} %get-tuple-element.138), channel_id=1, source_target_pairs={{0,16},{8,24},{16,0},{24,8},{1,17},{9,25},{17,1},{25,9},{2,18},{10... | collective-permute-start | bytes 786440 | tf_op jit(solution)/shard_map/ppermute | solution.py:22
  118.9 26.2 %collective-permute-start.5 = (bf16[64,2048]{1,0:T(8,128)(2,1)}, bf16[64,2048]{1,0:T(8,128)(2,1)S(1)}, u32[]{:S(2)}, u32[]{:S(2)}) collective-permute-start(bf16[64,2048]{1,0:T(8,128)(2,1)} %get-tuple-element.139), channel_id=1, source_target_pairs={{0,8},{8,16},{16,24},{24,0},{1,9},{9,17},{17,25},{25,1},{2,10},{10... | collective-permute-start | bytes 786440 | tf_op jit(solution)/shard_map/ppermute | solution.py:22
  145.2 355.0 %reduce-scatter.5.cloned.1.call-start = ((), (), s32[]{:S(2)}) async-start(), calls=%async_computation.13 | async-start | bytes 10485760 | tf_op jit(solution)/shard_map/reduce_scatter | solution.py:325
  147.8 27.1 %collective-permute-start.9 = (bf16[64,2048]{1,0:T(8,128)(2,1)}, bf16[64,2048]{1,0:T(8,128)(2,1)}, u32[]{:S(2)}, u32[]{:S(2)}) collective-permute-start(bf16[64,2048]{1,0:T(8,128)(2,1)} %get-tuple-element.141), channel_id=1, source_target_pairs={{0,24},{8,0},{16,8},{24,16},{1,25},{9,1},{17,9},{25,17},{2,26},{10... | collective-permute-start | bytes 786440 | tf_op jit(solution)/shard_map/ppermute | solution.py:22
  153.4 34.0 %collective-permute-start.6 = (bf16[64,2048]{1,0:T(8,128)(2,1)S(1)}, bf16[64,2048]{1,0:T(8,128)(2,1)}, u32[]{:S(2)}, u32[]{:S(2)}) collective-permute-start(bf16[64,2048]{1,0:T(8,128)(2,1)S(1)} %get-tuple-element.149.refs_0_), channel_id=1, source_target_pairs={{0,8},{8,16},{16,24},{24,0},{1,9},{9,17},{17,25},{25,1},{2,10},{10... | collective-permute-start | bytes 786440 | tf_op jit(solution)/shard_map/ppermute | solution.py:22
  153.5 45.7 %collective-permute-start.7 = (bf16[64,2048]{1,0:T(8,128)(2,1)S(1)}, bf16[64,2048]{1,0:T(8,128)(2,1)}, u32[]{:S(2)}, u32[]{:S(2)}) collective-permute-start(bf16[64,2048]{1,0:T(8,128)(2,1)S(1)} %get-tuple-element.149.refs_0_), channel_id=1, source_target_pairs={{0,16},{8,24},{16,0},{24,8},{1,17},{9,25},{17,1},{25,9},{2,18},{10... | collective-permute-start | bytes 786440 | tf_op jit(solution)/shard_map/ppermute | solution.py:22
  167.2 31.9 %collective-permute-start.8 = (bf16[64,2048]{1,0:T(8,128)(2,1)S(1)}, bf16[64,2048]{1,0:T(8,128)(2,1)}, u32[]{:S(2)}, u32[]{:S(2)}) collective-permute-start(bf16[64,2048]{1,0:T(8,128)(2,1)S(1)} %get-tuple-element.149.refs_0_), channel_id=1, source_target_pairs={{0,24},{8,0},{16,8},{24,16},{1,25},{9,1},{17,9},{25,17},{2,26},{10... | collective-permute-start | bytes 786440 | tf_op jit(solution)/shard_map/ppermute | solution.py:22
  178.0 40.9 %collective-permute-start.15 = (bf16[64,2048]{1,0:T(8,128)(2,1)}, bf16[64,2048]{1,0:T(8,128)(2,1)}, u32[]{:S(2)}, u32[]{:S(2)}) collective-permute-start(bf16[64,2048]{1,0:T(8,128)(2,1)} %get-tuple-element.160.refs_0_), channel_id=1, source_target_pairs={{0,8},{8,16},{16,24},{24,0},{1,9},{9,17},{17,25},{25,1},{2,10},{10... | collective-permute-start | bytes 786440 | tf_op jit(solution)/shard_map/ppermute | solution.py:22
  187.4 33.2 %collective-permute-start.16 = (bf16[64,2048]{1,0:T(8,128)(2,1)}, bf16[64,2048]{1,0:T(8,128)(2,1)}, u32[]{:S(2)}, u32[]{:S(2)}) collective-permute-start(bf16[64,2048]{1,0:T(8,128)(2,1)} %get-tuple-element.160.refs_0_), channel_id=1, source_target_pairs={{0,16},{8,24},{16,0},{24,8},{1,17},{9,25},{17,1},{25,9},{2,18},{10... | collective-permute-start | bytes 786440 | tf_op jit(solution)/shard_map/ppermute | solution.py:22
  187.5 33.2 %collective-permute-start.17 = (bf16[64,2048]{1,0:T(8,128)(2,1)}, bf16[64,2048]{1,0:T(8,128)(2,1)}, u32[]{:S(2)}, u32[]{:S(2)}) collective-permute-start(bf16[64,2048]{1,0:T(8,128)(2,1)} %get-tuple-element.160.refs_0_), channel_id=1, source_target_pairs={{0,24},{8,0},{16,8},{24,16},{1,25},{9,1},{17,9},{25,17},{2,26},{10... | collective-permute-start | bytes 786440 | tf_op jit(solution)/shard_map/ppermute | solution.py:22
  209.4 90.2 %collective-permute-start.24 = (bf16[512,2048]{1,0:T(8,128)(2,1)}, bf16[512,2048]{1,0:T(8,128)(2,1)S(1)}, u32[]{:S(2)}, u32[]{:S(2)}) collective-permute-start(bf16[512,2048]{1,0:T(8,128)(2,1)} %get-tuple-element.155.refs_0_.refs_4_.refs_8_.refs_12_.refs_16_), channel_id=1, source_target_pairs={{0,1},{1,0},{2,3},{3,2},{4,5},{5,4},{6,7},{7,6},{8,9},{9,8},{10,11... | collective-permute-start | bytes 6291464 | tf_op jit(solution)/shard_map/ppermute | solution.py:329
  218.8 26.2 %collective-permute-start.13 = (bf16[64,2048]{1,0:T(8,128)(2,1)}, bf16[64,2048]{1,0:T(8,128)(2,1)}, u32[]{:S(2)}, u32[]{:S(2)}) collective-permute-start(bf16[64,2048]{1,0:T(8,128)(2,1)} %get-tuple-element.158), channel_id=1, source_target_pairs={{0,16},{8,24},{16,0},{24,8},{1,17},{9,25},{17,1},{25,9},{2,18},{10... | collective-permute-start | bytes 786440 | tf_op jit(solution)/shard_map/ppermute | solution.py:22
  220.6 24.4 %collective-permute-start.14 = (bf16[64,2048]{1,0:T(8,128)(2,1)}, bf16[64,2048]{1,0:T(8,128)(2,1)}, u32[]{:S(2)}, u32[]{:S(2)}) collective-permute-start(bf16[64,2048]{1,0:T(8,128)(2,1)} %get-tuple-element.159), channel_id=1, source_target_pairs={{0,8},{8,16},{16,24},{24,0},{1,9},{9,17},{17,25},{25,1},{2,10},{10... | collective-permute-start | bytes 786440 | tf_op jit(solution)/shard_map/ppermute | solution.py:22
  228.7 70.9 %collective-permute-start.25 = (bf16[512,2048]{1,0:T(8,128)(2,1)}, bf16[512,2048]{1,0:T(8,128)(2,1)S(1)}, u32[]{:S(2)}, u32[]{:S(2)}) collective-permute-start(bf16[512,2048]{1,0:T(8,128)(2,1)} %get-tuple-element.164.refs_0_.refs_1_.refs_5_.refs_9_.refs_13_.refs_17_), channel_id=1, source_target_pairs={{0,1},{1,0},{2,3},{3,2},{4,5},{5,4},{6,7},{7,6},{8,9},{9,8},{10,11... | collective-permute-start | bytes 6291464 | tf_op jit(solution)/shard_map/ppermute | solution.py:329
  235.3 23.6 %collective-permute-start.18 = (bf16[64,2048]{1,0:T(8,128)(2,1)}, bf16[64,2048]{1,0:T(8,128)(2,1)S(1)}, u32[]{:S(2)}, u32[]{:S(2)}) collective-permute-start(bf16[64,2048]{1,0:T(8,128)(2,1)} %get-tuple-element.166), channel_id=1, source_target_pairs={{0,24},{8,0},{16,8},{24,16},{1,25},{9,1},{17,9},{25,17},{2,26},{10... | collective-permute-start | bytes 786440 | tf_op jit(solution)/shard_map/ppermute | solution.py:22
  245.1 33.0 %collective-permute-start.19 = (bf16[64,2048]{1,0:T(8,128)(2,1)}, bf16[64,2048]{1,0:T(8,128)(2,1)S(1)}, u32[]{:S(2)}, u32[]{:S(2)}) collective-permute-start(bf16[64,2048]{1,0:T(8,128)(2,1)} %get-tuple-element.167), channel_id=1, source_target_pairs={{0,16},{8,24},{16,0},{24,8},{1,17},{9,25},{17,1},{25,9},{2,18},{10... | collective-permute-start | bytes 786440 | tf_op jit(solution)/shard_map/ppermute | solution.py:22
  245.1 33.0 %collective-permute-start.20 = (bf16[64,2048]{1,0:T(8,128)(2,1)}, bf16[64,2048]{1,0:T(8,128)(2,1)S(1)}, u32[]{:S(2)}, u32[]{:S(2)}) collective-permute-start(bf16[64,2048]{1,0:T(8,128)(2,1)} %get-tuple-element.168), channel_id=1, source_target_pairs={{0,8},{8,16},{16,24},{24,0},{1,9},{9,17},{17,25},{25,1},{2,10},{10... | collective-permute-start | bytes 786440 | tf_op jit(solution)/shard_map/ppermute | solution.py:22
  258.8 22.2 %collective-permute-start.21 = (bf16[64,2048]{1,0:T(8,128)(2,1)S(1)}, bf16[64,2048]{1,0:T(8,128)(2,1)S(1)}, u32[]{:S(2)}, u32[]{:S(2)}) collective-permute-start(bf16[64,2048]{1,0:T(8,128)(2,1)S(1)} %get-tuple-element.181.refs_0_), channel_id=1, source_target_pairs={{0,8},{8,16},{16,24},{24,0},{1,9},{9,17},{17,25},{25,1},{2,10},{10... | collective-permute-start | bytes 786440 | tf_op jit(solution)/shard_map/ppermute | solution.py:22
  281.1 40.4 %collective-permute-start.29 = (bf16[64,2048]{1,0:T(8,128)(2,1)S(1)}, bf16[64,2048]{1,0:T(8,128)(2,1)S(1)}, u32[]{:S(2)}, u32[]{:S(2)}) collective-permute-start(bf16[64,2048]{1,0:T(8,128)(2,1)S(1)} %get-tuple-element.191.refs_0_), channel_id=1, source_target_pairs={{0,8},{8,16},{16,24},{24,0},{1,9},{9,17},{17,25},{25,1},{2,10},{10... | collective-permute-start | bytes 786440 | tf_op jit(solution)/shard_map/ppermute | solution.py:22
  299.5 23.9 %collective-permute-start.30 = (bf16[64,2048]{1,0:T(8,128)(2,1)S(1)}, bf16[64,2048]{1,0:T(8,128)(2,1)S(1)}, u32[]{:S(2)}, u32[]{:S(2)}) collective-permute-start(bf16[64,2048]{1,0:T(8,128)(2,1)S(1)} %get-tuple-element.191.refs_0_), channel_id=1, source_target_pairs={{0,16},{8,24},{16,0},{24,8},{1,17},{9,25},{17,1},{25,9},{2,18},{10... | collective-permute-start | bytes 786440 | tf_op jit(solution)/shard_map/ppermute | solution.py:22
  299.5 23.9 %collective-permute-start.31 = (bf16[64,2048]{1,0:T(8,128)(2,1)S(1)}, bf16[64,2048]{1,0:T(8,128)(2,1)S(1)}, u32[]{:S(2)}, u32[]{:S(2)}) collective-permute-start(bf16[64,2048]{1,0:T(8,128)(2,1)S(1)} %get-tuple-element.191.refs_0_), channel_id=1, source_target_pairs={{0,24},{8,0},{16,8},{24,16},{1,25},{9,1},{17,9},{25,17},{2,26},{10... | collective-permute-start | bytes 786440 | tf_op jit(solution)/shard_map/ppermute | solution.py:22
  313.8 23.8 %collective-permute-start.26 = (bf16[64,2048]{1,0:T(8,128)(2,1)}, bf16[64,2048]{1,0:T(8,128)(2,1)S(1)}, u32[]{:S(2)}, u32[]{:S(2)}) collective-permute-start(bf16[64,2048]{1,0:T(8,128)(2,1)} %get-tuple-element.188), channel_id=1, source_target_pairs={{0,24},{8,0},{16,8},{24,16},{1,25},{9,1},{17,9},{25,17},{2,26},{10... | collective-permute-start | bytes 786440 | tf_op jit(solution)/shard_map/ppermute | solution.py:22
  320.4 23.7 %collective-permute-start.27 = (bf16[64,2048]{1,0:T(8,128)(2,1)}, bf16[64,2048]{1,0:T(8,128)(2,1)S(1)}, u32[]{:S(2)}, u32[]{:S(2)}) collective-permute-start(bf16[64,2048]{1,0:T(8,128)(2,1)} %get-tuple-element.189), channel_id=1, source_target_pairs={{0,16},{8,24},{16,0},{24,8},{1,17},{9,25},{17,1},{25,9},{2,18},{10... | collective-permute-start | bytes 786440 | tf_op jit(solution)/shard_map/ppermute | solution.py:22
  321.4 22.6 %collective-permute-start.28 = (bf16[64,2048]{1,0:T(8,128)(2,1)}, bf16[64,2048]{1,0:T(8,128)(2,1)S(1)}, u32[]{:S(2)}, u32[]{:S(2)}) collective-permute-start(bf16[64,2048]{1,0:T(8,128)(2,1)} %get-tuple-element.190), channel_id=1, source_target_pairs={{0,8},{8,16},{16,24},{24,0},{1,9},{9,17},{17,25},{25,1},{2,10},{10... | collective-permute-start | bytes 786440 | tf_op jit(solution)/shard_map/ppermute | solution.py:22
  331.2 24.8 %collective-permute-start.36 = (bf16[512,1024]{1,0:T(8,128)(2,1)}, bf16[512,1024]{1,0:T(8,128)(2,1)S(1)}, u32[]{:S(2)}, u32[]{:S(2)}) collective-permute-start(bf16[512,1024]{1,0:T(8,128)(2,1)} %get-tuple-element.207), channel_id=1, source_target_pairs={{0,1},{1,0},{2,3},{3,2},{4,5},{5,4},{6,7},{7,6},{8,9},{9,8},{10,11... | collective-permute-start | bytes 3145736 | tf_op jit(solution)/shard_map/ppermute | solution.py:329
  331.2 27.2 %collective-permute-start.35 = (bf16[512,1024]{1,0:T(8,128)(2,1)S(1)}, bf16[512,1024]{1,0:T(8,128)(2,1)S(1)}, u32[]{:S(2)}, u32[]{:S(2)}) collective-permute-start(bf16[512,1024]{1,0:T(8,128)(2,1)S(1)} %copy-done.70), channel_id=1, source_target_pairs={{0,1},{1,0},{2,3},{3,2},{4,5},{5,4},{6,7},{7,6},{8,9},{9,8},{10,11... | collective-permute-start | bytes 3145736 | tf_op jit(solution)/shard_map/ppermute | solution.py:329
  337.6 36.1 %collective-permute-start.32 = (bf16[64,2048]{1,0:T(8,128)(2,1)}, bf16[64,2048]{1,0:T(8,128)(2,1)}, u32[]{:S(2)}, u32[]{:S(2)}) collective-permute-start(bf16[64,2048]{1,0:T(8,128)(2,1)} %get-tuple-element.198), channel_id=1, source_target_pairs={{0,24},{8,0},{16,8},{24,16},{1,25},{9,1},{17,9},{25,17},{2,26},{10... | collective-permute-start | bytes 786440 | tf_op jit(solution)/shard_map/ppermute | solution.py:22
  344.1 33.9 %collective-permute-start.33 = (bf16[64,2048]{1,0:T(8,128)(2,1)}, bf16[64,2048]{1,0:T(8,128)(2,1)}, u32[]{:S(2)}, u32[]{:S(2)}) collective-permute-start(bf16[64,2048]{1,0:T(8,128)(2,1)} %get-tuple-element.199), channel_id=1, source_target_pairs={{0,16},{8,24},{16,0},{24,8},{1,17},{9,25},{17,1},{25,9},{2,18},{10... | collective-permute-start | bytes 786440 | tf_op jit(solution)/shard_map/ppermute | solution.py:22
  344.1 33.9 %collective-permute-start.34 = (bf16[64,2048]{1,0:T(8,128)(2,1)}, bf16[64,2048]{1,0:T(8,128)(2,1)}, u32[]{:S(2)}, u32[]{:S(2)}) collective-permute-start(bf16[64,2048]{1,0:T(8,128)(2,1)} %get-tuple-element.200), channel_id=1, source_target_pairs={{0,8},{8,16},{16,24},{24,0},{1,9},{9,17},{17,25},{25,1},{2,10},{10... | collective-permute-start | bytes 786440 | tf_op jit(solution)/shard_map/ppermute | solution.py:22
  356.0 25.7 %collective-permute-start.37 = (bf16[64,2048]{1,0:T(8,128)(2,1)S(1)}, bf16[64,2048]{1,0:T(8,128)(2,1)}, u32[]{:S(2)}, u32[]{:S(2)}) collective-permute-start(bf16[64,2048]{1,0:T(8,128)(2,1)S(1)} %get-tuple-element.264.refs_0_), channel_id=1, source_target_pairs={{0,8},{8,16},{16,24},{24,0},{1,9},{9,17},{17,25},{25,1},{2,10},{10... | collective-permute-start | bytes 786440 | tf_op jit(solution)/shard_map/ppermute | solution.py:22
  358.4 32.7 %collective-permute-start.39 = (bf16[64,2048]{1,0:T(8,128)(2,1)S(1)}, bf16[64,2048]{1,0:T(8,128)(2,1)}, u32[]{:S(2)}, u32[]{:S(2)}) collective-permute-start(bf16[64,2048]{1,0:T(8,128)(2,1)S(1)} %get-tuple-element.264.refs_0_), channel_id=1, source_target_pairs={{0,16},{8,24},{16,0},{24,8},{1,17},{9,25},{17,1},{25,9},{2,18},{10... | collective-permute-start | bytes 786440 | tf_op jit(solution)/shard_map/ppermute | solution.py:22
  381.6 24.3 %collective-permute-start.40 = (bf16[64,2048]{1,0:T(8,128)(2,1)S(1)}, bf16[64,2048]{1,0:T(8,128)(2,1)S(1)}, u32[]{:S(2)}, u32[]{:S(2)}) collective-permute-start(bf16[64,2048]{1,0:T(8,128)(2,1)S(1)} %get-tuple-element.261.refs_1_), channel_id=1, source_target_pairs={{0,16},{8,24},{16,0},{24,8},{1,17},{9,25},{17,1},{25,9},{2,18},{10... | collective-permute-start | bytes 786440 | tf_op jit(solution)/shard_map/ppermute | solution.py:22
  381.6 24.3 %collective-permute-start.42 = (bf16[64,2048]{1,0:T(8,128)(2,1)S(1)}, bf16[64,2048]{1,0:T(8,128)(2,1)S(1)}, u32[]{:S(2)}, u32[]{:S(2)}) collective-permute-start(bf16[64,2048]{1,0:T(8,128)(2,1)S(1)} %get-tuple-element.261.refs_1_), channel_id=1, source_target_pairs={{0,24},{8,0},{16,8},{24,16},{1,25},{9,1},{17,9},{25,17},{2,26},{10... | collective-permute-start | bytes 786440 | tf_op jit(solution)/shard_map/ppermute | solution.py:22
  385.5 141.6 %reduce-scatter.3.cloned.1.call-start = ((), (), s32[]{:S(2)}) async-start(), calls=%async_computation.12 | async-start | bytes 5242880 | tf_op jit(solution)/shard_map/reduce_scatter | solution.py:325
  391.1 34.0 %collective-permute-start.43 = (bf16[512,2048]{1,0:T(8,128)(2,1)}, bf16[512,2048]{1,0:T(8,128)(2,1)}, u32[]{:S(2)}, u32[]{:S(2)}) collective-permute-start(bf16[512,2048]{1,0:T(8,128)(2,1)} %get-tuple-element.220.refs_0_.refs_1_.refs_2_.refs_3_), channel_id=1, source_target_pairs={{0,1},{1,0},{2,3},{3,2},{4,5},{5,4},{6,7},{7,6},{8,9},{9,8},{10,11... | collective-permute-start | bytes 6291464 | tf_op jit(solution)/shard_map/ppermute | solution.py:329
  451.5 48.6 %collective-permute-start.49 = (bf16[128,2048]{1,0:T(8,128)(2,1)}, bf16[128,2048]{1,0:T(8,128)(2,1)S(1)}, u32[]{:S(2)}, u32[]{:S(2)}) collective-permute-start(bf16[128,2048]{1,0:T(8,128)(2,1)} %get-tuple-element.228), channel_id=1, source_target_pairs={{0,8},{8,16},{16,24},{24,0},{1,9},{9,17},{17,25},{25,1},{2,10},{10... | collective-permute-start | bytes 1572872 | tf_op jit(solution)/shard_map/ppermute | solution.py:22
  451.5 48.6 %collective-permute-start.48 = (bf16[128,2048]{1,0:T(8,128)(2,1)}, bf16[128,2048]{1,0:T(8,128)(2,1)S(1)}, u32[]{:S(2)}, u32[]{:S(2)}) collective-permute-start(bf16[128,2048]{1,0:T(8,128)(2,1)} %get-tuple-element.227), channel_id=1, source_target_pairs={{0,16},{8,24},{16,0},{24,8},{1,17},{9,25},{17,1},{25,9},{2,18},{10... | collective-permute-start | bytes 1572872 | tf_op jit(solution)/shard_map/ppermute | solution.py:22
  464.8 33.6 %all-to-all-start.3 = ((f32[32,1,768]{2,1,0:T(1,128)}), f32[32,1,768]{2,1,0:T(1,128)S(1)}, u32[]{:S(2)}, u32[]{:S(2)}) async-start(f32[32,1,768]{2,1,0:T(1,128)} %all_to_all.28), calls=%async_computation.3 | async-start | bytes 196608 | tf_op jit(solution)/shard_map/all_to_all | solution.py:466
  506.0 30.6 %all-to-all-start.5 = ((bf16[4,64,2048]{2,1,0:T(8,128)(2,1)}), bf16[4,64,2048]{2,1,0:T(8,128)(2,1)S(1)}, u32[]{:S(2)}, u32[]{:S(2)}) async-start(bf16[4,64,2048]{2,1,0:T(8,128)(2,1)} %pad_maximum_fusion), calls=%async_computation.7 | async-start | bytes 2097152 | tf_op jit(solution)/shard_map/all_to_all | solution.py:316
  536.6 23.9 %all-to-all-start.4 = ((bf16[4,64,1536]{2,1,0:T(8,128)(2,1)}), bf16[4,64,1536]{2,1,0:T(8,128)(2,1)}, u32[]{:S(2)}, u32[]{:S(2)}) async-start(bf16[4,64,1536]{2,1,0:T(8,128)(2,1)} %pad_maximum_fusion.1), calls=%async_computation.6 | async-start | bytes 1572864 | tf_op jit(solution)/shard_map/all_to_all | solution.py:316
  (91 other events, 1305.3 us)
Sparse Core Ops, SparseCore 0:
  9.9 30.5 all-gather.4
  42.4 46.0 all-gather.6
  90.4 54.2 all-gather.8
  147.0 54.3 all-gather.10
  385.6 85.1 reduce-scatter.4
  473.9 53.1 reduce-scatter.2

commit v7 on v6

--- a/solution.py
+++ b/solution.py
@@ -733,10 +733,11 @@
         attn_far = to_partner(attn_sent)
         args = (tok_full, tok_far, mixed, mixed_far)
         qkv_far = to_partner(qkv_sent)
-        attn_low = attn_grad(c, *args, grad_qkv, qkv_far, grad_attn_full, attn_far)
+        last_split = split_product(c, grad_qkv, qkv_w, "last", nt=True)[0]
+        last_blocks = send_blocks(last_split)
+        attn_low = attn_grad(after(c, last_split), *args, grad_qkv, qkv_far, grad_attn_full, attn_far)
+        last_blocks[1], attn_low = lax.optimization_barrier((last_blocks[1], attn_low))
         attn_sum = sum_over(attn_low, "chip")
-        last_split = split_product(c, after(grad_qkv, attn_low), qkv_w, "last", nt=True)[0]
-        last_blocks = send_blocks(last_split)
         small_grads = small_sums(after(grad_qkv, last_blocks[1]))
         last_blocks[-1] = after(last_blocks[-1], small_grads)
         feed_sum = after(feed_sum, last_blocks)
@@ -745,7 +746,8 @@
         in_w_grad = join_columns(in_pieces, 1, 2, c)
         down_own, down_far = swap_rows(feed_sum[n:], (2, -1, half), 0, c)
         down_w_grad = join_halves(down_own.astype(f32), down_far.astype(f32), c)
-        attn_sum = after(attn_sum, in_far, down_own)
+        input_grad = (grad_h1 + total_of(last_blocks)).astype(bf16)
+        attn_sum = after(attn_sum, in_far, down_own, input_grad)
         attn_own, attn_far = swap_rows(attn_sum, (n, 2, -1, half), 1, c)
         split = 3 * part // 2
         pieces = jnp.concatenate([attn_own[:, :, :split], attn_far[:, :, :split]], 2)
@@ -763,8 +765,8 @@
         out_w_grad = sum_over(dot_tn(mixed, grad_attn_full).astype(bf16), DP).astype(f32)
         pieces = exchange(sum_over(attn_low.reshape(n, part, -1), DP))
         qkv_w_grad = join_columns(pieces, 3, 1, c)
-    last_blocks = after(last_blocks, small_grads)
-    input_grad = (grad_h1 + total_of(last_blocks)).astype(bf16)
+        last_blocks = after(last_blocks, small_grads)
+        input_grad = (grad_h1 + total_of(last_blocks)).astype(bf16)
     return (
         result[None],
         input_grad[None],

time: 571 us -> 569 us (level)
    ppermute x42, waiting for transfers between devices: 155 us -> 145 us  [shift(): return lax.ppermute(value, 'seq', [(i, (i + step) % n) for i in range(n)])]
  transfers between devices with their start and end apart: 64 -> 64, of which waited for: 26 -> 25; matrix products, arithmetic and copies ran while one was open for 7% -> 8% of each run, Pallas kernels for 22% -> 22%
where the time goes in v7:
time: 569 us; the launch traced here: 568 us
  waiting for transfers between devices  237 us (42%)
  Pallas kernels  126 us (22%)
  starting transfers between devices  110 us (19%)
  other arithmetic  32 us (6%)
  blocking collectives  26.7 us (5%)
  local copies, waits for them, and re-layouts  21.9 us (4%)
  between operations  15.1 us (3%)
    ppermute x42, waiting for transfers between devices, shift(): return lax.ppermute(value, 'seq', [(i, (i + step) % n) for i in range(n)])  145 us
    pallas_call x20, Pallas kernels, grid_call(): pl.pallas_call(kernel, grid_spec=grid_spec, out_shape=out_shape, compiler...  126 us
    ppermute x42, starting transfers between devices, shift(): return lax.ppermute(value, 'seq', [(i, (i + step) % n) for i in range(n)])  91.2 us
    all_to_all x1, waiting for transfers between devices, scatter_small(): mine = jnp.sum(lax.all_to_all(packed, ALL, 0, 0), axis=0)  32.6 us
    all_to_all x1, blocking collectives, exchange(): return lax.all_to_all(pieces, 'seq', 0, 0)  26.7 us
    reduce_scatter x2, waiting for transfers between devices, sum_over(): lax.psum_scatter(value, axes, scatter_dimension=value.ndim - 2, tiled=True)  19.6 us
    all_to_all x3, waiting for transfers between devices, exchange(): return lax.all_to_all(pieces, 'seq', 0, 0)  17.4 us
    all_to_all x1, waiting for transfers between devices, all_small(): lax.all_to_all(jnp.broadcast_to(packed[None], (count, packed.shape[0])),...  12.7 us
  transfers between devices with their start and end apart: 64, of which 25 were waited for; matrix products, arithmetic and copies ran while one was open for 8% of the time, Pallas kernels for 22%

profile of v7, /device:TPU:0, one launch (start us, length us, event | category | flops | bytes accessed | tf_op | source)
XLA Modules:
  0.0 568.1 jit_solution(15834997348409008333)
XLA Ops:
  10.1 26.7 %all_to_all.38 = bf16[4,64,1536]{2,1,0:T(8,128)(2,1)} all-to-all(bf16[4,64,1536]{2,1,0:T(8,128)(2,1)} %pack.2), channel_id=1, replica_groups=mesh['seq'=4,'chip'=4,'core'=2] {'seq'}, dimensions={0} | all-to-all | bytes 1572864 | tf_op jit(solution)/shard_map/all_to_all | solution.py:316
  36.8 3.7 all-gather.5.cloned.1.call-done.refs_1_.refs_8_
  53.8 4.2 collective-permute-done.refs_1_
  58.0 22.1 %collective-permute-done.1.refs_2_ = bf16[128,2048]{1,0:T(8,128)(2,1)S(1)} collective-permute-done((bf16[128,2048]{1,0:T(8,128)(2,1)S(1)}, bf16[128,2048]{1,0:T(8,128)(2,1)S(1)}, u32[]{:S(2)}, u32[]{:S(2)}) %collective-permute-start.1) | collective-permute-done | bytes 524320 | tf_op jit(solution)/shard_map/ppermute | solution.py:22
  80.2 12.7 %all-to-all-done.1 = bf16[32,2,384]{2,1,0:T(2,128)(2,1)S(1)} async-done(((bf16[32,2,384]{2,1,0:T(2,128)(2,1)}), bf16[32,2,384]{2,1,0:T(2,128)(2,1)S(1)}, u32[]{:S(2)}, u32[]{:S(2)}) %all-to-all-start.1) | async-done | bytes 49184 | tf_op jit(solution)/shard_map/all_to_all | solution.py:453
  92.9 3.5 all-to-all-start.2
  98.4 7.5 %qkv.1 = (bf16[512,1536]{1,0:T(8,128)(2,1)}, bf16[512,2048]{1,0:T(8,128)(2,1)}) custom-call(s32[1]{0:T(128)} %bitcast.1.sc.core, bf16[128,2048]{1,0:T(8,128)(2,1)} %bitcast.107, bf16[128,2048]{1,0:T(8,128)(2,1)} %copy-done.69, bf16[128,2048]{1,0:T(8,128)(2,1)} %copy-done.70, bf16[128,2048]{1,0:T(8,128)(2,1)} %copy-done.71, bf16[2048,1536]{1,0:T(8,128)(2,1)} %bitcast.123, ...), custom_call_target="tpu_custom_call" | custom-call | flops 3221225472 | bytes 9961472 | tf_op jit(solution)/shard_map/qkv/pallas_call | solution.py:73
  105.9 5.4 attend.1.refs_0_.refs_8_
  111.3 3.9 out.1
  115.2 3.8 collective-permute-start.3
  123.6 4.7 collective-permute-done.3
  128.3 16.9 %collective-permute-done.4 = bf16[64,2048]{1,0:T(8,128)(2,1)S(1)} collective-permute-done((bf16[64,2048]{1,0:T(8,128)(2,1)}, bf16[64,2048]{1,0:T(8,128)(2,1)S(1)}, u32[]{:S(2)}, u32[]{:S(2)}) %collective-permute-start.4) | collective-permute-done | bytes 262176 | tf_op jit(solution)/shard_map/ppermute | solution.py:22
  147.8 3.8 collective-permute-start.9
  154.2 13.0 %collective-permute-done.10 = bf16[64,2048]{1,0:T(8,128)(2,1)} collective-permute-done((bf16[64,2048]{1,0:T(8,128)(2,1)}, bf16[64,2048]{1,0:T(8,128)(2,1)}, u32[]{:S(2)}, u32[]{:S(2)}) %collective-permute-start.10) | collective-permute-done | bytes 262176 | tf_op jit(solution)/shard_map/ppermute | solution.py:22
  167.2 7.6 %collective-permute-done.9 = bf16[64,2048]{1,0:T(8,128)(2,1)} collective-permute-done((bf16[64,2048]{1,0:T(8,128)(2,1)}, bf16[64,2048]{1,0:T(8,128)(2,1)}, u32[]{:S(2)}, u32[]{:S(2)}) %collective-permute-start.9) | collective-permute-done | bytes 262176 | tf_op jit(solution)/shard_map/ppermute | solution.py:22
  177.9 9.6 %collective-permute-start.15 = (bf16[64,2048]{1,0:T(8,128)(2,1)}, bf16[64,2048]{1,0:T(8,128)(2,1)}, u32[]{:S(2)}, u32[]{:S(2)}) collective-permute-start(bf16[64,2048]{1,0:T(8,128)(2,1)} %get-tuple-element.158.refs_0_), channel_id=1, source_target_pairs={{0,8},{8,16},{16,24},{24,0},{1,9},{9,17},{17,25},{25,1},{2,10},{10... | collective-permute-start | bytes 786440 | tf_op jit(solution)/shard_map/ppermute | solution.py:22
  189.8 9.3 %collective-permute-done.7.refs_2_ = bf16[64,2048]{1,0:T(8,128)(2,1)} collective-permute-done((bf16[64,2048]{1,0:T(8,128)(2,1)S(1)}, bf16[64,2048]{1,0:T(8,128)(2,1)}, u32[]{:S(2)}, u32[]{:S(2)}) %collective-permute-start.7) | collective-permute-done | bytes 262176 | tf_op jit(solution)/shard_map/ppermute | solution.py:22
  201.5 8.0 %in.2 = (bf16[256,2048]{1,0:T(8,128)(2,1)}, bf16[512,2048]{1,0:T(8,128)(2,1)}) custom-call(s32[1]{0:T(128)} %bitcast.1.sc.core, bf16[64,2048]{1,0:T(8,128)(2,1)} %copy-done.16, bf16[64,2048]{1,0:T(8,128)(2,1)} %collective-permute-done.6.refs_1_, bf16[64,2048]{1,0:T(8,128)(2,1)} %collective-permute-done.7.refs_2_, ...), custom_call_target="tpu_custom_call" | custom-call | flops 2147483648 | bytes 10485760 | tf_op jit(solution)/shard_map/in/pallas_call | solution.py:73
  209.7 5.8 %down.2 = (f32[64,2048]{1,0:T(8,128)}, bf16[64,2048]{1,0:T(8,128)(2,1)}, bf16[64,2048]{1,0:T(8,128)(2,1)}, bf16[64,2048]{1,0:T(8,128)(2,1)}) custom-call(s32[1]{0:T(128)} %bitcast.1.sc.core, bf16[512,2048]{1,0:T(8,128)(2,1)} %get-tuple-element.153.refs_0_.refs_4_.refs_8_.refs_12_.refs_16_, bf16[2048,2048]{1,0:T(8,128)(2,1)} %all-gather.9.cloned.1.call-done.refs_1_.refs_4_), custom_call_target="tpu_custom_call" | custom-call | flops 2147483648 | bytes 10485760 | tf_op jit(solution)/shard_map/down/pallas_call | solution.py:73
  220.6 8.0 %in.3 = (bf16[256,2048]{1,0:T(8,128)(2,1)}, bf16[512,2048]{1,0:T(8,128)(2,1)}) custom-call(s32[1]{0:T(128)} %bitcast.1.sc.core, bf16[64,2048]{1,0:T(8,128)(2,1)} %get-tuple-element.158.refs_0_, bf16[64,2048]{1,0:T(8,128)(2,1)} %collective-permute-done.15.refs_1_, bf16[64,2048]{1,0:T(8,128)(2,1)} %collective-permute-done.16.refs_2_, ...), custom_call_target="tpu_custom_call" | custom-call | flops 2147483648 | bytes 10485760 | tf_op jit(solution)/shard_map/in/pallas_call | solution.py:73
  228.7 5.8 %down.3 = (f32[64,2048]{1,0:T(8,128)}, bf16[64,2048]{1,0:T(8,128)(2,1)}, bf16[64,2048]{1,0:T(8,128)(2,1)}, bf16[64,2048]{1,0:T(8,128)(2,1)}) custom-call(s32[1]{0:T(128)} %bitcast.1.sc.core, bf16[512,2048]{1,0:T(8,128)(2,1)} %get-tuple-element.162.refs_0_.refs_1_.refs_5_.refs_9_.refs_13_.refs_17_, bf16[2048,2048]{1,0:T(8,128)(2,1)} %all-gather.9.cloned.1.call-done.refs_1_.refs_4_), custom_call_target="tpu_custom_call" | custom-call | flops 2147483648 | bytes 10485760 | tf_op jit(solution)/shard_map/down/pallas_call | solution.py:73
  235.2 3.8 collective-permute-start.18
  239.0 5.9 %collective-permute-done.13 = bf16[64,2048]{1,0:T(8,128)(2,1)S(1)} collective-permute-done((bf16[64,2048]{1,0:T(8,128)(2,1)}, bf16[64,2048]{1,0:T(8,128)(2,1)S(1)}, u32[]{:S(2)}, u32[]{:S(2)}) %collective-permute-start.13) | collective-permute-done | bytes 262176 | tf_op jit(solution)/shard_map/ppermute | solution.py:22
  245.0 9.8 %collective-permute-start.20 = (bf16[64,2048]{1,0:T(8,128)(2,1)}, bf16[64,2048]{1,0:T(8,128)(2,1)S(1)}, u32[]{:S(2)}, u32[]{:S(2)}) collective-permute-start(bf16[64,2048]{1,0:T(8,128)(2,1)} %get-tuple-element.166), channel_id=1, source_target_pairs={{0,8},{8,16},{16,24},{24,0},{1,9},{9,17},{17,25},{25,1},{2,10},{10... | collective-permute-start | bytes 786440 | tf_op jit(solution)/shard_map/ppermute | solution.py:22
  262.2 15.9 %collective-permute-done.19 = bf16[64,2048]{1,0:T(8,128)(2,1)S(1)} collective-permute-done((bf16[64,2048]{1,0:T(8,128)(2,1)}, bf16[64,2048]{1,0:T(8,128)(2,1)S(1)}, u32[]{:S(2)}, u32[]{:S(2)}) %collective-permute-start.19) | collective-permute-done | bytes 262176 | tf_op jit(solution)/shard_map/ppermute | solution.py:22
  283.1 16.3 %collective-permute-done.22.refs_2_ = bf16[64,2048]{1,0:T(8,128)(2,1)S(1)} collective-permute-done((bf16[64,2048]{1,0:T(8,128)(2,1)S(1)}, bf16[64,2048]{1,0:T(8,128)(2,1)S(1)}, u32[]{:S(2)}, u32[]{:S(2)}) %collective-permute-start.22) | collective-permute-done | bytes 262176 | tf_op jit(solution)/shard_map/ppermute | solution.py:22
  300.3 7.7 %pre_grad.2 = (bf16[256,2048]{1,0:T(8,128)(2,1)}, bf16[512,1024]{1,0:T(8,128)(2,1)}, bf16[256,2048]{1,0:T(8,128)(2,1)}) custom-call(s32[1]{0:T(128)} %bitcast.1.sc.core, bf16[64,2048]{1,0:T(8,128)(2,1)} %copy-done.19, bf16[64,2048]{1,0:T(8,128)(2,1)} %copy-done.43, bf16[64,2048]{1,0:T(8,128)(2,1)} %copy-done.44, bf16[64,2048]{1,0:T(8,128)(2,1)} %copy-done.45, ...), custom_call_target="tpu_custom_call" | custom-call | flops 2147483648 | bytes 10485760 | tf_op jit(solution)/shard_map/pre_grad/pallas_call | solution.py:73
  308.0 5.9 %back.2 = (f32[64,2048]{1,0:T(8,128)}, bf16[64,2048]{1,0:T(8,128)(2,1)}, bf16[64,2048]{1,0:T(8,128)(2,1)}, bf16[64,2048]{1,0:T(8,128)(2,1)}) custom-call(s32[1]{0:T(128)} %bitcast.1.sc.core, bf16[256,2048]{1,0:T(8,128)(2,1)} %get-tuple-element.184.refs_0_.refs_20_, bf16[2048,2048]{1,0:T(8,128)(2,1)} %bitcast.102), custom_call_target="tpu_custom_call" | custom-call | flops 2147483648 | bytes 10485760 | tf_op jit(solution)/shard_map/back/pallas_call | solution.py:73
  313.9 6.5 %collective-permute-start.26 = (bf16[64,2048]{1,0:T(8,128)(2,1)}, bf16[64,2048]{1,0:T(8,128)(2,1)S(1)}, u32[]{:S(2)}, u32[]{:S(2)}) collective-permute-start(bf16[64,2048]{1,0:T(8,128)(2,1)} %get-tuple-element.186), channel_id=1, source_target_pairs={{0,24},{8,0},{16,8},{24,16},{1,25},{9,1},{17,9},{25,17},{2,26},{10... | collective-permute-start | bytes 786440 | tf_op jit(solution)/shard_map/ppermute | solution.py:22
  324.3 7.0 %pre_grad.3 = (bf16[256,2048]{1,0:T(8,128)(2,1)}, bf16[512,1024]{1,0:T(8,128)(2,1)}, bf16[256,2048]{1,0:T(8,128)(2,1)}) custom-call(s32[1]{0:T(128)} %bitcast.1.sc.core, bf16[64,2048]{1,0:T(8,128)(2,1)} %copy-done.18, bf16[64,2048]{1,0:T(8,128)(2,1)} %copy-done.46, bf16[64,2048]{1,0:T(8,128)(2,1)} %copy-done.47, bf16[64,2048]{1,0:T(8,128)(2,1)} %copy-done.48, ...), custom_call_target="tpu_custom_call" | custom-call | flops 2147483648 | bytes 10485760 | tf_op jit(solution)/shard_map/pre_grad/pallas_call | solution.py:73
  331.8 5.9 %back.3 = (f32[64,2048]{1,0:T(8,128)}, bf16[64,2048]{1,0:T(8,128)(2,1)}, bf16[64,2048]{1,0:T(8,128)(2,1)}, bf16[64,2048]{1,0:T(8,128)(2,1)}) custom-call(s32[1]{0:T(128)} %bitcast.1.sc.core, bf16[256,2048]{1,0:T(8,128)(2,1)} %get-tuple-element.194.refs_0_.refs_21_, bf16[2048,2048]{1,0:T(8,128)(2,1)} %bitcast.103), custom_call_target="tpu_custom_call" | custom-call | flops 2147483648 | bytes 10485760 | tf_op jit(solution)/shard_map/back/pallas_call | solution.py:73
  339.6 4.5 collective-permute-done.27
  344.1 9.4 %collective-permute-start.34 = (bf16[64,2048]{1,0:T(8,128)(2,1)}, bf16[64,2048]{1,0:T(8,128)(2,1)}, u32[]{:S(2)}, u32[]{:S(2)}) collective-permute-start(bf16[64,2048]{1,0:T(8,128)(2,1)} %get-tuple-element.198), channel_id=1, source_target_pairs={{0,8},{8,16},{16,24},{24,0},{1,9},{9,17},{17,25},{25,1},{2,10},{10... | collective-permute-start | bytes 786440 | tf_op jit(solution)/shard_map/ppermute | solution.py:22
  359.4 14.3 %feed_grads.1 = bf16[8,512,1024]{2,1,0:T(8,128)(2,1)} custom-call(s32[1]{0:T(128)} %bitcast.16.sc, bf16[512,2048]{1,0:T(8,128)(2,1)} %get-tuple-element.153.refs_0_.refs_4_.refs_8_.refs_12_.refs_16_, bf16[512,2048]{1,0:T(8,128)(2,1)} %get-tuple-element.162.refs_0_.refs_1_.refs_5_.refs_9_.refs_13_.refs_17_, bf16[512,2048]{1,0:T(8,128)(2,1)} %copy-done, ...), custom_call_target="tpu_custom_call" | custom-call | tf_op jit(solution)/shard_map/feed_grads/pallas_call | solution.py:73
  381.6 3.9 collective-permute-start.42
  385.7 5.4 collective-permute-done.39.refs_4_
  393.0 12.9 %collective-permute-done.40.refs_5_ = bf16[64,2048]{1,0:T(8,128)(2,1)S(1)} collective-permute-done((bf16[64,2048]{1,0:T(8,128)(2,1)S(1)}, bf16[64,2048]{1,0:T(8,128)(2,1)S(1)}, u32[]{:S(2)}, u32[]{:S(2)}) %collective-permute-start.40) | collective-permute-done | bytes 262176 | tf_op jit(solution)/shard_map/ppermute | solution.py:22
  407.3 5.7 mixed_grad.1
  413.0 9.0 %attend_back.1 = (bf16[512,1536]{1,0:T(8,128)(2,1)}, bf16[512,768]{1,0:T(8,128)(2,1)}) custom-call(s32[1]{0:T(128)} %bitcast.1.sc.core, s32[512,1]{1,0:T(8,128)} %copy.45.seg_col, s32[1,512]{1,0:T(1,128)} %bitcast.121, bf16[512,1536]{1,0:T(8,128)(2,1)} %get-tuple-element.133.q.k.v, bf16[512,1536]{1,0:T(8,128)(2,1)} %get-tuple-element.133.q.k.v, ...), custom_call_target="tpu_custom_call" | custom-call | flops 399999991808 | bytes 1 | tf_op jit(solution)/shard_map/attend_back/pallas_call | solution.py:73
  422.5 7.1 %last.1 = (f32[128,2048]{1,0:T(8,128)}, bf16[128,2048]{1,0:T(8,128)(2,1)}, bf16[128,2048]{1,0:T(8,128)(2,1)}, bf16[128,2048]{1,0:T(8,128)(2,1)}) custom-call(s32[1]{0:T(128)} %bitcast.1.sc.core, bf16[512,1536]{1,0:T(8,128)(2,1)} %get-tuple-element.228.refs_0_.refs_10_.refs_11_.refs_12_, bf16[2048,1536]{1,0:T(8,128)(2,1)} %bitcast.124), custom_call_target="tpu_custom_call" | custom-call | flops 3221225472 | bytes 9961472 | tf_op jit(solution)/shard_map/last/pallas_call | solution.py:73
  429.5 6.3 %collective-permute-start.43 = (bf16[128,2048]{1,0:T(8,128)(2,1)}, bf16[128,2048]{1,0:T(8,128)(2,1)S(1)}, u32[]{:S(2)}, u32[]{:S(2)}) collective-permute-start(bf16[128,2048]{1,0:T(8,128)(2,1)} %get-tuple-element.219), channel_id=1, source_target_pairs={{0,24},{8,0},{16,8},{24,16},{1,25},{9,1},{17,9},{25,17},{2,26},{10... | collective-permute-start | bytes 1572872 | tf_op jit(solution)/shard_map/ppermute | solution.py:22
  436.8 9.5 %attn_grad.1 = bf16[4,512,1024]{2,1,0:T(8,128)(2,1)} custom-call(s32[1]{0:T(128)} %bitcast.17.sc, bf16[512,2048]{1,0:T(8,128)(2,1)} %get-tuple-element.223.refs_0_.refs_1_.refs_2_.refs_3_, bf16[512,2048]{1,0:T(8,128)(2,1)} %get-tuple-element.223.refs_0_.refs_1_.refs_2_.refs_3_, bf16[512,2048]{1,0:T(8,128)(2,1)} %get-tuple-element.223.refs_0_.refs_1_.refs_2_.refs_3_, ...), custom_call_target="tpu_custom_call" | custom-call | tf_op jit(solution)/shard_map/attn_grad/pallas_call | solution.py:73
  451.2 4.8 collective-permute-start.48
  459.8 32.6 %all-to-all-done.3 = f32[32,1,768]{2,1,0:T(1,128)S(1)} async-done(((f32[32,1,768]{2,1,0:T(1,128)}), f32[32,1,768]{2,1,0:T(1,128)S(1)}, u32[]{:S(2)}, u32[]{:S(2)}) %all-to-all-start.3) | async-done | bytes 98336 | tf_op jit(solution)/shard_map/all_to_all | solution.py:466
  500.2 3.5 all-to-all-start.5
  507.6 19.6 %reduce-scatter.3.cloned.1.call-done = bf16[4,128,1024]{2,1,0:T(8,128)(2,1)} async-done(((bf16[4,512,1024]{2,1,0:T(8,128)(2,1)}), bf16[4,128,1024]{2,1,0:T(8,128)(2,1)}) %reduce-scatter.3.cloned.1.call-update) | async-done | bytes 1048592 | tf_op jit(solution)/shard_map/reduce_scatter | solution.py:325
  533.6 4.6 all-to-all-start.4
  545.0 13.9 %all-to-all-done.4.pieces_ref = bf16[4,64,1536]{2,1,0:T(8,128)(2,1)} async-done(((bf16[4,64,1536]{2,1,0:T(8,128)(2,1)}), bf16[4,64,1536]{2,1,0:T(8,128)(2,1)}, u32[]{:S(2)}, u32[]{:S(2)}) %all-to-all-start.4) | async-done | bytes 786464 | tf_op jit(solution)/shard_map/all_to_all | solution.py:316
  (357 shorter events, 115.2 us)
Async XLA Ops:
  7.2 33.4 %all-gather.5.cloned.1.call-start = ((), (), s32[]{:S(2)}) async-start(), calls=%async_computation.8 | async-start | bytes 2359296 | tf_op jit(solution)/shard_map/all_gather | solution.py:320
  7.9 90.5 %all-gather.7.cloned.1.call-start = ((), (), s32[]{:S(2)}) async-start(), calls=%async_computation.9 | async-start | bytes 7077888 | tf_op jit(solution)/shard_map/all_gather | solution.py:320
  40.6 134.3 %all-gather.9.cloned.1.call-start = ((), (), s32[]{:S(2)}) async-start(), calls=%async_computation.10 | async-start | bytes 9437184 | tf_op jit(solution)/shard_map/all_gather | solution.py:320
  42.8 37.3 %collective-permute-start.1 = (bf16[128,2048]{1,0:T(8,128)(2,1)S(1)}, bf16[128,2048]{1,0:T(8,128)(2,1)S(1)}, u32[]{:S(2)}, u32[]{:S(2)}) collective-permute-start(bf16[128,2048]{1,0:T(8,128)(2,1)S(1)} %bitcast.109), channel_id=1, source_target_pairs={{0,16},{8,24},{16,0},{24,8},{1,17},{9,25},{17,1},{25,9},{2,18},{10... | collective-permute-start | bytes 1572872 | tf_op jit(solution)/shard_map/ppermute | solution.py:22
  45.2 34.9 %collective-permute-start.2 = (bf16[128,2048]{1,0:T(8,128)(2,1)S(1)}, bf16[128,2048]{1,0:T(8,128)(2,1)S(1)}, u32[]{:S(2)}, u32[]{:S(2)}) collective-permute-start(bf16[128,2048]{1,0:T(8,128)(2,1)S(1)} %bitcast.110), channel_id=1, source_target_pairs={{0,24},{8,0},{16,8},{24,16},{1,25},{9,1},{17,9},{25,17},{2,26},{10... | collective-permute-start | bytes 1572872 | tf_op jit(solution)/shard_map/ppermute | solution.py:22
  49.0 43.9 %all-to-all-start.1 = ((bf16[32,2,384]{2,1,0:T(2,128)(2,1)}), bf16[32,2,384]{2,1,0:T(2,128)(2,1)S(1)}, u32[]{:S(2)}, u32[]{:S(2)}) async-start(bf16[32,2,384]{2,1,0:T(2,128)(2,1)} %reshape.330), calls=%async_computation.1 | async-start | bytes 98304 | tf_op jit(solution)/shard_map/all_to_all | solution.py:453
  92.9 30.7 %all-to-all-start.2 = ((bf16[4,64,2048]{2,1,0:T(8,128)(2,1)}), bf16[4,64,2048]{2,1,0:T(8,128)(2,1)S(1)}, u32[]{:S(2)}, u32[]{:S(2)}) async-start(bf16[4,64,2048]{2,1,0:T(8,128)(2,1)} %pack.3), calls=%async_computation.2 | async-start | bytes 2097152 | tf_op jit(solution)/shard_map/all_to_all | solution.py:316
  96.4 105.0 %all-gather.11.cloned.1.call-start = ((), (), s32[]{:S(2)}) async-start(), calls=%async_computation.11 | async-start | bytes 9437184 | tf_op jit(solution)/shard_map/all_gather | solution.py:320
  119.0 26.2 %collective-permute-start.4 = (bf16[64,2048]{1,0:T(8,128)(2,1)}, bf16[64,2048]{1,0:T(8,128)(2,1)S(1)}, u32[]{:S(2)}, u32[]{:S(2)}) collective-permute-start(bf16[64,2048]{1,0:T(8,128)(2,1)} %get-tuple-element.136), channel_id=1, source_target_pairs={{0,16},{8,24},{16,0},{24,8},{1,17},{9,25},{17,1},{25,9},{2,18},{10... | collective-permute-start | bytes 786440 | tf_op jit(solution)/shard_map/ppermute | solution.py:22
  119.0 26.2 %collective-permute-start.5 = (bf16[64,2048]{1,0:T(8,128)(2,1)}, bf16[64,2048]{1,0:T(8,128)(2,1)S(1)}, u32[]{:S(2)}, u32[]{:S(2)}) collective-permute-start(bf16[64,2048]{1,0:T(8,128)(2,1)} %get-tuple-element.137), channel_id=1, source_target_pairs={{0,8},{8,16},{16,24},{24,0},{1,9},{9,17},{17,25},{25,1},{2,10},{10... | collective-permute-start | bytes 786440 | tf_op jit(solution)/shard_map/ppermute | solution.py:22
  145.2 349.9 %reduce-scatter.5.cloned.1.call-start = ((), (), s32[]{:S(2)}) async-start(), calls=%async_computation.13 | async-start | bytes 10485760 | tf_op jit(solution)/shard_map/reduce_scatter | solution.py:325
  147.8 27.1 %collective-permute-start.9 = (bf16[64,2048]{1,0:T(8,128)(2,1)}, bf16[64,2048]{1,0:T(8,128)(2,1)}, u32[]{:S(2)}, u32[]{:S(2)}) collective-permute-start(bf16[64,2048]{1,0:T(8,128)(2,1)} %get-tuple-element.139), channel_id=1, source_target_pairs={{0,24},{8,0},{16,8},{24,16},{1,25},{9,1},{17,9},{25,17},{2,26},{10... | collective-permute-start | bytes 786440 | tf_op jit(solution)/shard_map/ppermute | solution.py:22
  153.4 34.0 %collective-permute-start.6 = (bf16[64,2048]{1,0:T(8,128)(2,1)S(1)}, bf16[64,2048]{1,0:T(8,128)(2,1)}, u32[]{:S(2)}, u32[]{:S(2)}) collective-permute-start(bf16[64,2048]{1,0:T(8,128)(2,1)S(1)} %get-tuple-element.147.refs_0_), channel_id=1, source_target_pairs={{0,8},{8,16},{16,24},{24,0},{1,9},{9,17},{17,25},{25,1},{2,10},{10... | collective-permute-start | bytes 786440 | tf_op jit(solution)/shard_map/ppermute | solution.py:22
  153.5 45.7 %collective-permute-start.7 = (bf16[64,2048]{1,0:T(8,128)(2,1)S(1)}, bf16[64,2048]{1,0:T(8,128)(2,1)}, u32[]{:S(2)}, u32[]{:S(2)}) collective-permute-start(bf16[64,2048]{1,0:T(8,128)(2,1)S(1)} %get-tuple-element.147.refs_0_), channel_id=1, source_target_pairs={{0,16},{8,24},{16,0},{24,8},{1,17},{9,25},{17,1},{25,9},{2,18},{10... | collective-permute-start | bytes 786440 | tf_op jit(solution)/shard_map/ppermute | solution.py:22
  167.2 31.9 %collective-permute-start.8 = (bf16[64,2048]{1,0:T(8,128)(2,1)S(1)}, bf16[64,2048]{1,0:T(8,128)(2,1)}, u32[]{:S(2)}, u32[]{:S(2)}) collective-permute-start(bf16[64,2048]{1,0:T(8,128)(2,1)S(1)} %get-tuple-element.147.refs_0_), channel_id=1, source_target_pairs={{0,24},{8,0},{16,8},{24,16},{1,25},{9,1},{17,9},{25,17},{2,26},{10... | collective-permute-start | bytes 786440 | tf_op jit(solution)/shard_map/ppermute | solution.py:22
  177.9 41.0 %collective-permute-start.15 = (bf16[64,2048]{1,0:T(8,128)(2,1)}, bf16[64,2048]{1,0:T(8,128)(2,1)}, u32[]{:S(2)}, u32[]{:S(2)}) collective-permute-start(bf16[64,2048]{1,0:T(8,128)(2,1)} %get-tuple-element.158.refs_0_), channel_id=1, source_target_pairs={{0,8},{8,16},{16,24},{24,0},{1,9},{9,17},{17,25},{25,1},{2,10},{10... | collective-permute-start | bytes 786440 | tf_op jit(solution)/shard_map/ppermute | solution.py:22
  187.4 33.2 %collective-permute-start.16 = (bf16[64,2048]{1,0:T(8,128)(2,1)}, bf16[64,2048]{1,0:T(8,128)(2,1)}, u32[]{:S(2)}, u32[]{:S(2)}) collective-permute-start(bf16[64,2048]{1,0:T(8,128)(2,1)} %get-tuple-element.158.refs_0_), channel_id=1, source_target_pairs={{0,16},{8,24},{16,0},{24,8},{1,17},{9,25},{17,1},{25,9},{2,18},{10... | collective-permute-start | bytes 786440 | tf_op jit(solution)/shard_map/ppermute | solution.py:22
  187.5 33.2 %collective-permute-start.17 = (bf16[64,2048]{1,0:T(8,128)(2,1)}, bf16[64,2048]{1,0:T(8,128)(2,1)}, u32[]{:S(2)}, u32[]{:S(2)}) collective-permute-start(bf16[64,2048]{1,0:T(8,128)(2,1)} %get-tuple-element.158.refs_0_), channel_id=1, source_target_pairs={{0,24},{8,0},{16,8},{24,16},{1,25},{9,1},{17,9},{25,17},{2,26},{10... | collective-permute-start | bytes 786440 | tf_op jit(solution)/shard_map/ppermute | solution.py:22
  209.4 90.1 %collective-permute-start.24 = (bf16[512,2048]{1,0:T(8,128)(2,1)}, bf16[512,2048]{1,0:T(8,128)(2,1)S(1)}, u32[]{:S(2)}, u32[]{:S(2)}) collective-permute-start(bf16[512,2048]{1,0:T(8,128)(2,1)} %get-tuple-element.153.refs_0_.refs_4_.refs_8_.refs_12_.refs_16_), channel_id=1, source_target_pairs={{0,1},{1,0},{2,3},{3,2},{4,5},{5,4},{6,7},{7,6},{8,9},{9,8},{10,11... | collective-permute-start | bytes 6291464 | tf_op jit(solution)/shard_map/ppermute | solution.py:329
  218.8 26.1 %collective-permute-start.13 = (bf16[64,2048]{1,0:T(8,128)(2,1)}, bf16[64,2048]{1,0:T(8,128)(2,1)S(1)}, u32[]{:S(2)}, u32[]{:S(2)}) collective-permute-start(bf16[64,2048]{1,0:T(8,128)(2,1)} %get-tuple-element.156), channel_id=1, source_target_pairs={{0,16},{8,24},{16,0},{24,8},{1,17},{9,25},{17,1},{25,9},{2,18},{10... | collective-permute-start | bytes 786440 | tf_op jit(solution)/shard_map/ppermute | solution.py:22
  220.6 24.3 %collective-permute-start.14 = (bf16[64,2048]{1,0:T(8,128)(2,1)}, bf16[64,2048]{1,0:T(8,128)(2,1)S(1)}, u32[]{:S(2)}, u32[]{:S(2)}) collective-permute-start(bf16[64,2048]{1,0:T(8,128)(2,1)} %get-tuple-element.157), channel_id=1, source_target_pairs={{0,8},{8,16},{16,24},{24,0},{1,9},{9,17},{17,25},{25,1},{2,10},{10... | collective-permute-start | bytes 786440 | tf_op jit(solution)/shard_map/ppermute | solution.py:22
  228.7 70.9 %collective-permute-start.25 = (bf16[512,2048]{1,0:T(8,128)(2,1)}, bf16[512,2048]{1,0:T(8,128)(2,1)S(1)}, u32[]{:S(2)}, u32[]{:S(2)}) collective-permute-start(bf16[512,2048]{1,0:T(8,128)(2,1)} %get-tuple-element.162.refs_0_.refs_1_.refs_5_.refs_9_.refs_13_.refs_17_), channel_id=1, source_target_pairs={{0,1},{1,0},{2,3},{3,2},{4,5},{5,4},{6,7},{7,6},{8,9},{9,8},{10,11... | collective-permute-start | bytes 6291464 | tf_op jit(solution)/shard_map/ppermute | solution.py:329
  235.2 23.8 %collective-permute-start.18 = (bf16[64,2048]{1,0:T(8,128)(2,1)}, bf16[64,2048]{1,0:T(8,128)(2,1)S(1)}, u32[]{:S(2)}, u32[]{:S(2)}) collective-permute-start(bf16[64,2048]{1,0:T(8,128)(2,1)} %get-tuple-element.164), channel_id=1, source_target_pairs={{0,24},{8,0},{16,8},{24,16},{1,25},{9,1},{17,9},{25,17},{2,26},{10... | collective-permute-start | bytes 786440 | tf_op jit(solution)/shard_map/ppermute | solution.py:22
  245.0 33.2 %collective-permute-start.19 = (bf16[64,2048]{1,0:T(8,128)(2,1)}, bf16[64,2048]{1,0:T(8,128)(2,1)S(1)}, u32[]{:S(2)}, u32[]{:S(2)}) collective-permute-start(bf16[64,2048]{1,0:T(8,128)(2,1)} %get-tuple-element.165), channel_id=1, source_target_pairs={{0,16},{8,24},{16,0},{24,8},{1,17},{9,25},{17,1},{25,9},{2,18},{10... | collective-permute-start | bytes 786440 | tf_op jit(solution)/shard_map/ppermute | solution.py:22
  245.0 33.1 %collective-permute-start.20 = (bf16[64,2048]{1,0:T(8,128)(2,1)}, bf16[64,2048]{1,0:T(8,128)(2,1)S(1)}, u32[]{:S(2)}, u32[]{:S(2)}) collective-permute-start(bf16[64,2048]{1,0:T(8,128)(2,1)} %get-tuple-element.166), channel_id=1, source_target_pairs={{0,8},{8,16},{16,24},{24,0},{1,9},{9,17},{17,25},{25,1},{2,10},{10... | collective-permute-start | bytes 786440 | tf_op jit(solution)/shard_map/ppermute | solution.py:22
  281.1 40.4 %collective-permute-start.29 = (bf16[64,2048]{1,0:T(8,128)(2,1)S(1)}, bf16[64,2048]{1,0:T(8,128)(2,1)S(1)}, u32[]{:S(2)}, u32[]{:S(2)}) collective-permute-start(bf16[64,2048]{1,0:T(8,128)(2,1)S(1)} %get-tuple-element.189.refs_0_), channel_id=1, source_target_pairs={{0,8},{8,16},{16,24},{24,0},{1,9},{9,17},{17,25},{25,1},{2,10},{10... | collective-permute-start | bytes 786440 | tf_op jit(solution)/shard_map/ppermute | solution.py:22
  299.5 24.0 %collective-permute-start.30 = (bf16[64,2048]{1,0:T(8,128)(2,1)S(1)}, bf16[64,2048]{1,0:T(8,128)(2,1)S(1)}, u32[]{:S(2)}, u32[]{:S(2)}) collective-permute-start(bf16[64,2048]{1,0:T(8,128)(2,1)S(1)} %get-tuple-element.189.refs_0_), channel_id=1, source_target_pairs={{0,16},{8,24},{16,0},{24,8},{1,17},{9,25},{17,1},{25,9},{2,18},{10... | collective-permute-start | bytes 786440 | tf_op jit(solution)/shard_map/ppermute | solution.py:22
  299.5 24.0 %collective-permute-start.31 = (bf16[64,2048]{1,0:T(8,128)(2,1)S(1)}, bf16[64,2048]{1,0:T(8,128)(2,1)S(1)}, u32[]{:S(2)}, u32[]{:S(2)}) collective-permute-start(bf16[64,2048]{1,0:T(8,128)(2,1)S(1)} %get-tuple-element.189.refs_0_), channel_id=1, source_target_pairs={{0,24},{8,0},{16,8},{24,16},{1,25},{9,1},{17,9},{25,17},{2,26},{10... | collective-permute-start | bytes 786440 | tf_op jit(solution)/shard_map/ppermute | solution.py:22
  313.9 23.8 %collective-permute-start.26 = (bf16[64,2048]{1,0:T(8,128)(2,1)}, bf16[64,2048]{1,0:T(8,128)(2,1)S(1)}, u32[]{:S(2)}, u32[]{:S(2)}) collective-permute-start(bf16[64,2048]{1,0:T(8,128)(2,1)} %get-tuple-element.186), channel_id=1, source_target_pairs={{0,24},{8,0},{16,8},{24,16},{1,25},{9,1},{17,9},{25,17},{2,26},{10... | collective-permute-start | bytes 786440 | tf_op jit(solution)/shard_map/ppermute | solution.py:22
  320.4 23.7 %collective-permute-start.27 = (bf16[64,2048]{1,0:T(8,128)(2,1)}, bf16[64,2048]{1,0:T(8,128)(2,1)S(1)}, u32[]{:S(2)}, u32[]{:S(2)}) collective-permute-start(bf16[64,2048]{1,0:T(8,128)(2,1)} %get-tuple-element.187), channel_id=1, source_target_pairs={{0,16},{8,24},{16,0},{24,8},{1,17},{9,25},{17,1},{25,9},{2,18},{10... | collective-permute-start | bytes 786440 | tf_op jit(solution)/shard_map/ppermute | solution.py:22
  331.3 24.7 %collective-permute-start.36 = (bf16[512,1024]{1,0:T(8,128)(2,1)}, bf16[512,1024]{1,0:T(8,128)(2,1)S(1)}, u32[]{:S(2)}, u32[]{:S(2)}) collective-permute-start(bf16[512,1024]{1,0:T(8,128)(2,1)} %get-tuple-element.205), channel_id=1, source_target_pairs={{0,1},{1,0},{2,3},{3,2},{4,5},{5,4},{6,7},{7,6},{8,9},{9,8},{10,11... | collective-permute-start | bytes 3145736 | tf_op jit(solution)/shard_map/ppermute | solution.py:329
  331.3 27.2 %collective-permute-start.35 = (bf16[512,1024]{1,0:T(8,128)(2,1)S(1)}, bf16[512,1024]{1,0:T(8,128)(2,1)S(1)}, u32[]{:S(2)}, u32[]{:S(2)}) collective-permute-start(bf16[512,1024]{1,0:T(8,128)(2,1)S(1)} %copy-done.68), channel_id=1, source_target_pairs={{0,1},{1,0},{2,3},{3,2},{4,5},{5,4},{6,7},{7,6},{8,9},{9,8},{10,11... | collective-permute-start | bytes 3145736 | tf_op jit(solution)/shard_map/ppermute | solution.py:329
  337.7 36.0 %collective-permute-start.32 = (bf16[64,2048]{1,0:T(8,128)(2,1)}, bf16[64,2048]{1,0:T(8,128)(2,1)S(1)}, u32[]{:S(2)}, u32[]{:S(2)}) collective-permute-start(bf16[64,2048]{1,0:T(8,128)(2,1)} %get-tuple-element.196), channel_id=1, source_target_pairs={{0,24},{8,0},{16,8},{24,16},{1,25},{9,1},{17,9},{25,17},{2,26},{10... | collective-permute-start | bytes 786440 | tf_op jit(solution)/shard_map/ppermute | solution.py:22
  344.1 33.9 %collective-permute-start.33 = (bf16[64,2048]{1,0:T(8,128)(2,1)}, bf16[64,2048]{1,0:T(8,128)(2,1)}, u32[]{:S(2)}, u32[]{:S(2)}) collective-permute-start(bf16[64,2048]{1,0:T(8,128)(2,1)} %get-tuple-element.197), channel_id=1, source_target_pairs={{0,16},{8,24},{16,0},{24,8},{1,17},{9,25},{17,1},{25,9},{2,18},{10... | collective-permute-start | bytes 786440 | tf_op jit(solution)/shard_map/ppermute | solution.py:22
  344.1 33.9 %collective-permute-start.34 = (bf16[64,2048]{1,0:T(8,128)(2,1)}, bf16[64,2048]{1,0:T(8,128)(2,1)}, u32[]{:S(2)}, u32[]{:S(2)}) collective-permute-start(bf16[64,2048]{1,0:T(8,128)(2,1)} %get-tuple-element.198), channel_id=1, source_target_pairs={{0,8},{8,16},{16,24},{24,0},{1,9},{9,17},{17,25},{25,1},{2,10},{10... | collective-permute-start | bytes 786440 | tf_op jit(solution)/shard_map/ppermute | solution.py:22
  356.0 25.6 %collective-permute-start.37 = (bf16[64,2048]{1,0:T(8,128)(2,1)S(1)}, bf16[64,2048]{1,0:T(8,128)(2,1)S(1)}, u32[]{:S(2)}, u32[]{:S(2)}) collective-permute-start(bf16[64,2048]{1,0:T(8,128)(2,1)S(1)} %get-tuple-element.260.refs_0_), channel_id=1, source_target_pairs={{0,8},{8,16},{16,24},{24,0},{1,9},{9,17},{17,25},{25,1},{2,10},{10... | collective-permute-start | bytes 786440 | tf_op jit(solution)/shard_map/ppermute | solution.py:22
  358.4 32.7 %collective-permute-start.39 = (bf16[64,2048]{1,0:T(8,128)(2,1)S(1)}, bf16[64,2048]{1,0:T(8,128)(2,1)S(1)}, u32[]{:S(2)}, u32[]{:S(2)}) collective-permute-start(bf16[64,2048]{1,0:T(8,128)(2,1)S(1)} %get-tuple-element.260.refs_0_), channel_id=1, source_target_pairs={{0,16},{8,24},{16,0},{24,8},{1,17},{9,25},{17,1},{25,9},{2,18},{10... | collective-permute-start | bytes 786440 | tf_op jit(solution)/shard_map/ppermute | solution.py:22
  381.5 24.4 %collective-permute-start.40 = (bf16[64,2048]{1,0:T(8,128)(2,1)S(1)}, bf16[64,2048]{1,0:T(8,128)(2,1)S(1)}, u32[]{:S(2)}, u32[]{:S(2)}) collective-permute-start(bf16[64,2048]{1,0:T(8,128)(2,1)S(1)} %get-tuple-element.257.refs_1_), channel_id=1, source_target_pairs={{0,16},{8,24},{16,0},{24,8},{1,17},{9,25},{17,1},{25,9},{2,18},{10... | collective-permute-start | bytes 786440 | tf_op jit(solution)/shard_map/ppermute | solution.py:22
  381.6 24.3 %collective-permute-start.42 = (bf16[64,2048]{1,0:T(8,128)(2,1)S(1)}, bf16[64,2048]{1,0:T(8,128)(2,1)S(1)}, u32[]{:S(2)}, u32[]{:S(2)}) collective-permute-start(bf16[64,2048]{1,0:T(8,128)(2,1)S(1)} %get-tuple-element.257.refs_1_), channel_id=1, source_target_pairs={{0,24},{8,0},{16,8},{24,16},{1,25},{9,1},{17,9},{25,17},{2,26},{10... | collective-permute-start | bytes 786440 | tf_op jit(solution)/shard_map/ppermute | solution.py:22
  385.5 141.8 %reduce-scatter.3.cloned.1.call-start = ((), (), s32[]{:S(2)}) async-start(), calls=%async_computation.12 | async-start | bytes 5242880 | tf_op jit(solution)/shard_map/reduce_scatter | solution.py:325
  391.1 44.7 %collective-permute-start.45 = (bf16[512,512]{1,0:T(8,128)(2,1)}, bf16[512,512]{1,0:T(8,128)(2,1)}, u32[]{:S(2)}, u32[]{:S(2)}) collective-permute-start(bf16[512,512]{1,0:T(8,128)(2,1)} %attend.1.refs_0_.refs_8_), channel_id=1, source_target_pairs={{0,1},{1,0},{2,3},{3,2},{4,5},{5,4},{6,7},{7,6},{8,9},{9,8},{10,11... | collective-permute-start | bytes 1572872 | tf_op jit(solution)/shard_map/ppermute | solution.py:329
  393.0 42.9 %collective-permute-start.44 = (bf16[512,2048]{1,0:T(8,128)(2,1)}, bf16[512,2048]{1,0:T(8,128)(2,1)}, u32[]{:S(2)}, u32[]{:S(2)}) collective-permute-start(bf16[512,2048]{1,0:T(8,128)(2,1)} %get-tuple-element.223.refs_0_.refs_1_.refs_2_.refs_3_), channel_id=1, source_target_pairs={{0,1},{1,0},{2,3},{3,2},{4,5},{5,4},{6,7},{7,6},{8,9},{9,8},{10,11... | collective-permute-start | bytes 6291464 | tf_op jit(solution)/shard_map/ppermute | solution.py:329
  413.0 22.9 %collective-permute-start.47 = (bf16[512,1024]{1,0:T(8,128)(2,1)}, bf16[512,1024]{1,0:T(8,128)(2,1)}, u32[]{:S(2)}, u32[]{:S(2)}) collective-permute-start(bf16[512,1024]{1,0:T(8,128)(2,1)} %get-tuple-element.226), channel_id=1, source_target_pairs={{0,1},{1,0},{2,3},{3,2},{4,5},{5,4},{6,7},{7,6},{8,9},{9,8},{10,11... | collective-permute-start | bytes 3145736 | tf_op jit(solution)/shard_map/ppermute | solution.py:329
  451.1 43.1 %collective-permute-start.49 = (bf16[128,2048]{1,0:T(8,128)(2,1)}, bf16[128,2048]{1,0:T(8,128)(2,1)S(1)}, u32[]{:S(2)}, u32[]{:S(2)}) collective-permute-start(bf16[128,2048]{1,0:T(8,128)(2,1)} %get-tuple-element.221), channel_id=1, source_target_pairs={{0,8},{8,16},{16,24},{24,0},{1,9},{9,17},{17,25},{25,1},{2,10},{10... | collective-permute-start | bytes 1572872 | tf_op jit(solution)/shard_map/ppermute | solution.py:22
  451.2 43.1 %collective-permute-start.48 = (bf16[128,2048]{1,0:T(8,128)(2,1)}, bf16[128,2048]{1,0:T(8,128)(2,1)S(1)}, u32[]{:S(2)}, u32[]{:S(2)}) collective-permute-start(bf16[128,2048]{1,0:T(8,128)(2,1)} %get-tuple-element.220), channel_id=1, source_target_pairs={{0,16},{8,24},{16,0},{24,8},{1,17},{9,25},{17,1},{25,9},{2,18},{10... | collective-permute-start | bytes 1572872 | tf_op jit(solution)/shard_map/ppermute | solution.py:22
  457.2 35.2 %all-to-all-start.3 = ((f32[32,1,768]{2,1,0:T(1,128)}), f32[32,1,768]{2,1,0:T(1,128)S(1)}, u32[]{:S(2)}, u32[]{:S(2)}) async-start(f32[32,1,768]{2,1,0:T(1,128)} %all_to_all.28), calls=%async_computation.3 | async-start | bytes 196608 | tf_op jit(solution)/shard_map/all_to_all | solution.py:466
  500.2 33.4 %all-to-all-start.5 = ((bf16[4,64,2048]{2,1,0:T(8,128)(2,1)}), bf16[4,64,2048]{2,1,0:T(8,128)(2,1)S(1)}, u32[]{:S(2)}, u32[]{:S(2)}) async-start(bf16[4,64,2048]{2,1,0:T(8,128)(2,1)} %pad_maximum_fusion), calls=%async_computation.7 | async-start | bytes 2097152 | tf_op jit(solution)/shard_map/all_to_all | solution.py:316
  533.6 25.3 %all-to-all-start.4 = ((bf16[4,64,1536]{2,1,0:T(8,128)(2,1)}), bf16[4,64,1536]{2,1,0:T(8,128)(2,1)}, u32[]{:S(2)}, u32[]{:S(2)}) async-start(bf16[4,64,1536]{2,1,0:T(8,128)(2,1)} %pad_maximum_fusion.1), calls=%async_computation.6 | async-start | bytes 1572864 | tf_op jit(solution)/shard_map/all_to_all | solution.py:316
  (89 other events, 1263.9 us)
Sparse Core Ops, SparseCore 0:
  9.9 30.5 all-gather.4
  42.4 46.0 all-gather.6
  90.4 54.2 all-gather.8
  147.0 54.3 all-gather.10
  385.6 85.5 reduce-scatter.4
  474.3 52.9 reduce-scatter.2
